TPU v7x, 32 devices: a whole 2x2x4 slice. The times are simulated.
32 devices in a mesh: seq: 8 (over y, x, core), fsdp: 4 (over z).
Axes of the slice: x: 2, y: 2, z: 4, core: 2. Of those that a mesh axis runs over, the one named last changes fastest.
Arguments:
- tokens: bfloat16 [4, 4096, 1600], P('fsdp', 'seq'), may hold values from -6 to 6
- ln1_gain: bfloat16 [1600], P('fsdp'), may hold values from 0.099609375 to 1.8984375
- ln1_bias: bfloat16 [1600], P('fsdp'), may hold values from -1.75 to 1.75
- qkv_weight: bfloat16 [1600, 4800], P('fsdp', 'seq'), may hold values from -0.15625 to 0.15625
- qv_bias: bfloat16 [3200], P('fsdp'), may hold values from -3 to 3
- out_weight: bfloat16 [1600, 1600], P('fsdp', 'seq'), may hold values from -2.5 to 2.5
- out_bias: bfloat16 [1600], P('fsdp'), may hold values from -1.75 to 1.75
- ln2_gain: bfloat16 [1600], P('fsdp'), may hold values from 0.099609375 to 1.8984375
- ln2_bias: bfloat16 [1600], P('fsdp'), may hold values from -1.75 to 1.75
- fc_weight: bfloat16 [1600, 6400], P('fsdp', 'seq'), may hold values from -0.15625 to 0.15625
- fc_bias: bfloat16 [6400], P('fsdp'), may hold values from -3 to 3
- proj_weight: bfloat16 [6400, 1600], P('fsdp', 'seq'), may hold values from -0.078125 to 0.078125
- proj_bias: bfloat16 [1600], P('fsdp'), may hold values from -1.75 to 1.75
- seg_lengths: int32 [4, 6], P('fsdp'), may hold values from 1 to 512, 2304 in all within a row
- parents: int32 [4, 6], P('fsdp'), may hold values from 0 to 2, as said below
- cotangent: bfloat16 [4, 4096, 1600], P('fsdp', 'seq'), may hold values from -6 to 6
Outputs:
- output: bfloat16 [4, 4096, 1600], P('fsdp', 'seq')
- input_grad: bfloat16 [4, 4096, 1600], P('fsdp', 'seq')
- ln1_gain_grad: float32 [1600], P('fsdp')
- ln1_bias_grad: float32 [1600], P('fsdp')
- qkv_weight_grad: float32 [1600, 4800], P('fsdp', 'seq')
- qv_bias_grad: float32 [3200], P('fsdp')
- out_weight_grad: float32 [1600, 1600], P('fsdp', 'seq')
- out_bias_grad: float32 [1600], P('fsdp')
- ln2_gain_grad: float32 [1600], P('fsdp')
- ln2_bias_grad: float32 [1600], P('fsdp')
- fc_weight_grad: float32 [1600, 6400], P('fsdp', 'seq')
- fc_bias_grad: float32 [6400], P('fsdp')
- proj_weight_grad: float32 [6400, 1600], P('fsdp', 'seq')
- proj_bias_grad: float32 [1600], P('fsdp')
Inputs may be any that keep to these rules, and one draw needn't show every extreme that they name: `seg_lengths`: valid tokens of each branch and leaf segment of a tree, in slot order; each row sums to 2304. `parents`: in each tree the first 2 entries are 0 (branches hang from the trunk); each of the other 4 entries names a branch segment 1 to 2, and each branch is named by exactly two of them.
All inputs are finite; a program needn't handle non-finite values.
Results may differ from a plain program's by a relative error of at most 0.018.
Values may be sent and summed in bfloat16 or wider, within the bound.
A program may use at most 448 MiB of HBM per device.

v0:
```python
import jax
import jax.numpy as jnp
from jax import lax
from jax.sharding import PartitionSpec as P

HEADS = 25


def layer_norm(values, gain, shift):
    centred = values - jnp.mean(values, -1, keepdims=True)
    spread = jnp.mean(centred * centred, -1, keepdims=True)
    return centred * lax.rsqrt(spread + 1e-05) * gain + shift


def pick_entry(table, position):
    spots = jnp.arange(table.shape[0], dtype=jnp.int32)
    return jnp.sum(jnp.where(spots == position, table, 0))


def segment_of(slot, trunk_slots):
    return jnp.where(slot < trunk_slots, 0, slot - trunk_slots + 1)


def key_mask(query_slot, key_slot, seg_len, parent_full, trunk_slots, block_rows):
    own_seg = segment_of(query_slot, trunk_slots)
    key_seg = segment_of(key_slot, trunk_slots)
    above = pick_entry(parent_full, own_seg)
    key_len = pick_entry(seg_len, key_seg)
    row_pos = jnp.arange(block_rows, dtype=jnp.int32)[:, None]
    col_pos = jnp.arange(block_rows, dtype=jnp.int32)[None, :]
    trunk_open = (key_seg == 0) & (
        key_slot * block_rows + col_pos <= query_slot * block_rows + row_pos
    )
    inside = col_pos < key_len
    other_open = (
        (key_seg == 0)
        | (key_seg == own_seg) & (col_pos <= row_pos) & inside
        | (key_seg == above) & inside
    )
    allowed = jnp.where(own_seg == 0, trunk_open, other_open)
    needed = jnp.where(
        own_seg == 0,
        key_slot <= query_slot,
        (key_seg == 0) | (key_slot == query_slot) | (key_seg == above),
    )
    return (allowed, needed)


def gather_weights(
    qkv_weight,
    out_weight,
    fc_weight,
    proj_weight,
    ln1_gain,
    ln1_bias,
    qv_bias,
    out_bias,
    ln2_gain,
    ln2_bias,
    fc_bias,
    proj_bias,
):
    widened = (
        lax.all_gather(qkv_weight, "seq", axis=1, tiled=True),
        lax.all_gather(out_weight, "seq", axis=1, tiled=True),
        lax.all_gather(fc_weight, "seq", axis=1, tiled=True),
        lax.all_gather(proj_weight, "seq", axis=1, tiled=True),
    )
    return (
        lax.all_gather(widened[0], "fsdp", axis=0, tiled=True),
        lax.all_gather(widened[1], "fsdp", axis=0, tiled=True),
        lax.all_gather(widened[2], "fsdp", axis=0, tiled=True),
        lax.all_gather(widened[3], "fsdp", axis=0, tiled=True),
        lax.all_gather(ln1_gain, "fsdp", axis=0, tiled=True),
        lax.all_gather(ln1_bias, "fsdp", axis=0, tiled=True),
        lax.all_gather(qv_bias, "fsdp", axis=0, tiled=True),
        lax.all_gather(out_bias, "fsdp", axis=0, tiled=True),
        lax.all_gather(ln2_gain, "fsdp", axis=0, tiled=True),
        lax.all_gather(ln2_bias, "fsdp", axis=0, tiled=True),
        lax.all_gather(fc_bias, "fsdp", axis=0, tiled=True),
        lax.all_gather(proj_bias, "fsdp", axis=0, tiled=True),
    )


def contract_rows(left, right):
    return lax.dot_general(
        left, right, (((0,), (0,)), ((), ())), preferred_element_type=jnp.float32
    )


def contract_cols(left, right):
    return lax.dot_general(
        left, right, (((1,), (1,)), ((), ())), preferred_element_type=jnp.float32
    )


def local(
    tokens,
    ln1_gain,
    ln1_bias,
    qkv_weight,
    qv_bias,
    out_weight,
    out_bias,
    ln2_gain,
    ln2_bias,
    fc_weight,
    fc_bias,
    proj_weight,
    proj_bias,
    seg_lengths,
    parents,
    cotangent,
):
    slot_count = lax.axis_size("seq")
    trunk_slots = slot_count // 4
    my_slot = lax.axis_index("seq")
    block_rows = tokens.shape[1]
    model_width = tokens.shape[2]
    head_count = HEADS
    head_width = model_width // head_count
    seg_len = jnp.concatenate([jnp.full((1,), trunk_slots * block_rows, jnp.int32), seg_lengths[0]])
    parent_full = jnp.concatenate([jnp.zeros((1,), jnp.int32), parents[0]])
    gathered = gather_weights(
        qkv_weight,
        out_weight,
        fc_weight,
        proj_weight,
        ln1_gain,
        ln1_bias,
        qv_bias,
        out_bias,
        ln2_gain,
        ln2_bias,
        fc_bias,
        proj_bias,
    )
    (
        qkv_full,
        out_full,
        fc_full,
        proj_full,
        gain_one,
        shift_one,
        bias_qv,
        bias_out,
        gain_two,
        shift_two,
        bias_fc,
        bias_proj,
    ) = gathered
    gain_one = gain_one.astype(jnp.float32)
    shift_one = shift_one.astype(jnp.float32)
    gain_two = gain_two.astype(jnp.float32)
    shift_two = shift_two.astype(jnp.float32)
    resid = tokens[0].astype(jnp.float32)
    normed_one = layer_norm(resid, gain_one, shift_one).astype(jnp.bfloat16)
    bias_three = jnp.concatenate(
        [bias_qv[:model_width], jnp.zeros((model_width,), jnp.bfloat16), bias_qv[model_width:]]
    ).astype(jnp.float32)
    projected = (
        jnp.dot(normed_one, qkv_full, preferred_element_type=jnp.float32) + bias_three
    ).astype(jnp.bfloat16)
    queries = projected[:, :model_width].reshape(block_rows, head_count, head_width)
    keys_mine = projected[:, model_width : 2 * model_width]
    values_mine = projected[:, 2 * model_width :]
    key_heads_mine = keys_mine.reshape(block_rows, head_count, head_width)
    value_heads_mine = values_mine.reshape(block_rows, head_count, head_width)
    start_state = (
        jnp.zeros((block_rows, head_count, head_width), jnp.float32),
        jnp.zeros((head_count, block_rows), jnp.float32),
    )
    key_piece = lax.all_gather(keys_mine, "seq", axis=0, tiled=True)
    value_piece = lax.all_gather(values_mine, "seq", axis=0, tiled=True)
    count = key_piece.shape[0] // block_rows

    def forward_one_block(inner_block, state):
        allowed, needed = key_mask(
            my_slot, inner_block, seg_len, parent_full, trunk_slots, block_rows
        )

        def forward_compute(inner_state):
            numerator, totals = inner_state
            key_rows = lax.dynamic_slice_in_dim(key_piece, inner_block * block_rows, block_rows, 0)
            value_rows = lax.dynamic_slice_in_dim(
                value_piece, inner_block * block_rows, block_rows, 0
            )
            key_heads = key_rows.reshape(block_rows, head_count, head_width)
            value_heads = value_rows.reshape(block_rows, head_count, head_width)
            scores = (
                jnp.einsum("qhd,khd->hqk", queries, key_heads, preferred_element_type=jnp.float32)
                * 0.125
            )
            weights_e = jnp.where(allowed[None], jnp.exp(scores), 0.0)
            numerator = numerator + jnp.einsum(
                "hqk,khd->qhd",
                weights_e.astype(jnp.bfloat16),
                value_heads,
                preferred_element_type=jnp.float32,
            )
            totals = totals + jnp.sum(weights_e, -1)
            return (numerator, totals)

        return lax.cond(needed, forward_compute, lambda inner_state: inner_state, state)

    numerator, totals = lax.fori_loop(0, count, forward_one_block, start_state)
    totals_rows = totals.T[:, :, None]
    attended = numerator / totals_rows
    attended_low = attended.reshape(block_rows, model_width).astype(jnp.bfloat16)
    middle = (
        resid
        + jnp.dot(attended_low, out_full, preferred_element_type=jnp.float32)
        + bias_out.astype(jnp.float32)
    )
    normed_two = layer_norm(middle, gain_two, shift_two).astype(jnp.bfloat16)
    hidden_pre = jnp.dot(normed_two, fc_full, preferred_element_type=jnp.float32) + bias_fc.astype(
        jnp.float32
    )
    hidden_act = jax.nn.gelu(hidden_pre, approximate=True).astype(jnp.bfloat16)
    result = (
        middle
        + jnp.dot(hidden_act, proj_full, preferred_element_type=jnp.float32)
        + bias_proj.astype(jnp.float32)
    )
    output = result.astype(jnp.bfloat16)[None]
    regathered = gather_weights(
        qkv_weight,
        out_weight,
        fc_weight,
        proj_weight,
        ln1_gain,
        ln1_bias,
        qv_bias,
        out_bias,
        ln2_gain,
        ln2_bias,
        fc_bias,
        proj_bias,
    )
    qkv_full, out_full, fc_full, proj_full = (
        regathered[0],
        regathered[1],
        regathered[2],
        regathered[3],
    )
    upstream = cotangent[0]
    upstream_f = upstream.astype(jnp.float32)
    grad_proj = contract_rows(hidden_act, upstream)
    grad_proj_bias = jnp.sum(upstream_f, 0)
    grad_act = contract_cols(upstream, proj_full)
    unused_value, gelu_back = jax.vjp(
        lambda inner: jax.nn.gelu(inner, approximate=True), hidden_pre
    )
    grad_pre = gelu_back(grad_act)[0].astype(jnp.bfloat16)
    grad_fc = contract_rows(normed_two, grad_pre)
    grad_fc_bias = jnp.sum(grad_pre.astype(jnp.float32), 0)
    grad_normed_two = contract_cols(grad_pre, fc_full)
    unused_norm, norm_two_back = jax.vjp(layer_norm, middle, gain_two, shift_two)
    grad_middle_norm, grad_gain_two, grad_shift_two = norm_two_back(grad_normed_two)
    grad_middle = upstream_f + grad_middle_norm
    grad_branch = grad_middle.astype(jnp.bfloat16)
    grad_out = contract_rows(attended_low, grad_branch)
    grad_out_bias = jnp.sum(grad_branch.astype(jnp.float32), 0)
    grad_attended = contract_cols(grad_branch, out_full).reshape(block_rows, head_count, head_width)
    delta_term = (jnp.sum(grad_attended * attended, -1) / totals.T).T
    grad_summed = (grad_attended / totals_rows).astype(jnp.bfloat16)
    query_key_piece = lax.all_gather(keys_mine, "seq", axis=0, tiled=True)
    query_value_piece = lax.all_gather(values_mine, "seq", axis=0, tiled=True)
    count = query_key_piece.shape[0] // block_rows

    def query_one_block(inner_block, grad_query):
        allowed, needed = key_mask(
            my_slot, inner_block, seg_len, parent_full, trunk_slots, block_rows
        )

        def query_compute(inner_grad):
            key_rows = lax.dynamic_slice_in_dim(
                query_key_piece, inner_block * block_rows, block_rows, 0
            )
            value_rows = lax.dynamic_slice_in_dim(
                query_value_piece, inner_block * block_rows, block_rows, 0
            )
            key_heads = key_rows.reshape(block_rows, head_count, head_width)
            value_heads = value_rows.reshape(block_rows, head_count, head_width)
            scores = (
                jnp.einsum("qhd,khd->hqk", queries, key_heads, preferred_element_type=jnp.float32)
                * 0.125
            )
            weights_e = jnp.where(allowed[None], jnp.exp(scores), 0.0)
            grad_weights = jnp.einsum(
                "qhd,khd->hqk", grad_summed, value_heads, preferred_element_type=jnp.float32
            )
            grad_scores = (0.125 * weights_e * (grad_weights - delta_term[:, :, None])).astype(
                jnp.bfloat16
            )
            return inner_grad + jnp.einsum(
                "hqk,khd->qhd", grad_scores, key_heads, preferred_element_type=jnp.float32
            )

        return lax.cond(needed, query_compute, lambda inner_grad: inner_grad, grad_query)

    grad_query = lax.fori_loop(
        0, count, query_one_block, jnp.zeros((block_rows, head_count, head_width), jnp.float32)
    )
    key_state = (
        jnp.zeros((block_rows, head_count, head_width), jnp.float32),
        jnp.zeros((block_rows, head_count, head_width), jnp.float32),
    )
    query_send = queries.reshape(block_rows, model_width).astype(jnp.float32)
    dsum_send = grad_summed.reshape(block_rows, model_width).astype(jnp.float32)
    delta_send = delta_term.T
    query_piece = lax.all_gather(query_send.astype(jnp.bfloat16), "seq", axis=0, tiled=True).astype(
        jnp.float32
    )
    dsum_piece = lax.all_gather(dsum_send.astype(jnp.bfloat16), "seq", axis=0, tiled=True).astype(
        jnp.float32
    )
    delta_piece = lax.all_gather(delta_send.astype(jnp.bfloat16), "seq", axis=0, tiled=True).astype(
        jnp.float32
    )
    count = query_piece.shape[0] // block_rows

    def key_one_block(inner_block, state):
        allowed, needed = key_mask(
            inner_block, my_slot, seg_len, parent_full, trunk_slots, block_rows
        )

        def key_compute(inner_state):
            key_acc, value_acc = inner_state
            query_rows = lax.dynamic_slice_in_dim(
                query_piece, inner_block * block_rows, block_rows, 0
            )
            dsum_rows = lax.dynamic_slice_in_dim(
                dsum_piece, inner_block * block_rows, block_rows, 0
            )
            delta_rows = lax.dynamic_slice_in_dim(
                delta_piece, inner_block * block_rows, block_rows, 0
            )
            query_heads = query_rows.astype(jnp.bfloat16).reshape(
                block_rows, head_count, head_width
            )
            dsum_heads = dsum_rows.astype(jnp.bfloat16).reshape(block_rows, head_count, head_width)
            scores = (
                jnp.einsum(
                    "qhd,khd->hqk", query_heads, key_heads_mine, preferred_element_type=jnp.float32
                )
                * 0.125
            )
            weights_e = jnp.where(allowed[None], jnp.exp(scores), 0.0)
            grad_weights = jnp.einsum(
                "qhd,khd->hqk", dsum_heads, value_heads_mine, preferred_element_type=jnp.float32
            )
            grad_scores = (0.125 * weights_e * (grad_weights - delta_rows.T[:, :, None])).astype(
                jnp.bfloat16
            )
            key_acc = key_acc + jnp.einsum(
                "hqk,qhd->khd", grad_scores, query_heads, preferred_element_type=jnp.float32
            )
            value_acc = value_acc + jnp.einsum(
                "hqk,qhd->khd",
                weights_e.astype(jnp.bfloat16),
                dsum_heads,
                preferred_element_type=jnp.float32,
            )
            return (key_acc, value_acc)

        return lax.cond(needed, key_compute, lambda inner_state: inner_state, state)

    key_acc, value_acc = lax.fori_loop(0, count, key_one_block, key_state)
    grad_projected = jnp.concatenate(
        [
            grad_query.reshape(block_rows, model_width),
            key_acc.reshape(block_rows, model_width),
            value_acc.reshape(block_rows, model_width),
        ],
        1,
    ).astype(jnp.bfloat16)
    grad_qkv = contract_rows(normed_one, grad_projected)
    column_sums = jnp.sum(grad_projected.astype(jnp.float32), 0)
    grad_qv = jnp.concatenate([column_sums[:model_width], column_sums[2 * model_width :]])
    grad_normed_one = contract_cols(grad_projected, qkv_full)
    unused_first, norm_one_back = jax.vjp(layer_norm, resid, gain_one, shift_one)
    grad_resid_norm, grad_gain_one, grad_shift_one = norm_one_back(grad_normed_one)
    input_grad = (grad_middle + grad_resid_norm).astype(jnp.bfloat16)[None]
    column_parts = (
        lax.psum_scatter(
            grad_qkv.astype(jnp.bfloat16), "seq", scatter_dimension=1, tiled=True
        ).astype(jnp.float32),
        lax.psum_scatter(
            grad_out.astype(jnp.bfloat16), "seq", scatter_dimension=1, tiled=True
        ).astype(jnp.float32),
        lax.psum_scatter(
            grad_fc.astype(jnp.bfloat16), "seq", scatter_dimension=1, tiled=True
        ).astype(jnp.float32),
        lax.psum_scatter(
            grad_proj.astype(jnp.bfloat16), "seq", scatter_dimension=1, tiled=True
        ).astype(jnp.float32),
    )
    vector_whole = (
        lax.psum(grad_gain_one.astype(jnp.bfloat16), "seq").astype(jnp.float32),
        lax.psum(grad_shift_one.astype(jnp.bfloat16), "seq").astype(jnp.float32),
        lax.psum(grad_qv.astype(jnp.bfloat16), "seq").astype(jnp.float32),
        lax.psum(grad_out_bias.astype(jnp.bfloat16), "seq").astype(jnp.float32),
        lax.psum(grad_gain_two.astype(jnp.bfloat16), "seq").astype(jnp.float32),
        lax.psum(grad_shift_two.astype(jnp.bfloat16), "seq").astype(jnp.float32),
        lax.psum(grad_fc_bias.astype(jnp.bfloat16), "seq").astype(jnp.float32),
        lax.psum(grad_proj_bias.astype(jnp.bfloat16), "seq").astype(jnp.float32),
    )
    both_parts = (
        lax.psum_scatter(
            column_parts[0].astype(jnp.bfloat16), "fsdp", scatter_dimension=0, tiled=True
        ).astype(jnp.float32),
        lax.psum_scatter(
            column_parts[1].astype(jnp.bfloat16), "fsdp", scatter_dimension=0, tiled=True
        ).astype(jnp.float32),
        lax.psum_scatter(
            column_parts[2].astype(jnp.bfloat16), "fsdp", scatter_dimension=0, tiled=True
        ).astype(jnp.float32),
        lax.psum_scatter(
            column_parts[3].astype(jnp.bfloat16), "fsdp", scatter_dimension=0, tiled=True
        ).astype(jnp.float32),
        lax.psum_scatter(
            vector_whole[0].astype(jnp.bfloat16), "fsdp", scatter_dimension=0, tiled=True
        ).astype(jnp.float32),
        lax.psum_scatter(
            vector_whole[1].astype(jnp.bfloat16), "fsdp", scatter_dimension=0, tiled=True
        ).astype(jnp.float32),
        lax.psum_scatter(
            vector_whole[2].astype(jnp.bfloat16), "fsdp", scatter_dimension=0, tiled=True
        ).astype(jnp.float32),
        lax.psum_scatter(
            vector_whole[3].astype(jnp.bfloat16), "fsdp", scatter_dimension=0, tiled=True
        ).astype(jnp.float32),
        lax.psum_scatter(
            vector_whole[4].astype(jnp.bfloat16), "fsdp", scatter_dimension=0, tiled=True
        ).astype(jnp.float32),
        lax.psum_scatter(
            vector_whole[5].astype(jnp.bfloat16), "fsdp", scatter_dimension=0, tiled=True
        ).astype(jnp.float32),
        lax.psum_scatter(
            vector_whole[6].astype(jnp.bfloat16), "fsdp", scatter_dimension=0, tiled=True
        ).astype(jnp.float32),
        lax.psum_scatter(
            vector_whole[7].astype(jnp.bfloat16), "fsdp", scatter_dimension=0, tiled=True
        ).astype(jnp.float32),
    )
    matrix_parts = both_parts[:4]
    vector_parts = both_parts[4:]
    return (
        output,
        input_grad,
        vector_parts[0],
        vector_parts[1],
        matrix_parts[0],
        vector_parts[2],
        matrix_parts[1],
        vector_parts[3],
        vector_parts[4],
        vector_parts[5],
        matrix_parts[2],
        vector_parts[6],
        matrix_parts[3],
        vector_parts[7],
    )


def solution(mesh):
    in_specs = (
        P("fsdp", "seq", None),
        P("fsdp"),
        P("fsdp"),
        P("fsdp", "seq"),
        P("fsdp"),
        P("fsdp", "seq"),
        P("fsdp"),
        P("fsdp"),
        P("fsdp"),
        P("fsdp", "seq"),
        P("fsdp"),
        P("fsdp", "seq"),
        P("fsdp"),
        P("fsdp", None),
        P("fsdp", None),
        P("fsdp", "seq", None),
    )
    out_specs = (
        P("fsdp", "seq", None),
        P("fsdp", "seq", None),
        P("fsdp"),
        P("fsdp"),
        P("fsdp", "seq"),
        P("fsdp"),
        P("fsdp", "seq"),
        P("fsdp"),
        P("fsdp"),
        P("fsdp"),
        P("fsdp", "seq"),
        P("fsdp"),
        P("fsdp", "seq"),
        P("fsdp"),
    )
    return jax.shard_map(local, mesh=mesh, in_specs=in_specs, out_specs=out_specs, check_vma=False)
```

profile of v0, /device:TPU:3, one launch (start us, length us, event | category | flops | bytes accessed | tf_op | source)
XLA Modules:
  0.0 2572.9 jit_solution(10772226682592462577)
XLA Ops:
  8.0 39.9 %all-gather.35.cloned.1.call-done = bf16[8,600,400]{1,2,0:T(8,128)(2,1)} async-done(((bf16[1,600,400]{1,2,0:T(8,128)(2,1)}), bf16[8,600,400]{1,2,0:T(8,128)(2,1)}) %all-gather.35.cloned.1.call-update) | async-done | bytes 3840016 | tf_op jit(solution)/shard_map/all_gather | solution.py:64
  67.9 30.8 %all-reduce.21 = (bf16[1600]{0:T(1024)(128)(2,1)S(1)}, bf16[1600]{0:T(1024)(128)(2,1)S(1)}, bf16[3200]{0:T(1024)(128)(2,1)S(1)}, bf16[6400]{0:T(1024)(128)(2,1)S...) all-reduce(bf16[1600]{0:T(1024)(128)(2,1)S(1)} %dynamic-update-slic, ...), channel_id=1, replica_groups=mesh['seq'=8,'fsdp'=4] {'fsdp'}, use_global_device_ids=true, to_apply=%add.1 | all-reduce | flops 17600 | bytes 70400
  100.4 228.3 %all-gather.15.cloned.1.call-done = bf16[1600,4800]{1,0:T(8,128)(2,1)} async-done(((bf16[400,4800]{1,0:T(8,128)(2,1)}), bf16[1600,4800]{1,0:T(8,128)(2,1)}) %all-gather.15.cloned.1.call-update) | async-done | bytes 15360016 | tf_op jit(solution)/shard_map/all_gather | solution.py:70
  328.7 14.5 add_convert_fusion
  359.4 41.2 %all-gather.37.cloned.1.call-done = bf16[8,800,400]{1,2,0:T(8,128)(2,1)} async-done(((bf16[1,800,400]{1,2,0:T(8,128)(2,1)}), bf16[8,800,400]{1,2,0:T(8,128)(2,1)}) %all-gather.37.cloned.1.call-update) | async-done | bytes 5120016 | tf_op jit(solution)/shard_map/all_gather | solution.py:66
  417.0 26.7 %all-gather.27.cloned.1.call-done = bf16[1600,1600]{0,1:T(8,128)(2,1)} async-done(((bf16[1600,200]{0,1:T(8,128)(2,1)}), bf16[1600,1600]{0,1:T(8,128)(2,1)}) %all-gather.27.cloned.1.call-update) | async-done | bytes 5120016 | tf_op jit(solution)/shard_map/all_gather | solution.py:67
  456.3 66.0 %all-gather.17.cloned.1.call-done = bf16[4096,1600]{0,1:T(8,128)(2,1)} async-done(((bf16[512,1600]{0,1:T(8,128)(2,1)}), bf16[4096,1600]{0,1:T(8,128)(2,1)}) %all-gather.17.cloned.1.call-update) | async-done | bytes 13107216 | tf_op jit(solution)/shard_map/all_gather | solution.py:174
  522.4 79.3 %all-gather.19.cloned.1.call-done = bf16[4096,1600]{0,1:T(8,128)(2,1)} async-done(((bf16[512,1600]{0,1:T(8,128)(2,1)}), bf16[4096,1600]{0,1:T(8,128)(2,1)}) %all-gather.19.cloned.1.call-update) | async-done | bytes 13107216 | tf_op jit(solution)/shard_map/all_gather | solution.py:173
  602.1 130.2 %while.61 = (s32[]{:T(128)}, f32[512,25,64]{0,2,1:T(8,128)S(1)}, f32[25,512]{1,0:T(8,128)S(1)}, s32[]{:T(128)}, s32[]{:T(128)}, /*index=5*/s32[7]{0:T(128)}, pre...) while((s32[]{:T(128)}, f32[512,25,64]{0,2,1:T(8,128)S(1)}, ...), condition=%wide.region_8.9_spmd, body=%wide.region_2.8_spmd.sunk | while | flops 1719961600 | bytes 82211536 | solution.py:206
  606.3 32.3 %conditional.6 = ((f32[512,25,64]{0,2,1:T(8,128)S(1)}, f32[25,512]{1,0:T(8,128)S(1)})) conditional(s32[]{:T(128)} %convert_element_type.399, (f32[512,25,64]{0,2,1:T(8,128)S(1)}, f32[25,512]{1,0:T(8,128)S(1)}) %tuple.238, (s32[]{:T(128)}, bf16[4096,1600]{0,1:T(8,128)(2,1)}, pred[]{:T(512)}, pred[]{:T(512)}, s32[1,512]{1,0:T(1,128)S(1)}, ...), branch_computations={%region_4.4_spmd, %region_5.7_spmd} | conditional | flops 1719961600 | bytes 80109784 | solution.py:204
  642.7 31.8 %conditional.6 = ((f32[512,25,64]{0,2,1:T(8,128)S(1)}, f32[25,512]{1,0:T(8,128)S(1)})) conditional(s32[]{:T(128)} %convert_element_type.399, (f32[512,25,64]{0,2,1:T(8,128)S(1)}, f32[25,512]{1,0:T(8,128)S(1)}) %tuple.238, (s32[]{:T(128)}, bf16[4096,1600]{0,1:T(8,128)(2,1)}, pred[]{:T(512)}, pred[]{:T(512)}, s32[1,512]{1,0:T(1,128)S(1)}, ...), branch_computations={%region_4.4_spmd, %region_5.7_spmd} | conditional | flops 1719961600 | bytes 80109784 | solution.py:204
  682.8 32.9 %conditional.6 = ((f32[512,25,64]{0,2,1:T(8,128)S(1)}, f32[25,512]{1,0:T(8,128)S(1)})) conditional(s32[]{:T(128)} %convert_element_type.399, (f32[512,25,64]{0,2,1:T(8,128)S(1)}, f32[25,512]{1,0:T(8,128)S(1)}) %tuple.238, (s32[]{:T(128)}, bf16[4096,1600]{0,1:T(8,128)(2,1)}, pred[]{:T(512)}, pred[]{:T(512)}, s32[1,512]{1,0:T(1,128)S(1)}, ...), branch_computations={%region_4.4_spmd, %region_5.7_spmd} | conditional | flops 1719961600 | bytes 80109784 | solution.py:204
  743.2 308.5 %all-gather.25.cloned.1.call-done = bf16[1600,6400]{1,0:T(8,128)(2,1)} async-done(((bf16[400,6400]{1,0:T(8,128)(2,1)}), bf16[1600,6400]{1,0:T(8,128)(2,1)}) %all-gather.25.cloned.1.call-update) | async-done | bytes 20480016 | tf_op jit(solution)/shard_map/all_gather | solution.py:72
  1051.7 21.3 convolution_add_fusion
  1073.0 341.0 %all-gather.29.cloned.1.call-done = bf16[6400,1600]{1,0:T(8,128)(2,1)} async-done(((bf16[1600,1600]{1,0:T(8,128)(2,1)}), bf16[6400,1600]{1,0:T(8,128)(2,1)}) %all-gather.29.cloned.1.call-update) | async-done | bytes 20480016 | tf_op jit(solution)/shard_map/all_gather | solution.py:73
  1414.0 25.1 fusion.82
  1439.1 21.2 multiply_reduce_fusion
  1480.4 19.3 convolution_convert_fusion.1
  1499.8 34.6 %reduce-scatter.36.cloned.1.call-done = bf16[1600,200]{0,1:T(8,128)(2,1)} async-done(((bf16[1600,1600]{0,1:T(8,128)(2,1)}), bf16[1600,200]{0,1:T(8,128)(2,1)}) %reduce-scatter.36.cloned.1.call-update) | async-done | bytes 640016
  1536.7 19.2 convolution_convert_fusion
  1562.1 143.0 %while.62 = (s32[]{:T(128)}, f32[512,25,64]{0,2,1:T(8,128)}, s32[]{:T(128)}, s32[]{:T(128)}, s32[7]{0:T(128)}, /*index=5*/pred[]{:T(512)}, bf16[4096,1600]{0,1:T...) while((s32[]{:T(128)}, f32[512,25,64]{0,2,1:T(8,128)}, ...), condition=%wide.region_19.20_spmd, body=%wide.region_14.19_spmd.sunk | while | flops 2558822400 | bytes 85072576 | solution.py:302
  1565.7 40.1 %conditional.7 = (f32[512,25,64]{0,2,1:T(8,128)}) conditional(s32[]{:T(128)} %convert_element_type.400, f32[512,25,64]{0,2,1:T(8,128)} %get-tuple-element.2478, (s32[]{:T(128)}, bf16[4096,1600]{0,1:T(8,128)(2,1)}, pred[]{:T(512)}, pred[]{:T(512)}, s32[1,512]{1,0:T(1,128)S(1)}, /*index=5*/s32[]{:T(128)}, s32[512,1]{0,1:T(1,128)S(1)}, s32[]{:T(128)}, ...), branch_computations={%region_16.16_spmd, %region_17.18_spmd} | conditional | flops 2558822400 | bytes 82970824 | solution.py:300
  1584.7 21.1 bitcast_add_fusion.1
  1608.9 39.3 %conditional.7 = (f32[512,25,64]{0,2,1:T(8,128)}) conditional(s32[]{:T(128)} %convert_element_type.400, f32[512,25,64]{0,2,1:T(8,128)} %get-tuple-element.2478, (s32[]{:T(128)}, bf16[4096,1600]{0,1:T(8,128)(2,1)}, pred[]{:T(512)}, pred[]{:T(512)}, s32[1,512]{1,0:T(1,128)S(1)}, /*index=5*/s32[]{:T(128)}, s32[512,1]{0,1:T(1,128)S(1)}, s32[]{:T(128)}, ...), branch_computations={%region_16.16_spmd, %region_17.18_spmd} | conditional | flops 2558822400 | bytes 82970824 | solution.py:300
  1627.0 21.2 bitcast_add_fusion.1
  1654.5 38.1 %conditional.7 = (f32[512,25,64]{0,2,1:T(8,128)}) conditional(s32[]{:T(128)} %convert_element_type.400, f32[512,25,64]{0,2,1:T(8,128)} %get-tuple-element.2478, (s32[]{:T(128)}, bf16[4096,1600]{0,1:T(8,128)(2,1)}, pred[]{:T(512)}, pred[]{:T(512)}, s32[1,512]{1,0:T(1,128)S(1)}, /*index=5*/s32[]{:T(128)}, s32[512,1]{0,1:T(1,128)S(1)}, s32[]{:T(128)}, ...), branch_computations={%region_16.16_spmd, %region_17.18_spmd} | conditional | flops 2558822400 | bytes 82970824 | solution.py:300
  1671.7 20.9 bitcast_add_fusion.1
  1709.1 57.1 %all_gather.93 = bf16[4096,25]{0,1:T(8,128)(2,1)S(1)} all-gather(bf16[512,25]{0,1:T(8,128)(2,1)S(1)} %divide_convert_fusion.1), channel_id=1, replica_groups=mesh['seq'=8,'fsdp'=4] {'seq'}, dimensions={0}, use_global_device_ids=true | all-gather | bytes 230400 | tf_op jit(solution)/shard_map/all_gather | solution.py:318
  1771.3 192.3 %while.63 = (s32[]{:T(128)}, f32[512,25,64]{0,2,1:T(8,128)}, f32[512,25,64]{0,2,1:T(8,128)}, s32[]{:T(128)}, pred[]{:T(512)}, /*index=5*/s32[7]{0:T(128)}, s32[]...) while((s32[]{:T(128)}, f32[512,25,64]{0,2,1:T(8,128)}, ...), condition=%wide.region_25.26_spmd, body=%wide.region_20.25_spmd.sunk | while | flops 3418163200 | bytes 119843576 | solution.py:369
  1787.8 51.7 %conditional.8 = ((f32[512,25,64]{0,2,1:T(8,128)}, f32[512,25,64]{0,2,1:T(8,128)})) conditional(s32[]{:T(128)} %convert_element_type.401, (f32[512,25,64]{0,2,1:T(8,128)}, f32[512,25,64]{0,2,1:T(8,128)}) %tuple.243, (s32[]{:T(128)}, bf16[4096,1600]{0,1:T(8,128)(2,1)}, pred[]{:T(512)}, pred[]{:T(512)}, s32[]{:T(128)}, ...), branch_computations={%region_22.22_spmd, %region_23.24_spmd} | conditional | flops 3418163200 | bytes 117741792 | solution.py:367
  1806.7 18.5 bitcast_add_fusion.3
  1825.2 14.3 bitcast_add_fusion.2
  1847.7 52.6 %conditional.8 = ((f32[512,25,64]{0,2,1:T(8,128)}, f32[512,25,64]{0,2,1:T(8,128)})) conditional(s32[]{:T(128)} %convert_element_type.401, (f32[512,25,64]{0,2,1:T(8,128)}, f32[512,25,64]{0,2,1:T(8,128)}) %tuple.243, (s32[]{:T(128)}, bf16[4096,1600]{0,1:T(8,128)(2,1)}, pred[]{:T(512)}, pred[]{:T(512)}, s32[]{:T(128)}, ...), branch_computations={%region_22.22_spmd, %region_23.24_spmd} | conditional | flops 3418163200 | bytes 117741792 | solution.py:367
  1866.1 17.7 bitcast_add_fusion.3
  1883.8 16.5 bitcast_add_fusion.2
  1904.4 55.1 %conditional.8 = ((f32[512,25,64]{0,2,1:T(8,128)}, f32[512,25,64]{0,2,1:T(8,128)})) conditional(s32[]{:T(128)} %convert_element_type.401, (f32[512,25,64]{0,2,1:T(8,128)}, f32[512,25,64]{0,2,1:T(8,128)}) %tuple.243, (s32[]{:T(128)}, bf16[4096,1600]{0,1:T(8,128)(2,1)}, pred[]{:T(512)}, pred[]{:T(512)}, s32[]{:T(128)}, ...), branch_computations={%region_22.22_spmd, %region_23.24_spmd} | conditional | flops 3418163200 | bytes 117741792 | solution.py:367
  1926.3 18.3 bitcast_add_fusion.3
  1944.5 14.9 bitcast_add_fusion.2
  1970.6 16.0 convolution_convert_fusion.2
  1999.9 44.3 %reduce-scatter.38.cloned.1.call-done = bf16[6400,200]{0,1:T(8,128)(2,1)} async-done(((bf16[6400,1600]{0,1:T(8,128)(2,1)}), bf16[6400,200]{0,1:T(8,128)(2,1)}) %reduce-scatter.38.cloned.1.call-update) | async-done | bytes 2560016
  2048.9 18.7 fusion.73
  2069.4 16.0 all-reduce.20
  2086.0 229.7 %all-reduce.19 = (bf16[400]{0:T(512)(128)(2,1)S(1)}, bf16[400]{0:T(512)(128)(2,1)S(1)}, bf16[800]{0:T(1024)(128)(2,1)S(1)}, bf16[400]{0:T(512)(128)(2,1)S(1)}, b...) all-reduce(bf16[400]{0:T(512)(128)(2,1)S(1)} %dynamic-slice.9, ...), channel_id=1, replica_groups=mesh['seq'=8,'fsdp'=4] {'seq'}, use_global_device_ids=true, to_apply=%region_29.30 | all-reduce | flops 4800 | bytes 19200 | tf_op jit(solution)/shard_map/psum | solution.py:400
  2325.1 69.8 %reduce-scatter.34.cloned.1.call-done = bf16[1600,600]{0,1:T(8,128)(2,1)} async-done(((bf16[1600,4800]{0,1:T(8,128)(2,1)}), bf16[1600,600]{0,1:T(8,128)(2,1)}) %reduce-scatter.34.cloned.1.call-update) | async-done | bytes 1920016
  2398.9 18.6 fusion.57
  2417.5 35.5 %reduce-scatter.30.cloned.1.call-done = bf16[400,800]{1,0:T(8,128)(2,1)} async-done(((bf16[1600,800]{1,0:T(8,128)(2,1)}), bf16[400,800]{1,0:T(8,128)(2,1)}) %reduce-scatter.30.cloned.1.call-update) | async-done | bytes 640016
  2455.9 61.8 %reduce-scatter.32.cloned.1.call-done = bf16[1600,200]{1,0:T(8,128)(2,1)} async-done(((bf16[6400,200]{1,0:T(8,128)(2,1)}), bf16[1600,200]{1,0:T(8,128)(2,1)}) %reduce-scatter.32.cloned.1.call-update) | async-done | bytes 640016
  2520.3 42.8 %reduce-scatter.26.cloned.1.call-done = bf16[400,600]{1,0:T(8,128)(2,1)} async-done(((bf16[1600,600]{1,0:T(8,128)(2,1)}), bf16[400,600]{1,0:T(8,128)(2,1)}) %reduce-scatter.26.cloned.1.call-update) | async-done | bytes 480016
  (517 shorter events, 444.5 us)
Async XLA Ops:
  7.2 40.7 %all-gather.35.cloned.1.call-start = ((), (), s32[]{:S(2)}) async-start(), calls=%async_computation.19 | async-start | bytes 4608000 | tf_op jit(solution)/shard_map/all_gather | solution.py:64
  7.9 320.8 %all-gather.15.cloned.1.call-start = ((), (), s32[]{:S(2)}) async-start(), calls=%async_computation.8 | async-start | bytes 19456000 | tf_op jit(solution)/shard_map/all_gather | solution.py:70
  60.6 5.5 copy-start.44
  60.6 5.8 copy-start.45
  60.6 6.0 copy-start.46
  60.6 6.3 copy-start.47
  60.6 6.5 copy-start.48
  60.6 6.8 copy-start.41
  60.6 7.1 copy-start.43
  60.6 38.3 %copy-start.5 = (bf16[1,512,1600]{1,2,0:T(8,128)(2,1)S(1)}, bf16[1,512,1600]{1,2,0:T(8,128)(2,1)}, u32[]{:S(2)}) copy-start(bf16[1,512,1600]{1,2,0:T(8,128)(2,1)} %param.28) | copy-start | bytes 4915204
  60.7 294.9 %all-gather.21.cloned.1.call-start = ((), (), s32[]{:S(2)}) async-start(), calls=%async_computation.11 | async-start | bytes 1843200 | tf_op jit(solution)/shard_map/all_gather | solution.py:65
  62.3 338.2 %all-gather.37.cloned.1.call-start = ((), (), s32[]{:S(2)}) async-start(), calls=%async_computation.20 | async-start | bytes 6451200 | tf_op jit(solution)/shard_map/all_gather | solution.py:66
  62.9 380.8 %all-gather.27.cloned.1.call-start = ((), (), s32[]{:S(2)}) async-start(), calls=%async_computation.14 | async-start | bytes 5990400 | tf_op jit(solution)/shard_map/all_gather | solution.py:67
  63.5 458.9 %all-gather.17.cloned.1.call-start = ((), (), s32[]{:S(2)}) async-start(), calls=%async_computation.9 | async-start | bytes 14745600 | tf_op jit(solution)/shard_map/all_gather | solution.py:174
  99.0 244.3 %copy-start.21 = (f32[1600]{0:T(1024)}, f32[1600]{0:T(1024)S(1)}, u32[]{:S(2)}) copy-start(f32[1600]{0:T(1024)S(1)} %convert_element_type.257) | copy-start | bytes 19204
  99.0 244.2 %copy-start.35 = (f32[1600]{0:T(1024)}, f32[1600]{0:T(1024)S(1)}, u32[]{:S(2)}) copy-start(f32[1600]{0:T(1024)S(1)} %convert_element_type.258) | copy-start | bytes 19204
  99.3 243.9 %copy-start.23 = (f32[512]{0:T(512)}, f32[512]{0:T(512)S(1)}, u32[]{:S(2)}) copy-start(f32[512]{0:T(512)S(1)} %broadcast_multiply_fusion.1) | copy-start | bytes 6148
  100.4 242.9 %copy-start.27 = (f32[512]{0:T(512)}, f32[512]{0:T(512)S(1)}, u32[]{:S(2)}) copy-start(f32[512]{0:T(512)S(1)} %fusion.67) | copy-start | bytes 6148
  345.7 256.1 %all-gather.19.cloned.1.call-start = ((), (), s32[]{:S(2)}) async-start(), calls=%async_computation.10 | async-start | bytes 14745600 | tf_op jit(solution)/shard_map/all_gather | solution.py:173
  346.4 387.6 %all-gather.23.cloned.1.call-start = ((), (), s32[]{:S(2)}) async-start(), calls=%async_computation.12 | async-start | bytes 6656000 | tf_op jit(solution)/shard_map/all_gather | solution.py:71
  359.1 692.6 %all-gather.25.cloned.1.call-start = ((), (), s32[]{:S(2)}) async-start(), calls=%async_computation.13 | async-start | bytes 25600000 | tf_op jit(solution)/shard_map/all_gather | solution.py:72
  417.0 997.0 %all-gather.29.cloned.1.call-start = ((), (), s32[]{:S(2)}) async-start(), calls=%async_computation.15 | async-start | bytes 26624000 | tf_op jit(solution)/shard_map/all_gather | solution.py:73
  453.3 1081.1 %reduce-scatter.36.cloned.1.call-start = ((), (), s32[]{:S(2)}) async-start(), calls=%async_computation.26 | async-start | bytes 5990400
  613.7 14.0 copy-start
  649.9 13.8 copy-start
  689.9 13.7 copy-start
  732.3 8.7 copy-start.19
  741.1 310.6 %copy-start.25 = (f32[1600]{0:T(1024)S(1)}, f32[1600]{0:T(1024)}, u32[]{:S(2)}) copy-start(f32[1600]{0:T(1024)} %convert_element_type.265) | copy-start | bytes 19204
  741.1 310.6 %copy-start.26 = (f32[6400]{0:T(1024)S(1)}, f32[6400]{0:T(1024)}, u32[]{:S(2)}) copy-start(f32[6400]{0:T(1024)} %convert_element_type.268) | copy-start | bytes 76804
  741.1 310.6 %copy-start.37 = (f32[1600]{0:T(1024)S(1)}, f32[1600]{0:T(1024)}, u32[]{:S(2)}) copy-start(f32[1600]{0:T(1024)} %convert_element_type.266) | copy-start | bytes 19204
  1414.0 25.1 copy-start.11
  1471.2 295.8 %all-gather.31.cloned.1.call-start = ((), (), s32[]{:S(2)}) async-start(), calls=%async_computation.16 | async-start | bytes 14745600 | tf_op jit(solution)/shard_map/all_gather | solution.py:312
  1471.8 295.2 %all-gather.33.cloned.1.call-start = ((), (), s32[]{:S(2)}) async-start(), calls=%async_computation.17 | async-start | bytes 14745600 | tf_op jit(solution)/shard_map/all_gather | solution.py:315
  1480.3 506.4 %reduce-scatter.24.cloned.1.call-start = ((), (), s32[]{:S(2)}) async-start(), calls=%async_computation.18 | async-start | bytes 23961600 | tf_op jit(solution)/shard_map/reduce_scatter | solution.py:392
  1499.7 495.0 %reduce-scatter.28.cloned.1.call-start = ((), (), s32[]{:S(2)}) async-start(), calls=%async_computation.22 | async-start | bytes 1024000
  1536.7 507.5 %reduce-scatter.38.cloned.1.call-start = ((), (), s32[]{:S(2)}) async-start(), calls=%async_computation.27 | async-start | bytes 23040000
  1555.9 839.0 %reduce-scatter.34.cloned.1.call-start = ((), (), s32[]{:S(2)}) async-start(), calls=%async_computation.25 | async-start | bytes 17971200
  1608.9 4.1 copy-start.2
  1986.6 5.5 copy-start.9
  1986.7 466.4 %reduce-scatter.30.cloned.1.call-start = ((), (), s32[]{:S(2)}) async-start(), calls=%async_computation.23 | async-start | bytes 3584000
  1992.1 525.5 %reduce-scatter.32.cloned.1.call-start = ((), (), s32[]{:S(2)}) async-start(), calls=%async_computation.24 | async-start | bytes 4096000
  1999.9 49.0 %copy-start.15 = (bf16[512,25,64]{0,2,1:T(8,128)(2,1)S(1)}, bf16[512,25,64]{0,2,1:T(8,128)(2,1)}, u32[]{:S(2)}) copy-start(bf16[512,25,64]{0,2,1:T(8,128)(2,1)} %convert.21) | copy-start | bytes 4915204
  2048.8 18.9 copy-start.32
  2048.8 514.3 %reduce-scatter.26.cloned.1.call-start = ((), (), s32[]{:S(2)}) async-start(), calls=%async_computation.21 | async-start | bytes 2560000
  2048.9 18.8 copy-start.7
  2067.7 252.8 %copy-start.4 = (f32[512,1600]{0,1:T(8,128)S(1)}, f32[512,1600]{0,1:T(8,128)}, u32[]{:S(2)}) copy-start(f32[512,1600]{0,1:T(8,128)} %copy-done.3) | copy-start | bytes 9830404
  2067.7 252.8 %copy-start.30 = (f32[512]{0:T(512)S(1)}, f32[512]{0:T(512)}, u32[]{:S(2)}) copy-start(f32[512]{0:T(512)} %copy-done.29) | copy-start | bytes 6148
  2325.1 73.8 %copy-start.12 = (f32[512,1600]{0,1:T(8,128)S(1)}, f32[512,1600]{0,1:T(8,128)}, u32[]{:S(2)}) copy-start(f32[512,1600]{0,1:T(8,128)} %copy-done.10) | copy-start | bytes 9830404
  (30 other events, 74.3 us)
Sparse Core Ops, SparseCore 0:
  9.9 37.9 all-gather.34
  60.8 267.8 all-gather.14
  331.2 24.3 all-gather.20
  357.3 43.1 all-gather.36
  402.3 41.4 all-gather.26
  445.5 76.8 all-gather.16
  524.8 76.8 all-gather.18
  603.8 99.1 all-gather.22
  704.6 347.0 all-gather.24
  1053.1 360.8 all-gather.28
  1471.3 63.0 reduce-scatter.35
  1536.9 77.5 all-gather.30
  1616.5 76.8 all-gather.32
  1697.4 145.6 reduce-scatter.23
  1846.0 23.3 reduce-scatter.27
  1873.2 170.9 reduce-scatter.37
  2046.4 348.4 reduce-scatter.33
  2397.2 55.8 reduce-scatter.29
  2455.5 62.1 reduce-scatter.31
  2519.9 43.0 reduce-scatter.25
where the time goes:
time: 2590 us; the launch traced here: 2570 us
  waiting for transfers between devices  1430 us (55%)
  matrix products  501 us (19%)
  blocking collectives  334 us (13%)
  local copies, waits for them, and re-layouts  165 us (6%)
  other arithmetic  102 us (4%)
    all_gather x1, waiting for transfers between devices, gather_weights(): lax.all_gather(widened[3], 'fsdp', axis=0, tiled=True)  341 us
    all_gather x1, waiting for transfers between devices, gather_weights(): lax.all_gather(widened[2], 'fsdp', axis=0, tiled=True)  309 us
    unnamed x27, waiting for transfers between devices  292 us
    psum x1, blocking collectives, local(): lax.psum(grad_gain_one.astype(jnp.bfloat16), 'seq').astype(jnp.float32)  230 us
    all_gather x1, waiting for transfers between devices, gather_weights(): lax.all_gather(widened[0], 'fsdp', axis=0, tiled=True)  228 us
    all_gather x1, waiting for transfers between devices, local(): key_piece = lax.all_gather(keys_mine, 'seq', axis=0, tiled=True)  79.3 us
    dot_general x4, matrix products, contract_cols(): lax.dot_general(left, right, (((1,), (1,)), ((), ())), preferred_element_...  73.5 us
    all_gather x1, waiting for transfers between devices, local(): value_piece = lax.all_gather(values_mine, 'seq', axis=0, tiled=True)  66 us
  transfers between devices with their start and end apart: 20, of which 15 were waited for; matrix products, arithmetic and copies ran while one was open for 27% of the time, Pallas kernels for 0%

commit v1 on v0

v1 whole, which is shorter than its diff:
```python
import functools
import math

import jax
import jax.numpy as jnp
from jax import lax
from jax.experimental import pallas as pl
from jax.experimental.pallas import tpu as pltpu
from jax.sharding import PartitionSpec as P

MESH = pl.DeviceIdType.MESH
HEADS = 25


def route_bits(n):
    bits = []
    b = 2
    while b < n:
        bits.append(b)
        b *= 2
    return bits


def flip(a, b):
    return jnp.where(lax.rem(lax.div(a, b), 2) == 0, a + b, a - b)


def place(me, r, n):
    if isinstance(r, int):
        for b in [1] + route_bits(n):
            if r & b:
                me = flip(me, b)
        return me
    for b in [1] + route_bits(n):
        me = jnp.where(lax.rem(lax.div(r, b), 2) == 0, me, flip(me, b))
    return me


def pick(table, q):
    value = jnp.int32(table[0])
    for i, entry in enumerate(table[1:]):
        value = jnp.where(q == i + 1, jnp.int32(entry), value)
    return value


def greet(ids):
    barrier = pltpu.get_barrier_semaphore()
    for i in ids:
        pl.semaphore_signal(barrier, inc=1, device_id=i, device_id_type=MESH)
    pl.semaphore_wait(barrier, len(ids))


def remote(src, dst, send, recv, device):
    return pltpu.make_async_remote_copy(
        src_ref=src, dst_ref=dst, send_sem=send, recv_sem=recv, device_id=device, device_id_type=MESH
    )


def arrival_order(n):
    bits = route_bits(n)
    orders = [bits, bits[::-1]]
    lists = []
    for order in orders:
        held, phases = [0], [-1]
        for i, b in enumerate(order):
            fresh = [h ^ b for h in held]
            held, phases = held + fresh, phases + [i] * len(fresh)
        lists.append(list(zip(held, phases)))
    entries = []
    for i in range(n // 2):
        for odd in (0, 1):
            for half in (0, 1):
                k, phase = lists[half][i]
                entries.append((half, k ^ odd, phase, odd))
    return orders, entries


def gather_kernel(n, h, body, n_const, n_out, relative, *refs):
    x_ref = refs[0]
    consts = refs[1 : 1 + n_const]
    all_ref = refs[1 + n_const]
    outs = refs[2 + n_const : 2 + n_const + n_out]
    held = refs[2 + n_const + n_out]
    stages = refs[3 + n_const + n_out : 3 + n_const + 2 * n_out]
    send, recv, keep, store = refs[3 + n_const + 2 * n_out :]
    me = lax.axis_index("seq")
    orders, entries = arrival_order(n)
    bits = orders[0]
    nb = len(bits)

    def device(b):
        return {"seq": flip(me, b)}

    def spot(half, k):
        return 2 * (k if relative else place(me, k, n)) + half

    def ship(half, k, b):
        at = spot(half, k)
        src = x_ref.at[pl.ds(half * h, h)] if isinstance(k, int) and k == 0 else held.at[at]
        lane = 0 if b == 1 else 1 + bits.index(b)
        to = k ^ b if isinstance(k, int) else place(k, b, n)
        dst = 2 * to + half if relative else at
        return remote(src, held.at[dst], send.at[half, lane, k], recv.at[half, to], device(b))

    greet([device(b) for b in [1] + bits])
    for i in range(nb):
        for half in (0, 1):
            ship(half, 0, orders[half][i]).start()
    for half in (0, 1):
        ship(half, 0, 1).start()

    def output(o, q, at):
        slot = lax.rem(q, 2)
        return pltpu.make_async_copy(stages[o].at[slot], outs[o].at[at], store.at[o, slot])

    def entry(q, at, value):
        results = body(value, *consts)
        for o in range(n_out):

            @pl.when(q >= 2)
            def _(o=o):
                output(o, q, at).wait()

            stages[o][lax.rem(q, 2)] = results[o]
            output(o, q, at).start()

    def step(q, carry):
        half = pick([e[0] for e in entries], q)
        k = pick([e[1] for e in entries], q)
        phase = pick([e[2] for e in entries], q)
        odd = pick([e[3] for e in entries], q)
        at = spot(half, k)

        @pl.when(k == 0)
        def _():
            held[at] = x_ref[pl.ds(pl.multiple_of(half * h, h), h)]

        @pl.when(k != 0)
        def _():
            remote(held.at[at], held.at[at], send.at[0, 0, 0], recv.at[half, k], device(1)).wait_recv()

        for side in (0, 1):
            for i in range(nb):

                @pl.when((half == side) & (odd == 0) & (k != 0) & (phase < i))
                def _(side=side, i=i):
                    ship(side, k, orders[side][i]).start()

            @pl.when((half == side) & (odd == 0) & (k != 0))
            def _(side=side):
                ship(side, k, 1).start()

        pltpu.make_async_copy(held.at[at], all_ref.at[at], keep.at[q]).start()
        if n_out:
            entry(q, at, held[at])
        return carry

    lax.fori_loop(0, 2 * n, step, 0)
    for q, (half, k, phase, odd) in enumerate(entries):
        at = spot(half, k)
        pltpu.make_async_copy(held.at[at], all_ref.at[at], keep.at[q]).wait()
        if q >= 2 * n - 2:
            for o in range(n_out):
                output(o, jnp.int32(q), at).wait()
        if not odd:
            for i in range(nb):
                if phase < i:
                    ship(half, k, orders[half][i]).wait_send()
            ship(half, k, 1).wait_send()


def seq_gather(x, n, ident, name, body=None, consts=(), outs=(), relative=False):
    rows, cols = x.shape
    h = rows // 2
    nb = len(route_bits(n))
    shapes = [jax.ShapeDtypeStruct((2 * n, h, c), d) for c, d in outs]
    vmem = pl.BlockSpec(memory_space=pltpu.VMEM)
    hbm = pl.BlockSpec(memory_space=pl.ANY)
    out = pl.pallas_call(
        functools.partial(gather_kernel, n, h, body, len(consts), len(outs), relative),
        out_shape=[jax.ShapeDtypeStruct((2 * n, h, cols), x.dtype)] + shapes,
        in_specs=[vmem] * (1 + len(consts)),
        out_specs=[hbm] * (1 + len(outs)),
        scratch_shapes=[pltpu.VMEM((2 * n, h, cols), x.dtype)]
        + [pltpu.VMEM((2, h, c), d) for c, d in outs]
        + [
            pltpu.SemaphoreType.DMA((2, nb + 1, n)),
            pltpu.SemaphoreType.DMA((2, n)),
            pltpu.SemaphoreType.DMA((2 * n,)),
            pltpu.SemaphoreType.DMA((max(len(outs), 1), 2)),
        ],
        compiler_params=pltpu.CompilerParams(
            collective_id=ident, has_side_effects=True, vmem_limit_bytes=60 << 20
        ),
        cost_estimate=pl.CostEstimate(
            flops=0, bytes_accessed=34 * n * rows * cols, transcendentals=0
        ),
        name=name,
    )(x, *consts)
    return [o.reshape(2 * n * h, o.shape[2]) for o in out]


def scatter_order(n):
    bits = route_bits(n)
    orders = [bits, bits[::-1]]
    lists = [
        sorted(range(0, n, 2), key=lambda k: [-int(bool(k & b)) for b in order]) for order in orders
    ]
    return orders, [(half, lists[half][i]) for i in range(n // 2) for half in (0, 1)]


def scatter_kernel(n, h, body, n_in, n_const, n_out, modes, *refs):
    ins = refs[:n_in]
    consts = refs[n_in : n_in + n_const]
    at = n_in + n_const
    sum_ref = refs[at]
    outs = refs[at + 1 : at + 1 + n_out]
    at += 1 + n_out
    give, pair, own, far, total = refs[at : at + 5]
    at += 5
    loads = refs[at : at + n_in]
    stages = refs[at + n_in : at + n_in + n_out]
    pair_send, pair_recv, far_send, far_recv, load, store, done = refs[at + n_in + n_out :]
    me = lax.axis_index("seq")
    orders, entries = scatter_order(n)
    bits = orders[0]
    slots = give.shape[0]
    index = {e: j for j, e in enumerate(entries)}

    def device(b):
        return {"seq": flip(me, b)}

    def phase_of(half, k):
        for i, b in enumerate(orders[half]):
            if k & b:
                return i
        return len(bits)

    landing = {}
    for half in (0, 1):
        for i, b in enumerate(orders[half]):
            for k in range(0, n, 2):
                if phase_of(half, k) == i:
                    landing[half, i, k ^ b] = len(landing)

    halves = [e[0] for e in entries]
    ks = [e[1] for e in entries]

    def spot(q, relative):
        j = lax.div(q, 2)
        k = pick(ks, j)
        k = jnp.where(lax.rem(q, 2) == 0, flip(k, 1), k)
        return 2 * (k if relative else place(me, k, n)) + pick(halves, j)

    def fetch(q):
        slot = lax.rem(q, 2)
        return [
            pltpu.make_async_copy(ins[i].at[spot(q, modes[0][i])], loads[i].at[slot], load.at[i, slot])
            for i in range(n_in)
        ]

    def output(o, q):
        slot = lax.rem(q, 2)
        return pltpu.make_async_copy(stages[o].at[slot], outs[o].at[spot(q, modes[1][o])], store.at[o, slot])

    def hand(j):
        slot = lax.rem(j, slots)
        return remote(give.at[slot], pair.at[j], pair_send.at[j], pair_recv.at[j], device(1))

    def launch(half, k):
        i = phase_of(half, k)
        b = orders[half][i]
        to = landing[half, i, k ^ b]
        return remote(own.at[index[half, k]], far.at[to], far_send.at[to], far_recv.at[to], device(b))

    def join(j):
        hand(j).wait_recv()
        own[j] = (own[j].astype(jnp.float32) + pair[j].astype(jnp.float32)).astype(own.dtype)
        for e, (half, k) in enumerate(entries):
            if phase_of(half, k) == 0:

                @pl.when(j == e)
                def _(half=half, k=k):
                    launch(half, k).start()

    for c in fetch(jnp.int32(0)):
        c.start()
    greet([device(b) for b in [1] + bits])

    def step(q, carry):
        j = lax.div(q, 2)
        slot = lax.rem(q, 2)

        @pl.when(q + 1 < 2 * n)
        def _():
            for c in fetch(q + 1):
                c.start()

        for c in fetch(q):
            c.wait()
        part, *results = body(*[r[slot] for r in loads], *consts)
        for o in range(n_out):

            @pl.when(q >= 2)
            def _(o=o):
                output(o, q).wait()

            stages[o][slot] = results[o]
            output(o, q).start()

        @pl.when(slot == 0)
        def _():
            @pl.when(j >= slots)
            def _():
                hand(j - slots).wait_send()

            give[lax.rem(j, slots)] = part.astype(give.dtype)
            hand(j).start()

        @pl.when(slot == 1)
        def _():
            own[j] = part.astype(own.dtype)

            @pl.when(j >= 1)
            def _():
                join(j - 1)

        return carry

    lax.fori_loop(0, 2 * n, step, 0)
    join(jnp.int32(n - 1))
    for i in range(len(bits)):
        for half in (0, 1):
            order = orders[half]
            for k in [k for hh, k in entries if hh == half and phase_of(half, k) > i]:
                to = landing[half, i, k]
                remote(far.at[to], far.at[to], far_send.at[to], far_recv.at[to], device(1)).wait_recv()
                j = index[half, k]
                rows = pl.ds(half * h, h)
                if i == len(bits) - 1:
                    total[rows] = own[j].astype(jnp.float32) + far[to].astype(jnp.float32)
                    pltpu.make_async_copy(total.at[rows], sum_ref.at[rows], done.at[half]).start()
                else:
                    own[j] = (own[j].astype(jnp.float32) + far[to].astype(jnp.float32)).astype(own.dtype)
                    if phase_of(half, k) == i + 1:
                        launch(half, k).start()
    for half in (0, 1):
        rows = pl.ds(half * h, h)
        pltpu.make_async_copy(total.at[rows], sum_ref.at[rows], done.at[half]).wait()
    for q in (2 * n - 2, 2 * n - 1):
        for o in range(n_out):
            output(o, jnp.int32(q)).wait()
    for j in range(max(n - slots, 0), n):
        hand(jnp.int32(j)).wait_send()
    for half, k in entries:
        if phase_of(half, k) < len(bits):
            launch(half, k).wait_send()


def seq_scatter(n, cols, ident, name, body, ins, consts, outs=(), modes=None):
    h = ins[0].shape[0] // (2 * n)
    low = jnp.bfloat16
    slots = min(4, n)
    split = [a.reshape(2 * n, h, a.shape[1]) for a in ins]
    vmem = pl.BlockSpec(memory_space=pltpu.VMEM)
    hbm = pl.BlockSpec(memory_space=pl.ANY)
    reach = n - 2
    out = pl.pallas_call(
        functools.partial(scatter_kernel, n, h, body, len(ins), len(consts), len(outs), modes or ([0] * len(ins), [0] * len(outs))),
        out_shape=[jax.ShapeDtypeStruct((2 * h, cols), jnp.float32)]
        + [jax.ShapeDtypeStruct((2 * n, h, c), d) for c, d in outs],
        in_specs=[hbm] * len(ins) + [vmem] * len(consts),
        out_specs=[hbm] * (1 + len(outs)),
        scratch_shapes=[
            pltpu.VMEM((slots, h, cols), low),
            pltpu.VMEM((n, h, cols), low),
            pltpu.VMEM((n, h, cols), low),
            pltpu.VMEM((reach, h, cols), low),
            pltpu.VMEM((2 * h, cols), jnp.float32),
        ]
        + [pltpu.VMEM((2, h, a.shape[2]), a.dtype) for a in split]
        + [pltpu.VMEM((2, h, c), d) for c, d in outs]
        + [
            pltpu.SemaphoreType.DMA((n,)),
            pltpu.SemaphoreType.DMA((n,)),
            pltpu.SemaphoreType.DMA((reach,)),
            pltpu.SemaphoreType.DMA((reach,)),
            pltpu.SemaphoreType.DMA((len(ins), 2)),
            pltpu.SemaphoreType.DMA((max(len(outs), 1), 2)),
            pltpu.SemaphoreType.DMA((2,)),
        ],
        compiler_params=pltpu.CompilerParams(
            collective_id=ident, has_side_effects=True, vmem_limit_bytes=60 << 20
        ),
        cost_estimate=pl.CostEstimate(flops=0, bytes_accessed=68 * n * h * cols, transcendentals=0),
        name=name,
    )(*split, *consts)
    return [out[0]] + [o.reshape(2 * n * h, o.shape[2]) for o in out[1:]]


def exchange_kernel(n, nf, h, w_ref, p_ref, c_ref, v_ref, w_all, p_all, c_all, v_all, send, recv, p_send, p_recv, c_send, c_recv, v_send, v_recv, local):
    me = lax.axis_index("seq")
    f = lax.axis_index("fsdp")
    bits = route_bits(n)
    orders = [bits, bits[::-1]]
    group = n // nf

    def device(r):
        return {"seq": place(me, r, n)}

    def rows(half):
        return pl.ds(0, h) if half == 0 else pl.ds(h, w_ref.shape[0] - h)

    planes = [{"fsdp": lax.rem(f + d, nf)} for d in range(1, nf)]
    greet([device(r) for r in range(1, n)] + planes)
    started = []

    def ship(half, r, b):
        owner = place(me, r, n)
        src = w_ref if r == 0 else w_all.at[owner]
        c = remote(
            src.at[rows(half)],
            w_all.at[owner].at[rows(half)],
            send.at[half, r, 0 if b == 1 else 1 + bits.index(b)],
            recv.at[half, r ^ b],
            device(b),
        )
        c.start()
        started.append(c)

    def arrive(half, k):
        dst = w_all.at[place(me, k, n)].at[rows(half)]
        remote(dst, dst, send.at[half, 0, 0], recv.at[half, k], device(1)).wait_recv()

    for d in range(1, nf):
        c = remote(v_ref, v_all.at[f], v_send.at[d - 1], v_recv.at[d - 1], planes[d - 1])
        c.start()
        started.append(c)
    for i in range(len(bits)):
        for half in (0, 1):
            ship(half, 0, orders[half][i])
    for half in (0, 1):
        ship(half, 0, 1)
    mine = [
        pltpu.make_async_copy(w_ref, w_all.at[me], local.at[0]),
        pltpu.make_async_copy(p_ref.at[me], p_all.at[me], local.at[1]),
        pltpu.make_async_copy(v_ref, v_all.at[f], local.at[2]),
    ]
    for c in mine:
        c.start()
    for i in range(len(bits)):
        for half in (0, 1):
            order = orders[half]
            had = [0]
            for b in order[:i]:
                had = had + [k ^ b for k in had]
            for k0 in had:
                k = k0 ^ order[i]
                arrive(half, k)
                for b in order[i + 1 :]:
                    ship(half, k, b)
                ship(half, k, 1)
        if i == 0:
            for r in range(1, n):
                c = remote(p_ref.at[place(me, r, n)], p_all.at[me], p_send.at[r - 1], p_recv.at[r - 1], device(r))
                c.start()
                started.append(c)
            for i2 in range(nf):
                to = lax.rem(me, group) * nf + i2
                slot = lax.div(me, group)

                @pl.when(to != me)
                def _(i2=i2, to=to, slot=slot):
                    remote(c_ref.at[i2], c_all.at[slot], c_send.at[i2], c_recv.at[slot], {"seq": to}).start()

                @pl.when(to == me)
                def _(i2=i2, slot=slot):
                    pltpu.make_async_copy(c_ref.at[i2], c_all.at[slot], local.at[3]).start()

    for half in (0, 1):
        for k in range(1, n, 2):
            arrive(half, k)
    for r in range(1, n):
        dst = p_all.at[place(me, r, n)]
        remote(dst, dst, p_send.at[0], p_recv.at[r - 1], device(r)).wait_recv()
    for p in range(nf):
        source = p * group + lax.div(me, nf)

        @pl.when(source != me)
        def _(p=p):
            remote(c_all.at[p], c_all.at[p], c_send.at[0], c_recv.at[p], device(1)).wait_recv()

        @pl.when(source == me)
        def _(p=p):
            pltpu.make_async_copy(c_all.at[p], c_all.at[p], local.at[3]).wait()

    for d in range(1, nf):
        dst = v_all.at[lax.rem(f + nf - d, nf)]
        remote(dst, dst, v_send.at[0], v_recv.at[d - 1], planes[0]).wait_recv()
    for c in mine:
        c.wait()
    for i2 in range(nf):
        to = lax.rem(me, group) * nf + i2

        @pl.when(to != me)
        def _(i2=i2):
            remote(c_ref.at[i2], c_ref.at[i2], c_send.at[i2], c_recv.at[0], device(1)).wait_send()

    for c in started:
        c.wait_send()


def exchange(w, p, c, v, n, nf, ident):
    rows, cols = w.shape
    h = (rows // 2 + 7) // 8 * 8
    nb = len(route_bits(n))
    hbm = pl.BlockSpec(memory_space=pl.ANY)
    dma = pltpu.SemaphoreType.DMA
    return pl.pallas_call(
        functools.partial(exchange_kernel, n, nf, h),
        out_shape=[
            jax.ShapeDtypeStruct((n, rows, cols), w.dtype),
            jax.ShapeDtypeStruct(p.shape, p.dtype),
            jax.ShapeDtypeStruct(c.shape, c.dtype),
            jax.ShapeDtypeStruct((nf,) + v.shape, v.dtype),
        ],
        in_specs=[hbm] * 4,
        out_specs=[hbm] * 4,
        scratch_shapes=[
            dma((2, n, nb + 1)),
            dma((2, n)),
            dma((n - 1,)),
            dma((n - 1,)),
            dma((nf,)),
            dma((nf,)),
            dma((nf - 1,)),
            dma((nf - 1,)),
            dma((4,)),
        ],
        compiler_params=pltpu.CompilerParams(collective_id=ident, has_side_effects=True),
        cost_estimate=pl.CostEstimate(flops=0, bytes_accessed=60 << 20, transcendentals=0),
        name="exchange",
    )(w, p, c, v)


def swap_kernel(n, wide, to_heads, x_ref, o_ref, send, recv, local):
    me = lax.axis_index("seq")

    def lanes(i):
        return pl.ds(pl.multiple_of(i * wide, 128), wide)

    def source(i):
        return x_ref.at[:, lanes(i)] if to_heads else x_ref.at[i]

    def target(i):
        return o_ref.at[i] if to_heads else o_ref.at[:, lanes(i)]

    greet([{"seq": place(me, r, n)} for r in range(1, n)])
    copies = []
    for r in range(n - 1, 0, -1):
        to = place(me, r, n)
        c = remote(source(to), target(me), send.at[r - 1], recv.at[r - 1], {"seq": to})
        c.start()
        copies.append(c)
    mine = pltpu.make_async_copy(source(me), target(me), local)
    mine.start()
    for r in range(1, n):
        dst = target(place(me, r, n))
        remote(dst, dst, send.at[0], recv.at[r - 1], {"seq": place(me, r, n)}).wait_recv()
    mine.wait()
    for c in copies:
        c.wait_send()


def swap(x, n, wide, to_heads, ident):
    rows = x.shape[0] if to_heads else x.shape[1]
    hbm = pl.BlockSpec(memory_space=pl.ANY)
    shape = (n, rows, wide) if to_heads else (rows, n * wide)
    return pl.pallas_call(
        functools.partial(swap_kernel, n, wide, to_heads),
        out_shape=jax.ShapeDtypeStruct(shape, x.dtype),
        in_specs=[hbm],
        out_specs=hbm,
        scratch_shapes=[
            pltpu.SemaphoreType.DMA((n - 1,)),
            pltpu.SemaphoreType.DMA((n - 1,)),
            pltpu.SemaphoreType.DMA,
        ],
        compiler_params=pltpu.CompilerParams(collective_id=ident, has_side_effects=True),
        cost_estimate=pl.CostEstimate(flops=0, bytes_accessed=40 << 20, transcendentals=0),
        name="to_heads" if to_heads else "to_tokens",
    )(x)


HEAD=64
SCALE=0.125*math.log2(math.e)

def block_table(lengths, parents, slots, trunk, block):
    branches=lengths.shape[0]//3
    rows=[]
    for t in range(slots):
        if t<trunk:
            keys=[(c,0 if c==t else block,block) for c in range(t+1)]
        else:
            m=t-trunk
            keys=[(c,block,block) for c in range(trunk)]
            if m>=branches:
                keys.append((trunk-1+parents[m],block,jnp.sum(jnp.where(jnp.arange(lengths.shape[0])==parents[m]-1,lengths,0))))
            keys.append((t,0,lengths[m]))
        for i,(c,shift,count) in enumerate(keys):
            masked=jnp.where(jnp.logical_or(shift==0,count<block),1,0)
            rows.append(jnp.stack([jnp.asarray(v,jnp.int32) for v in (t,c,shift,count,masked,int(i==0),int(i==len(keys)-1))]))
    return jnp.stack(rows,1)

def lane_half(shape):
    return lax.broadcasted_iota(jnp.int32,shape,len(shape)-1)<HEAD

def nt(a,b):
    return lax.dot_general(a,b,(((1,),(1,)),((),())),preferred_element_type=jnp.float32)

def mm(a,b):
    return jnp.dot(a,b,preferred_element_type=jnp.float32)

def attend_kernel(width, block, tab, qkv, low, att, tot, acc):
    p=pl.program_id(0)
    qs,ks,shift,count,masked=tab[0,p],tab[1,p],tab[2,p],tab[3,p],tab[4,p]
    first,last=tab[5,p],tab[6,p]
    qrow=pl.ds(pl.multiple_of(qs*block,block),block)
    krow=pl.ds(pl.multiple_of(ks*block,block),block)
    left=lane_half((block,2*HEAD))
    @pl.when(first==1)
    def _(): acc[...]=jnp.zeros_like(acc)
    def step(mask):
        for j in range(width//(2*HEAD)):
            q=qkv[qrow,j*2*HEAD:(j+1)*2*HEAD]
            k=qkv[krow,width+j*2*HEAD:width+(j+1)*2*HEAD]
            v=qkv[krow,2*width+j*2*HEAD:2*width+(j+1)*2*HEAD]
            for h in range(2):
                here=left if h==0 else jnp.logical_not(left)
                s=nt(jnp.where(here,q,0),k)
                e=jnp.exp2(s*SCALE)
                if mask is not None: e=jnp.where(mask,e,0.0)
                acc[2*j+h]+=mm(e.astype(jnp.bfloat16),jnp.where(here,v,1))
    @pl.when(masked==0)
    def _(): step(None)
    @pl.when(masked==1)
    def _():
        row=lax.broadcasted_iota(jnp.int32,(block,block),0)
        col=lax.broadcasted_iota(jnp.int32,(block,block),1)
        step((col<=row+shift)&(col<count))
    @pl.when(last==1)
    def _():
        for j in range(width//(2*HEAD)):
            a,b=acc[2*j],acc[2*j+1]
            total=jnp.where(left,pltpu.roll(a,HEAD,1),pltpu.roll(b,HEAD,1))
            value=jnp.where(left,a,b)/total
            lanes=slice(j*2*HEAD,(j+1)*2*HEAD)
            low[:,lanes]=value.astype(jnp.bfloat16)
            att[:,lanes]=value
            tot[:,lanes]=total

def attend(table, qkv, block):
    rows,width=qkv.shape[0],qkv.shape[1]//3
    steps=table.shape[1]
    by_q=lambda p,t:(t[0,p],0)
    heads=width//HEAD
    return pl.pallas_call(functools.partial(attend_kernel,width,block),
        out_shape=(jax.ShapeDtypeStruct((rows,width),jnp.bfloat16),jax.ShapeDtypeStruct((rows,width),jnp.float32),jax.ShapeDtypeStruct((rows,width),jnp.float32)),
        grid_spec=pltpu.PrefetchScalarGridSpec(num_scalar_prefetch=1,grid=(steps,),
            in_specs=[pl.BlockSpec((rows,3*width),lambda p,t:(0,0),pipeline_mode=pl.Buffered(1))],
            out_specs=[pl.BlockSpec((block,width),by_q)]*3,
            scratch_shapes=[pltpu.VMEM((heads,block,2*HEAD),jnp.float32)]),
        compiler_params=pltpu.CompilerParams(dimension_semantics=("arbitrary",),vmem_limit_bytes=50<<20),
        cost_estimate=pl.CostEstimate(flops=4*steps*heads*block*block*4*HEAD,bytes_accessed=rows*width*16,transcendentals=steps*heads*block*block),
        name="attend")(table,qkv)

def attend_back_kernel(width, block, tab, qkv, kt, datt, att, tot, out, dk, dv, dqt, aug):
    p=pl.program_id(0)
    qs,ks,shift,count,masked=tab[0,p],tab[1,p],tab[2,p],tab[3,p],tab[4,p]
    first,last=tab[5,p],tab[6,p]
    qrow=pl.ds(pl.multiple_of(qs*block,block),block)
    krow=pl.ds(pl.multiple_of(ks*block,block),block)
    left=lane_half((block,2*HEAD))
    lane=lax.broadcasted_iota(jnp.int32,(block,2*HEAD),1)
    pairs=width//(2*HEAD)
    @pl.when(p==0)
    def _():
        dk[...]=jnp.zeros_like(dk)
        dv[...]=jnp.zeros_like(dv)
    @pl.when(first==1)
    def _():
        dqt[...]=jnp.zeros_like(dqt)
        for j in range(pairs):
            lanes=slice(j*2*HEAD,(j+1)*2*HEAD)
            d=datt[:,lanes].astype(jnp.float32)
            total=tot[:,lanes]
            low=(d/total).astype(jnp.bfloat16)
            prod=d*att[:,lanes]/total
            for h in range(2):
                here=left if h==0 else jnp.logical_not(left)
                delta=-jnp.sum(jnp.where(here,prod,0.0),1,keepdims=True)
                hi=delta.astype(jnp.bfloat16).astype(jnp.float32)
                mid=(delta-hi).astype(jnp.bfloat16).astype(jnp.float32)
                rest=delta-hi-mid
                at=HEAD*(1-h)
                extra=jnp.where(lane==at,hi,jnp.where(lane==at+1,mid,jnp.where(lane==at+2,rest,0.0)))
                aug[2*j+h]=jnp.where(here,low.astype(jnp.float32),extra).astype(jnp.bfloat16)
    def step(mask):
        for j in range(pairs):
            q=qkv[qrow,j*2*HEAD:(j+1)*2*HEAD]
            k=qkv[krow,width+j*2*HEAD:width+(j+1)*2*HEAD]
            v=qkv[krow,2*width+j*2*HEAD:2*width+(j+1)*2*HEAD]
            lanes=slice(j*2*HEAD,(j+1)*2*HEAD)
            dvs,dks=[],[]
            for h in range(2):
                here=left if h==0 else jnp.logical_not(left)
                qh=jnp.where(here,q,0)
                e=jnp.exp2(nt(k,qh)*SCALE)
                if mask is not None: e=jnp.where(mask,e,0.0)
                dod=aug[2*j+h]
                ds=(e*nt(jnp.where(here,v*0.125,0.125).astype(jnp.bfloat16),dod)).astype(jnp.bfloat16)
                dvs.append(mm(e.astype(jnp.bfloat16),dod))
                dks.append(mm(ds,qh))
                at=j*2*HEAD+h*HEAD
                dqt[at:at+HEAD]+=mm(kt[at:at+HEAD,krow],ds)
            dv[krow,lanes]+=jnp.where(left,dvs[0],dvs[1])
            dk[krow,lanes]+=dks[0]+dks[1]
    @pl.when(masked==0)
    def _(): step(None)
    @pl.when(masked==1)
    def _():
        col=lax.broadcasted_iota(jnp.int32,(block,block),0)
        row=lax.broadcasted_iota(jnp.int32,(block,block),1)
        step((col<=row+shift)&(col<count))
    @pl.when(last==1)
    def _():
        out[qrow,0:width]=dqt[...].T.astype(jnp.bfloat16)
    @pl.when(p==pl.num_programs(0)-1)
    def _():
        out[:,width:2*width]=dk[...].astype(jnp.bfloat16)
        out[:,2*width:]=dv[...].astype(jnp.bfloat16)

def attend_back(table, qkv, datt, att, tot, block):
    rows,width=qkv.shape[0],qkv.shape[1]//3
    steps=table.shape[1]
    by_q=lambda p,t:(t[0,p],0)
    heads=width//HEAD
    kt=qkv[:,width:2*width].T
    whole=lambda s:pl.BlockSpec(s,lambda p,t:(0,0),pipeline_mode=pl.Buffered(1))
    return pl.pallas_call(functools.partial(attend_back_kernel,width,block),
        out_shape=jax.ShapeDtypeStruct((rows,3*width),jnp.bfloat16),
        grid_spec=pltpu.PrefetchScalarGridSpec(num_scalar_prefetch=1,grid=(steps,),
            in_specs=[whole((rows,3*width)),whole((width,rows))]+[pl.BlockSpec((block,width),by_q)]*3,
            out_specs=whole((rows,3*width)),
            scratch_shapes=[pltpu.VMEM((rows,width),jnp.float32),pltpu.VMEM((rows,width),jnp.float32),pltpu.VMEM((width,block),jnp.float32),pltpu.VMEM((heads,block,2*HEAD),jnp.bfloat16)]),
        compiler_params=pltpu.CompilerParams(dimension_semantics=("arbitrary",),vmem_limit_bytes=60<<20),
        cost_estimate=pl.CostEstimate(flops=10*steps*heads*block*block*2*HEAD,bytes_accessed=rows*width*32,transcendentals=steps*heads*block*block),
        name="attend_back")(table,qkv,kt,datt,att,tot)


def layer_norm(values, gain, shift):
    centred = values - jnp.mean(values, -1, keepdims=True)
    spread = jnp.mean(centred * centred, -1, keepdims=True)
    return centred * lax.rsqrt(spread + 1e-05) * gain + shift


def contract_rows(left, right):
    return lax.dot_general(
        left, right, (((0,), (0,)), ((), ())), preferred_element_type=jnp.float32
    )


def contract_cols(left, right):
    return lax.dot_general(
        left, right, (((1,), (1,)), ((), ())), preferred_element_type=jnp.float32
    )


def sum_kernel(n, nf, v_ref, o_ref, planes, sums, send_z, recv_z, send_s, recv_s):
    s = lax.axis_index("seq")
    f = lax.axis_index("fsdp")
    others = [{"fsdp": lax.rem(f + d, nf)} for d in range(1, nf)]
    peers = [{"seq": lax.rem(s + d, n)} for d in range(1, n)]
    greet(others + peers)
    copies = []
    for d in range(1, nf):
        c = pltpu.make_async_remote_copy(
            src_ref=v_ref.at[lax.rem(f + d, nf)],
            dst_ref=planes.at[d - 1],
            send_sem=send_z.at[d - 1],
            recv_sem=recv_z.at[d - 1],
            device_id=others[d - 1],
            device_id_type=MESH,
        )
        c.start()
        copies.append(c)
    total = v_ref[f]
    for d, c in enumerate(copies):
        c.wait_recv()
        total = total + planes[d]
    sums[0] = total
    spread = []
    for d in range(1, n):
        c = pltpu.make_async_remote_copy(
            src_ref=sums.at[0],
            dst_ref=sums.at[d],
            send_sem=send_s.at[d - 1],
            recv_sem=recv_s.at[d - 1],
            device_id=peers[d - 1],
            device_id_type=MESH,
        )
        c.start()
        spread.append(c)
    for d, c in enumerate(spread):
        c.wait_recv()
        total = total + sums[d + 1]
    o_ref[...] = total
    for c in copies + spread:
        c.wait_send()


def sum_vectors(blocks, n, nf):
    k = blocks.shape[1]
    rows = -(-k // 1024) * 8
    padded = jnp.pad(blocks, ((0, 0), (0, rows * 128 - k))).reshape(nf, rows, 128)
    out = pl.pallas_call(
        functools.partial(sum_kernel, n, nf),
        out_shape=jax.ShapeDtypeStruct((rows, 128), jnp.float32),
        in_specs=[pl.BlockSpec(memory_space=pltpu.VMEM)],
        out_specs=pl.BlockSpec(memory_space=pltpu.VMEM),
        scratch_shapes=[
            pltpu.VMEM((nf - 1, rows, 128), jnp.float32),
            pltpu.VMEM((n, rows, 128), jnp.float32),
            pltpu.SemaphoreType.DMA((nf - 1,)),
            pltpu.SemaphoreType.DMA((nf - 1,)),
            pltpu.SemaphoreType.DMA((n - 1,)),
            pltpu.SemaphoreType.DMA((n - 1,)),
        ],
        compiler_params=pltpu.CompilerParams(collective_id=7, has_side_effects=True),
        name="sum_vectors",
    )(padded)
    return out.reshape(-1)[:k]


def local(
    tokens,
    ln1_gain,
    ln1_bias,
    qkv_weight,
    qv_bias,
    out_weight,
    out_bias,
    ln2_gain,
    ln2_bias,
    fc_weight,
    fc_bias,
    proj_weight,
    proj_bias,
    seg_lengths,
    parents,
    cotangent,
):
    n = lax.axis_size("seq")
    nf = lax.axis_size("fsdp")
    s = lax.axis_index("seq")
    f = lax.axis_index("fsdp")
    trunk = n // 4
    block, width = tokens.shape[1], tokens.shape[2]
    rows = width // nf
    hidden = fc_weight.shape[1] * n
    piece = hidden // (n * nf)
    group = n // nf
    wide = 2 * HEAD * (-(-HEADS // (2 * n)))
    low = jnp.bfloat16
    wider = jnp.float32

    vectors = [ln1_gain, ln1_bias, qv_bias, out_bias, ln2_gain, ln2_bias, fc_bias, proj_bias]
    sizes = [v.shape[0] for v in vectors]
    joined = jnp.concatenate(vectors)
    joined = jnp.pad(joined, (0, -joined.shape[0] % 2048)).reshape(-1, 128)
    qkv_cols = qkv_weight.shape[1]
    turned = jnp.pad(qkv_weight.T, ((0, 0 if qkv_cols % 8 == 0 else -qkv_cols % 16), (0, 0)))
    out_turned = lax.all_gather(out_weight, "fsdp", axis=0, tiled=True).T
    turned, proj_blocks, fc_blocks, joined = exchange(
        turned,
        proj_weight.reshape(n, piece, width // n),
        fc_weight.reshape(rows, nf, piece).transpose(1, 0, 2),
        joined,
        n,
        nf,
        0,
    )
    joined = joined.reshape(nf, -1)
    whole = []
    at = 0
    for size in sizes:
        whole.append(joined[:, at : at + size].reshape(-1).astype(wider))
        at += size
    gain_one, shift_one, bias_qv, bias_out, gain_two, shift_two, bias_fc, bias_proj = whole
    bias_three = jnp.stack([bias_qv[:width], jnp.zeros((width,), wider), bias_qv[width:]])
    bias_three = jnp.pad(bias_three, ((0, 0), (0, n * wide - width)))
    bias_mine = lax.dynamic_slice_in_dim(bias_three, s * wide, wide, 1).reshape(-1)
    bias_hidden = lax.dynamic_index_in_dim(bias_fc.reshape(nf, n, piece), s, 1, False)
    bias_hidden = bias_hidden.reshape(1, -1)

    turned = turned[:, :qkv_cols].reshape(3, width, rows)
    turned = jnp.pad(turned, ((0, 0), (0, n * wide - width), (0, 0)))
    turned = lax.dynamic_slice_in_dim(turned, s * wide, wide, 1)
    qkv_rows = turned.transpose(2, 0, 1).reshape(rows, 3 * wide)
    qkv_mine = lax.all_gather(qkv_rows, "fsdp", axis=0, tiled=True)
    out_turned = lax.all_gather(out_turned, "seq", axis=0, tiled=True)
    fc_rows = fc_blocks.transpose(1, 0, 2).reshape(rows, nf * piece)
    fc_mine = lax.all_gather(fc_rows, "fsdp", axis=0, tiled=True)
    proj_rows = proj_blocks.transpose(1, 0, 2).reshape(piece, width)
    proj_mine = lax.all_gather(proj_rows, "fsdp", axis=0, tiled=True)

    table = block_table(seg_lengths[0], parents[0], n, trunk, block)

    resid = tokens[0].astype(wider)
    (normed_one,) = seq_gather(
        layer_norm(resid, gain_one, shift_one).astype(low), n, 1, "gather_one"
    )
    projected = (
        jnp.dot(normed_one, qkv_mine, preferred_element_type=wider) + bias_mine
    ).astype(low)

    upstream = cotangent[0].astype(wider)
    sent, normed_one = lax.optimization_barrier((cotangent[0], normed_one))
    pieces = {}
    bits = route_bits(n)
    for half, order in enumerate([bits, bits[::-1]]):
        held = {0: sent[half * block // 2 : (half + 1) * block // 2]}
        for b in order:
            pairs = [(i, i ^ b) for i in range(n)]
            held.update({k ^ b: lax.ppermute(v, "seq", pairs) for k, v in held.items()})
        pairs = [(i, i ^ 1) for i in range(n)]
        held.update({k ^ 1: lax.ppermute(v, "seq", pairs) for k, v in held.items()})
        pieces.update({2 * k + half: v for k, v in held.items()})
    upstream_all = jnp.concatenate([pieces[i] for i in range(2 * n)])

    attended_low, attended, totals = attend(table, projected, block)
    attended_mine = swap(attended_low.reshape(n, block, wide), n, wide, False, 2)[:, :width]
    middle = resid + contract_cols(attended_mine, out_turned) + bias_out
    normed_two = layer_norm(middle, gain_two, shift_two).astype(low)
    ff = nf * piece

    def expand(value, weight, bias):
        pre = mm(value, weight[...]) + bias[...]
        bend = math.sqrt(2 / math.pi)
        inner = jnp.tanh(bend * (pre + 0.044715 * (pre * pre * pre)))
        act = 0.5 * pre * (1 + inner)
        slope = 0.5 * (1 + inner) + 0.5 * pre * (1 - inner * inner) * (
            bend * (1 + 3 * 0.044715 * (pre * pre))
        )
        return act.astype(low), slope.astype(low)

    normed_two, hidden_act, hidden_slope = seq_gather(
        normed_two, n, 3, "gather_two", expand, (fc_mine, bias_hidden), ((ff, low), (ff, low)), True
    )

    def shrink(up, act, slope, proj, fc):
        mixed = mm(act, proj[...])
        grad = (nt(up, proj[...]) * slope.astype(wider)).astype(low)
        return nt(grad, fc[...]), grad, mixed.astype(low)

    grad_normed_two, grad_pre, mixed = seq_scatter(
        n,
        width,
        4,
        "scatter_two",
        shrink,
        (upstream_all, hidden_act, hidden_slope),
        (proj_mine, fc_mine),
        ((ff, low), (width, low)),
        ((1, 1, 1), (1, 0)),
    )
    unused_two, norm_two_back = jax.vjp(layer_norm, middle, gain_two, shift_two)
    grad_middle_norm, grad_gain_two, grad_shift_two = norm_two_back(grad_normed_two)
    grad_middle = upstream + grad_middle_norm
    grad_branch = grad_middle.astype(low)
    grad_attended = jnp.dot(grad_branch, out_turned, preferred_element_type=wider).astype(low)
    grad_attended = jnp.pad(grad_attended, ((0, 0), (0, n * wide - width)))
    grad_attended = swap(grad_attended, n, wide, True, 5).reshape(n * block, wide)
    mixed, grad_attended = lax.optimization_barrier((mixed, grad_attended))
    mixed = lax.psum_scatter(mixed, "seq", scatter_dimension=0, tiled=True).astype(wider)
    output = (middle + mixed + bias_proj).astype(low)[None]
    grad_projected = attend_back(table, projected, grad_attended, attended, totals, block)
    grad_qkv = contract_rows(normed_one, grad_projected).astype(low)
    (grad_normed_one,) = seq_scatter(
        n, width, 6, "scatter_one", lambda g, w: (nt(g, w[...]),), (grad_projected,), (qkv_mine,)
    )
    unused_one, norm_one_back = jax.vjp(layer_norm, resid, gain_one, shift_one)
    grad_resid_norm, grad_gain_one, grad_shift_one = norm_one_back(grad_normed_one)
    input_grad = (grad_middle + grad_resid_norm).astype(low)[None]

    grad_proj = contract_rows(hidden_act, upstream_all).astype(low)
    grad_fc = contract_rows(normed_two, grad_pre).astype(low)
    grad_out = contract_rows(grad_branch, attended_mine).astype(low)
    proj_part = lax.psum_scatter(grad_proj, "fsdp", scatter_dimension=0, tiled=True)
    proj_out = lax.all_to_all(proj_part, "seq", 1, 0, tiled=True).astype(wider)
    fc_part = lax.psum_scatter(grad_fc, "fsdp", scatter_dimension=0, tiled=True)
    fc_part = fc_part.reshape(rows, nf, piece).transpose(1, 0, 2)
    fc_part = lax.all_to_all(jnp.repeat(fc_part, group, axis=0), "seq", 0, 0, tiled=True)
    fc_part = lax.dynamic_index_in_dim(
        fc_part.reshape(group, nf, rows, piece), lax.rem(s, group), 0, False
    )
    fc_out = fc_part.transpose(1, 0, 2).reshape(rows, nf * piece).astype(wider)
    out_part = lax.psum_scatter(grad_out, "seq", scatter_dimension=0, tiled=True).T
    out_out = lax.psum_scatter(out_part, "fsdp", scatter_dimension=0, tiled=True).astype(wider)
    qkv_part = lax.psum_scatter(grad_qkv, "fsdp", scatter_dimension=0, tiled=True)
    qkv_part = lax.all_gather(qkv_part.reshape(rows, 3, wide), "seq", axis=2, tiled=True)
    qkv_part = qkv_part[:, :, :width].reshape(rows, 3 * width)
    qkv_out = lax.dynamic_slice_in_dim(qkv_part, s * qkv_cols, qkv_cols, 1).astype(wider)

    column_sums = jnp.sum(grad_projected.astype(wider), 0).reshape(3, wide)
    placed = lax.dynamic_update_slice_in_dim(
        jnp.zeros((3, n * wide), wider), column_sums, s * wide, 1
    )[:, :width]
    grad_qv = jnp.concatenate([placed[0], placed[2]])
    hidden_sums = jnp.sum(grad_pre.astype(wider), 0).reshape(nf, 1, piece)
    grad_fc_bias = lax.dynamic_update_slice_in_dim(
        jnp.zeros((nf, n, piece), wider), hidden_sums, s, 1
    )
    parts = [
        grad_gain_one,
        grad_shift_one,
        grad_qv,
        jnp.sum(grad_branch.astype(wider), 0),
        grad_gain_two,
        grad_shift_two,
        grad_fc_bias,
        jnp.sum(upstream, 0),
    ]
    summed = sum_vectors(jnp.concatenate([p.reshape(nf, -1) for p in parts], 1), n, nf)
    vector_out = []
    at = 0
    for size in sizes:
        vector_out.append(summed[at : at + size])
        at += size
    return (
        output,
        input_grad,
        vector_out[0],
        vector_out[1],
        qkv_out,
        vector_out[2],
        out_out,
        vector_out[3],
        vector_out[4],
        vector_out[5],
        fc_out,
        vector_out[6],
        proj_out,
        vector_out[7],
    )


def solution(mesh):
    in_specs = (
        P("fsdp", "seq", None),
        P("fsdp"),
        P("fsdp"),
        P("fsdp", "seq"),
        P("fsdp"),
        P("fsdp", "seq"),
        P("fsdp"),
        P("fsdp"),
        P("fsdp"),
        P("fsdp", "seq"),
        P("fsdp"),
        P("fsdp", "seq"),
        P("fsdp"),
        P("fsdp", None),
        P("fsdp", None),
        P("fsdp", "seq", None),
    )
    out_specs = (
        P("fsdp", "seq", None),
        P("fsdp", "seq", None),
        P("fsdp"),
        P("fsdp"),
        P("fsdp", "seq"),
        P("fsdp"),
        P("fsdp", "seq"),
        P("fsdp"),
        P("fsdp"),
        P("fsdp"),
        P("fsdp", "seq"),
        P("fsdp"),
        P("fsdp", "seq"),
        P("fsdp"),
    )
    return jax.shard_map(local, mesh=mesh, in_specs=in_specs, out_specs=out_specs, check_vma=False)
```

time: 2590 us -> 1090 us (0.42)
  waiting for transfers between devices: 1430 us -> 129 us
  Pallas kernels: 0 us -> 568 us
  matrix products: 501 us -> 93.9 us
  blocking collectives: 334 us -> 23.7 us
  other arithmetic: 102 us -> 41.7 us
    all_gather x12 -> x5, waiting for transfers between devices: 1140 us -> 12.7 us  [the longest x1 12.6 us: local(): lax.all_gather(qkv_part.reshape(rows, 3, wide), 'seq', axis=2, tiled=True)]
    pallas_call x0 -> x10, Pallas kernels: none -> 568 us  [the longest x2 152 us: seq_gather(): pl.pallas_call(functools.partial(gather_kernel, n, h, body, len(consts),...]
    dot_general x25 -> x2, matrix products: 368 us -> 25.7 us  [the longest x1 17.3 us: local(): jnp.dot(normed_one, qkv_mine, preferred_element_type=wider) + bias_mine]
    unnamed x27 -> x14, waiting for transfers between devices: 292 us -> 0.87 us
    psum x1 -> x0, blocking collectives: 230 us -> none  [local(): lax.psum(grad_gain_one.astype(jnp.bfloat16), 'seq').astype(jnp.float32)]
    reduce_scatter x1 -> x3, waiting for transfers between devices: 0.02 us -> 102 us  [the longest x1 80.7 us: local(): lax.psum_scatter(mixed, 'seq', scatter_dimension=0, tiled=True)]
    dot_general x4 -> x1, matrix products: 73.5 us -> 7.11 us  [contract_cols(): lax.dot_general(left, right, (((1,), (1,)), ((), ())), preferred_element_...]
    unnamed x2 -> x0, blocking collectives: 46.9 us -> none
  transfers between devices with their start and end apart: 20 -> 27, of which waited for: 15 -> 7; matrix products, arithmetic and copies ran while one was open for 27% -> 24% of each run, Pallas kernels for 0% -> 41%
where the time goes in v1:
time: 1090 us; the launch traced here: 1080 us
  Pallas kernels  568 us (52%)
  local copies, waits for them, and re-layouts  176 us (16%)
  waiting for transfers between devices  129 us (12%)
  matrix products  93.9 us (9%)
  other arithmetic  41.7 us (4%)
  blocking collectives  23.7 us (2%)
  between operations  22.9 us (2%)
  starting transfers between devices  21 us (2%)
    pallas_call x2, Pallas kernels, seq_gather(): pl.pallas_call(functools.partial(gather_kernel, n, h, body, len(consts),...  152 us
    pallas_call x2, Pallas kernels, seq_scatter(): pl.pallas_call(functools.partial(scatter_kernel, n, h, body, len(ins), le...  150 us
    pallas_call x1, Pallas kernels, attend_back(): pl.pallas_call(functools.partial(attend_back_kernel, width, block), out_s...  89.7 us
    reduce_scatter x1, waiting for transfers between devices, local(): lax.psum_scatter(mixed, 'seq', scatter_dimension=0, tiled=True)  80.7 us
    pallas_call x2, Pallas kernels, swap(): pl.pallas_call(functools.partial(swap_kernel, n, wide, to_heads), out_sha...  67.2 us
    dot_general x4, matrix products, contract_rows(): lax.dot_general(left, right, (((0,), (0,)), ((), ())), preferred_element_...  61.1 us
    unnamed x122, local copies, waits for them, and re-layouts  46.4 us
    pallas_call x1, Pallas kernels, exchange(): pl.pallas_call(functools.partial(exchange_kernel, n, nf, h), out_shape=[j...  44.1 us
  transfers between devices with their start and end apart: 27, of which 7 were waited for; matrix products, arithmetic and copies ran while one was open for 24% of the time, Pallas kernels for 41%

profile of v1, /device:TPU:3, one launch (start us, length us, event | category | flops | bytes accessed | tf_op | source)
XLA Modules:
  0.0 1076.4 jit_solution(15336901928453083009)
XLA Ops:
  7.2 5.7 concatenate.18
  20.5 44.1 %exchange.1 = (bf16[8,600,400]{2,1,0:T(8,128)(2,1)}, bf16[8,200,200]{2,1,0:T(8,128)(2,1)}, bf16[4,400,200]{2,1,0:T(8,128)(2,1)}, bf16[4,48,128]{2,1,0:T(8,128)(2,1)}) custom-call(bf16[600,400]{1,0:T(8,128)(2,1)} %bitcast.163, bf16[8,200,200]{2,1,0:T(8,128)(2,1)} %bitcast.159, bf16[4,400,200]{2,1,0:T(8,128)(2,1)} %bitcast.158, ...), custom_call_target="tpu_custom_call" | custom-call | bytes 62914560 | tf_op jit(solution)/shard_map/exchange/pallas_call | solution.py:519
  64.6 10.6 copy.240
  77.9 23.7 %all_gather.19 = bf16[1600,200]{1,0:T(8,128)(2,1)S(1)} all-gather(bf16[400,200]{1,0:T(8,128)(2,1)S(1)} %copy-done.16), channel_id=1, replica_groups=mesh['seq'=8,'fsdp'=4] {'fsdp'}, dimensions={0}, use_global_device_ids=true | all-gather | bytes 800000 | tf_op jit(solution)/shard_map/all_gather | solution.py:883
  107.6 3.2 copy.245
  115.9 84.8 %gather_one.1 = bf16[16,256,1600]{2,1,0:T(8,128)(2,1)} custom-call(bf16[512,1600]{1,0:T(8,128)(2,1)} %fusion.9.refs_0_), custom_call_target="tpu_custom_call" | custom-call | bytes 222822400 | tf_op jit(solution)/shard_map/gather_one/pallas_call | solution.py:179
  234.8 7.7 collective-permute-done.3
  264.0 4.9 collective-permute-done.10
  283.6 17.3 %add_convert_fusion = bf16[4096,768]{0,1:T(8,128)(2,1)} fusion(bf16[4096,1600]{1,0:T(8,128)(2,1)} %bitcast.150, bf16[1600,768]{1,0:T(8,128)(2,1)} %all-gather.6.cloned.1.call-done.refs_1_, f32[768]{0:T(1024)S(1)} %add.147), kind=kOutput, calls=%fused_computation.2 | convolution fusion | flops 10072621056 | bytes 21859328 | tf_op jit(solution)/shard_map/dot_general | solution.py:924
  300.9 8.7 copy.242.qkv
  309.6 42.6 %attend.1 = (bf16[4096,256]{1,0:T(8,128)(2,1)S(1)}, f32[4096,256]{1,0:T(8,128)}, f32[4096,256]{1,0:T(8,128)}) custom-call(s32[7,25]{1,0:T(8,128)S(1)} %stack.191.tab, bf16[4096,768]{1,0:T(8,128)(2,1)} %copy.242.qkv), custom_call_target="tpu_custom_call" | custom-call | flops 26843545600 | bytes 16777216 | tf_op jit(solution)/shard_map/attend/pallas_call | solution.py:667
  353.5 25.7 %to_tokens.1 = bf16[512,2048]{1,0:T(8,128)(2,1)} custom-call(bf16[8,512,256]{2,1,0:T(8,128)(2,1)} %bitcast.145), custom_call_target="tpu_custom_call" | custom-call | bytes 41943040 | tf_op jit(solution)/shard_map/to_tokens/pallas_call | solution.py:579
  379.2 7.1 fusion.34
  388.6 67.7 %gather_two.1 = (bf16[16,256,1600]{2,1,0:T(8,128)(2,1)}, bf16[16,256,800]{2,1,0:T(8,128)(2,1)}, bf16[16,256,800]{2,1,0:T(8,128)(2,1)}) custom-call(bf16[512,1600]{1,0:T(8,128)(2,1)} %add_convert_fusion.3.refs_0_, bf16[1600,800]{1,0:T(8,128)(2,1)} %all-gather.10.cloned.1.call-done.refs_1_.refs_4_, f32[1,800]{1,0:T(1,128)} %reshape.311.refs_2_), custom_call_target="tpu_custom_call" | custom-call | bytes 222822400 | tf_op jit(solution)/shard_map/gather_two/pallas_call | solution.py:179
  456.3 82.0 %scatter_two.1 = (f32[512,1600]{1,0:T(8,128)}, bf16[16,256,800]{2,1,0:T(8,128)(2,1)}, bf16[16,256,1600]{2,1,0:T(8,128)(2,1)}) custom-call(bf16[16,256,1600]{2,1,0:T(8,128)(2,1)} %bitcast.149, bf16[16,256,800]{2,1,0:T(8,128)(2,1)} %get-tuple-element.36.refs_1_, bf16[16,256,800]{2,1,0:T(8,128)(2,1)} %get-tuple-element.37.refs_2_, ...), custom_call_target="tpu_custom_call" | custom-call | bytes 222822400 | tf_op jit(solution)/shard_map/scatter_two/pallas_call | solution.py:368
  538.3 3.2 multiply_reduce_fusion
  545.6 5.5 convolution_convert_fusion
  551.2 3.3 slice_bitcast_fusion.kt
  554.5 8.4 convolution_convert_fusion.3
  562.9 3.6 copy.268
  566.6 3.1 pad.23.x_ref
  569.7 41.6 %to_heads.1 = bf16[8,512,256]{2,1,0:T(8,128)(2,1)} custom-call(bf16[512,2048]{1,0:T(8,128)(2,1)} %pad.23.x_ref), custom_call_target="tpu_custom_call" | custom-call | bytes 41943040 | tf_op jit(solution)/shard_map/to_heads/pallas_call | solution.py:579
  611.2 89.7 %attend_back.1 = bf16[4096,768]{1,0:T(8,128)(2,1)} custom-call(s32[7,25]{1,0:T(8,128)} %copy-done.1, bf16[4096,768]{1,0:T(8,128)(2,1)} %copy.242.qkv, bf16[256,4096]{1,0:T(8,128)(2,1)} %slice_bitcast_fusion.kt, bf16[4096,256]{1,0:T(8,128)(2,1)} %bitcast.164, f32[4096,256]{1,0:T(8,128)} %get-tuple-element.43.att, f32[4096,256]{1,0:T(8,128)} %get-tuple-element.44.tot), custom_call_target="tpu_custom_call" | custom-call | flops 33554432000 | bytes 33554432 | tf_op jit(solution)/shard_map/attend_back/pallas_call | solution.py:750
  700.9 17.9 %convolution_convert_fusion.2 = bf16[1600,768]{1,0:T(8,128)(2,1)} fusion(bf16[4096,1600]{1,0:T(8,128)(2,1)} %bitcast.151, bf16[4096,768]{1,0:T(8,128)(2,1)} %attend_back.1), kind=kOutput, calls=%fused_computation.34 | convolution fusion | flops 10067558400 | bytes 21856256 | tf_op jit(solution)/shard_map/dot_general | solution.py:768
  718.9 18.4 %convolution_convert_fusion.1 = bf16[800,1600]{1,0:T(8,128)(2,1)} fusion(bf16[4096,800]{1,0:T(8,128)(2,1)} %bitcast.153, bf16[4096,1600]{1,0:T(8,128)(2,1)} %constant_dynamic-update-slice_fusion), kind=kOutput, calls=%fused_computation.20 | convolution fusion | flops 10487040000 | bytes 22220800 | tf_op jit(solution)/shard_map/dot_general | solution.py:768
  737.4 19.2 %bitcast_convert_fusion = bf16[1600,800]{1,0:T(8,128)(2,1)} fusion(bf16[16,256,1600]{2,1,0:T(8,128)(2,1)} %get-tuple-element.47, bf16[16,256,800]{2,1,0:T(8,128)(2,1)} %get-tuple-element.45), kind=kOutput, calls=%fused_computation.5 | convolution fusion | flops 10487040000 | bytes 22220800 | tf_op jit(solution)/shard_map/dot_general | solution.py:768
  759.0 11.6 %reduce-scatter.15.cloned.1.call-done = bf16[400,768]{1,0:T(8,128)(2,1)} async-done(((bf16[1600,768]{1,0:T(8,128)(2,1)}), bf16[400,768]{1,0:T(8,128)(2,1)}) %reduce-scatter.15.cloned.1.call-update) | async-done | bytes 614416 | tf_op jit(solution)/shard_map/reduce_scatter | solution.py:1010
  770.7 2.8 reshape.327
  774.3 4.2 convert_reduce_fusion
  781.5 3.7 convert_reduce_fusion.1
  785.2 68.1 %scatter_one.1 = f32[512,1600]{1,0:T(8,128)} custom-call(bf16[16,256,768]{2,1,0:T(8,128)(2,1)} %bitcast.148, bf16[1600,768]{1,0:T(8,128)(2,1)} %all-gather.6.cloned.1.call-done.refs_1_), custom_call_target="tpu_custom_call" | custom-call | bytes 222822400 | tf_op jit(solution)/shard_map/scatter_one/pallas_call | solution.py:368
  853.3 3.5 fusion.26
  859.7 3.1 all_to_all.14
  865.1 5.8 all-to-all-start.1
  874.1 9.8 reduce-scatter.17.cloned.1.call-done
  883.9 3.3 reshape.329
  891.8 5.6 all-to-all-start
  898.1 21.9 %sum_vectors.1 = f32[40,128]{1,0:T(8,128)} custom-call(f32[4,40,128]{2,1,0:T(8,128)} %bitcast.168), custom_call_target="tpu_custom_call" | custom-call | tf_op jit(solution)/shard_map/sum_vectors/pallas_call | solution.py:826
  922.7 5.8 fusion.16
  928.6 3.6 copy.276
  935.3 3.0 copy.278
  942.0 3.2 reshape.340
  948.8 12.6 %all-gather.14.cloned.1.call-done = bf16[400,3,2048]{2,1,0:T(4,128)(2,1)} async-done(((bf16[400,3,256]{2,1,0:T(4,128)(2,1)}), bf16[400,3,2048]{2,1,0:T(4,128)(2,1)}) %all-gather.14.cloned.1.call-update) | async-done | bytes 4915216 | tf_op jit(solution)/shard_map/all_gather | solution.py:1011
  961.4 6.7 slice.202
  968.1 11.5 %reshape.328 = bf16[400,4800]{1,0:T(8,128)(2,1)} reshape(bf16[400,3,1600]{2,1,0:T(4,128)(2,1)} %slice.202) | data formatting | bytes 7680000 | tf_op jit(solution)/shard_map/reshape | solution.py:1012
  982.0 80.7 %reduce-scatter.13.cloned.1.call-done = bf16[512,1600]{1,0:T(8,128)(2,1)} async-done(((bf16[4096,1600]{1,0:T(8,128)(2,1)}), bf16[512,1600]{1,0:T(8,128)(2,1)}) %reduce-scatter.13.cloned.1.call-update) | async-done | bytes 1638416 | tf_op jit(solution)/shard_map/reduce_scatter | solution.py:985
  1062.7 3.1 fusion.15
  1065.8 3.6 copy.275
  (296 shorter events, 126.7 us)
Async XLA Ops:
  7.2 276.4 %all-gather.6.cloned.1.call-start = ((), (), s32[]{:S(2)}) async-start(), calls=%async_computation.8 | async-start | bytes 3072000 | tf_op jit(solution)/shard_map/all_gather | solution.py:910
  76.9 26.0 %copy-start.12 = (bf16[4,400,200]{2,1,0:T(8,128)(2,1)S(1)}, bf16[4,400,200]{2,1,0:T(8,128)(2,1)}, u32[]{:S(2)}) copy-start(bf16[4,400,200]{2,1,0:T(8,128)(2,1)} %get-tuple-element.35) | copy-start | bytes 1920004
  77.9 301.3 %all-gather.8.cloned.1.call-start = ((), (), s32[]{:S(2)}) async-start(), calls=%async_computation.9 | async-start | bytes 5990400 | tf_op jit(solution)/shard_map/all_gather | solution.py:911
  102.8 285.8 %all-gather.10.cloned.1.call-start = ((), (), s32[]{:S(2)}) async-start(), calls=%async_computation.10 | async-start | bytes 3584000 | tf_op jit(solution)/shard_map/all_gather | solution.py:913
  104.8 351.5 %all-gather.12.cloned.1.call-start = ((), (), s32[]{:S(2)}) async-start(), calls=%async_computation.11 | async-start | bytes 3328000 | tf_op jit(solution)/shard_map/all_gather | solution.py:915
  110.8 101.1 %copy-start.5 = (bf16[1,512,1600]{2,1,0:T(8,128)(2,1)}, bf16[1,512,1600]{2,1,0:T(8,128)(2,1)S(1)}, u32[]{:S(2)}) copy-start(bf16[1,512,1600]{2,1,0:T(8,128)(2,1)S(1)} %copy.245) | copy-start | bytes 4915204
  202.0 43.6 %collective-permute-start.6 = (bf16[256,1600]{0,1:T(8,128)(2,1)}, bf16[256,1600]{0,1:T(8,128)(2,1)}, u32[]{:S(2)}, u32[]{:S(2)}) collective-permute-start(bf16[256,1600]{0,1:T(8,128)(2,1)} %copy.246), channel_id=1, source_target_pairs={{0,16},{4,20},{8,24},{12,28},{16,0},{20,4},{24,8},{28,12},{1,17},{... | collective-permute-start | bytes 2457608 | tf_op jit(solution)/shard_map/ppermute | solution.py:935
  204.7 26.4 %collective-permute-start.2 = (bf16[256,1600]{0,1:T(8,128)(2,1)}, bf16[256,1600]{0,1:T(8,128)(2,1)}, u32[]{:S(2)}, u32[]{:S(2)}) collective-permute-start(bf16[256,1600]{0,1:T(8,128)(2,1)} %copy.246), channel_id=1, source_target_pairs={{0,8},{4,12},{8,0},{12,4},{16,24},{20,28},{24,16},{28,20},{1,9},{5... | collective-permute-start | bytes 2457608 | tf_op jit(solution)/shard_map/ppermute | solution.py:935
  204.8 27.7 %collective-permute-start = (bf16[256,1600]{0,1:T(8,128)(2,1)}, bf16[256,1600]{0,1:T(8,128)(2,1)}, u32[]{:S(2)}, u32[]{:S(2)}) collective-permute-start(bf16[256,1600]{0,1:T(8,128)(2,1)} %copy.246), channel_id=1, source_target_pairs={{0,4},{4,0},{8,12},{12,8},{16,20},{20,16},{24,28},{28,24},{1,5},{5... | collective-permute-start | bytes 2457608 | tf_op jit(solution)/shard_map/ppermute | solution.py:937
  206.6 35.8 %collective-permute-start.3 = (bf16[256,1600]{0,1:T(8,128)(2,1)}, bf16[256,1600]{0,1:T(8,128)(2,1)S(1)}, u32[]{:S(2)}, u32[]{:S(2)}) collective-permute-start(bf16[256,1600]{0,1:T(8,128)(2,1)} %copy.247), channel_id=1, source_target_pairs={{0,8},{4,12},{8,0},{12,4},{16,24},{20,28},{24,16},{28,20},{1,9},{5... | collective-permute-start | bytes 2457608 | tf_op jit(solution)/shard_map/ppermute | solution.py:935
  207.5 38.3 %collective-permute-start.1 = (bf16[256,1600]{0,1:T(8,128)(2,1)}, bf16[256,1600]{0,1:T(8,128)(2,1)}, u32[]{:S(2)}, u32[]{:S(2)}) collective-permute-start(bf16[256,1600]{0,1:T(8,128)(2,1)} %copy.247), channel_id=1, source_target_pairs={{0,4},{4,0},{8,12},{12,8},{16,20},{20,16},{24,28},{28,24},{1,5},{5... | collective-permute-start | bytes 2457608 | tf_op jit(solution)/shard_map/ppermute | solution.py:937
  209.5 22.7 %copy-start.32 = (s32[7,1]{1,0:T(8,128)S(1)}, s32[7,1]{1,0:T(8,128)}, u32[]{:S(2)}) copy-start(s32[7,1]{1,0:T(8,128)} %constant.134.clone.1) | copy-start | bytes 88
  209.5 22.7 %copy-start.33 = (s32[7,1]{1,0:T(8,128)S(1)}, s32[7,1]{1,0:T(8,128)}, u32[]{:S(2)}) copy-start(s32[7,1]{1,0:T(8,128)} %constant.133.clone.1) | copy-start | bytes 88
  209.6 22.7 %copy-start.34 = (s32[7,1]{1,0:T(8,128)S(1)}, s32[7,1]{1,0:T(8,128)}, u32[]{:S(2)}) copy-start(s32[7,1]{1,0:T(8,128)} %constant.130.clone.1) | copy-start | bytes 88
  209.6 22.7 %copy-start.35 = (s32[7,1]{1,0:T(8,128)S(1)}, s32[7,1]{1,0:T(8,128)}, u32[]{:S(2)}) copy-start(s32[7,1]{1,0:T(8,128)} %constant.129.clone.1) | copy-start | bytes 88
  209.6 22.7 %copy-start.36 = (s32[7,1]{1,0:T(8,128)S(1)}, s32[7,1]{1,0:T(8,128)}, u32[]{:S(2)}) copy-start(s32[7,1]{1,0:T(8,128)} %constant.126.clone.1) | copy-start | bytes 88
  209.6 22.7 %copy-start.37 = (s32[7,1]{1,0:T(8,128)S(1)}, s32[7,1]{1,0:T(8,128)}, u32[]{:S(2)}) copy-start(s32[7,1]{1,0:T(8,128)} %constant.125.clone.1) | copy-start | bytes 88
  209.6 22.7 %copy-start.38 = (s32[7,1]{1,0:T(8,128)S(1)}, s32[7,1]{1,0:T(8,128)}, u32[]{:S(2)}) copy-start(s32[7,1]{1,0:T(8,128)} %constant.116.clone.1) | copy-start | bytes 88
  209.6 22.7 %copy-start.39 = (s32[7,1]{1,0:T(8,128)S(1)}, s32[7,1]{1,0:T(8,128)}, u32[]{:S(2)}) copy-start(s32[7,1]{1,0:T(8,128)} %constant.115.clone.1) | copy-start | bytes 88
  209.6 22.7 %copy-start.40 = (s32[7,1]{1,0:T(8,128)S(1)}, s32[7,1]{1,0:T(8,128)}, u32[]{:S(2)}) copy-start(s32[7,1]{1,0:T(8,128)} %constant.113.clone.1) | copy-start | bytes 88
  209.6 22.7 %copy-start.41 = (s32[7,1]{1,0:T(8,128)S(1)}, s32[7,1]{1,0:T(8,128)}, u32[]{:S(2)}) copy-start(s32[7,1]{1,0:T(8,128)} %constant.112.clone.1) | copy-start | bytes 88
  209.7 22.7 %copy-start.42 = (s32[7,1]{1,0:T(8,128)S(1)}, s32[7,1]{1,0:T(8,128)}, u32[]{:S(2)}) copy-start(s32[7,1]{1,0:T(8,128)} %constant.108.clone.1) | copy-start | bytes 88
  209.7 22.7 %copy-start.43 = (s32[7,1]{1,0:T(8,128)S(1)}, s32[7,1]{1,0:T(8,128)}, u32[]{:S(2)}) copy-start(s32[7,1]{1,0:T(8,128)} %constant.107.clone.1) | copy-start | bytes 88
  209.7 22.7 %copy-start.44 = (s32[7,1]{1,0:T(8,128)S(1)}, s32[7,1]{1,0:T(8,128)}, u32[]{:S(2)}) copy-start(s32[7,1]{1,0:T(8,128)} %constant.106.clone.1) | copy-start | bytes 88
  209.7 22.7 %copy-start.45 = (s32[7,1]{1,0:T(8,128)S(1)}, s32[7,1]{1,0:T(8,128)}, u32[]{:S(2)}) copy-start(s32[7,1]{1,0:T(8,128)} %constant.105.clone.1) | copy-start | bytes 88
  211.5 545.2 %reduce-scatter.21.cloned.1.call-start = ((), (), s32[]{:S(2)}) async-start(), calls=%async_computation.17 | async-start | bytes 5990400
  231.1 20.3 %collective-permute-start.7 = (bf16[256,1600]{0,1:T(8,128)(2,1)}, bf16[256,1600]{0,1:T(8,128)(2,1)}, u32[]{:S(2)}, u32[]{:S(2)}) collective-permute-start(bf16[256,1600]{0,1:T(8,128)(2,1)} %copy.247), channel_id=1, source_target_pairs={{0,16},{4,20},{8,24},{12,28},{16,0},{20,4},{24,8},{28,12},{1,17},{... | collective-permute-start | bytes 2457608 | tf_op jit(solution)/shard_map/ppermute | solution.py:935
  232.5 77.1 %copy-start.1 = (s32[7,25]{1,0:T(8,128)}, s32[7,25]{1,0:T(8,128)S(1)}, u32[]{:S(2)}) copy-start(s32[7,25]{1,0:T(8,128)S(1)} %stack.191.tab) | copy-start | bytes 2104
  232.5 23.3 %collective-permute-start.4 = (bf16[256,1600]{0,1:T(8,128)(2,1)}, bf16[256,1600]{0,1:T(8,128)(2,1)}, u32[]{:S(2)}, u32[]{:S(2)}) collective-permute-start(bf16[256,1600]{0,1:T(8,128)(2,1)} %collective-permute-done.2), channel_id=1, source_target_pairs={{0,4},{4,0},{8,12},{12,8},{16,20},{20,16},{24,28},{28,24},{1,5},{5... | collective-permute-start | bytes 2457608 | tf_op jit(solution)/shard_map/ppermute | solution.py:937
  242.5 16.5 %collective-permute-start.5 = (bf16[256,1600]{0,1:T(8,128)(2,1)S(1)}, bf16[256,1600]{0,1:T(8,128)(2,1)}, u32[]{:S(2)}, u32[]{:S(2)}) collective-permute-start(bf16[256,1600]{0,1:T(8,128)(2,1)S(1)} %collective-permute-done.3), channel_id=1, source_target_pairs={{0,4},{4,0},{8,12},{12,8},{16,20},{20,16},{24,28},{28,24},{1,5},{5... | collective-permute-start | bytes 2457608 | tf_op jit(solution)/shard_map/ppermute | solution.py:937
  245.6 23.3 %collective-permute-start.10 = (bf16[256,1600]{0,1:T(8,128)(2,1)}, bf16[256,1600]{0,1:T(8,128)(2,1)}, u32[]{:S(2)}, u32[]{:S(2)}) collective-permute-start(bf16[256,1600]{0,1:T(8,128)(2,1)} %collective-permute-done.2), channel_id=1, source_target_pairs={{0,16},{4,20},{8,24},{12,28},{16,0},{20,4},{24,8},{28,12},{1,17},{... | collective-permute-start | bytes 2457608 | tf_op jit(solution)/shard_map/ppermute | solution.py:935
  245.7 16.7 %collective-permute-start.8 = (bf16[256,1600]{0,1:T(8,128)(2,1)}, bf16[256,1600]{0,1:T(8,128)(2,1)}, u32[]{:S(2)}, u32[]{:S(2)}) collective-permute-start(bf16[256,1600]{0,1:T(8,128)(2,1)} %collective-permute-done.6), channel_id=1, source_target_pairs={{0,4},{4,0},{8,12},{12,8},{16,20},{20,16},{24,28},{28,24},{1,5},{5... | collective-permute-start | bytes 2457608 | tf_op jit(solution)/shard_map/ppermute | solution.py:937
  251.4 21.3 %collective-permute-start.11 = (bf16[256,1600]{0,1:T(8,128)(2,1)}, bf16[256,1600]{0,1:T(8,128)(2,1)}, u32[]{:S(2)}, u32[]{:S(2)}) collective-permute-start(bf16[256,1600]{0,1:T(8,128)(2,1)} %collective-permute-done.7), channel_id=1, source_target_pairs={{0,8},{4,12},{8,0},{12,4},{16,24},{20,28},{24,16},{28,20},{1,9},{5... | collective-permute-start | bytes 2457608 | tf_op jit(solution)/shard_map/ppermute | solution.py:935
  255.8 16.8 %collective-permute-start.9 = (bf16[256,1600]{0,1:T(8,128)(2,1)}, bf16[256,1600]{0,1:T(8,128)(2,1)}, u32[]{:S(2)}, u32[]{:S(2)}) collective-permute-start(bf16[256,1600]{0,1:T(8,128)(2,1)} %collective-permute-done.7), channel_id=1, source_target_pairs={{0,4},{4,0},{8,12},{12,8},{16,20},{20,16},{24,28},{28,24},{1,5},{5... | collective-permute-start | bytes 2457608 | tf_op jit(solution)/shard_map/ppermute | solution.py:937
  268.9 11.3 %collective-permute-start.12 = (bf16[256,1600]{0,1:T(8,128)(2,1)}, bf16[256,1600]{0,1:T(8,128)(2,1)S(1)}, u32[]{:S(2)}, u32[]{:S(2)}) collective-permute-start(bf16[256,1600]{0,1:T(8,128)(2,1)} %collective-permute-done.10), channel_id=1, source_target_pairs={{0,4},{4,0},{8,12},{12,8},{16,20},{20,16},{24,28},{28,24},{1,5},{5... | collective-permute-start | bytes 2457608 | tf_op jit(solution)/shard_map/ppermute | solution.py:937
  272.6 9.2 collective-permute-start.13
  551.2 219.5 %reduce-scatter.15.cloned.1.call-start = ((), (), s32[]{:S(2)}) async-start(), calls=%async_computation.13 | async-start | bytes 3072000 | tf_op jit(solution)/shard_map/reduce_scatter | solution.py:1010
  718.9 140.8 %reduce-scatter.23.cloned.1.call-start = ((), (), s32[]{:S(2)}) async-start(), calls=%async_computation.18 | async-start | bytes 3328000
  737.3 146.6 %reduce-scatter.17.cloned.1.call-start = ((), (), s32[]{:S(2)}) async-start(), calls=%async_computation.15 | async-start | bytes 3584000 | tf_op jit(solution)/shard_map/reduce_scatter | solution.py:1001
  756.6 188.6 %reduce-scatter.19.cloned.1.call-start = ((), (), s32[]{:S(2)}) async-start(), calls=%async_computation.16 | async-start | bytes 1024000
  759.0 202.4 %all-gather.14.cloned.1.call-start = ((), (), s32[]{:S(2)}) async-start(), calls=%async_computation.14 | async-start | bytes 7372800 | tf_op jit(solution)/shard_map/all_gather | solution.py:1011
  773.5 289.2 %reduce-scatter.13.cloned.1.call-start = ((), (), s32[]{:S(2)}) async-start(), calls=%async_computation.12 | async-start | bytes 15335424 | tf_op jit(solution)/shard_map/reduce_scatter | solution.py:985
  785.2 68.1 %copy-start.15 = (f32[1600]{0:T(1024)S(1)}, f32[1600]{0:T(1024)}, u32[]{:S(2)}) copy-start(f32[1600]{0:T(1024)} %copy-done.14) | copy-start | bytes 19204
  785.2 68.1 %copy-start.19 = (f32[512]{0:T(512)S(1)}, f32[512]{0:T(512)}, u32[]{:S(2)}) copy-start(f32[512]{0:T(512)} %copy-done.18) | copy-start | bytes 6148
  865.1 24.3 %all-to-all-start.1 = ((bf16[200,8,200]{2,0,1:T(8,128)(2,1)}), bf16[200,8,200]{2,0,1:T(8,128)(2,1)}, u32[]{:S(2)}, u32[]{:S(2)}) async-start(bf16[200,8,200]{2,0,1:T(8,128)(2,1)} %copy.274), calls=%async_computation.4 | async-start | bytes 1638400 | tf_op jit(solution)/shard_map/all_to_all | solution.py:1000
  889.4 33.4 %copy-start.26 = (f32[512]{0:T(512)S(1)}, f32[512]{0:T(512)}, u32[]{:S(2)}) copy-start(f32[512]{0:T(512)} %copy-done.25) | copy-start | bytes 6148
  889.4 33.4 %copy-start.28 = (f32[512]{0:T(512)S(1)}, f32[512]{0:T(512)}, u32[]{:S(2)}) copy-start(f32[512]{0:T(512)} %copy-done.27) | copy-start | bytes 6148
  891.8 46.4 %all-to-all-start = ((bf16[8,400,200]{2,1,0:T(8,128)(2,1)}), bf16[8,400,200]{2,1,0:T(8,128)(2,1)}, u32[]{:S(2)}, u32[]{:S(2)}) async-start(bf16[8,400,200]{2,1,0:T(8,128)(2,1)} %bitcast.154), calls=%async_computation.3 | async-start | bytes 3276800 | tf_op jit(solution)/shard_map/all_to_all | solution.py:1003
  (26 other events, 119.1 us)
Sparse Core Ops, SparseCore 0:
  78.0 56.6 all-gather.5
  137.1 60.6 all-gather.7
  199.9 60.1 all-gather.9
  262.2 54.2 all-gather.11
  551.3 82.2 reduce-scatter.20
  719.0 51.6 reduce-scatter.14
  773.1 52.2 reduce-scatter.22
  827.8 56.0 reduce-scatter.16
  886.3 24.7 reduce-scatter.18
  913.5 47.7 all-gather.13
  965.3 97.3 reduce-scatter.12

commit v2 on v1

v2 whole, which is shorter than its diff:
```python
import functools
import math

import jax
import jax.numpy as jnp
import numpy as np
from jax import lax
from jax.experimental import pallas as pl
from jax.experimental.layout import Layout, with_layout_constraint
from jax.experimental.pallas import tpu as pltpu
from jax.sharding import PartitionSpec as P

MESH = pl.DeviceIdType.MESH
HEADS = 25
SMALL = pl.CostEstimate(flops=0, bytes_accessed=1 << 20, transcendentals=0)


def route_bits(n):
    bits = []
    b = 2
    while b < n:
        bits.append(b)
        b *= 2
    return bits


def flip(a, b):
    return jnp.where(lax.rem(lax.div(a, b), 2) == 0, a + b, a - b)


def place(me, r, n):
    if isinstance(r, int):
        for b in [1] + route_bits(n):
            if r & b:
                me = flip(me, b)
        return me
    for b in [1] + route_bits(n):
        me = jnp.where(lax.rem(lax.div(r, b), 2) == 0, me, flip(me, b))
    return me


def pick(table, q):
    value = jnp.int32(table[0])
    for i, entry in enumerate(table[1:]):
        value = jnp.where(q == i + 1, jnp.int32(entry), value)
    return value


def greet(ids):
    barrier = pltpu.get_barrier_semaphore()
    for i in ids:
        pl.semaphore_signal(barrier, inc=1, device_id=i, device_id_type=MESH)
    pl.semaphore_wait(barrier, len(ids))


def remote(src, dst, send, recv, device):
    return pltpu.make_async_remote_copy(
        src_ref=src, dst_ref=dst, send_sem=send, recv_sem=recv, device_id=device, device_id_type=MESH
    )


class Blocks:
    def __init__(self, axis, size, same, source, target, send, recv, local):
        self.axis, self.size, self.same = axis, size, same
        self.source, self.target = source, target
        self.send, self.recv, self.local = send, recv, local
        self.me = lax.axis_index(axis)

    @staticmethod
    def scratch(size):
        dma = pltpu.SemaphoreType.DMA
        return [dma((size - 1,)), dma((size - 1,)), dma]

    def peers(self):
        return [{self.axis: lax.rem(self.me + d, self.size)} for d in range(1, self.size)]

    def copy(self, d):
        to = lax.rem(self.me + d, self.size)
        src = self.source if self.same else self.source.at[to]
        return remote(src, self.target.at[self.me], self.send.at[d - 1], self.recv.at[d - 1], {self.axis: to})

    def own(self):
        src = self.source if self.same else self.source.at[self.me]
        return pltpu.make_async_copy(src, self.target.at[self.me], self.local)

    def start(self):
        for d in range(1, self.size):
            self.copy(d).start()
        self.own().start()

    def finish(self):
        for d in range(1, self.size):
            dst = self.target.at[lax.rem(self.me + self.size - d, self.size)]
            remote(dst, dst, self.send.at[d - 1], self.recv.at[d - 1], {self.axis: self.me}).wait_recv()
        self.own().wait()
        for d in range(1, self.size):
            self.copy(d).wait_send()


def blocks_shape(x, size, same):
    return jax.ShapeDtypeStruct(((size,) + x.shape) if same else x.shape, x.dtype)


def arrival_order(n):
    bits = route_bits(n)
    orders = [bits, bits[::-1]]
    lists = []
    for order in orders:
        held, phases = [0], [-1]
        for i, b in enumerate(order):
            fresh = [h ^ b for h in held]
            held, phases = held + fresh, phases + [i] * len(fresh)
        lists.append(list(zip(held, phases)))
    entries = []
    for i in range(n // 2):
        for odd in (0, 1):
            for half in (0, 1):
                k, phase = lists[half][i]
                entries.append((half, k ^ odd, phase, odd))
    return orders, entries


def gather_kernel(n, h, body, n_const, n_out, relative, modes, nf, same, second, *refs):
    if second:
        at = 1 + n_const
        out = at + 1 + min(nf, 1) + 1 + n_out
        w_ref, w_all = refs[at], refs[out]
        w_send, w_recv, w_keep = refs[-3:]
        refs = refs[:at] + refs[at + 1 : out] + refs[out + 1 : -3]
        w_half = w_ref.shape[1] // 2
    refs, rider = split_rider(refs, nf, same, 1 + n_const, 1 + n_out)
    x_ref = refs[0]
    consts = refs[1 : 1 + n_const]
    all_ref = refs[1 + n_const]
    outs = refs[2 + n_const : 2 + n_const + n_out]
    held = refs[2 + n_const + n_out]
    stages = refs[3 + n_const + n_out : 3 + n_const + 2 * n_out]
    send, recv, keep, store = refs[3 + n_const + 2 * n_out :]
    me = lax.axis_index("seq")
    orders, entries = arrival_order(n)
    bits = orders[0]
    nb = len(bits)

    def device(b):
        return {"seq": flip(me, b)}

    def spot(half, k):
        return 2 * (k if relative else place(me, k, n)) + half

    def ship(half, k, b):
        at = spot(half, k)
        src = x_ref.at[pl.ds(half * h, h)] if isinstance(k, int) and k == 0 else held.at[at]
        lane = 0 if b == 1 else 1 + bits.index(b)
        to = k ^ b if isinstance(k, int) else place(k, b, n)
        dst = 2 * to + half if relative else at
        first = remote(src, held.at[dst], send.at[half, lane, k], recv.at[half, to], device(b))
        if not second:
            return [first]
        owner = place(me, k, n)
        lanes = pl.ds(half * w_half, w_half)
        src = w_ref if isinstance(k, int) and k == 0 else w_all.at[owner]
        other = remote(
            src.at[:, lanes], w_all.at[owner].at[:, lanes], w_send.at[half, lane, k], w_recv.at[half, to], device(b)
        )
        return [first, other]

    def each(copies, act):
        for c in copies:
            act(c)

    def w_arrive(half, k):
        dst = w_all.at[place(me, k, n)].at[:, pl.ds(0, w_half)]
        remote(dst, dst, w_send.at[0, 0, 0], w_recv.at[half, k], device(1)).wait_recv()

    greet([device(b) for b in [1] + bits] + (rider.peers() if nf else []))
    for i in range(nb):
        for half in (0, 1):
            each(ship(half, 0, orders[half][i]), lambda c: c.start())
    for half in (0, 1):
        each(ship(half, 0, 1), lambda c: c.start())
    if second:
        pltpu.make_async_copy(w_ref, w_all.at[me], w_keep).start()
    if nf:
        rider.start()

    def output(o, q, at):
        slot = lax.rem(q, 2)
        return pltpu.make_async_copy(stages[o].at[slot], outs[o].at[at], store.at[o, slot])

    def entry(q, at, value):
        results = body(value, *consts)
        for o in range(n_out):

            @pl.when(q >= 2)
            def _(o=o):
                output(o, q, at[modes[o]]).wait()

            stages[o][lax.rem(q, 2)] = results[o]
            output(o, q, at[modes[o]]).start()

    def step(q, carry):
        half = pick([e[0] for e in entries], q)
        k = pick([e[1] for e in entries], q)
        phase = pick([e[2] for e in entries], q)
        odd = pick([e[3] for e in entries], q)
        at = spot(half, k)

        @pl.when(k == 0)
        def _():
            held[at] = x_ref[pl.ds(pl.multiple_of(half * h, h), h)]

        @pl.when(k != 0)
        def _():
            remote(held.at[at], held.at[at], send.at[0, 0, 0], recv.at[half, k], device(1)).wait_recv()
            if second:
                w_arrive(half, k)

        for side in (0, 1):
            for i in range(nb):

                @pl.when((half == side) & (odd == 0) & (k != 0) & (phase < i))
                def _(side=side, i=i):
                    each(ship(side, k, orders[side][i]), lambda c: c.start())

            @pl.when((half == side) & (odd == 0) & (k != 0))
            def _(side=side):
                each(ship(side, k, 1), lambda c: c.start())

        pltpu.make_async_copy(held.at[at], all_ref.at[at], keep.at[q]).start()
        if n_out:
            entry(q, (2 * place(me, k, n) + half, 2 * k + half), held[at])
        return carry

    lax.fori_loop(0, 2 * n, step, 0)
    for q, (half, k, phase, odd) in enumerate(entries):
        at = spot(half, k)
        pltpu.make_async_copy(held.at[at], all_ref.at[at], keep.at[q]).wait()
        if q >= 2 * n - 2:
            for o in range(n_out):
                output(o, jnp.int32(q), at).wait()
        if not odd:
            for i in range(nb):
                if phase < i:
                    each(ship(half, k, orders[half][i]), lambda c: c.wait_send())
            each(ship(half, k, 1), lambda c: c.wait_send())
    if second:
        pltpu.make_async_copy(w_ref, w_all.at[me], w_keep).wait()
    if nf:
        rider.finish()


def split_rider(refs, nf, same, n_in, n_out):
    if not nf:
        return refs, None
    source = refs[n_in]
    target = refs[n_in + 1 + n_out]
    rider = Blocks("fsdp", nf, same, source, target, *refs[-3:])
    return refs[:n_in] + refs[n_in + 1 : n_in + 1 + n_out] + refs[n_in + 2 + n_out : -3], rider


def rider_parts(rider):
    if rider is None:
        return [], [], [], [], 0, False
    x, same, nf = rider
    hbm = [pl.BlockSpec(memory_space=pl.ANY)]
    return [x], hbm, [blocks_shape(x, nf, same)], Blocks.scratch(nf), nf, same


def seq_gather(x, n, ident, name, body=None, consts=(), outs=(), relative=False, modes=None, rider=None, second=None):
    rows, cols = x.shape
    h = rows // 2
    nb = len(route_bits(n))
    shapes = [jax.ShapeDtypeStruct((2 * n, h, c), d) for c, d in outs]
    vmem = pl.BlockSpec(memory_space=pltpu.VMEM)
    hbm = pl.BlockSpec(memory_space=pl.ANY)
    more, spec, shape, scratch, nf, same = rider_parts(rider)
    also = [] if second is None else [second]
    out = pl.pallas_call(
        functools.partial(
            gather_kernel, n, h, body, len(consts), len(outs), relative, modes, nf, same, second is not None
        ),
        out_shape=[jax.ShapeDtypeStruct((2 * n, h, cols), x.dtype)]
        + shapes
        + [jax.ShapeDtypeStruct((n,) + w.shape, w.dtype) for w in also]
        + shape,
        in_specs=[vmem] * (1 + len(consts)) + [hbm] * len(also) + spec,
        out_specs=[hbm] * (1 + len(outs)) + [hbm] * len(also) + spec,
        scratch_shapes=[pltpu.VMEM((2 * n, h, cols), x.dtype)]
        + [pltpu.VMEM((2, h, c), d) for c, d in outs]
        + [
            pltpu.SemaphoreType.DMA((2, nb + 1, n)),
            pltpu.SemaphoreType.DMA((2, n)),
            pltpu.SemaphoreType.DMA((2 * n,)),
            pltpu.SemaphoreType.DMA((max(len(outs), 1), 2)),
        ]
        + scratch
        + [
            pltpu.SemaphoreType.DMA((2, nb + 1, n)),
            pltpu.SemaphoreType.DMA((2, n)),
            pltpu.SemaphoreType.DMA,
        ]
        * len(also),
        compiler_params=pltpu.CompilerParams(
            collective_id=ident, has_side_effects=True, vmem_limit_bytes=60 << 20
        ),
        cost_estimate=SMALL,
        name=name,
    )(x, *consts, *also, *more)
    return [o.reshape(2 * n * h, o.shape[2]) for o in out[: 1 + len(outs)]] + list(out[1 + len(outs) :])


class Side:
    def __init__(self, count, product, refs):
        self.count, self.product = count, product
        self.a, self.b, self.grad, self.made, self.acc, self.abuf, self.bbuf, self.mbuf, self.load, self.store = refs

    def fetch(self, i):
        slot = lax.rem(i, 2)
        return [
            pltpu.make_async_copy(self.a.at[i], self.abuf.at[slot], self.load.at[0, slot]),
            pltpu.make_async_copy(self.b.at[i], self.bbuf.at[slot], self.load.at[1, slot]),
        ]

    def output(self, i):
        slot = lax.rem(i, 2)
        return pltpu.make_async_copy(self.mbuf.at[slot], self.made.at[i], self.store.at[slot])

    def begin(self):
        self.acc[...] = jnp.zeros_like(self.acc)
        for c in self.fetch(jnp.int32(0)):
            c.start()

    def run(self, first, last):
        def step(i, carry):
            @pl.when(i + 1 < self.count)
            def _():
                for c in self.fetch(i + 1):
                    c.start()

            for c in self.fetch(i):
                c.wait()
            slot = lax.rem(i, 2)
            a, b = self.abuf[slot], self.bbuf[slot]
            self.acc[...] += lax.dot_general(
                a, b, (((0,), (0,)), ((), ())), preferred_element_type=jnp.float32
            )
            if self.product is not None:

                @pl.when(i >= 2)
                def _():
                    self.output(i).wait()

                self.mbuf[slot] = self.product(a)
                self.output(i).start()
            return carry

        lax.fori_loop(first, last, step, 0)

    def end(self):
        self.grad[...] = self.acc[...].astype(self.grad.dtype)
        if self.product is not None:
            for i in (self.count - 2, self.count - 1):
                self.output(jnp.int32(i)).wait()


def side_parts(side, count):
    if side is None:
        return [], [], [], [], []
    a, b, product, made = side
    h = a.shape[0] // count
    low = jnp.bfloat16
    made = made or 128
    hbm = pl.BlockSpec(memory_space=pl.ANY)
    vmem = pl.BlockSpec(memory_space=pltpu.VMEM)
    dma = pltpu.SemaphoreType.DMA
    return (
        [x.reshape(count, h, x.shape[1]) for x in (a, b)],
        [
            jax.ShapeDtypeStruct((a.shape[1], b.shape[1]), low),
            jax.ShapeDtypeStruct((count, h, made), low),
        ],
        [hbm, hbm],
        [vmem, hbm],
        [
            pltpu.VMEM((a.shape[1], b.shape[1]), jnp.float32),
            pltpu.VMEM((2, h, a.shape[1]), low),
            pltpu.VMEM((2, h, b.shape[1]), low),
            pltpu.VMEM((2, h, made), low),
            dma((2, 2)),
            dma((2,)),
        ],
    )


def scatter_order(n):
    bits = route_bits(n)
    orders = [bits, bits[::-1]]
    lists = [
        sorted(range(0, n, 2), key=lambda k: [-int(bool(k & b)) for b in order]) for order in orders
    ]
    return orders, [(half, lists[half][i]) for i in range(n // 2) for half in (0, 1)]


def scatter_kernel(n, h, body, n_in, n_const, n_out, modes, nf, same, product, *refs):
    side = None
    if product is not False:
        at = n_in + n_const
        out = at + 2 + min(nf, 1) + 1 + n_out
        extra = refs[at : at + 2] + refs[out : out + 2] + refs[-6:]
        refs = refs[:at] + refs[at + 2 : out] + refs[out + 2 : -6]
        consts = refs[n_in : n_in + n_const]
        make = None if product is None else lambda a: product(a, *consts)
        side = Side(2 * n, make, extra)
    refs, rider = split_rider(refs, nf, same, n_in + n_const, 1 + n_out)
    ins = refs[:n_in]
    consts = refs[n_in : n_in + n_const]
    at = n_in + n_const
    sum_ref = refs[at]
    outs = refs[at + 1 : at + 1 + n_out]
    at += 1 + n_out
    give, pair, own, far, total = refs[at : at + 5]
    at += 5
    loads = refs[at : at + n_in]
    stages = refs[at + n_in : at + n_in + n_out]
    pair_send, pair_recv, far_send, far_recv, load, store, done = refs[at + n_in + n_out :]
    me = lax.axis_index("seq")
    orders, entries = scatter_order(n)
    bits = orders[0]
    slots = give.shape[0]
    index = {e: j for j, e in enumerate(entries)}

    def device(b):
        return {"seq": flip(me, b)}

    def phase_of(half, k):
        for i, b in enumerate(orders[half]):
            if k & b:
                return i
        return len(bits)

    landing = {}
    for half in (0, 1):
        for i, b in enumerate(orders[half]):
            for k in range(0, n, 2):
                if phase_of(half, k) == i:
                    landing[half, i, k ^ b] = len(landing)

    halves = [e[0] for e in entries]
    ks = [e[1] for e in entries]

    def spot(q, relative):
        j = lax.div(q, 2)
        k = pick(ks, j)
        k = jnp.where(lax.rem(q, 2) == 0, flip(k, 1), k)
        return 2 * (k if relative else place(me, k, n)) + pick(halves, j)

    def fetch(q):
        slot = lax.rem(q, 2)
        return [
            pltpu.make_async_copy(ins[i].at[spot(q, modes[0][i])], loads[i].at[slot], load.at[i, slot])
            for i in range(n_in)
        ]

    def output(o, q):
        slot = lax.rem(q, 2)
        return pltpu.make_async_copy(stages[o].at[slot], outs[o].at[spot(q, modes[1][o])], store.at[o, slot])

    def hand(j):
        slot = lax.rem(j, slots)
        return remote(give.at[slot], pair.at[j], pair_send.at[j], pair_recv.at[j], device(1))

    def launch(half, k):
        i = phase_of(half, k)
        b = orders[half][i]
        to = landing[half, i, k ^ b]
        return remote(own.at[index[half, k]], far.at[to], far_send.at[to], far_recv.at[to], device(b))

    def join(j):
        hand(j).wait_recv()
        own[j] = (own[j].astype(jnp.float32) + pair[j].astype(jnp.float32)).astype(own.dtype)
        for e, (half, k) in enumerate(entries):
            if phase_of(half, k) == 0:

                @pl.when(j == e)
                def _(half=half, k=k):
                    launch(half, k).start()

    for c in fetch(jnp.int32(0)):
        c.start()
    greet([device(b) for b in [1] + bits] + (rider.peers() if nf else []))
    if nf:
        rider.start()

    def step(q, carry):
        j = lax.div(q, 2)
        slot = lax.rem(q, 2)

        @pl.when(q + 1 < 2 * n)
        def _():
            for c in fetch(q + 1):
                c.start()

        for c in fetch(q):
            c.wait()
        part, *results = body(*[r[slot] for r in loads], *consts)
        for o in range(n_out):

            @pl.when(q >= 2)
            def _(o=o):
                output(o, q).wait()

            stages[o][slot] = results[o]
            output(o, q).start()

        @pl.when(slot == 0)
        def _():
            @pl.when(j >= slots)
            def _():
                hand(j - slots).wait_send()

            give[lax.rem(j, slots)] = part.astype(give.dtype)
            hand(j).start()

        @pl.when(slot == 1)
        def _():
            own[j] = part.astype(own.dtype)

            @pl.when(j >= 1)
            def _():
                join(j - 1)

        return carry

    lax.fori_loop(0, 2 * n, step, 0)
    if side:
        side.begin()
    join(jnp.int32(n - 1))
    first = n // 2
    cuts = [0, first] + [first + (2 * n - first) * i // (len(bits) - 1) for i in range(1, len(bits))]
    for i in range(len(bits)):
        if side:
            side.run(cuts[i], cuts[i + 1])
        for half in (0, 1):
            order = orders[half]
            for k in [k for hh, k in entries if hh == half and phase_of(half, k) > i]:
                to = landing[half, i, k]
                remote(far.at[to], far.at[to], far_send.at[to], far_recv.at[to], device(1)).wait_recv()
                j = index[half, k]
                rows = pl.ds(half * h, h)
                if i == len(bits) - 1:
                    total[rows] = own[j].astype(jnp.float32) + far[to].astype(jnp.float32)
                    pltpu.make_async_copy(total.at[rows], sum_ref.at[rows], done.at[half]).start()
                else:
                    own[j] = (own[j].astype(jnp.float32) + far[to].astype(jnp.float32)).astype(own.dtype)
                    if phase_of(half, k) == i + 1:
                        launch(half, k).start()
    for half in (0, 1):
        rows = pl.ds(half * h, h)
        pltpu.make_async_copy(total.at[rows], sum_ref.at[rows], done.at[half]).wait()
    for q in (2 * n - 2, 2 * n - 1):
        for o in range(n_out):
            output(o, jnp.int32(q)).wait()
    for j in range(max(n - slots, 0), n):
        hand(jnp.int32(j)).wait_send()
    for half, k in entries:
        if phase_of(half, k) < len(bits):
            launch(half, k).wait_send()
    if nf:
        rider.finish()
    if side:
        side.end()


def seq_scatter(n, cols, ident, name, body, ins, consts, outs=(), modes=None, rider=None, side=None):
    h = ins[0].shape[0] // (2 * n)
    low = jnp.bfloat16
    slots = min(4, n)
    split = [a.reshape(2 * n, h, a.shape[1]) for a in ins]
    vmem = pl.BlockSpec(memory_space=pltpu.VMEM)
    hbm = pl.BlockSpec(memory_space=pl.ANY)
    reach = n - 2
    modes = modes or ([0] * len(ins), [0] * len(outs))
    more, spec, shape, scratch, nf, same = rider_parts(rider)
    s_ins, s_shapes, s_in_specs, s_out_specs, s_scratch = side_parts(side, 2 * n)
    product = False if side is None else side[2]
    out = pl.pallas_call(
        functools.partial(
            scatter_kernel, n, h, body, len(ins), len(consts), len(outs), modes, nf, same, product
        ),
        out_shape=[jax.ShapeDtypeStruct((2 * h, cols), jnp.float32)]
        + [jax.ShapeDtypeStruct((2 * n, h, c), d) for c, d in outs]
        + s_shapes
        + shape,
        in_specs=[hbm] * len(ins) + [vmem] * len(consts) + s_in_specs + spec,
        out_specs=[hbm] * (1 + len(outs)) + s_out_specs + spec,
        scratch_shapes=[
            pltpu.VMEM((slots, h, cols), low),
            pltpu.VMEM((n, h, cols), low),
            pltpu.VMEM((n, h, cols), low),
            pltpu.VMEM((reach, h, cols), low),
            pltpu.VMEM((2 * h, cols), jnp.float32),
        ]
        + [pltpu.VMEM((2, h, a.shape[2]), a.dtype) for a in split]
        + [pltpu.VMEM((2, h, c), d) for c, d in outs]
        + [
            pltpu.SemaphoreType.DMA((n,)),
            pltpu.SemaphoreType.DMA((n,)),
            pltpu.SemaphoreType.DMA((reach,)),
            pltpu.SemaphoreType.DMA((reach,)),
            pltpu.SemaphoreType.DMA((len(ins), 2)),
            pltpu.SemaphoreType.DMA((max(len(outs), 1), 2)),
            pltpu.SemaphoreType.DMA((2,)),
        ]
        + scratch
        + s_scratch,
        compiler_params=pltpu.CompilerParams(
            collective_id=ident, has_side_effects=True, vmem_limit_bytes=60 << 20
        ),
        cost_estimate=SMALL,
        name=name,
    )(*split, *consts, *s_ins, *more)
    many = 1 + len(outs)
    sides = [] if side is None else [out[many], out[many + 1].reshape(2 * n * h, -1)]
    more = list(out[many + len(sides) :])
    return [out[0]] + [o.reshape(2 * n * h, o.shape[2]) for o in out[1:many]] + sides + more


class Rows:
    def __init__(self, n, held, width, wide, back):
        moves = []
        for to in range(n):
            for third in range(3):
                at, end = third * width + to * wide, third * width + min((to + 1) * wide, width)
                row = third * wide
                while at < end:
                    source = at // held
                    count = min(end, (source + 1) * held) - at
                    moves.append((source, at - source * held, to, row, count))
                    at, row = at + count, row + count
        self.n = n
        self.moves = [(c, d, a, b, e) if back else (a, b, c, d, e) for a, b, c, d, e in moves]
        self.out = [[m for m in self.moves if m[0] == i] for i in range(n)]
        self.into = [[m for m in self.moves if m[2] == i] for i in range(n)]
        self.most = max(len(v) for v in self.out + self.into)

    def scratch(self):
        dma = pltpu.SemaphoreType.DMA
        return [dma((self.most,)), dma((self.most,)), dma((self.most,))]

    def bind(self, source, target, send, recv, local):
        self.source, self.target, self.send, self.recv, self.local = source, target, send, recv, local
        return self

    def copy(self, i, m):
        src = self.source.at[pl.ds(m[1], m[4])]
        dst = self.target.at[pl.ds(m[3], m[4])]
        if m[0] == m[2]:
            return pltpu.make_async_copy(src, dst, self.local.at[i])
        return remote(src, dst, self.send.at[i], self.recv.at[self.into[m[2]].index(m)], {"seq": m[2]})

    def start(self):
        me = lax.axis_index("seq")
        for s in range(self.n):

            @pl.when(me == s)
            def _(s=s):
                for i, m in enumerate(self.out[s]):
                    self.copy(i, m).start()

    def finish(self):
        me = lax.axis_index("seq")
        for s in range(self.n):

            @pl.when(me == s)
            def _(s=s):
                for i, m in enumerate(self.into[s]):
                    if m[0] != s:
                        dst = self.target.at[pl.ds(m[3], m[4])]
                        remote(dst, dst, self.send.at[0], self.recv.at[i], {"seq": s}).wait_recv()
                for i, m in enumerate(self.out[s]):
                    if m[0] == m[2]:
                        self.copy(i, m).wait()
                    else:
                        self.copy(i, m).wait_send()


class Units:
    def __init__(self, n, nf, back, source, target, send, recv, local):
        self.n, self.nf, self.back = n, nf, back
        self.source, self.target, self.send, self.recv, self.local = source, target, send, recv, local
        self.me = lax.axis_index("seq")

    @staticmethod
    def scratch(nf):
        dma = pltpu.SemaphoreType.DMA
        return [dma((nf,)), dma((nf,)), dma]

    def ends(self, i):
        group = self.n // self.nf
        if self.back:
            return i * group + lax.div(self.me, self.nf), lax.rem(self.me, self.nf)
        return lax.rem(self.me, group) * self.nf + i, lax.div(self.me, group)

    def comes(self, i):
        group = self.n // self.nf
        if self.back:
            return lax.rem(self.me, group) * self.nf + i
        return i * group + lax.div(self.me, self.nf)

    def each(self, i, there, here):
        to, slot = self.ends(i)

        @pl.when(to != self.me)
        def _():
            there(remote(self.source.at[i], self.target.at[slot], self.send.at[i], self.recv.at[slot], {"seq": to}))

        @pl.when(to == self.me)
        def _():
            here(pltpu.make_async_copy(self.source.at[i], self.target.at[slot], self.local))

    def start(self):
        for i in range(self.nf):
            self.each(i, lambda c: c.start(), lambda c: c.start())

    def finish(self):
        for i in range(self.nf):
            source = self.comes(i)

            @pl.when(source != self.me)
            def _(i=i):
                dst = self.target.at[i]
                remote(dst, dst, self.send.at[0], self.recv.at[i], {"seq": self.me}).wait_recv()

        for i in range(self.nf):
            self.each(i, lambda c: c.wait_send(), lambda c: c.wait())


def all_peers(n, nf):
    me, f = lax.axis_index("seq"), lax.axis_index("fsdp")
    return [{"seq": place(me, r, n)} for r in range(1, n)] + [
        {"fsdp": lax.rem(f + d, nf)} for d in range(1, nf)
    ]


def exchange_kernel(n, nf, rows, count, *refs):
    ins, outs, sems = refs[: 4 + count], refs[4 + count : 8 + 2 * count], list(refs[8 + 2 * count :])
    take = lambda k: [sems.pop(0) for _ in range(k)]
    parts = []
    if rows is not None:
        parts.append(rows.bind(ins[0], outs[0], *take(3)))
    vectors = [Blocks("fsdp", nf, True, ins[4 + i], outs[4 + i], *take(3)) for i in range(count)]
    later = [
        Blocks("fsdp", nf, True, ins[3], outs[3], *take(3)),
        Units(n, nf, False, ins[2], outs[2], *take(3)),
        Blocks("seq", n, False, ins[1], outs[1], *take(3)),
    ]
    parts = vectors + parts + later
    greet(all_peers(n, nf))
    for p in parts:
        p.start()
    for p in parts:
        p.finish()


def exchange(w, p, c, o, vectors, n, nf, rows, wide, ident):
    hbm = pl.BlockSpec(memory_space=pl.ANY)
    count = len(vectors)
    out = pl.pallas_call(
        functools.partial(exchange_kernel, n, nf, rows, count),
        out_shape=[
            jax.ShapeDtypeStruct((3 * wide, w.shape[1]) if rows is not None else w.shape, w.dtype),
            blocks_shape(p, n, False),
            blocks_shape(c, nf, False),
            blocks_shape(o, nf, True),
        ]
        + [blocks_shape(v, nf, True) for v in vectors],
        in_specs=[hbm] * (4 + count),
        out_specs=[hbm] * (4 + count),
        scratch_shapes=(rows.scratch() if rows is not None else [])
        + sum([Blocks.scratch(nf) for _ in vectors], [])
        + Blocks.scratch(nf)
        + Units.scratch(nf)
        + Blocks.scratch(n),
        compiler_params=pltpu.CompilerParams(collective_id=ident, has_side_effects=True),
        cost_estimate=SMALL,
        name="exchange",
    )(w, p, c, o, *vectors)
    return out[0], out[1], out[2], out[3], out[4:]


def to_tokens_kernel(n, wide, x_ref, o_ref, send, recv, local):
    me = lax.axis_index("seq")

    def target(i):
        return o_ref.at[:, pl.ds(pl.multiple_of(i * wide, 128), wide)]

    greet([{"seq": place(me, r, n)} for r in range(1, n)])
    copies = []
    for r in range(n - 1, 0, -1):
        to = place(me, r, n)
        c = remote(x_ref.at[to], target(me), send.at[r - 1], recv.at[r - 1], {"seq": to})
        c.start()
        copies.append(c)
    mine = pltpu.make_async_copy(x_ref.at[me], target(me), local)
    mine.start()
    for r in range(1, n):
        dst = target(place(me, r, n))
        remote(dst, dst, send.at[0], recv.at[r - 1], {"seq": place(me, r, n)}).wait_recv()
    mine.wait()
    for c in copies:
        c.wait_send()


def to_tokens(x, n, wide, ident):
    rows = x.shape[1]
    hbm = pl.BlockSpec(memory_space=pl.ANY)
    return pl.pallas_call(
        functools.partial(to_tokens_kernel, n, wide),
        out_shape=jax.ShapeDtypeStruct((rows, n * wide), x.dtype),
        in_specs=[hbm],
        out_specs=hbm,
        scratch_shapes=Blocks.scratch(n),
        compiler_params=pltpu.CompilerParams(collective_id=ident, has_side_effects=True),
        cost_estimate=SMALL,
        name="to_tokens",
    )(x)


def to_heads_kernel(n, wide, x_ref, w_ref, a_ref, b_ref, o_ref, g_ref, m_ref, made, send, recv, local, *extra):
    me = lax.axis_index("seq")
    side = Side(2 * n, None, (a_ref, b_ref, g_ref, m_ref) + extra)
    side.begin()
    greet([{"seq": place(me, r, n)} for r in range(1, n)])

    def copy(r):
        to = place(me, r, n)
        return remote(made.at[r], o_ref.at[me], send.at[r - 1], recv.at[r - 1], {"seq": to})

    def mine():
        return pltpu.make_async_copy(made.at[0], o_ref.at[me], local)

    def step(i, carry):
        r = n - 1 - i
        lanes = pl.ds(pl.multiple_of(place(me, r, n) * wide, 128), wide)
        made[r] = mm(x_ref[...], w_ref[:, lanes]).astype(made.dtype)

        @pl.when(r > 0)
        def _():
            copy(r).start()

        return carry

    lax.fori_loop(0, n, step, 0)
    mine().start()
    side.run(0, 2 * n)
    for r in range(1, n):
        dst = o_ref.at[place(me, r, n)]
        remote(dst, dst, send.at[0], recv.at[r - 1], {"seq": me}).wait_recv()
    mine().wait()
    for r in range(1, n):
        copy(r).wait_send()
    side.end()


def to_heads(x, w, n, wide, ident, a, b):
    rows = x.shape[0]
    vmem = pl.BlockSpec(memory_space=pltpu.VMEM)
    hbm = pl.BlockSpec(memory_space=pl.ANY)
    s_ins, s_shapes, s_in_specs, s_out_specs, s_scratch = side_parts((a, b, None, 0), 2 * n)
    out = pl.pallas_call(
        functools.partial(to_heads_kernel, n, wide),
        out_shape=[jax.ShapeDtypeStruct((n, rows, wide), x.dtype)] + s_shapes,
        in_specs=[vmem, vmem] + s_in_specs,
        out_specs=[hbm] + s_out_specs,
        scratch_shapes=[pltpu.VMEM((n, rows, wide), x.dtype)] + Blocks.scratch(n) + s_scratch,
        compiler_params=pltpu.CompilerParams(
            collective_id=ident, has_side_effects=True, vmem_limit_bytes=60 << 20
        ),
        cost_estimate=SMALL,
        name="to_heads",
    )(x, w, *s_ins)
    return out[0], out[1]


def project_kernel(x_ref, w_ref, b_ref, o_ref):
    o_ref[...] = (mm(x_ref[...], w_ref[...]) + b_ref[...]).astype(o_ref.dtype)


def project(x, w, bias, tile):
    rows, cols = x.shape[0], w.shape[1]
    still = lambda shape: pl.BlockSpec(shape, lambda i: (0, 0), pipeline_mode=pl.Buffered(1))
    return pl.pallas_call(
        project_kernel,
        out_shape=jax.ShapeDtypeStruct((rows, cols), x.dtype),
        grid=(rows // tile,),
        in_specs=[pl.BlockSpec((tile, x.shape[1]), lambda i: (i, 0)), still(w.shape), still((1, cols))],
        out_specs=pl.BlockSpec((tile, cols), lambda i: (i, 0)),
        compiler_params=pltpu.CompilerParams(vmem_limit_bytes=40 << 20),
        cost_estimate=SMALL,
        name="project",
    )(x, w, bias)


def contract_kernel(a_ref, b_ref, ready, o_ref, acc):
    i = pl.program_id(0)
    part = lax.dot_general(
        a_ref[...], b_ref[...], (((0,), (0,)), ((), ())), preferred_element_type=jnp.float32
    )

    @pl.when(i == 0)
    def _():
        acc[...] = part

    @pl.when(i > 0)
    def _():
        acc[...] += part

    @pl.when(i == pl.num_programs(0) - 1)
    def _():
        o_ref[...] = acc[...].astype(o_ref.dtype)


def contract(a, b, ready, tile):
    rows = a.shape[0]
    shape = (a.shape[1], b.shape[1])
    still = lambda s: pl.BlockSpec(s, lambda i: (0,) * len(s), pipeline_mode=pl.Buffered(1))
    return pl.pallas_call(
        contract_kernel,
        out_shape=jax.ShapeDtypeStruct(shape, a.dtype),
        grid=(rows // tile,),
        in_specs=[
            pl.BlockSpec((tile, shape[0]), lambda i: (i, 0)),
            pl.BlockSpec((tile, shape[1]), lambda i: (i, 0)),
            still(ready.shape),
        ],
        out_specs=still(shape),
        scratch_shapes=[pltpu.VMEM(shape, jnp.float32)],
        compiler_params=pltpu.CompilerParams(
            dimension_semantics=("arbitrary",), vmem_limit_bytes=40 << 20
        ),
        cost_estimate=SMALL,
        name="contract",
    )(a, b, ready)


def give_back_kernel(
    n, nf, rows, v_ref, w_ref, p_ref, c_ref, o_ref, v_out, w_out, p_out, c_out, o_out, planes, sums, *sems
):
    s = lax.axis_index("seq")
    f = lax.axis_index("fsdp")
    sems = list(sems)
    take = lambda k: [sems.pop(0) for _ in range(k)]
    send_z, recv_z, send_s, recv_s = take(4)
    parts = []
    if rows is not None:
        parts.append(rows.bind(w_ref, w_out, *take(3)))
    parts.append(Units(n, nf, True, c_ref, c_out, *take(3)))
    parts.append(Blocks("seq", n, False, p_ref, p_out, *take(3)))
    parts.append(Blocks("fsdp", nf, False, o_ref, o_out, *take(3)))
    others = [{"fsdp": lax.rem(f + d, nf)} for d in range(1, nf)]
    peers = [{"seq": place(s, r, n)} for r in range(1, n)]
    greet(peers + others)
    copies = []
    for d in range(1, nf):
        c = remote(v_ref.at[lax.rem(f + d, nf)], planes.at[d - 1], send_z.at[d - 1], recv_z.at[d - 1], others[d - 1])
        c.start()
        copies.append(c)
    for p in parts[:1]:
        p.start()
    total = v_ref[f]
    for d, c in enumerate(copies):
        c.wait_recv()
        total = total + planes[d]
    sums[0] = total
    spread = []
    for r in range(1, n):
        c = remote(sums.at[0], sums.at[r], send_s.at[r - 1], recv_s.at[r - 1], peers[r - 1])
        c.start()
        spread.append(c)
    for p in parts[1:]:
        p.start()
    for r, c in enumerate(spread):
        c.wait_recv()
        total = total + sums[r + 1]
    v_out[...] = total
    for p in parts:
        p.finish()
    for c in copies + spread:
        c.wait_send()


def give_back(vectors, w, held, p, c, o, n, nf, rows, ident):
    k = vectors.shape[1]
    tiles = -(-k // 1024) * 8
    padded = jnp.pad(vectors, ((0, 0), (0, tiles * 128 - k))).reshape(nf, tiles, 128)
    vmem = pl.BlockSpec(memory_space=pltpu.VMEM)
    hbm = pl.BlockSpec(memory_space=pl.ANY)
    dma = pltpu.SemaphoreType.DMA
    out = pl.pallas_call(
        functools.partial(give_back_kernel, n, nf, rows),
        out_shape=[
            jax.ShapeDtypeStruct((tiles, 128), jnp.float32),
            jax.ShapeDtypeStruct((held, w.shape[1]), w.dtype),
            blocks_shape(p, n, False),
            blocks_shape(c, nf, False),
            blocks_shape(o, nf, False),
        ],
        in_specs=[vmem, hbm, hbm, hbm, hbm],
        out_specs=[vmem, hbm, hbm, hbm, hbm],
        scratch_shapes=[
            pltpu.VMEM((nf - 1, tiles, 128), jnp.float32),
            pltpu.VMEM((n, tiles, 128), jnp.float32),
            dma((nf - 1,)),
            dma((nf - 1,)),
            dma((n - 1,)),
            dma((n - 1,)),
        ]
        + (rows.scratch() if rows is not None else [])
        + Units.scratch(nf)
        + Blocks.scratch(n)
        + Blocks.scratch(nf),
        compiler_params=pltpu.CompilerParams(collective_id=ident, has_side_effects=True),
        cost_estimate=SMALL,
        name="give_back",
    )(padded, w, p, c, o)
    return out[0].reshape(-1)[:k], out[1], out[2], out[3], out[4]


HEAD=64
SCALE=0.125*math.log2(math.e)

def block_table(lengths, parents, slots, trunk, block):
    count=lengths.shape[0]
    branches=count//3
    fixed,owner,child=[],[],[]
    for t in range(slots):
        m=t-trunk
        if t<trunk:
            keys=[(c,0 if c==t else block,-1,-1) for c in range(t+1)]
        else:
            keys=[(c,block,-1,-1) for c in range(trunk)]
            if m>=branches:
                keys.append((trunk-1,block,-1,m))
            keys.append((t,0,m,-1))
        for i,(c,shift,own,leaf) in enumerate(keys):
            fixed.append((t,c,shift,int(i==0),int(i==len(keys)-1)))
            owner.append(own)
            child.append(leaf)
    fixed=np.array(fixed,np.int32).T
    segments=np.arange(count)
    own=np.array(owner)[None,:]==segments[:,None]
    leaf=np.array(child)[None,:]==segments[:,None]
    above=jnp.sum(jnp.where(leaf,parents[:,None],0),0)
    source=own|(segments[:,None]+1==above[None,:])
    closed=(np.array(owner)<0)&(np.array(child)<0)
    reach=jnp.where(closed,block,jnp.sum(jnp.where(source,lengths[:,None],0),0))
    masked=jnp.where((fixed[2]==0)|(reach<block),1,0)
    return jnp.stack([fixed[0],fixed[1]+above,fixed[2],reach,masked,fixed[3],fixed[4]]).astype(jnp.int32)

def lane_half(shape):
    return lax.broadcasted_iota(jnp.int32,shape,len(shape)-1)<HEAD

def nt(a,b):
    return lax.dot_general(a,b,(((1,),(1,)),((),())),preferred_element_type=jnp.float32)

def mm(a,b):
    return jnp.dot(a,b,preferred_element_type=jnp.float32)

def attend_kernel(width, block, tab, qkv, low, att, tot, acc):
    p=pl.program_id(0)
    qs,ks,shift,count,masked=tab[0,p],tab[1,p],tab[2,p],tab[3,p],tab[4,p]
    first,last=tab[5,p],tab[6,p]
    qrow=pl.ds(pl.multiple_of(qs*block,block),block)
    krow=pl.ds(pl.multiple_of(ks*block,block),block)
    left=lane_half((block,2*HEAD))
    @pl.when(first==1)
    def _(): acc[...]=jnp.zeros_like(acc)
    def step(mask):
        for j in range(width//(2*HEAD)):
            q=qkv[qrow,j*2*HEAD:(j+1)*2*HEAD]
            k=qkv[krow,width+j*2*HEAD:width+(j+1)*2*HEAD]
            v=qkv[krow,2*width+j*2*HEAD:2*width+(j+1)*2*HEAD]
            for h in range(2):
                here=left if h==0 else jnp.logical_not(left)
                s=nt(jnp.where(here,q,0),k)
                e=jnp.exp2(s*SCALE)
                if mask is not None: e=jnp.where(mask,e,0.0)
                acc[2*j+h]+=mm(e.astype(jnp.bfloat16),jnp.where(here,v,1))
    @pl.when(masked==0)
    def _(): step(None)
    @pl.when(masked==1)
    def _():
        row=lax.broadcasted_iota(jnp.int32,(block,block),0)
        col=lax.broadcasted_iota(jnp.int32,(block,block),1)
        step((col<=row+shift)&(col<count))
    @pl.when(last==1)
    def _():
        for j in range(width//(2*HEAD)):
            a,b=acc[2*j],acc[2*j+1]
            total=jnp.where(left,pltpu.roll(a,HEAD,1),pltpu.roll(b,HEAD,1))
            value=jnp.where(left,a,b)/total
            lanes=slice(j*2*HEAD,(j+1)*2*HEAD)
            low[:,lanes]=value.astype(jnp.bfloat16)
            att[:,lanes]=value
            tot[:,lanes]=total

def attend(table, qkv, block):
    rows,width=qkv.shape[0],qkv.shape[1]//3
    steps=table.shape[1]
    by_q=lambda p,t:(t[0,p],0)
    heads=width//HEAD
    return pl.pallas_call(functools.partial(attend_kernel,width,block),
        out_shape=(jax.ShapeDtypeStruct((rows,width),jnp.bfloat16),jax.ShapeDtypeStruct((rows,width),jnp.float32),jax.ShapeDtypeStruct((rows,width),jnp.float32)),
        grid_spec=pltpu.PrefetchScalarGridSpec(num_scalar_prefetch=1,grid=(steps,),
            in_specs=[pl.BlockSpec((rows,3*width),lambda p,t:(0,0),pipeline_mode=pl.Buffered(1))],
            out_specs=[pl.BlockSpec((block,width),by_q)]*3,
            scratch_shapes=[pltpu.VMEM((heads,block,2*HEAD),jnp.float32)]),
        compiler_params=pltpu.CompilerParams(dimension_semantics=("arbitrary",),vmem_limit_bytes=50<<20),
        cost_estimate=SMALL,
        name="attend")(table,qkv)

def attend_back_kernel(width, block, tab, qkv, kt, datt, att, tot, out, dk, dv, dqt, aug):
    p=pl.program_id(0)
    qs,ks,shift,count,masked=tab[0,p],tab[1,p],tab[2,p],tab[3,p],tab[4,p]
    first,last=tab[5,p],tab[6,p]
    qrow=pl.ds(pl.multiple_of(qs*block,block),block)
    krow=pl.ds(pl.multiple_of(ks*block,block),block)
    left=lane_half((block,2*HEAD))
    lane=lax.broadcasted_iota(jnp.int32,(block,2*HEAD),1)
    pairs=width//(2*HEAD)
    @pl.when(p==0)
    def _():
        dk[...]=jnp.zeros_like(dk)
        dv[...]=jnp.zeros_like(dv)
    @pl.when(first==1)
    def _():
        dqt[...]=jnp.zeros_like(dqt)
        for j in range(pairs):
            lanes=slice(j*2*HEAD,(j+1)*2*HEAD)
            d=datt[:,lanes].astype(jnp.float32)
            total=tot[:,lanes]
            low=(d/total).astype(jnp.bfloat16)
            prod=d*att[:,lanes]/total
            for h in range(2):
                here=left if h==0 else jnp.logical_not(left)
                delta=-jnp.sum(jnp.where(here,prod,0.0),1,keepdims=True)
                hi=delta.astype(jnp.bfloat16).astype(jnp.float32)
                mid=(delta-hi).astype(jnp.bfloat16).astype(jnp.float32)
                rest=delta-hi-mid
                at=HEAD*(1-h)
                extra=jnp.where(lane==at,hi,jnp.where(lane==at+1,mid,jnp.where(lane==at+2,rest,0.0)))
                aug[2*j+h]=jnp.where(here,low.astype(jnp.float32),extra).astype(jnp.bfloat16)
    def step(mask):
        for j in range(pairs):
            q=qkv[qrow,j*2*HEAD:(j+1)*2*HEAD]
            k=qkv[krow,width+j*2*HEAD:width+(j+1)*2*HEAD]
            v=qkv[krow,2*width+j*2*HEAD:2*width+(j+1)*2*HEAD]
            lanes=slice(j*2*HEAD,(j+1)*2*HEAD)
            dvs,dks=[],[]
            for h in range(2):
                here=left if h==0 else jnp.logical_not(left)
                qh=jnp.where(here,q,0)
                e=jnp.exp2(nt(k,qh)*SCALE)
                if mask is not None: e=jnp.where(mask,e,0.0)
                dod=aug[2*j+h]
                ds=(e*nt(jnp.where(here,v*0.125,0.125).astype(jnp.bfloat16),dod)).astype(jnp.bfloat16)
                dvs.append(mm(e.astype(jnp.bfloat16),dod))
                dks.append(mm(ds,qh))
                at=j*2*HEAD+h*HEAD
                dqt[at:at+HEAD]+=mm(kt[at:at+HEAD,krow],ds)
            dv[krow,lanes]+=jnp.where(left,dvs[0],dvs[1])
            dk[krow,lanes]+=dks[0]+dks[1]
    @pl.when(masked==0)
    def _(): step(None)
    @pl.when(masked==1)
    def _():
        col=lax.broadcasted_iota(jnp.int32,(block,block),0)
        row=lax.broadcasted_iota(jnp.int32,(block,block),1)
        step((col<=row+shift)&(col<count))
    @pl.when(last==1)
    def _():
        out[qrow,0:width]=dqt[...].T.astype(jnp.bfloat16)
    @pl.when(p==pl.num_programs(0)-1)
    def _():
        out[:,width:2*width]=dk[...].astype(jnp.bfloat16)
        out[:,2*width:]=dv[...].astype(jnp.bfloat16)

def attend_back(table, qkv, datt, att, tot, block):
    rows,width=qkv.shape[0],qkv.shape[1]//3
    steps=table.shape[1]
    by_q=lambda p,t:(t[0,p],0)
    heads=width//HEAD
    kt=qkv[:,width:2*width].T
    whole=lambda s:pl.BlockSpec(s,lambda p,t:(0,0),pipeline_mode=pl.Buffered(1))
    return pl.pallas_call(functools.partial(attend_back_kernel,width,block),
        out_shape=jax.ShapeDtypeStruct((rows,3*width),jnp.bfloat16),
        grid_spec=pltpu.PrefetchScalarGridSpec(num_scalar_prefetch=1,grid=(steps,),
            in_specs=[whole((rows,3*width)),whole((width,rows))]+[pl.BlockSpec((block,width),by_q)]*3,
            out_specs=whole((rows,3*width)),
            scratch_shapes=[pltpu.VMEM((rows,width),jnp.float32),pltpu.VMEM((rows,width),jnp.float32),pltpu.VMEM((width,block),jnp.float32),pltpu.VMEM((heads,block,2*HEAD),jnp.bfloat16)]),
        compiler_params=pltpu.CompilerParams(dimension_semantics=("arbitrary",),vmem_limit_bytes=60<<20),
        cost_estimate=SMALL,
        name="attend_back")(table,qkv,kt,datt,att,tot)


def layer_norm(values, gain, shift):
    centred = values - jnp.mean(values, -1, keepdims=True)
    spread = jnp.mean(centred * centred, -1, keepdims=True)
    return centred * lax.rsqrt(spread + 1e-05) * gain + shift


def contract_rows(left, right):
    return lax.dot_general(
        left, right, (((0,), (0,)), ((), ())), preferred_element_type=jnp.float32
    )


def contract_cols(left, right):
    return lax.dot_general(
        left, right, (((1,), (1,)), ((), ())), preferred_element_type=jnp.float32
    )


def after(value, other):
    return value + (other[(0,) * other.ndim] * 0).astype(value.dtype)


def row_major(x):
    return with_layout_constraint(x, Layout(major_to_minor=tuple(range(x.ndim))))


def local(
    tokens,
    ln1_gain,
    ln1_bias,
    qkv_weight,
    qv_bias,
    out_weight,
    out_bias,
    ln2_gain,
    ln2_bias,
    fc_weight,
    fc_bias,
    proj_weight,
    proj_bias,
    seg_lengths,
    parents,
    cotangent,
):
    n = lax.axis_size("seq")
    nf = lax.axis_size("fsdp")
    s = lax.axis_index("seq")
    f = lax.axis_index("fsdp")
    trunk = n // 4
    block, width = tokens.shape[1], tokens.shape[2]
    rows = width // nf
    hidden = fc_weight.shape[1] * n
    piece = hidden // (n * nf)
    group = n // nf
    wide = 2 * HEAD * (-(-HEADS // (2 * n)))
    low = jnp.bfloat16
    wider = jnp.float32

    vectors = [ln1_gain, ln1_bias, qv_bias, out_bias, ln2_gain, ln2_bias, fc_bias, proj_bias]
    sizes = [v.shape[0] for v in vectors]
    qkv_cols = qkv_weight.shape[1]
    even = qkv_cols % 8 == 0
    forth = Rows(n, qkv_cols, width, wide, False) if even else None
    back = Rows(n, qkv_cols, width, wide, True) if even else None
    turned, proj_blocks, fc_blocks, out_blocks, gathered = exchange(
        qkv_weight.T,
        proj_weight.reshape(n, piece, width // n),
        fc_weight.reshape(rows, nf, piece).transpose(1, 0, 2),
        out_weight,
        [v.reshape(1, -1) for v in vectors],
        n,
        nf,
        forth,
        wide,
        0,
    )
    whole = [v.reshape(-1).astype(wider) for v in gathered]
    gain_one, shift_one, bias_qv, bias_out, gain_two, shift_two, bias_fc, bias_proj = whole
    bias_three = jnp.stack([bias_qv[:width], jnp.zeros((width,), wider), bias_qv[width:]])
    bias_three = jnp.pad(bias_three, ((0, 0), (0, n * wide - width)))
    bias_mine = lax.dynamic_slice_in_dim(bias_three, s * wide, wide, 1).reshape(1, -1)
    bias_hidden = lax.dynamic_index_in_dim(bias_fc.reshape(nf, n, piece), s, 1, False)
    bias_hidden = bias_hidden.reshape(1, -1)

    if even:
        turned = turned.reshape(3, wide, rows)
        kept = lax.broadcasted_iota(jnp.int32, turned.shape, 1) + s * wide < width
        turned = jnp.where(kept, turned, 0).reshape(3 * wide, rows)
    else:
        turned = lax.all_gather(qkv_weight.T, "seq", axis=0, tiled=True).reshape(3, width, rows)
        turned = jnp.pad(turned, ((0, 0), (0, n * wide - width), (0, 0)))
        turned = lax.dynamic_slice_in_dim(turned, s * wide, wide, 1).reshape(3 * wide, rows)
    table = block_table(seg_lengths[0], parents[0], n, trunk, block)

    resid = tokens[0].astype(wider)
    out_turned = jnp.pad(out_blocks.reshape(width, width // n).T, ((0, 0), (0, n * wide - width)))
    normed_one, out_turned, qkv_mine = seq_gather(
        layer_norm(resid, gain_one, shift_one).astype(low),
        n,
        1,
        "gather_one",
        rider=(turned.T, True, nf),
        second=out_turned,
    )
    out_turned = out_turned.reshape(width, n * wide)
    qkv_mine = qkv_mine.reshape(width, 3 * wide)
    fc_rows = fc_blocks.transpose(1, 0, 2).reshape(rows, nf * piece)
    fc_mine = lax.all_gather(fc_rows, "fsdp", axis=0, tiled=True)

    upstream = cotangent[0].astype(wider)
    projected = project(normed_one, qkv_mine, bias_mine, block // 2)
    sent = row_major(after(after(cotangent[0], fc_mine), projected))
    upstream_all = row_major(lax.all_gather(sent, "seq", axis=0, tiled=True))
    table = after(table, sent)
    attended_low, attended, totals = attend(table, projected, block)
    proj_rows = proj_blocks.transpose(1, 0, 2).reshape(piece, width)
    proj_mine = lax.all_gather(after(proj_rows, attended_low), "fsdp", axis=0, tiled=True)
    attended_mine = to_tokens(attended_low.reshape(n, block, wide), n, wide, 2)
    middle = after(resid, upstream_all) + contract_cols(attended_mine, out_turned) + bias_out
    normed_two = layer_norm(middle, gain_two, shift_two).astype(low)
    ff = nf * piece

    def expand(value, fc, bias):
        pre = mm(value, fc[...]) + bias[...]
        bend = math.sqrt(2 / math.pi)
        square = pre * pre
        inner = jnp.tanh(pre * (bend + bend * 0.044715 * square))
        half = 0.5 + 0.5 * inner
        act = (pre * half).astype(low)
        slope = half + 0.5 * pre * (1 - inner * inner) * (bend + 3 * bend * 0.044715 * square)
        return act, slope.astype(low)

    normed_two, hidden_act, hidden_slope = seq_gather(
        normed_two,
        n,
        3,
        "gather_two",
        expand,
        (fc_mine, bias_hidden),
        ((ff, low), (ff, low)),
        modes=(0, 0),
    )

    def shrink(up, slope, proj, fc):
        grad = (nt(up, proj[...]) * slope.astype(wider)).astype(low)
        return nt(grad, fc[...]), grad

    grad_normed_two, grad_pre, grad_proj, mixed = seq_scatter(
        n,
        width,
        4,
        "scatter_two",
        shrink,
        (upstream_all, hidden_slope),
        (proj_mine, fc_mine),
        ((ff, low),),
        side=(hidden_act, upstream_all, lambda a, proj, fc: mm(a, proj[...]).astype(low), width),
    )
    mixed = lax.psum_scatter(mixed, "seq", scatter_dimension=0, tiled=True).astype(wider)
    proj_part = lax.psum_scatter(
        grad_proj.reshape(nf, piece, width), "fsdp", scatter_dimension=0, tiled=False
    )
    unused_two, norm_two_back = jax.vjp(layer_norm, middle, gain_two, shift_two)
    grad_middle_norm, grad_gain_two, grad_shift_two = norm_two_back(grad_normed_two)
    grad_middle = upstream + grad_middle_norm
    grad_branch = grad_middle.astype(low)
    grad_attended, grad_fc = to_heads(
        grad_branch, out_turned, n, wide, 5, normed_two, grad_pre
    )
    grad_attended = grad_attended.reshape(n * block, wide)
    fc_part = lax.psum_scatter(grad_fc, "fsdp", scatter_dimension=0, tiled=True)
    grad_projected = attend_back(table, projected, grad_attended, attended, totals, block)
    output = (after(middle, grad_projected) + mixed + bias_proj).astype(low)[None]
    ready = output[0, :8, :128].astype(wider)
    grad_qkv = contract(normed_one, grad_projected, ready, block)
    grad_normed_one, qkv_parts = seq_scatter(
        n,
        width,
        6,
        "scatter_one",
        lambda g, w: (nt(g, w[...]),),
        (grad_projected,),
        (qkv_mine,),
        rider=(grad_qkv.reshape(nf, rows, 3 * wide), False, nf),
    )
    unused_one, norm_one_back = jax.vjp(layer_norm, resid, gain_one, shift_one)
    grad_resid_norm, grad_gain_one, grad_shift_one = norm_one_back(grad_normed_one)
    input_grad = (grad_middle + grad_resid_norm).astype(low)[None]

    proj_part = after(proj_part, grad_normed_one).reshape(piece, n, width // n).transpose(1, 0, 2)
    fc_part = after(fc_part, grad_normed_one).reshape(rows, nf, piece).transpose(1, 0, 2)
    grad_out = contract_rows(
        after(grad_branch, grad_attended), attended_mine[:, :width]
    ).astype(low)
    out_part = lax.psum_scatter(grad_out, "seq", scatter_dimension=0, tiled=True).T
    out_part = after(out_part, grad_normed_one).reshape(nf, rows, width // n)
    qkv_part = jnp.sum(qkv_parts.astype(wider), 0).astype(low).T

    column_sums = jnp.sum(grad_projected.astype(wider), 0).reshape(3, wide)
    placed = lax.dynamic_update_slice_in_dim(
        jnp.zeros((3, n * wide), wider), column_sums, s * wide, 1
    )[:, :width]
    grad_qv = jnp.concatenate([placed[0], placed[2]])
    hidden_sums = jnp.sum(grad_pre.astype(wider), 0).reshape(nf, 1, piece)
    grad_fc_bias = lax.dynamic_update_slice_in_dim(
        jnp.zeros((nf, n, piece), wider), hidden_sums, s, 1
    )
    parts = [
        grad_gain_one,
        grad_shift_one,
        grad_qv,
        jnp.sum(grad_branch.astype(wider), 0),
        grad_gain_two,
        grad_shift_two,
        grad_fc_bias,
        jnp.sum(upstream, 0),
    ]
    summed, qkv_out, proj_out, fc_out, out_out = give_back(
        jnp.concatenate([p.reshape(nf, -1) for p in parts], 1),
        qkv_part,
        qkv_cols,
        proj_part,
        fc_part,
        out_part,
        n,
        nf,
        back,
        7,
    )
    if not even:
        qkv_part = qkv_part.reshape(3, wide, rows)
        qkv_out = lax.all_gather(qkv_part, "seq", axis=1, tiled=True)[:, :width]
        qkv_out = qkv_out.reshape(3 * width, rows)
        qkv_out = lax.dynamic_slice_in_dim(qkv_out, s * qkv_cols, qkv_cols, 0)
    out_out = jnp.sum(out_out.astype(wider), 0)
    qkv_out = qkv_out.T.astype(wider)
    proj_out = proj_out.reshape(n * piece, width // n).astype(wider)
    fc_out = fc_out.transpose(1, 0, 2).reshape(rows, nf * piece).astype(wider)
    vector_out = []
    at = 0
    for size in sizes:
        vector_out.append(summed[at : at + size])
        at += size
    return (
        output,
        input_grad,
        vector_out[0],
        vector_out[1],
        qkv_out,
        vector_out[2],
        out_out,
        vector_out[3],
        vector_out[4],
        vector_out[5],
        fc_out,
        vector_out[6],
        proj_out,
        vector_out[7],
    )


def solution(mesh):
    in_specs = (
        P("fsdp", "seq", None),
        P("fsdp"),
        P("fsdp"),
        P("fsdp", "seq"),
        P("fsdp"),
        P("fsdp", "seq"),
        P("fsdp"),
        P("fsdp"),
        P("fsdp"),
        P("fsdp", "seq"),
        P("fsdp"),
        P("fsdp", "seq"),
        P("fsdp"),
        P("fsdp", None),
        P("fsdp", None),
        P("fsdp", "seq", None),
    )
    out_specs = (
        P("fsdp", "seq", None),
        P("fsdp", "seq", None),
        P("fsdp"),
        P("fsdp"),
        P("fsdp", "seq"),
        P("fsdp"),
        P("fsdp", "seq"),
        P("fsdp"),
        P("fsdp"),
        P("fsdp"),
        P("fsdp", "seq"),
        P("fsdp"),
        P("fsdp", "seq"),
        P("fsdp"),
    )
    return jax.shard_map(local, mesh=mesh, in_specs=in_specs, out_specs=out_specs, check_vma=False)
```

time: 1090 us -> 889 us (0.82)
  local copies, waits for them, and re-layouts: 176 us -> 71.3 us
  Pallas kernels: 568 us -> 657 us
  matrix products: 93.9 us -> 13.6 us
  waiting for transfers between devices: 129 us -> 64.7 us
  blocking collectives: 23.7 us -> 0 us
  starting transfers between devices: 21 us -> 0.88 us
    reduce_scatter x1, waiting for transfers between devices: 80.7 us -> 0.02 us  [local(): lax.psum_scatter(mixed, 'seq', scatter_dimension=0, tiled=True)]
    pallas_call x4 -> x6, Pallas kernels: 133 us -> 199 us  [the longest x1 49.6 us: to_tokens(): pl.pallas_call(functools.partial(to_tokens_kernel, n, wide), out_shape=ja...]
    unnamed x14 -> x9, waiting for transfers between devices: 0.87 us -> 56.9 us
    dot_general x4 -> x1, matrix products: 61.1 us -> 5.57 us  [contract_rows(): lax.dot_general(left, right, (((0,), (0,)), ((), ())), preferred_element_...]
    dot_general x2 -> x0, matrix products: 25.7 us -> none  [the longest x1 17.3 us: local(): jnp.dot(normed_one, qkv_mine, preferred_element_type=wider) + bias_mine]
    all_gather x1 -> x0, blocking collectives: 23.7 us -> none  [local(): out_turned = lax.all_gather(out_weight, 'fsdp', axis=0, tiled=True).T]
    reshape x6 -> x11, local copies, waits for them, and re-layouts: 30.6 us -> 7.85 us  [the longest x8 4.67 us: local(): v.reshape(1, -1)]
    unnamed x122 -> x117, local copies, waits for them, and re-layouts: 46.4 us -> 26.8 us
  transfers between devices with their start and end apart: 27 -> 7, of which waited for: 7 -> 2; matrix products, arithmetic and copies ran while one was open for 24% -> 8% of each run, Pallas kernels for 41% -> 57%
where the time goes in v2:
time: 889 us; the launch traced here: 879 us
  Pallas kernels  657 us (74%)
  local copies, waits for them, and re-layouts  71.3 us (8%)
  waiting for transfers between devices  64.7 us (7%)
  other arithmetic  50.9 us (6%)
  between operations  21.1 us (2%)
  matrix products  13.6 us (2%)
    pallas_call x2, Pallas kernels, seq_scatter(): pl.pallas_call(functools.partial(scatter_kernel, n, h, body, len(ins), le...  168 us
    pallas_call x2, Pallas kernels, seq_gather(): pl.pallas_call(functools.partial(gather_kernel, n, h, body, len(consts),...  159 us
    pallas_call x1, Pallas kernels, attend_back(): pl.pallas_call(functools.partial(attend_back_kernel, width, block), out_s...  88.7 us
    unnamed x9, waiting for transfers between devices  56.9 us
    pallas_call x1, Pallas kernels, to_tokens(): pl.pallas_call(functools.partial(to_tokens_kernel, n, wide), out_shape=ja...  49.6 us
    pallas_call x1, Pallas kernels, to_heads(): pl.pallas_call(functools.partial(to_heads_kernel, n, wide), out_shape=[ja...  45.6 us
    pallas_call x1, Pallas kernels, attend(): pl.pallas_call(functools.partial(attend_kernel, width, block), out_shape=...  42.1 us
    pallas_call x1, Pallas kernels, give_back(): pl.pallas_call(functools.partial(give_back_kernel, n, nf, rows), out_shap...  35.7 us
  transfers between devices with their start and end apart: 7, of which 2 were waited for; matrix products, arithmetic and copies ran while one was open for 8% of the time, Pallas kernels for 57%

profile of v2, /device:TPU:3, one launch (start us, length us, event | category | flops | bytes accessed | tf_op | source)
XLA Modules:
  0.0 879.4 jit_solution(8739443630711064448)
XLA Ops:
  7.3 2.7 reshape.323
  18.0 32.7 %exchange.1 = (bf16[768,400]{1,0:T(8,128)(2,1)}, bf16[8,200,200]{2,1,0:T(8,128)(2,1)}, bf16[4,400,200]{2,1,0:T(8,128)(2,1)}, bf16[4,400,200]{2,1,0:T(8,128)(2,1)...) custom-call(bf16[600,400]{1,0:T(8,128)(2,1)} %bitcast.156, ...), custom_call_target="tpu_custom_call" | custom-call | bytes 1048576 | tf_op jit(solution)/shard_map/exchange/pallas_call | solution.py:768
  50.7 1.6 copy.104
  52.3 1.5 reshape.332
  55.5 1.9 copy.107
  57.5 1.5 copy.123
  62.2 1.8 fusion.9.refs_0_
  64.0 92.4 %gather_one.1 = (bf16[16,256,1600]{2,1,0:T(8,128)(2,1)}, bf16[8,200,2048]{2,1,0:T(8,128)(2,1)}, bf16[4,400,768]{2,1,0:T(8,128)(2,1)}) custom-call(bf16[512,1600]{1,0:T(8,128)(2,1)} %fusion.9.refs_0_, bf16[200,2048]{1,0:T(8,128)(2,1)} %pad.12.refs_1_, bf16[400,768]{1,0:T(8,128)(2,1)} %select_bitcast_fusion.refs_2_), custom_call_target="tpu_custom_call" | custom-call | bytes 1048576 | tf_op jit(solution)/shard_map/gather_one/pallas_call | solution.py:278
  156.4 1.7 copy-done.2
  158.1 17.7 %project.1.qkv = bf16[4096,768]{1,0:T(8,128)(2,1)S(1)} custom-call(bf16[4096,1600]{1,0:T(8,128)(2,1)} %bitcast.140, bf16[1600,768]{1,0:T(8,128)(2,1)S(1)} %bitcast.136, f32[1,768]{1,0:T(1,128)S(1)} %bitcast.139), custom_call_target="tpu_custom_call" | custom-call | bytes 1048576 | tf_op jit(solution)/shard_map/project/pallas_call | solution.py:892
  175.8 2.6 copy-done.1
  183.2 1.4 add_bitcast_fusion
  187.1 42.1 %attend.1 = (bf16[4096,256]{1,0:T(8,128)(2,1)S(1)}, f32[4096,256]{1,0:T(8,128)}, f32[4096,256]{1,0:T(8,128)}) custom-call(s32[7,25]{1,0:T(8,128)S(1)} %broadcast_add_fusion.2.tab, bf16[4096,768]{1,0:T(8,128)(2,1)} %copy-done.1), custom_call_target="tpu_custom_call" | custom-call | bytes 1048576 | tf_op jit(solution)/shard_map/attend/pallas_call | solution.py:1112
  230.7 1.8 add.202
  233.8 49.6 %to_tokens.1 = bf16[512,2048]{1,0:T(8,128)(2,1)} custom-call(bf16[8,512,256]{2,1,0:T(8,128)(2,1)} %bitcast.138), custom_call_target="tpu_custom_call" | custom-call | bytes 1048576 | tf_op jit(solution)/shard_map/to_tokens/pallas_call | solution.py:817
  283.4 7.7 all-gather.6.cloned.1.call-done
  292.9 8.1 fusion.32
  301.5 1.9 add_convert_fusion.2.refs_0_
  303.4 66.9 %gather_two.1 = (bf16[16,256,1600]{2,1,0:T(8,128)(2,1)}, bf16[16,256,800]{2,1,0:T(8,128)(2,1)}, bf16[16,256,800]{2,1,0:T(8,128)(2,1)}) custom-call(bf16[512,1600]{1,0:T(8,128)(2,1)} %add_convert_fusion.2.refs_0_, bf16[1600,800]{1,0:T(8,128)(2,1)} %all-gather.4.cloned.1.call-done.refs_1_.refs_3_, f32[1,800]{1,0:T(1,128)} %reshape.340.refs_2_), custom_call_target="tpu_custom_call" | custom-call | bytes 1048576 | tf_op jit(solution)/shard_map/gather_two/pallas_call | solution.py:278
  370.3 86.2 %scatter_two.1 = (f32[512,1600]{1,0:T(8,128)}, bf16[16,256,800]{2,1,0:T(8,128)(2,1)}, bf16[800,1600]{1,0:T(8,128)(2,1)}, bf16[16,256,1600]{2,1,0:T(8,128)(2,1)}) custom-call(bf16[16,256,1600]{2,1,0:T(8,128)(2,1)} %bitcast.142, bf16[16,256,800]{2,1,0:T(8,128)(2,1)} %get-tuple-element.62.refs_1_, bf16[800,1600]{1,0:T(8,128)(2,1)} %all-gather.8.cloned.1.call-done.refs_2_, ...), custom_call_target="tpu_custom_call" | custom-call | bytes 1048576 | tf_op jit(solution)/shard_map/scatter_two/pallas_call | solution.py:586
  456.8 3.2 multiply_reduce_fusion
  461.5 2.0 convert_reduce_fusion.4
  463.5 45.6 %to_heads.1 = (bf16[8,512,256]{2,1,0:T(8,128)(2,1)}, bf16[1600,800]{1,0:T(8,128)(2,1)}, bf16[16,256,128]{2,1,0:T(8,128)(2,1)}) custom-call(bf16[512,1600]{1,0:T(8,128)(2,1)} %get-tuple-element.150.x_ref, bf16[1600,2048]{1,0:T(8,128)(2,1)} %bitcast.147, bf16[16,256,1600]{2,1,0:T(8,128)(2,1)} %get-tuple-element.66.a_ref, ...), custom_call_target="tpu_custom_call" | custom-call | bytes 1048576 | tf_op jit(solution)/shard_map/to_heads/pallas_call | solution.py:870
  511.0 5.6 convolution_convert_fusion
  519.0 2.9 copy.124
  522.1 1.7 convert_reduce_fusion.2
  523.9 88.7 %attend_back.1.b_ref = bf16[4096,768]{1,0:T(8,128)(2,1)} custom-call(s32[7,25]{1,0:T(8,128)} %copy-done.5, bf16[4096,768]{1,0:T(8,128)(2,1)} %copy-done.1, bf16[256,4096]{1,0:T(8,128)(2,1)} %bitcast.145, bf16[4096,256]{1,0:T(8,128)(2,1)} %bitcast.158, f32[4096,256]{1,0:T(8,128)} %get-tuple-element.69.att, f32[4096,256]{1,0:T(8,128)} %get-tuple-element.70.tot), custom_call_target="tpu_custom_call" | custom-call | bytes 1048576 | tf_op jit(solution)/shard_map/attend_back/pallas_call | solution.py:1195
  614.4 4.0 convert_reduce_fusion.1
  618.9 4.3 convert_reduce_fusion
  623.5 2.1 fusion.17
  627.3 17.6 %contract.1 = bf16[1600,768]{1,0:T(8,128)(2,1)S(1)} custom-call(bf16[4096,1600]{1,0:T(8,128)(2,1)} %bitcast.141, bf16[4096,768]{1,0:T(8,128)(2,1)S(1)} %copy-done, f32[8,128]{1,0:T(8,128)S(1)} %fusion.23.ready), custom_call_target="tpu_custom_call" | custom-call | bytes 1048576 | tf_op jit(solution)/shard_map/contract/pallas_call | solution.py:927
  644.9 1.5 copy-done.3
  646.4 81.7 %scatter_one.1 = (f32[512,1600]{1,0:T(8,128)}, bf16[4,400,768]{2,1,0:T(8,128)(2,1)}) custom-call(bf16[16,256,768]{2,1,0:T(8,128)(2,1)} %bitcast.134, bf16[1600,768]{1,0:T(8,128)(2,1)} %bitcast.135, bf16[4,400,768]{2,1,0:T(8,128)(2,1)} %bitcast.137), custom_call_target="tpu_custom_call" | custom-call | bytes 1048576 | tf_op jit(solution)/shard_map/scatter_one/pallas_call | solution.py:586
  735.4 2.8 fusion.28
  738.2 55.8 %reduce-scatter.13.cloned.1.call-done = bf16[1,200,1600]{2,1,0:T(8,128)(2,1)} async-done(((bf16[4,200,1600]{2,1,0:T(8,128)(2,1)}), bf16[1,200,1600]{2,1,0:T(8,128)(2,1)}) %reduce-scatter.13.cloned.1.call-update) | async-done | bytes 640016
  797.4 3.1 fusion.10
  801.6 3.2 reduce_sum.211
  804.7 2.2 copy.113
  807.0 35.7 %give_back.1 = (f32[40,128]{1,0:T(8,128)}, bf16[600,400]{1,0:T(8,128)(2,1)}, bf16[8,200,200]{2,1,0:T(8,128)(2,1)}, bf16[4,400,200]{2,1,0:T(8,128)(2,1)}, bf16[4,400,200]{2,1,0:T(8,128)(2,1)}) custom-call(f32[4,40,128]{2,1,0:T(8,128)} %bitcast.161, bf16[768,400]{1,0:T(8,128)(2,1)} %bitcast.153, bf16[8,200,200]{2,1,0:T(8,128)(2,1)} %bitcast.150, ...), custom_call_target="tpu_custom_call" | custom-call | bytes 1048576 | tf_op jit(solution)/shard_map/give_back/pallas_call | solution.py:999
  842.6 1.4 fusion.31
  846.8 2.5 copy.118
  851.7 2.2 reshape.370
  855.1 1.6 copy.121
  856.7 2.4 convert_bitcast_fusion.3
  859.1 2.6 copy.120
  861.7 2.1 convert_reduce_fusion.5
  863.8 4.7 fusion.18
  868.5 3.6 copy.119
  (223 shorter events, 47.7 us)
Async XLA Ops:
  7.2 3.9 copy-start.22
  7.2 5.1 copy-start.23
  7.2 6.1 copy-start.32
  7.2 6.7 copy-start.33
  7.2 7.3 copy-start.34
  7.2 7.9 copy-start.35
  7.2 8.5 copy-start.36
  7.3 9.0 %copy-start.37 = (bf16[400]{0:T(512)(128)(2,1)S(1)}, bf16[400]{0:T(512)(128)(2,1)}, u32[]{:S(2)}) copy-start(bf16[400]{0:T(512)(128)(2,1)} %param.33) | copy-start | bytes 2404
  7.3 9.6 %copy-start.38 = (bf16[400]{0:T(512)(128)(2,1)S(1)}, bf16[400]{0:T(512)(128)(2,1)}, u32[]{:S(2)}) copy-start(bf16[400]{0:T(512)(128)(2,1)} %param.34) | copy-start | bytes 2404
  7.3 10.2 %copy-start.39 = (bf16[400]{0:T(512)(128)(2,1)S(1)}, bf16[400]{0:T(512)(128)(2,1)}, u32[]{:S(2)}) copy-start(bf16[400]{0:T(512)(128)(2,1)} %param.38) | copy-start | bytes 2404
  7.3 174.1 %all-gather.4.cloned.1.call-start = ((), (), s32[]{:S(2)}) async-start(), calls=%async_computation.4 | async-start | bytes 3584000 | tf_op jit(solution)/shard_map/all_gather | solution.py:1313
  13.3 40.7 %copy-start.19 = (bf16[1,512,1600]{1,2,0:T(8,128)(2,1)S(1)}, bf16[1,512,1600]{1,2,0:T(8,128)(2,1)}, u32[]{:S(2)}) copy-start(bf16[1,512,1600]{1,2,0:T(8,128)(2,1)} %param.26) | copy-start | bytes 4915204
  53.8 5.2 copy-start.25
  53.8 237.3 %all-gather.6.cloned.1.call-start = ((), (), s32[]{:S(2)}) async-start(), calls=%async_computation.5 | async-start | bytes 15335424 | tf_op jit(solution)/shard_map/all_gather | solution.py:1318
  55.4 6.7 copy-start.8
  158.1 20.9 %copy-start.20 = (bf16[1,512,1600]{1,2,0:T(8,128)(2,1)S(1)}, bf16[1,512,1600]{1,2,0:T(8,128)(2,1)}, u32[]{:S(2)}) copy-start(bf16[1,512,1600]{1,2,0:T(8,128)(2,1)} %param.41) | copy-start | bytes 4915204
  179.0 5.9 copy-start.41
  179.0 5.9 copy-start.42
  179.0 6.0 copy-start.40
  179.0 6.0 copy-start.43
  179.0 6.0 copy-start.44
  179.0 6.1 copy-start.45
  179.0 6.1 copy-start.46
  179.0 6.1 copy-start.47
  180.4 6.7 copy-start.10
  180.4 4.7 copy-start.48
  180.4 4.7 copy-start.49
  180.4 4.7 copy-start.50
  180.5 4.7 copy-start.51
  184.6 45.8 %copy-start.21 = (bf16[8,200,200]{2,1,0:T(8,128)(2,1)S(1)}, bf16[8,200,200]{2,1,0:T(8,128)(2,1)}, u32[]{:S(2)}) copy-start(bf16[8,200,200]{2,1,0:T(8,128)(2,1)} %get-tuple-element.63) | copy-start | bytes 1920004
  184.6 185.7 %all-gather.8.cloned.1.call-start = ((), (), s32[]{:S(2)}) async-start(), calls=%async_computation.6 | async-start | bytes 3328000 | tf_op jit(solution)/shard_map/all_gather | solution.py:1322
  187.1 43.4 %copy-start.5 = (s32[7,25]{1,0:T(8,128)}, s32[7,25]{1,0:T(8,128)S(1)}, u32[]{:S(2)}) copy-start(s32[7,25]{1,0:T(8,128)S(1)} %broadcast_add_fusion.2.tab) | copy-start | bytes 2104
  229.2 4.6 copy-start.4
  229.2 3.6 copy-start.27
  229.2 3.7 copy-start.24
  232.5 391.0 %reduce-scatter.9.cloned.1.call-start = ((), (), s32[]{:S(2)}) async-start(), calls=%async_computation.7 | async-start | bytes 15335424 | tf_op jit(solution)/shard_map/reduce_scatter | solution.py:1364
  301.0 159.0 %copy-start.6 = (f32[512,1600]{1,0:T(8,128)}, f32[512,1600]{1,0:T(8,128)S(1)}, u32[]{:S(2)}) copy-start(f32[512,1600]{1,0:T(8,128)S(1)} %get-tuple-element.162) | copy-start | bytes 9830404
  456.5 273.4 %reduce-scatter.15.cloned.1.call-start = ((), (), s32[]{:S(2)}) async-start(), calls=%async_computation.10 | async-start | bytes 5990400
  463.5 47.5 %copy-start.17 = (bf16[512,1600]{1,0:T(8,128)(2,1)S(1)}, bf16[512,1600]{1,0:T(8,128)(2,1)}, u32[]{:S(2)}) copy-start(bf16[512,1600]{1,0:T(8,128)(2,1)} %get-tuple-element.150.x_ref) | copy-start | bytes 4915204
  463.5 47.5 %copy-start.18 = (bf16[512,2048]{1,0:T(8,128)(2,1)S(1)}, bf16[512,2048]{1,0:T(8,128)(2,1)}, u32[]{:S(2)}) copy-start(bf16[512,2048]{1,0:T(8,128)(2,1)} %to_tokens.1) | copy-start | bytes 6291460
  516.6 215.9 %reduce-scatter.11.cloned.1.call-start = ((), (), s32[]{:S(2)}) async-start(), calls=%async_computation.8 | async-start | bytes 3584000 | tf_op jit(solution)/shard_map/reduce_scatter | solution.py:1376
  517.2 276.8 %reduce-scatter.13.cloned.1.call-start = ((), (), s32[]{:S(2)}) async-start(), calls=%async_computation.9 | async-start | bytes 3328000
  517.9 4.0 copy-start.26
  618.9 4.7 copy-start.7
  623.5 3.7 copy-start
  730.0 5.4 copy-start.9
  801.5 45.3 %copy-start.16 = (bf16[1,512,1600]{2,1,0:T(8,128)(2,1)S(1)}, bf16[1,512,1600]{2,1,0:T(8,128)(2,1)}, u32[]{:S(2)}) copy-start(bf16[1,512,1600]{2,1,0:T(8,128)(2,1)} %copy-done.15) | copy-start | bytes 4915204
  856.7 7.1 copy-start.12
  (12 other events, 28.7 us)
Sparse Core Ops, SparseCore 0:
  53.9 103.6 all-gather.3
  184.7 106.3 all-gather.5
  293.3 55.0 all-gather.7
  456.7 108.5 reduce-scatter.8
  568.5 64.6 reduce-scatter.14
  635.5 95.2 reduce-scatter.10
  733.2 60.6 reduce-scatter.12

commit v3 on v2

--- a/solution.py
+++ b/solution.py
@@ -95,6 +95,83 @@
         self.own().wait()
         for d in range(1, self.size):
             self.copy(d).wait_send()
+
+
+class Spread:
+    def __init__(self, n, source, target, send, recv, local):
+        self.n, self.source, self.target = n, source, target
+        self.send, self.recv, self.local = send, recv, local
+        self.me = lax.axis_index("seq")
+        self.bits = route_bits(n)
+        self.orders = [self.bits, self.bits[::-1]]
+        self.h = source.shape[0] // 2
+
+    @staticmethod
+    def scratch(n):
+        dma = pltpu.SemaphoreType.DMA
+        return [dma((2, len(route_bits(n)) + 1, n)), dma((2, n)), dma]
+
+    def device(self, b):
+        return {"seq": flip(self.me, b)}
+
+    def peers(self):
+        return [self.device(b) for b in [1] + self.bits]
+
+    def rows(self, half):
+        return pl.ds(half * self.h, self.h)
+
+    def ship(self, half, k, b):
+        owner = place(self.me, k, self.n)
+        src = self.source if k == 0 else self.target.at[owner]
+        lane = 0 if b == 1 else 1 + self.bits.index(b)
+        return remote(
+            src.at[self.rows(half)],
+            self.target.at[owner].at[self.rows(half)],
+            self.send.at[half, lane, k],
+            self.recv.at[half, k ^ b],
+            self.device(b),
+        )
+
+    def arrive(self, half, k):
+        dst = self.target.at[place(self.me, k, self.n)].at[self.rows(half)]
+        remote(dst, dst, self.send.at[half, 0, 0], self.recv.at[half, k], self.device(1)).wait_recv()
+
+    def own(self):
+        return pltpu.make_async_copy(self.source, self.target.at[self.me], self.local)
+
+    def fresh(self, half, i):
+        had = [0]
+        for b in self.orders[half][:i]:
+            had = had + [k ^ b for k in had]
+        return [k ^ self.orders[half][i] for k in had]
+
+    def start(self):
+        for i in range(len(self.bits)):
+            for half in (0, 1):
+                self.ship(half, 0, self.orders[half][i]).start()
+        for half in (0, 1):
+            self.ship(half, 0, 1).start()
+        self.own().start()
+
+    def phase(self, i):
+        for half in (0, 1):
+            for k in self.fresh(half, i):
+                self.arrive(half, k)
+                for b in self.orders[half][i + 1 :] + [1]:
+                    self.ship(half, k, b).start()
+
+    def finish(self):
+        for half in (0, 1):
+            for k in range(1, self.n, 2):
+                self.arrive(half, k)
+        self.own().wait()
+        for half in (0, 1):
+            for b in self.orders[half] + [1]:
+                self.ship(half, 0, b).wait_send()
+            for i in range(len(self.bits)):
+                for k in self.fresh(half, i):
+                    for b in self.orders[half][i + 1 :] + [1]:
+                        self.ship(half, k, b).wait_send()
 
 
 def blocks_shape(x, size, same):
@@ -310,9 +387,9 @@
 
 
 class Side:
-    def __init__(self, count, product, refs):
-        self.count, self.product = count, product
-        self.a, self.b, self.grad, self.made, self.acc, self.abuf, self.bbuf, self.mbuf, self.load, self.store = refs
+    def __init__(self, count, refs):
+        self.count = count
+        self.a, self.b, self.grad, self.sums, self.acc, self.abuf, self.bbuf, self.load = refs
 
     def fetch(self, i):
         slot = lax.rem(i, 2)
@@ -321,12 +398,9 @@
             pltpu.make_async_copy(self.b.at[i], self.bbuf.at[slot], self.load.at[1, slot]),
         ]
 
-    def output(self, i):
-        slot = lax.rem(i, 2)
-        return pltpu.make_async_copy(self.mbuf.at[slot], self.made.at[i], self.store.at[slot])
-
     def begin(self):
         self.acc[...] = jnp.zeros_like(self.acc)
+        self.sums[...] = jnp.zeros_like(self.sums)
         for c in self.fetch(jnp.int32(0)):
             c.start()
 
@@ -344,50 +418,36 @@
             self.acc[...] += lax.dot_general(
                 a, b, (((0,), (0,)), ((), ())), preferred_element_type=jnp.float32
             )
-            if self.product is not None:
-
-                @pl.when(i >= 2)
-                def _():
-                    self.output(i).wait()
-
-                self.mbuf[slot] = self.product(a)
-                self.output(i).start()
+            self.sums[...] += jnp.sum(b.astype(jnp.float32), 0, keepdims=True)
             return carry
 
         lax.fori_loop(first, last, step, 0)
 
     def end(self):
         self.grad[...] = self.acc[...].astype(self.grad.dtype)
-        if self.product is not None:
-            for i in (self.count - 2, self.count - 1):
-                self.output(jnp.int32(i)).wait()
 
 
 def side_parts(side, count):
     if side is None:
         return [], [], [], [], []
-    a, b, product, made = side
+    a, b = side
     h = a.shape[0] // count
     low = jnp.bfloat16
-    made = made or 128
     hbm = pl.BlockSpec(memory_space=pl.ANY)
     vmem = pl.BlockSpec(memory_space=pltpu.VMEM)
-    dma = pltpu.SemaphoreType.DMA
     return (
         [x.reshape(count, h, x.shape[1]) for x in (a, b)],
         [
             jax.ShapeDtypeStruct((a.shape[1], b.shape[1]), low),
-            jax.ShapeDtypeStruct((count, h, made), low),
+            jax.ShapeDtypeStruct((1, b.shape[1]), jnp.float32),
         ],
         [hbm, hbm],
-        [vmem, hbm],
+        [vmem, vmem],
         [
             pltpu.VMEM((a.shape[1], b.shape[1]), jnp.float32),
             pltpu.VMEM((2, h, a.shape[1]), low),
             pltpu.VMEM((2, h, b.shape[1]), low),
-            pltpu.VMEM((2, h, made), low),
-            dma((2, 2)),
-            dma((2,)),
+            pltpu.SemaphoreType.DMA((2, 2)),
         ],
     )
 
@@ -401,16 +461,17 @@
     return orders, [(half, lists[half][i]) for i in range(n // 2) for half in (0, 1)]
 
 
-def scatter_kernel(n, h, body, n_in, n_const, n_out, modes, nf, same, product, *refs):
+def scatter_kernel(n, h, body, n_in, n_const, n_out, modes, nf, same, has_side, carried, *refs):
+    if carried:
+        out = n_in + n_const + 2 * has_side + min(nf, 1) + 2 + n_out + 2 * has_side + min(nf, 1)
+        refs = refs[1:out] + refs[out + 1 :]
     side = None
-    if product is not False:
+    if has_side:
         at = n_in + n_const
         out = at + 2 + min(nf, 1) + 1 + n_out
-        extra = refs[at : at + 2] + refs[out : out + 2] + refs[-6:]
-        refs = refs[:at] + refs[at + 2 : out] + refs[out + 2 : -6]
-        consts = refs[n_in : n_in + n_const]
-        make = None if product is None else lambda a: product(a, *consts)
-        side = Side(2 * n, make, extra)
+        extra = refs[at : at + 2] + refs[out : out + 2] + refs[-4:]
+        refs = refs[:at] + refs[at + 2 : out] + refs[out + 2 : -4]
+        side = Side(2 * n, extra)
     refs, rider = split_rider(refs, nf, same, n_in + n_const, 1 + n_out)
     ins = refs[:n_in]
     consts = refs[n_in : n_in + n_const]
@@ -571,7 +632,7 @@
         side.end()
 
 
-def seq_scatter(n, cols, ident, name, body, ins, consts, outs=(), modes=None, rider=None, side=None):
+def seq_scatter(n, cols, ident, name, body, ins, consts, outs=(), modes=None, rider=None, side=None, carry=None):
     h = ins[0].shape[0] // (2 * n)
     low = jnp.bfloat16
     slots = min(4, n)
@@ -582,17 +643,19 @@
     modes = modes or ([0] * len(ins), [0] * len(outs))
     more, spec, shape, scratch, nf, same = rider_parts(rider)
     s_ins, s_shapes, s_in_specs, s_out_specs, s_scratch = side_parts(side, 2 * n)
-    product = False if side is None else side[2]
+    carries = [] if carry is None else [carry]
     out = pl.pallas_call(
         functools.partial(
-            scatter_kernel, n, h, body, len(ins), len(consts), len(outs), modes, nf, same, product
+            scatter_kernel, n, h, body, len(ins), len(consts), len(outs), modes, nf, same, int(side is not None), carry is not None
         ),
         out_shape=[jax.ShapeDtypeStruct((2 * h, cols), jnp.float32)]
         + [jax.ShapeDtypeStruct((2 * n, h, c), d) for c, d in outs]
         + s_shapes
-        + shape,
-        in_specs=[hbm] * len(ins) + [vmem] * len(consts) + s_in_specs + spec,
-        out_specs=[hbm] * (1 + len(outs)) + s_out_specs + spec,
+        + shape
+        + [jax.ShapeDtypeStruct(x.shape, x.dtype) for x in carries],
+        in_specs=[hbm] * (len(carries) + len(ins)) + [vmem] * len(consts) + s_in_specs + spec,
+        out_specs=[hbm] * (1 + len(outs)) + s_out_specs + spec + [hbm] * len(carries),
+        input_output_aliases={0: 1 + len(outs) + len(s_shapes) + len(shape)} if carries else {},
         scratch_shapes=[
             pltpu.VMEM((slots, h, cols), low),
             pltpu.VMEM((n, h, cols), low),
@@ -618,9 +681,9 @@
         ),
         cost_estimate=SMALL,
         name=name,
-    )(*split, *consts, *s_ins, *more)
+    )(*carries, *split, *consts, *s_ins, *more)
     many = 1 + len(outs)
-    sides = [] if side is None else [out[many], out[many + 1].reshape(2 * n * h, -1)]
+    sides = [] if side is None else list(out[many : many + 2])
     more = list(out[many + len(sides) :])
     return [out[0]] + [o.reshape(2 * n * h, o.shape[2]) for o in out[1:many]] + sides + more
 
@@ -826,11 +889,14 @@
     )(x)
 
 
-def to_heads_kernel(n, wide, x_ref, w_ref, a_ref, b_ref, o_ref, g_ref, m_ref, made, send, recv, local, *extra):
+def to_heads_kernel(n, nf, wide, x_ref, w_ref, a_ref, b_ref, z_ref, o_ref, g_ref, m_ref, z_out, made, send, recv, local, *extra):
     me = lax.axis_index("seq")
-    side = Side(2 * n, None, (a_ref, b_ref, g_ref, m_ref) + extra)
+    rider = Blocks("fsdp", nf, False, z_ref, z_out, *extra[-3:])
+    extra = extra[:-3]
+    side = Side(2 * n, (a_ref, b_ref, g_ref, m_ref) + extra)
     side.begin()
-    greet([{"seq": place(me, r, n)} for r in range(1, n)])
+    greet([{"seq": place(me, r, n)} for r in range(1, n)] + rider.peers())
+    rider.start()
 
     def copy(r):
         to = place(me, r, n)
@@ -860,45 +926,32 @@
     for r in range(1, n):
         copy(r).wait_send()
     side.end()
-
-
-def to_heads(x, w, n, wide, ident, a, b):
+    rider.finish()
+
+
+def to_heads(x, w, n, nf, wide, ident, a, b, z):
     rows = x.shape[0]
     vmem = pl.BlockSpec(memory_space=pltpu.VMEM)
     hbm = pl.BlockSpec(memory_space=pl.ANY)
-    s_ins, s_shapes, s_in_specs, s_out_specs, s_scratch = side_parts((a, b, None, 0), 2 * n)
+    s_ins, s_shapes, s_in_specs, s_out_specs, s_scratch = side_parts((a, b), 2 * n)
     out = pl.pallas_call(
-        functools.partial(to_heads_kernel, n, wide),
-        out_shape=[jax.ShapeDtypeStruct((n, rows, wide), x.dtype)] + s_shapes,
-        in_specs=[vmem, vmem] + s_in_specs,
-        out_specs=[hbm] + s_out_specs,
-        scratch_shapes=[pltpu.VMEM((n, rows, wide), x.dtype)] + Blocks.scratch(n) + s_scratch,
+        functools.partial(to_heads_kernel, n, nf, wide),
+        out_shape=[jax.ShapeDtypeStruct((n, rows, wide), x.dtype)]
+        + s_shapes
+        + [blocks_shape(z, nf, False)],
+        in_specs=[vmem, vmem] + s_in_specs + [hbm],
+        out_specs=[hbm] + s_out_specs + [hbm],
+        scratch_shapes=[pltpu.VMEM((n, rows, wide), x.dtype)]
+        + Blocks.scratch(n)
+        + s_scratch
+        + Blocks.scratch(nf),
         compiler_params=pltpu.CompilerParams(
             collective_id=ident, has_side_effects=True, vmem_limit_bytes=60 << 20
         ),
         cost_estimate=SMALL,
         name="to_heads",
-    )(x, w, *s_ins)
-    return out[0], out[1]
-
-
-def project_kernel(x_ref, w_ref, b_ref, o_ref):
-    o_ref[...] = (mm(x_ref[...], w_ref[...]) + b_ref[...]).astype(o_ref.dtype)
-
-
-def project(x, w, bias, tile):
-    rows, cols = x.shape[0], w.shape[1]
-    still = lambda shape: pl.BlockSpec(shape, lambda i: (0, 0), pipeline_mode=pl.Buffered(1))
-    return pl.pallas_call(
-        project_kernel,
-        out_shape=jax.ShapeDtypeStruct((rows, cols), x.dtype),
-        grid=(rows // tile,),
-        in_specs=[pl.BlockSpec((tile, x.shape[1]), lambda i: (i, 0)), still(w.shape), still((1, cols))],
-        out_specs=pl.BlockSpec((tile, cols), lambda i: (i, 0)),
-        compiler_params=pltpu.CompilerParams(vmem_limit_bytes=40 << 20),
-        cost_estimate=SMALL,
-        name="project",
-    )(x, w, bias)
+    )(x, w, *s_ins, z)
+    return out
 
 
 def contract_kernel(a_ref, b_ref, ready, o_ref, acc):
@@ -1029,178 +1082,355 @@
 HEAD=64
 SCALE=0.125*math.log2(math.e)
 
-def block_table(lengths, parents, slots, trunk, block):
-    count=lengths.shape[0]
-    branches=count//3
-    fixed,owner,child=[],[],[]
+
+def block_pairs(slots, trunk):
+    branches = (slots - trunk) // 3
+    pairs = []
     for t in range(slots):
-        m=t-trunk
-        if t<trunk:
-            keys=[(c,0 if c==t else block,-1,-1) for c in range(t+1)]
+        m = t - trunk
+        if t < trunk:
+            keys = [(c, int(c == t), -1, -1) for c in range(t + 1)]
         else:
-            keys=[(c,block,-1,-1) for c in range(trunk)]
-            if m>=branches:
-                keys.append((trunk-1,block,-1,m))
-            keys.append((t,0,m,-1))
-        for i,(c,shift,own,leaf) in enumerate(keys):
-            fixed.append((t,c,shift,int(i==0),int(i==len(keys)-1)))
-            owner.append(own)
-            child.append(leaf)
-    fixed=np.array(fixed,np.int32).T
-    segments=np.arange(count)
-    own=np.array(owner)[None,:]==segments[:,None]
-    leaf=np.array(child)[None,:]==segments[:,None]
-    above=jnp.sum(jnp.where(leaf,parents[:,None],0),0)
-    source=own|(segments[:,None]+1==above[None,:])
-    closed=(np.array(owner)<0)&(np.array(child)<0)
-    reach=jnp.where(closed,block,jnp.sum(jnp.where(source,lengths[:,None],0),0))
-    masked=jnp.where((fixed[2]==0)|(reach<block),1,0)
-    return jnp.stack([fixed[0],fixed[1]+above,fixed[2],reach,masked,fixed[3],fixed[4]]).astype(jnp.int32)
+            keys = [(c, 0, -1, -1) for c in range(trunk)]
+            if m >= branches:
+                keys.append((trunk, 0, -1, m))
+            keys.append((t, 1, m, -1))
+        for i, (c, causal, own, leaf) in enumerate(keys):
+            pairs.append((t, c, causal, own, leaf, int(i == 0), int(i == len(keys) - 1)))
+    return pairs
+
+
+def block_fields(p, slots, trunk):
+    branches = (slots - trunk) // 3
+    counts = [t + 1 for t in range(trunk)] + [trunk + 1] * branches
+    counts += [trunk + 2] * (slots - trunk - branches)
+    starts = [sum(counts[:t]) for t in range(slots)]
+    t, begin, end = jnp.int32(0), jnp.int32(0), jnp.int32(counts[0])
+    for i in range(1, slots):
+        here = p >= starts[i]
+        t = jnp.where(here, i, t)
+        begin = jnp.where(here, starts[i], begin)
+        end = jnp.where(here, starts[i] + counts[i], end)
+    i = p - begin
+    last = p == end - 1
+    leaf = (t >= trunk + branches) & (i == trunk)
+    key = jnp.where((t >= trunk) & last, t, i)
+    return t, key, last, leaf, i == 0, last
+
+
+def block_values(lengths, parents, pairs, block):
+    count = lengths.shape[0]
+    segments = np.arange(count)
+    own = np.array([p[3] for p in pairs])[None, :] == segments[:, None]
+    leaf = np.array([p[4] for p in pairs])[None, :] == segments[:, None]
+    above = jnp.sum(jnp.where(leaf, parents[:, None], 0), 0)
+    source = own | (segments[:, None] + 1 == above[None, :])
+    closed = np.array([p[3] < 0 and p[4] < 0 for p in pairs])
+    reach = jnp.where(closed, block, jnp.sum(jnp.where(source, lengths[:, None], 0), 0))
+    return jnp.stack([jnp.maximum(above - 1, 0), reach]).astype(jnp.int32)
+
 
 def lane_half(shape):
-    return lax.broadcasted_iota(jnp.int32,shape,len(shape)-1)<HEAD
-
-def nt(a,b):
-    return lax.dot_general(a,b,(((1,),(1,)),((),())),preferred_element_type=jnp.float32)
-
-def mm(a,b):
-    return jnp.dot(a,b,preferred_element_type=jnp.float32)
-
-def attend_kernel(width, block, tab, qkv, low, att, tot, acc):
-    p=pl.program_id(0)
-    qs,ks,shift,count,masked=tab[0,p],tab[1,p],tab[2,p],tab[3,p],tab[4,p]
-    first,last=tab[5,p],tab[6,p]
-    qrow=pl.ds(pl.multiple_of(qs*block,block),block)
-    krow=pl.ds(pl.multiple_of(ks*block,block),block)
-    left=lane_half((block,2*HEAD))
-    @pl.when(first==1)
-    def _(): acc[...]=jnp.zeros_like(acc)
+    return lax.broadcasted_iota(jnp.int32, shape, len(shape) - 1) < HEAD
+
+
+def nt(a, b):
+    return lax.dot_general(a, b, (((1,), (1,)), ((), ())), preferred_element_type=jnp.float32)
+
+
+def mm(a, b):
+    return jnp.dot(a, b, preferred_element_type=jnp.float32)
+
+
+def attend_kernel(width, block, trunk, n, values, x_ref, w_ref, b_ref, c_ref, qkv, low, att, tot, kt, c_all, acc, xbuf, xsem, *sems):
+    p = pl.program_id(0)
+    slot, key, causal, leaf, first, last = block_fields(p, n, trunk)
+    rows = lambda slot: pl.ds(pl.multiple_of(slot * block, block), block)
+    qrow = rows(slot)
+    above = values[0, p]
+    reach = values[1, p]
+    branches = (n - trunk) // 3
+    left = lane_half((block, 2 * HEAD))
+    spread = Spread(n, c_ref, c_all, *sems)
+
+    def fetch(i):
+        slot = lax.rem(i, 2)
+        return pltpu.make_async_copy(x_ref.at[i], xbuf.at[slot], xsem.at[slot])
+
+    @pl.when(p == 0)
+    def _():
+        fetch(jnp.int32(0)).start()
+        greet(spread.peers())
+        spread.start()
+
+        def step(i, carry):
+            @pl.when(i + 1 < n)
+            def _():
+                fetch(i + 1).start()
+
+            fetch(i).wait()
+            made = (mm(xbuf[lax.rem(i, 2)], w_ref[...]) + b_ref[...]).astype(qkv.dtype)
+            qkv[rows(i)] = made
+            kt[:, rows(i)] = made[:, width : 2 * width].T
+            return carry
+
+        lax.fori_loop(0, n, step, 0)
+        for i in range(len(spread.bits) - 1):
+            spread.phase(i)
+
+    @pl.when(first)
+    def _():
+        acc[...] = jnp.zeros_like(acc)
+
+    def keyed(mask, read):
+        got = read(rows(key))
+        if mask is not None:
+            for b in range(1, branches):
+                got = jnp.where(leaf & (above == b), read(pl.ds((trunk + b) * block, block)), got)
+        return got
+
     def step(mask):
-        for j in range(width//(2*HEAD)):
-            q=qkv[qrow,j*2*HEAD:(j+1)*2*HEAD]
-            k=qkv[krow,width+j*2*HEAD:width+(j+1)*2*HEAD]
-            v=qkv[krow,2*width+j*2*HEAD:2*width+(j+1)*2*HEAD]
+        for j in range(width // (2 * HEAD)):
+            lanes = slice(j * 2 * HEAD, (j + 1) * 2 * HEAD)
+            q = qkv[qrow, lanes]
+            k = keyed(mask, lambda at: qkv[at, width + j * 2 * HEAD : width + (j + 1) * 2 * HEAD])
+            v = keyed(mask, lambda at: qkv[at, 2 * width + j * 2 * HEAD : 2 * width + (j + 1) * 2 * HEAD])
             for h in range(2):
-                here=left if h==0 else jnp.logical_not(left)
-                s=nt(jnp.where(here,q,0),k)
-                e=jnp.exp2(s*SCALE)
-                if mask is not None: e=jnp.where(mask,e,0.0)
-                acc[2*j+h]+=mm(e.astype(jnp.bfloat16),jnp.where(here,v,1))
-    @pl.when(masked==0)
-    def _(): step(None)
-    @pl.when(masked==1)
+                here = left if h == 0 else jnp.logical_not(left)
+                s = nt(jnp.where(here, q, 0), k)
+                e = jnp.exp2(s * SCALE)
+                if mask is not None:
+                    e = jnp.where(mask, e, 0.0)
+                acc[2 * j + h] += mm(e.astype(jnp.bfloat16), jnp.where(here, v, 1))
+
+    closes = causal | leaf
+    shift = jnp.where(causal, 0, block)
+
+    @pl.when(jnp.logical_not(closes))
     def _():
-        row=lax.broadcasted_iota(jnp.int32,(block,block),0)
-        col=lax.broadcasted_iota(jnp.int32,(block,block),1)
-        step((col<=row+shift)&(col<count))
-    @pl.when(last==1)
+        step(None)
+
+    @pl.when(closes)
     def _():
-        for j in range(width//(2*HEAD)):
-            a,b=acc[2*j],acc[2*j+1]
-            total=jnp.where(left,pltpu.roll(a,HEAD,1),pltpu.roll(b,HEAD,1))
-            value=jnp.where(left,a,b)/total
-            lanes=slice(j*2*HEAD,(j+1)*2*HEAD)
-            low[:,lanes]=value.astype(jnp.bfloat16)
-            att[:,lanes]=value
-            tot[:,lanes]=total
-
-def attend(table, qkv, block):
-    rows,width=qkv.shape[0],qkv.shape[1]//3
-    steps=table.shape[1]
-    by_q=lambda p,t:(t[0,p],0)
-    heads=width//HEAD
-    return pl.pallas_call(functools.partial(attend_kernel,width,block),
-        out_shape=(jax.ShapeDtypeStruct((rows,width),jnp.bfloat16),jax.ShapeDtypeStruct((rows,width),jnp.float32),jax.ShapeDtypeStruct((rows,width),jnp.float32)),
-        grid_spec=pltpu.PrefetchScalarGridSpec(num_scalar_prefetch=1,grid=(steps,),
-            in_specs=[pl.BlockSpec((rows,3*width),lambda p,t:(0,0),pipeline_mode=pl.Buffered(1))],
-            out_specs=[pl.BlockSpec((block,width),by_q)]*3,
-            scratch_shapes=[pltpu.VMEM((heads,block,2*HEAD),jnp.float32)]),
-        compiler_params=pltpu.CompilerParams(dimension_semantics=("arbitrary",),vmem_limit_bytes=50<<20),
+        row = lax.broadcasted_iota(jnp.int32, (block, block), 0)
+        col = lax.broadcasted_iota(jnp.int32, (block, block), 1)
+        step((col <= row + shift) & (col < reach))
+
+    @pl.when(last)
+    def _():
+        for j in range(width // (2 * HEAD)):
+            a, b = acc[2 * j], acc[2 * j + 1]
+            total = jnp.where(left, pltpu.roll(a, HEAD, 1), pltpu.roll(b, HEAD, 1))
+            value = jnp.where(left, a, b) / total
+            lanes = slice(j * 2 * HEAD, (j + 1) * 2 * HEAD)
+            low[:, lanes] = value.astype(jnp.bfloat16)
+            att[:, lanes] = value
+            tot[:, lanes] = total
+
+    @pl.when(p == pl.num_programs(0) - 1)
+    def _():
+        spread.phase(len(spread.bits) - 1)
+        spread.finish()
+
+
+def attend(values, pairs, x, w, bias, block, trunk, sent, n, ident):
+    rows, width = x.shape[0], w.shape[1] // 3
+    by_q = lambda p: (block_fields(p, n, trunk)[0], 0)
+    heads = width // HEAD
+    once = lambda s: pl.BlockSpec(s, lambda p: (0,) * len(s), pipeline_mode=pl.Buffered(1))
+    hbm = pl.BlockSpec(memory_space=pl.ANY)
+    out = pl.pallas_call(
+        functools.partial(attend_kernel, width, block, trunk, n),
+        grid=(len(pairs),),
+        out_shape=(
+            jax.ShapeDtypeStruct((rows, 3 * width), x.dtype),
+            jax.ShapeDtypeStruct((rows, width), x.dtype),
+            jax.ShapeDtypeStruct((rows, width), jnp.float32),
+            jax.ShapeDtypeStruct((rows, width), jnp.float32),
+            jax.ShapeDtypeStruct((width, rows), x.dtype),
+            jax.ShapeDtypeStruct((n,) + sent.shape, sent.dtype),
+        ),
+        in_specs=[pl.BlockSpec(memory_space=pltpu.SMEM), hbm, once(w.shape), once(bias.shape), hbm],
+        out_specs=[once((rows, 3 * width))]
+        + [pl.BlockSpec((block, width), by_q)] * 3
+        + [once((width, rows)), hbm],
+        scratch_shapes=[
+            pltpu.VMEM((heads, block, 2 * HEAD), jnp.float32),
+            pltpu.VMEM((2, block, x.shape[1]), x.dtype),
+            pltpu.SemaphoreType.DMA((2,)),
+        ]
+        + Spread.scratch(n),
+        compiler_params=pltpu.CompilerParams(
+            dimension_semantics=("arbitrary",),
+            vmem_limit_bytes=60 << 20,
+            collective_id=ident,
+            has_side_effects=True,
+        ),
         cost_estimate=SMALL,
-        name="attend")(table,qkv)
-
-def attend_back_kernel(width, block, tab, qkv, kt, datt, att, tot, out, dk, dv, dqt, aug):
-    p=pl.program_id(0)
-    qs,ks,shift,count,masked=tab[0,p],tab[1,p],tab[2,p],tab[3,p],tab[4,p]
-    first,last=tab[5,p],tab[6,p]
-    qrow=pl.ds(pl.multiple_of(qs*block,block),block)
-    krow=pl.ds(pl.multiple_of(ks*block,block),block)
-    left=lane_half((block,2*HEAD))
-    lane=lax.broadcasted_iota(jnp.int32,(block,2*HEAD),1)
-    pairs=width//(2*HEAD)
-    @pl.when(p==0)
+        name="attend",
+    )(values, x.reshape(n, block, x.shape[1]), w, bias, sent)
+    return out[:5] + (out[5].reshape(n * sent.shape[0], sent.shape[1]),)
+
+
+def attend_back_kernel(width, block, slots, trunk, branches, nf, count, *refs):
+    values, qkv, kt, datt, att, tot = refs[:6]
+    sources = refs[6 : 6 + count]
+    out, sums = refs[6 + count : 8 + count]
+    targets = refs[8 + count : 8 + 2 * count]
+    dk, dv, dqt, aug = refs[8 + 2 * count : 12 + 2 * count]
+    sems = refs[12 + 2 * count :]
+    riders = [
+        Blocks("fsdp", nf, False, sources[i], targets[i], *sems[3 * i : 3 * i + 3]) for i in range(count)
+    ]
+    p = pl.program_id(0)
+    slot, key, causal, leaf, first, last = block_fields(p, slots, trunk)
+    rows = lambda slot: pl.ds(pl.multiple_of(slot * block, block), block)
+    above = values[0, p]
+    reach = values[1, p]
+    qrow = rows(slot)
+    left = lane_half((block, 2 * HEAD))
+    lane = lax.broadcasted_iota(jnp.int32, (block, 2 * HEAD), 1)
+    columns = width // (2 * HEAD)
+
+    @pl.when(p == 0)
     def _():
-        dk[...]=jnp.zeros_like(dk)
-        dv[...]=jnp.zeros_like(dv)
-    @pl.when(first==1)
+        greet(riders[0].peers())
+        for r in riders:
+            r.start()
+        dk[...] = jnp.zeros_like(dk)
+        dv[...] = jnp.zeros_like(dv)
+
+    @pl.when(first)
     def _():
-        dqt[...]=jnp.zeros_like(dqt)
-        for j in range(pairs):
-            lanes=slice(j*2*HEAD,(j+1)*2*HEAD)
-            d=datt[:,lanes].astype(jnp.float32)
-            total=tot[:,lanes]
-            low=(d/total).astype(jnp.bfloat16)
-            prod=d*att[:,lanes]/total
+        dqt[...] = jnp.zeros_like(dqt)
+        for j in range(columns):
+            lanes = slice(j * 2 * HEAD, (j + 1) * 2 * HEAD)
+            d = datt[:, lanes].astype(jnp.float32)
+            total = tot[:, lanes]
+            low = (d / total).astype(jnp.bfloat16)
+            prod = d * att[:, lanes] / total
             for h in range(2):
-                here=left if h==0 else jnp.logical_not(left)
-                delta=-jnp.sum(jnp.where(here,prod,0.0),1,keepdims=True)
-                hi=delta.astype(jnp.bfloat16).astype(jnp.float32)
-                mid=(delta-hi).astype(jnp.bfloat16).astype(jnp.float32)
-                rest=delta-hi-mid
-                at=HEAD*(1-h)
-                extra=jnp.where(lane==at,hi,jnp.where(lane==at+1,mid,jnp.where(lane==at+2,rest,0.0)))
-                aug[2*j+h]=jnp.where(here,low.astype(jnp.float32),extra).astype(jnp.bfloat16)
+                here = left if h == 0 else jnp.logical_not(left)
+                delta = -jnp.sum(jnp.where(here, prod, 0.0), 1, keepdims=True)
+                hi = delta.astype(jnp.bfloat16).astype(jnp.float32)
+                mid = (delta - hi).astype(jnp.bfloat16).astype(jnp.float32)
+                rest = delta - hi - mid
+                at = HEAD * (1 - h)
+                extra = jnp.where(
+                    lane == at, hi, jnp.where(lane == at + 1, mid, jnp.where(lane == at + 2, rest, 0.0))
+                )
+                aug[2 * j + h] = jnp.where(here, low.astype(jnp.float32), extra).astype(jnp.bfloat16)
+
+    def add(lanes, dks, dvs):
+        @pl.when(jnp.logical_not(leaf))
+        def _():
+            at = rows(key)
+            dk[at, lanes] += dks
+            dv[at, lanes] += dvs
+
+        @pl.when(leaf)
+        def _():
+            for b in range(branches):
+                at = pl.ds((trunk + b) * block, block)
+                dk[at, lanes] += jnp.where(above == b, dks, 0.0)
+                dv[at, lanes] += jnp.where(above == b, dvs, 0.0)
+
+    def keyed(mask, read):
+        got = read(rows(key))
+        if mask is not None:
+            for b in range(1, branches):
+                got = jnp.where(leaf & (above == b), read(pl.ds((trunk + b) * block, block)), got)
+        return got
+
     def step(mask):
-        for j in range(pairs):
-            q=qkv[qrow,j*2*HEAD:(j+1)*2*HEAD]
-            k=qkv[krow,width+j*2*HEAD:width+(j+1)*2*HEAD]
-            v=qkv[krow,2*width+j*2*HEAD:2*width+(j+1)*2*HEAD]
-            lanes=slice(j*2*HEAD,(j+1)*2*HEAD)
-            dvs,dks=[],[]
+        for j in range(columns):
+            lanes = slice(j * 2 * HEAD, (j + 1) * 2 * HEAD)
+            q = qkv[qrow, lanes]
+            k = keyed(mask, lambda at: qkv[at, width + j * 2 * HEAD : width + (j + 1) * 2 * HEAD])
+            v = keyed(mask, lambda at: qkv[at, 2 * width + j * 2 * HEAD : 2 * width + (j + 1) * 2 * HEAD])
+            dvs, dks = [], []
             for h in range(2):
-                here=left if h==0 else jnp.logical_not(left)
-                qh=jnp.where(here,q,0)
-                e=jnp.exp2(nt(k,qh)*SCALE)
-                if mask is not None: e=jnp.where(mask,e,0.0)
-                dod=aug[2*j+h]
-                ds=(e*nt(jnp.where(here,v*0.125,0.125).astype(jnp.bfloat16),dod)).astype(jnp.bfloat16)
-                dvs.append(mm(e.astype(jnp.bfloat16),dod))
-                dks.append(mm(ds,qh))
-                at=j*2*HEAD+h*HEAD
-                dqt[at:at+HEAD]+=mm(kt[at:at+HEAD,krow],ds)
-            dv[krow,lanes]+=jnp.where(left,dvs[0],dvs[1])
-            dk[krow,lanes]+=dks[0]+dks[1]
-    @pl.when(masked==0)
-    def _(): step(None)
-    @pl.when(masked==1)
+                here = left if h == 0 else jnp.logical_not(left)
+                qh = jnp.where(here, q, 0)
+                e = jnp.exp2(nt(k, qh) * SCALE)
+                if mask is not None:
+                    e = jnp.where(mask, e, 0.0)
+                dod = aug[2 * j + h]
+                ds = (e * nt(jnp.where(here, v * 0.125, 0.125).astype(jnp.bfloat16), dod)).astype(
+                    jnp.bfloat16
+                )
+                dvs.append(mm(e.astype(jnp.bfloat16), dod))
+                dks.append(mm(ds, qh))
+                at = j * 2 * HEAD + h * HEAD
+                dqt[at : at + HEAD] += mm(keyed(mask, lambda i: kt[at : at + HEAD, i]), ds)
+            add(lanes, dks[0] + dks[1], jnp.where(left, dvs[0], dvs[1]))
+
+    closes = causal | leaf
+    shift = jnp.where(causal, 0, block)
+
+    @pl.when(jnp.logical_not(closes))
     def _():
-        col=lax.broadcasted_iota(jnp.int32,(block,block),0)
-        row=lax.broadcasted_iota(jnp.int32,(block,block),1)
-        step((col<=row+shift)&(col<count))
-    @pl.when(last==1)
+        step(None)
+
+    @pl.when(closes)
     def _():
-        out[qrow,0:width]=dqt[...].T.astype(jnp.bfloat16)
-    @pl.when(p==pl.num_programs(0)-1)
+        col = lax.broadcasted_iota(jnp.int32, (block, block), 0)
+        row = lax.broadcasted_iota(jnp.int32, (block, block), 1)
+        step((col <= row + shift) & (col < reach))
+
+    @pl.when(last)
     def _():
-        out[:,width:2*width]=dk[...].astype(jnp.bfloat16)
-        out[:,2*width:]=dv[...].astype(jnp.bfloat16)
-
-def attend_back(table, qkv, datt, att, tot, block):
-    rows,width=qkv.shape[0],qkv.shape[1]//3
-    steps=table.shape[1]
-    by_q=lambda p,t:(t[0,p],0)
-    heads=width//HEAD
-    kt=qkv[:,width:2*width].T
-    whole=lambda s:pl.BlockSpec(s,lambda p,t:(0,0),pipeline_mode=pl.Buffered(1))
-    return pl.pallas_call(functools.partial(attend_back_kernel,width,block),
-        out_shape=jax.ShapeDtypeStruct((rows,3*width),jnp.bfloat16),
-        grid_spec=pltpu.PrefetchScalarGridSpec(num_scalar_prefetch=1,grid=(steps,),
-            in_specs=[whole((rows,3*width)),whole((width,rows))]+[pl.BlockSpec((block,width),by_q)]*3,
-            out_specs=whole((rows,3*width)),
-            scratch_shapes=[pltpu.VMEM((rows,width),jnp.float32),pltpu.VMEM((rows,width),jnp.float32),pltpu.VMEM((width,block),jnp.float32),pltpu.VMEM((heads,block,2*HEAD),jnp.bfloat16)]),
-        compiler_params=pltpu.CompilerParams(dimension_semantics=("arbitrary",),vmem_limit_bytes=60<<20),
+        out[qrow, 0:width] = dqt[...].T.astype(jnp.bfloat16)
+
+    @pl.when(p == pl.num_programs(0) - 1)
+    def _():
+        out[:, width : 2 * width] = dk[...].astype(jnp.bfloat16)
+        out[:, 2 * width :] = dv[...].astype(jnp.bfloat16)
+        for t in range(3):
+            lanes = slice(t * width, (t + 1) * width)
+            sums[:, lanes] = jnp.sum(out[:, lanes].astype(jnp.float32), 0, keepdims=True)
+        for r in riders:
+            r.finish()
+
+
+def attend_back(values, pairs, qkv, kt, datt, att, tot, block, trunk, nf, riders, ident):
+    rows, width = qkv.shape[0], qkv.shape[1] // 3
+    by_q = lambda p: (block_fields(p, rows // block, trunk)[0], 0)
+    heads = width // HEAD
+    branches = (rows // block - trunk) // 3
+    once = lambda s: pl.BlockSpec(s, lambda p: (0,) * len(s), pipeline_mode=pl.Buffered(1))
+    hbm = pl.BlockSpec(memory_space=pl.ANY)
+    out = pl.pallas_call(
+        functools.partial(
+            attend_back_kernel, width, block, rows // block, trunk, branches, nf, len(riders)
+        ),
+        grid=(len(pairs),),
+        out_shape=[
+            jax.ShapeDtypeStruct((rows, 3 * width), jnp.bfloat16),
+            jax.ShapeDtypeStruct((1, 3 * width), jnp.float32),
+        ]
+        + [blocks_shape(r, nf, False) for r in riders],
+        in_specs=[pl.BlockSpec(memory_space=pltpu.SMEM), once((rows, 3 * width)), once((width, rows))]
+        + [pl.BlockSpec((block, width), by_q)] * 3
+        + [hbm] * len(riders),
+        out_specs=[once((rows, 3 * width)), once((1, 3 * width))] + [hbm] * len(riders),
+        scratch_shapes=[
+            pltpu.VMEM((rows, width), jnp.float32),
+            pltpu.VMEM((rows, width), jnp.float32),
+            pltpu.VMEM((width, block), jnp.float32),
+            pltpu.VMEM((heads, block, 2 * HEAD), jnp.bfloat16),
+        ]
+        + sum([Blocks.scratch(nf) for _ in riders], []),
+        compiler_params=pltpu.CompilerParams(
+            dimension_semantics=("arbitrary",),
+            vmem_limit_bytes=60 << 20,
+            collective_id=ident,
+            has_side_effects=True,
+        ),
         cost_estimate=SMALL,
-        name="attend_back")(table,qkv,kt,datt,att,tot)
+        name="attend_back",
+    )(values, qkv, kt, datt, att, tot, *riders)
+    return out[0], out[1], out[2:]
 
 
 def layer_norm(values, gain, shift):
@@ -1295,7 +1525,8 @@
         turned = lax.all_gather(qkv_weight.T, "seq", axis=0, tiled=True).reshape(3, width, rows)
         turned = jnp.pad(turned, ((0, 0), (0, n * wide - width), (0, 0)))
         turned = lax.dynamic_slice_in_dim(turned, s * wide, wide, 1).reshape(3 * wide, rows)
-    table = block_table(seg_lengths[0], parents[0], n, trunk, block)
+    pairs = block_pairs(n, trunk)
+    table = block_values(seg_lengths[0], parents[0], pairs, block)
 
     resid = tokens[0].astype(wider)
     out_turned = jnp.pad(out_blocks.reshape(width, width // n).T, ((0, 0), (0, n * wide - width)))
@@ -1313,19 +1544,17 @@
     fc_mine = lax.all_gather(fc_rows, "fsdp", axis=0, tiled=True)
 
     upstream = cotangent[0].astype(wider)
-    projected = project(normed_one, qkv_mine, bias_mine, block // 2)
-    sent = row_major(after(after(cotangent[0], fc_mine), projected))
-    upstream_all = row_major(lax.all_gather(sent, "seq", axis=0, tiled=True))
-    table = after(table, sent)
-    attended_low, attended, totals = attend(table, projected, block)
     proj_rows = proj_blocks.transpose(1, 0, 2).reshape(piece, width)
-    proj_mine = lax.all_gather(after(proj_rows, attended_low), "fsdp", axis=0, tiled=True)
+    proj_mine = lax.all_gather(after(proj_rows, normed_one), "fsdp", axis=0, tiled=True)
+    projected, attended_low, attended, totals, keys_turned, upstream_all = attend(
+        table, pairs, normed_one, qkv_mine, bias_mine, block, trunk, cotangent[0], n, 8
+    )
     attended_mine = to_tokens(attended_low.reshape(n, block, wide), n, wide, 2)
-    middle = after(resid, upstream_all) + contract_cols(attended_mine, out_turned) + bias_out
+    middle = resid + contract_cols(attended_mine, out_turned) + bias_out
     normed_two = layer_norm(middle, gain_two, shift_two).astype(low)
     ff = nf * piece
 
-    def expand(value, fc, bias):
+    def expand(value, fc, bias, proj):
         pre = mm(value, fc[...]) + bias[...]
         bend = math.sqrt(2 / math.pi)
         square = pre * pre
@@ -1333,24 +1562,24 @@
         half = 0.5 + 0.5 * inner
         act = (pre * half).astype(low)
         slope = half + 0.5 * pre * (1 - inner * inner) * (bend + 3 * bend * 0.044715 * square)
-        return act, slope.astype(low)
-
-    normed_two, hidden_act, hidden_slope = seq_gather(
+        return act, slope.astype(low), mm(act, proj[...]).astype(low)
+
+    normed_two, hidden_act, hidden_slope, mixed = seq_gather(
         normed_two,
         n,
         3,
         "gather_two",
         expand,
-        (fc_mine, bias_hidden),
-        ((ff, low), (ff, low)),
-        modes=(0, 0),
+        (fc_mine, bias_hidden, proj_mine),
+        ((ff, low), (ff, low), (width, low)),
+        modes=(0, 0, 0),
     )
 
     def shrink(up, slope, proj, fc):
         grad = (nt(up, proj[...]) * slope.astype(wider)).astype(low)
         return nt(grad, fc[...]), grad
 
-    grad_normed_two, grad_pre, grad_proj, mixed = seq_scatter(
+    grad_normed_two, grad_pre, grad_proj, unused_sums, mixed = seq_scatter(
         n,
         width,
         4,
@@ -1359,22 +1588,34 @@
         (upstream_all, hidden_slope),
         (proj_mine, fc_mine),
         ((ff, low),),
-        side=(hidden_act, upstream_all, lambda a, proj, fc: mm(a, proj[...]).astype(low), width),
+        side=(hidden_act, upstream_all),
+        carry=mixed,
     )
     mixed = lax.psum_scatter(mixed, "seq", scatter_dimension=0, tiled=True).astype(wider)
-    proj_part = lax.psum_scatter(
-        grad_proj.reshape(nf, piece, width), "fsdp", scatter_dimension=0, tiled=False
-    )
+    grad_proj = grad_proj.reshape(nf, piece, width)
+    cut = piece // 16 * 8
     unused_two, norm_two_back = jax.vjp(layer_norm, middle, gain_two, shift_two)
     grad_middle_norm, grad_gain_two, grad_shift_two = norm_two_back(grad_normed_two)
     grad_middle = upstream + grad_middle_norm
     grad_branch = grad_middle.astype(low)
-    grad_attended, grad_fc = to_heads(
-        grad_branch, out_turned, n, wide, 5, normed_two, grad_pre
+    grad_attended, grad_fc, hidden_sums, proj_first = to_heads(
+        grad_branch, out_turned, n, nf, wide, 5, normed_two, grad_pre, grad_proj[:, :cut]
     )
     grad_attended = grad_attended.reshape(n * block, wide)
-    fc_part = lax.psum_scatter(grad_fc, "fsdp", scatter_dimension=0, tiled=True)
-    grad_projected = attend_back(table, projected, grad_attended, attended, totals, block)
+    grad_projected, column_sums, (fc_parts, proj_second) = attend_back(
+        table,
+        pairs,
+        projected,
+        keys_turned,
+        grad_attended,
+        attended,
+        totals,
+        block,
+        trunk,
+        nf,
+        (grad_fc.reshape(nf, rows, ff), grad_proj[:, cut:]),
+        9,
+    )
     output = (after(middle, grad_projected) + mixed + bias_proj).astype(low)[None]
     ready = output[0, :8, :128].astype(wider)
     grad_qkv = contract(normed_one, grad_projected, ready, block)
@@ -1392,8 +1633,11 @@
     grad_resid_norm, grad_gain_one, grad_shift_one = norm_one_back(grad_normed_one)
     input_grad = (grad_middle + grad_resid_norm).astype(low)[None]
 
-    proj_part = after(proj_part, grad_normed_one).reshape(piece, n, width // n).transpose(1, 0, 2)
-    fc_part = after(fc_part, grad_normed_one).reshape(rows, nf, piece).transpose(1, 0, 2)
+    proj_part = jnp.concatenate([proj_first, proj_second], 1)
+    proj_part = jnp.sum(proj_part.astype(wider), 0).astype(low)
+    proj_part = proj_part.reshape(piece, n, width // n).transpose(1, 0, 2)
+    fc_part = jnp.sum(fc_parts.astype(wider), 0).astype(low)
+    fc_part = fc_part.reshape(rows, nf, piece).transpose(1, 0, 2)
     grad_out = contract_rows(
         after(grad_branch, grad_attended), attended_mine[:, :width]
     ).astype(low)
@@ -1401,12 +1645,12 @@
     out_part = after(out_part, grad_normed_one).reshape(nf, rows, width // n)
     qkv_part = jnp.sum(qkv_parts.astype(wider), 0).astype(low).T
 
-    column_sums = jnp.sum(grad_projected.astype(wider), 0).reshape(3, wide)
+    column_sums = column_sums.reshape(3, wide)
     placed = lax.dynamic_update_slice_in_dim(
         jnp.zeros((3, n * wide), wider), column_sums, s * wide, 1
     )[:, :width]
     grad_qv = jnp.concatenate([placed[0], placed[2]])
-    hidden_sums = jnp.sum(grad_pre.astype(wider), 0).reshape(nf, 1, piece)
+    hidden_sums = hidden_sums.reshape(nf, 1, piece)
     grad_fc_bias = lax.dynamic_update_slice_in_dim(
         jnp.zeros((nf, n, piece), wider), hidden_sums, s, 1
     )

time: 889 us -> 813 us (0.915)
  waiting for transfers between devices: 64.7 us -> 0.1 us
    unnamed x9 -> x5, waiting for transfers between devices: 56.9 us -> 0.08 us
    pallas_call x4 -> x3, Pallas kernels: 194 us -> 224 us  [the longest x1 100 us: attend_back(): pl.pallas_call(functools.partial(attend_back_kernel, width, block, rows /...]
    pallas_call x1, Pallas kernels: 49.6 us -> 25.3 us  [to_tokens(): pl.pallas_call(functools.partial(to_tokens_kernel, n, wide), out_shape=ja...]
    pallas_call x2, Pallas kernels: 168 us -> 148 us  [seq_scatter(): pl.pallas_call(functools.partial(scatter_kernel, n, h, body, len(ins), le...]
    reshape x4 -> x6, local copies, waits for them, and re-layouts: 1.79 us -> 11.3 us  [the longest x2 5.87 us: local(): fc_part = fc_part.reshape(rows, nf, piece).transpose(1, 0, 2)]
    unnamed x117 -> x90, local copies, waits for them, and re-layouts: 26.8 us -> 25.6 us
  transfers between devices with their start and end apart: 7 -> 4, of which waited for: 2 -> 0; matrix products, arithmetic and copies ran while one was open for 8% -> 8% of each run, Pallas kernels for 57% -> 42%
where the time goes in v3:
time: 813 us; the launch traced here: 804 us
  Pallas kernels  649 us (80%)
  local copies, waits for them, and re-layouts  76.4 us (9%)
  other arithmetic  44.6 us (5%)
  between operations  17.3 us (2%)
  matrix products  15.6 us (2%)
    pallas_call x2, Pallas kernels, seq_gather(): pl.pallas_call(functools.partial(gather_kernel, n, h, body, len(consts),...  165 us
    pallas_call x2, Pallas kernels, seq_scatter(): pl.pallas_call(functools.partial(scatter_kernel, n, h, body, len(ins), le...  148 us
    pallas_call x1, Pallas kernels, attend_back(): pl.pallas_call(functools.partial(attend_back_kernel, width, block, rows /...  100 us
    pallas_call x1, Pallas kernels, attend(): pl.pallas_call(functools.partial(attend_kernel, width, block, trunk, n),...  75.6 us
    pallas_call x1, Pallas kernels, to_heads(): pl.pallas_call(functools.partial(to_heads_kernel, n, nf, wide), out_shape...  48.6 us
    pallas_call x1, Pallas kernels, give_back(): pl.pallas_call(functools.partial(give_back_kernel, n, nf, rows), out_shap...  36.3 us
    pallas_call x1, Pallas kernels, exchange(): pl.pallas_call(functools.partial(exchange_kernel, n, nf, rows, count), ou...  32.7 us
    unnamed x90, local copies, waits for them, and re-layouts  25.6 us
  transfers between devices with their start and end apart: 4, of which 0 were waited for; matrix products, arithmetic and copies ran while one was open for 8% of the time, Pallas kernels for 42%

profile of v3, /device:TPU:3, one launch (start us, length us, event | category | flops | bytes accessed | tf_op | source)
XLA Modules:
  0.0 804.0 jit_solution(5770639827927398399)
XLA Ops:
  7.3 2.8 reshape.317
  12.4 2.1 copy.93
  19.1 32.7 %exchange.1 = (bf16[768,400]{1,0:T(8,128)(2,1)}, bf16[8,200,200]{2,1,0:T(8,128)(2,1)}, bf16[4,400,200]{2,1,0:T(8,128)(2,1)}, bf16[4,400,200]{2,1,0:T(8,128)(2,1)...) custom-call(bf16[600,400]{1,0:T(8,128)(2,1)} %bitcast.139, ...), custom_call_target="tpu_custom_call" | custom-call | bytes 1048576 | tf_op jit(solution)/shard_map/exchange/pallas_call | solution.py:831
  56.5 1.5 copy.114
  59.8 1.9 fusion.9.refs_0_
  61.7 92.4 %gather_one.1 = (bf16[16,256,1600]{2,1,0:T(8,128)(2,1)}, bf16[8,200,2048]{2,1,0:T(8,128)(2,1)}, bf16[4,400,768]{2,1,0:T(8,128)(2,1)}) custom-call(bf16[512,1600]{1,0:T(8,128)(2,1)} %fusion.9.refs_0_, bf16[200,2048]{1,0:T(8,128)(2,1)} %pad.12.refs_1_, bf16[400,768]{1,0:T(8,128)(2,1)} %select_bitcast_fusion.refs_2_), custom_call_target="tpu_custom_call" | custom-call | bytes 1048576 | tf_op jit(solution)/shard_map/gather_one/pallas_call | solution.py:355
  156.4 1.8 add.150
  158.7 1.5 reshape.331
  161.6 2.4 copy.98
  164.8 75.6 %attend.1 = (bf16[4096,768]{1,0:T(8,128)(2,1)}, bf16[4096,256]{1,0:T(8,128)(2,1)}, f32[4096,256]{1,0:T(8,128)}, f32[4096,256]{1,0:T(8,128)}, bf16[256,4096]{1,0:T(8,128)(2,1)}, /*index=5*/bf16[8,512,1600]{2,1,0:T(8,128)(2,1)}) custom-call(s32[2,25]{1,0:T(2,128)} %pad_add_fusion.values.refs_0_, bf16[8,512,1600]{2,1,0:T(8,128)(2,1)} %bitcast.119, ...), custom_call_target="tpu_custom_call" | custom-call | bytes 1048576 | tf_op jit(solution)/shard_map/attend/pallas_call | solution.py:1242
  240.4 25.3 %to_tokens.1 = bf16[512,2048]{1,0:T(8,128)(2,1)} custom-call(bf16[8,512,256]{2,1,0:T(8,128)(2,1)} %bitcast.142), custom_call_target="tpu_custom_call" | custom-call | bytes 1048576 | tf_op jit(solution)/shard_map/to_tokens/pallas_call | solution.py:880
  267.0 8.1 %fusion.29 = (f32[512]{0:T(512)S(1)}, f32[512,1600]{1,0:T(8,128)S(1)}) fusion(f32[1600]{0:T(1024)S(1)} %reshape.356, bf16[512,2048]{1,0:T(8,128)(2,1)} %to_tokens.1, bf16[1600,2048]{1,0:T(8,128)(2,1)} %bitcast.127, bf16[1,512,1600]{2,1,0:T(8,128)(2,1)} %copy-done.2), kind=kOutput, calls=%fused_computation.86 | convolution fusion | flops 3358719488 | bytes 13574400 | tf_op jit(solution)/shard_map/dot_general | solution.py:1449
  275.5 1.8 add_convert_fusion.2.refs_0_
  277.3 72.9 %gather_two.1 = (bf16[16,256,1600]{2,1,0:T(8,128)(2,1)}, bf16[16,256,800]{2,1,0:T(8,128)(2,1)}, bf16[16,256,800]{2,1,0:T(8,128)(2,1)}, bf16[16,256,1600]{2,1,0:T(8,128)(2,1)}) custom-call(bf16[512,1600]{1,0:T(8,128)(2,1)} %add_convert_fusion.2.refs_0_, bf16[1600,800]{1,0:T(8,128)(2,1)} %all-gather.3.cloned.1.call-done.refs_1_.refs_4_, ...), custom_call_target="tpu_custom_call" | custom-call | bytes 1048576 | tf_op jit(solution)/shard_map/gather_two/pallas_call | solution.py:355
  350.3 77.5 %scatter_two.1 = (f32[512,1600]{1,0:T(8,128)}, bf16[16,256,800]{2,1,0:T(8,128)(2,1)}, bf16[800,1600]{1,0:T(8,128)(2,1)}, f32[1,1600]{1,0:T(1,128)}, bf16[4096,1600]{1,0:T(8,128)(2,1)}) custom-call(bf16[4096,1600]{1,0:T(8,128)(2,1)} %bitcast.123, bf16[16,256,1600]{2,1,0:T(8,128)(2,1)} %bitcast.121, ...), custom_call_target="tpu_custom_call", output_to_operand_aliasing={{4}: (0, {})} | custom-call | bytes 1048576 | tf_op jit(solution)/shard_map/scatter_two/pallas_call | solution.py:647
  428.0 2.4 slice.97.z_ref
  430.5 3.2 multiply_reduce_fusion
  435.7 1.9 convert_reduce_fusion.2
  437.6 48.6 %to_heads.1 = (bf16[8,512,256]{2,1,0:T(8,128)(2,1)}, bf16[1600,800]{1,0:T(8,128)(2,1)}, f32[1,800]{1,0:T(1,128)}, bf16[4,96,1600]{2,1,0:T(8,128)(2,1)}) custom-call(bf16[512,1600]{1,0:T(8,128)(2,1)} %get-tuple-element.170.x_ref, bf16[1600,2048]{1,0:T(8,128)(2,1)} %bitcast.128, bf16[16,256,1600]{2,1,0:T(8,128)(2,1)} %get-tuple-element.80.a_ref, ...), custom_call_target="tpu_custom_call" | custom-call | bytes 1048576 | tf_op jit(solution)/shard_map/to_heads/pallas_call | solution.py:937
  488.1 7.6 convolution_convert_fusion
  496.4 2.6 slice.98.refs_7_
  499.1 100.2 %attend_back.1 = (bf16[4096,768]{1,0:T(8,128)(2,1)}, f32[1,768]{1,0:T(1,128)}, bf16[4,400,800]{2,1,0:T(8,128)(2,1)}, bf16[4,104,1600]{2,1,0:T(8,128)(2,1)}) custom-call(s32[2,25]{1,0:T(2,128)} %pad_add_fusion.values.refs_0_, bf16[4096,768]{1,0:T(8,128)(2,1)} %get-tuple-element.68.refs_1_, bf16[256,4096]{1,0:T(8,128)(2,1)} %get-tuple-element.69.refs_2_, ...), custom_call_target="tpu_custom_call" | custom-call | bytes 1048576 | tf_op jit(solution)/shard_map/attend_back/pallas_call | solution.py:1403
  601.1 3.2 maximum_reduce_fusion
  604.3 3.1 reshape.350
  607.5 2.2 copy.123
  610.5 3.3 reduce_sum.223
  613.9 3.7 reshape.351
  617.6 2.1 copy.122
  619.8 2.0 fusion.15
  623.0 2.8 copy-done
  625.7 17.4 %contract.1 = bf16[1600,768]{1,0:T(8,128)(2,1)S(1)} custom-call(bf16[4096,1600]{1,0:T(8,128)(2,1)} %bitcast.120, bf16[4096,768]{1,0:T(8,128)(2,1)S(1)} %copy-done, f32[8,128]{1,0:T(8,128)S(1)} %fusion.21.ready), custom_call_target="tpu_custom_call" | custom-call | bytes 1048576 | tf_op jit(solution)/shard_map/contract/pallas_call | solution.py:980
  643.2 1.4 copy-done.1
  644.6 70.4 %scatter_one.1 = (f32[512,1600]{1,0:T(8,128)}, bf16[4,400,768]{2,1,0:T(8,128)(2,1)}) custom-call(bf16[16,256,768]{2,1,0:T(8,128)(2,1)} %bitcast.116, bf16[1600,768]{1,0:T(8,128)(2,1)} %bitcast.126, bf16[4,400,768]{2,1,0:T(8,128)(2,1)} %bitcast.117), custom_call_target="tpu_custom_call" | custom-call | bytes 1048576 | tf_op jit(solution)/shard_map/scatter_one/pallas_call | solution.py:647
  717.0 2.8 fusion.25
  722.1 3.1 fusion.10
  726.2 3.2 reduce_sum.218
  729.4 2.2 copy.104
  731.6 36.3 %give_back.1 = (f32[40,128]{1,0:T(8,128)}, bf16[600,400]{1,0:T(8,128)(2,1)}, bf16[8,200,200]{2,1,0:T(8,128)(2,1)}, bf16[4,400,200]{2,1,0:T(8,128)(2,1)}, bf16[4,400,200]{2,1,0:T(8,128)(2,1)}) custom-call(f32[4,40,128]{2,1,0:T(8,128)} %bitcast.145, bf16[768,400]{1,0:T(8,128)(2,1)} %bitcast.134, bf16[8,200,200]{2,1,0:T(8,128)(2,1)} %bitcast.129, ...), custom_call_target="tpu_custom_call" | custom-call | bytes 1048576 | tf_op jit(solution)/shard_map/give_back/pallas_call | solution.py:1052
  767.9 1.4 fusion.28
  769.4 1.4 slice.109
  772.1 2.4 copy.109
  776.8 2.2 reshape.363
  780.3 1.6 copy.112
  781.9 2.4 convert_bitcast_fusion.2
  784.3 2.6 copy.111
  786.9 2.1 convert_reduce_fusion.3
  789.0 4.7 fusion.16
  793.7 3.6 copy.110
  (179 shorter events, 36.1 us)
Async XLA Ops:
  7.2 4.0 copy-start.14
  7.2 7.3 copy-start.23
  7.2 7.9 copy-start.26
  7.2 8.4 %copy-start.27 = (bf16[400]{0:T(512)(128)(2,1)S(1)}, bf16[400]{0:T(512)(128)(2,1)}, u32[]{:S(2)}) copy-start(bf16[400]{0:T(512)(128)(2,1)} %param.21) | copy-start | bytes 2404
  7.2 9.0 %copy-start.28 = (bf16[400]{0:T(512)(128)(2,1)S(1)}, bf16[400]{0:T(512)(128)(2,1)}, u32[]{:S(2)}) copy-start(bf16[400]{0:T(512)(128)(2,1)} %param.22) | copy-start | bytes 2404
  7.2 9.6 %copy-start.29 = (bf16[400]{0:T(512)(128)(2,1)S(1)}, bf16[400]{0:T(512)(128)(2,1)}, u32[]{:S(2)}) copy-start(bf16[400]{0:T(512)(128)(2,1)} %param.26) | copy-start | bytes 2404
  7.2 10.1 %copy-start.30 = (bf16[400]{0:T(512)(128)(2,1)S(1)}, bf16[400]{0:T(512)(128)(2,1)}, u32[]{:S(2)}) copy-start(bf16[400]{0:T(512)(128)(2,1)} %param.27) | copy-start | bytes 2404
  7.3 10.7 %copy-start.31 = (bf16[400]{0:T(512)(128)(2,1)S(1)}, bf16[400]{0:T(512)(128)(2,1)}, u32[]{:S(2)}) copy-start(bf16[400]{0:T(512)(128)(2,1)} %param.28) | copy-start | bytes 2404
  7.3 11.3 %copy-start.32 = (bf16[400]{0:T(512)(128)(2,1)S(1)}, bf16[400]{0:T(512)(128)(2,1)}, u32[]{:S(2)}) copy-start(bf16[400]{0:T(512)(128)(2,1)} %param.32) | copy-start | bytes 2404
  7.3 270.1 %all-gather.5.cloned.1.call-start = ((), (), s32[]{:S(2)}) async-start(), calls=%async_computation.3 | async-start | bytes 3328000 | tf_op jit(solution)/shard_map/all_gather | solution.py:1548
  10.2 42.6 %copy-start.10 = (bf16[1,512,1600]{1,2,0:T(8,128)(2,1)S(1)}, bf16[1,512,1600]{1,2,0:T(8,128)(2,1)}, u32[]{:S(2)}) copy-start(bf16[1,512,1600]{1,2,0:T(8,128)(2,1)} %param.20) | copy-start | bytes 4915204
  54.1 5.7 copy-start.2
  55.0 6.7 copy-start.16
  61.7 94.4 %copy-start.13 = (bf16[8,200,200]{2,1,0:T(8,128)(2,1)S(1)}, bf16[8,200,200]{2,1,0:T(8,128)(2,1)}, u32[]{:S(2)}) copy-start(bf16[8,200,200]{2,1,0:T(8,128)(2,1)} %get-tuple-element.74) | copy-start | bytes 1920004
  154.2 4.1 copy-start.12
  156.3 4.2 copy-start.18
  156.4 5.2 copy-start.11
  158.2 119.2 %all-gather.3.cloned.1.call-start = ((), (), s32[]{:S(2)}) async-start(), calls=%async_computation.2 | async-start | bytes 3584000 | tf_op jit(solution)/shard_map/all_gather | solution.py:1544
  158.2 5.8 copy-start.34
  158.2 5.8 copy-start.36
  158.2 5.9 copy-start.33
  158.3 5.8 copy-start.37
  158.3 5.8 copy-start.38
  158.3 5.9 copy-start.35
  160.2 459.6 %reduce-scatter.5.cloned.1.call-start = ((), (), s32[]{:S(2)}) async-start(), calls=%async_computation.4 | async-start | bytes 15335424 | tf_op jit(solution)/shard_map/reduce_scatter | solution.py:1594
  240.4 25.3 %copy-start.21 = (bf16[4,1,400]{2,1,0:T(2,128)(2,1)S(1)}, bf16[4,1,400]{2,1,0:T(2,128)(2,1)}, u32[]{:S(2)}) copy-start(bf16[4,1,400]{2,1,0:T(2,128)(2,1)} %get-tuple-element.67) | copy-start | bytes 9604
  240.4 25.3 %copy-start.22 = (bf16[4,1,400]{2,1,0:T(2,128)(2,1)S(1)}, bf16[4,1,400]{2,1,0:T(2,128)(2,1)}, u32[]{:S(2)}) copy-start(bf16[4,1,400]{2,1,0:T(2,128)(2,1)} %get-tuple-element.71) | copy-start | bytes 9604
  240.4 25.6 %copy-start.20 = (bf16[4,1,400]{2,1,0:T(2,128)(2,1)S(1)}, bf16[4,1,400]{2,1,0:T(2,128)(2,1)}, u32[]{:S(2)}) copy-start(bf16[4,1,400]{2,1,0:T(2,128)(2,1)} %get-tuple-element.70) | copy-start | bytes 9604
  240.4 25.7 %copy-start.15 = (bf16[4,1,1600]{2,1,0:T(2,128)(2,1)S(1)}, bf16[4,1,1600]{2,1,0:T(2,128)(2,1)}, u32[]{:S(2)}) copy-start(bf16[4,1,1600]{2,1,0:T(2,128)(2,1)} %get-tuple-element.73) | copy-start | bytes 38404
  427.8 292.0 %reduce-scatter.7.cloned.1.call-start = ((), (), s32[]{:S(2)}) async-start(), calls=%async_computation.5 | async-start | bytes 5990400
  430.5 3.2 copy-start.7
  433.7 2.0 copy-start.5
  434.8 2.8 copy-start.4
  495.6 0.7 copy-start.19
  599.3 10.4 %copy-start.25 = (f32[1,768]{1,0:T(1,128)S(1)}, f32[1,768]{1,0:T(1,128)}, u32[]{:S(2)}) copy-start(f32[1,768]{1,0:T(1,128)} %get-tuple-element.91) | copy-start | bytes 9220
  599.3 10.7 %copy-start.24 = (f32[1,800]{1,0:T(1,128)S(1)}, f32[1,800]{1,0:T(1,128)}, u32[]{:S(2)}) copy-start(f32[1,800]{1,0:T(1,128)} %get-tuple-element.92) | copy-start | bytes 9604
  621.7 1.2 copy-start.8
  623.0 2.8 copy-start
  643.2 1.5 copy-start.1
  644.6 72.3 %copy-start.3 = (bf16[1,512,1600]{2,1,0:T(8,128)(2,1)S(1)}, bf16[1,512,1600]{2,1,0:T(8,128)(2,1)}, u32[]{:S(2)}) copy-start(bf16[1,512,1600]{2,1,0:T(8,128)(2,1)} %copy-done.2) | copy-start | bytes 4915204
  717.0 5.2 copy-start.17
  726.2 45.9 %copy-start.9 = (bf16[1,512,1600]{2,1,0:T(8,128)(2,1)S(1)}, bf16[1,512,1600]{2,1,0:T(8,128)(2,1)}, u32[]{:S(2)}) copy-start(bf16[1,512,1600]{2,1,0:T(8,128)(2,1)} %copy-done.8) | copy-start | bytes 4915204
  781.9 7.1 copy-start.6
Sparse Core Ops, SparseCore 0:
  158.3 55.0 all-gather.4
  215.5 57.6 all-gather.2
  427.9 108.3 reduce-scatter.4
  539.6 64.7 reduce-scatter.6

commit v4 on v3

--- a/solution.py
+++ b/solution.py
@@ -172,6 +172,33 @@
                 for k in self.fresh(half, i):
                     for b in self.orders[half][i + 1 :] + [1]:
                         self.ship(half, k, b).wait_send()
+
+
+class PlaneSum(Blocks):
+    def __init__(self, size, source, low, target, send, recv, local):
+        super().__init__("fsdp", size, False, source, target, send, recv, local)
+        self.window = pl.ds(low, target.shape[1])
+
+    @staticmethod
+    def scratch(size, rows, cols):
+        return [pltpu.VMEM((size, rows, cols), jnp.bfloat16)] + Blocks.scratch(size)
+
+    def copy(self, d):
+        to = lax.rem(self.me + d, self.size)
+        src = self.source.at[to].at[self.window]
+        return remote(src, self.target.at[self.me], self.send.at[d - 1], self.recv.at[d - 1], {self.axis: to})
+
+    def own(self):
+        src = self.source.at[self.me].at[self.window]
+        return pltpu.make_async_copy(src, self.target.at[self.me], self.local)
+
+    def store(self, out):
+        total = self.target[0].astype(jnp.float32)
+        for i in range(1, self.size):
+            total = total + self.target[i].astype(jnp.float32)
+        cols = out.shape[2]
+        for i in range(out.shape[0]):
+            out[i] = total[:, i * cols : (i + 1) * cols].astype(out.dtype)
 
 
 def blocks_shape(x, size, same):
@@ -461,10 +488,12 @@
     return orders, [(half, lists[half][i]) for i in range(n // 2) for half in (0, 1)]
 
 
-def scatter_kernel(n, h, body, n_in, n_const, n_out, modes, nf, same, has_side, carried, *refs):
-    if carried:
-        out = n_in + n_const + 2 * has_side + min(nf, 1) + 2 + n_out + 2 * has_side + min(nf, 1)
-        refs = refs[1:out] + refs[out + 1 :]
+def scatter_kernel(n, h, body, n_in, n_const, n_out, modes, nf, same, has_side, has_norm, *refs):
+    if has_norm:
+        out = n_in + 3 + n_const + 2 * has_side + min(nf, 1)
+        values, gain, joins = refs[:3]
+        x_grad, g_grad, b_grad = refs[out], refs[out + 1], refs[out + 2]
+        refs = refs[3:out] + (None,) + refs[out + 3 :]
     side = None
     if has_side:
         at = n_in + n_const
@@ -610,12 +639,32 @@
                 rows = pl.ds(half * h, h)
                 if i == len(bits) - 1:
                     total[rows] = own[j].astype(jnp.float32) + far[to].astype(jnp.float32)
-                    pltpu.make_async_copy(total.at[rows], sum_ref.at[rows], done.at[half]).start()
+                    if not has_norm:
+                        pltpu.make_async_copy(total.at[rows], sum_ref.at[rows], done.at[half]).start()
                 else:
                     own[j] = (own[j].astype(jnp.float32) + far[to].astype(jnp.float32)).astype(own.dtype)
                     if phase_of(half, k) == i + 1:
                         launch(half, k).start()
-    for half in (0, 1):
+    if has_norm:
+        g_grad[...] = jnp.zeros_like(g_grad)
+        b_grad[...] = jnp.zeros_like(b_grad)
+
+        def tile(i, carry):
+            rows = pl.ds(pl.multiple_of(i * 64, 64), 64)
+            x = values[rows].astype(jnp.float32)
+            centred = x - jnp.mean(x, -1, keepdims=True)
+            scale = lax.rsqrt(jnp.mean(centred * centred, -1, keepdims=True) + 1e-05)
+            xhat = centred * scale
+            grad = total[rows]
+            g_grad[...] += jnp.sum(grad * xhat, 0, keepdims=True)
+            b_grad[...] += jnp.sum(grad, 0, keepdims=True)
+            e = gain[...] * grad
+            inner = e - jnp.mean(e, -1, keepdims=True) - xhat * jnp.mean(e * xhat, -1, keepdims=True)
+            x_grad[rows] = (joins[rows].astype(jnp.float32) + scale * inner).astype(x_grad.dtype)
+            return carry
+
+        lax.fori_loop(0, 2 * h // 64, tile, 0)
+    for half in (0, 1) if not has_norm else ():
         rows = pl.ds(half * h, h)
         pltpu.make_async_copy(total.at[rows], sum_ref.at[rows], done.at[half]).wait()
     for q in (2 * n - 2, 2 * n - 1):
@@ -632,7 +681,7 @@
         side.end()
 
 
-def seq_scatter(n, cols, ident, name, body, ins, consts, outs=(), modes=None, rider=None, side=None, carry=None):
+def seq_scatter(n, cols, ident, name, body, ins, consts, outs=(), modes=None, rider=None, side=None, norm=None):
     h = ins[0].shape[0] // (2 * n)
     low = jnp.bfloat16
     slots = min(4, n)
@@ -643,19 +692,22 @@
     modes = modes or ([0] * len(ins), [0] * len(outs))
     more, spec, shape, scratch, nf, same = rider_parts(rider)
     s_ins, s_shapes, s_in_specs, s_out_specs, s_scratch = side_parts(side, 2 * n)
-    carries = [] if carry is None else [carry]
+    sums = [jax.ShapeDtypeStruct((2 * h, cols), jnp.float32)]
+    norms = []
+    if norm is not None:
+        norms = list(norm[:3])
+        line = jax.ShapeDtypeStruct((1, cols), jnp.float32)
+        sums = [jax.ShapeDtypeStruct((2 * h, cols), norm[3]), line, line]
     out = pl.pallas_call(
         functools.partial(
-            scatter_kernel, n, h, body, len(ins), len(consts), len(outs), modes, nf, same, int(side is not None), carry is not None
+            scatter_kernel, n, h, body, len(ins), len(consts), len(outs), modes, nf, same, int(side is not None), norm is not None
         ),
-        out_shape=[jax.ShapeDtypeStruct((2 * h, cols), jnp.float32)]
+        out_shape=sums
         + [jax.ShapeDtypeStruct((2 * n, h, c), d) for c, d in outs]
         + s_shapes
-        + shape
-        + [jax.ShapeDtypeStruct(x.shape, x.dtype) for x in carries],
-        in_specs=[hbm] * (len(carries) + len(ins)) + [vmem] * len(consts) + s_in_specs + spec,
-        out_specs=[hbm] * (1 + len(outs)) + s_out_specs + spec + [hbm] * len(carries),
-        input_output_aliases={0: 1 + len(outs) + len(s_shapes) + len(shape)} if carries else {},
+        + shape,
+        in_specs=[vmem] * len(norms) + [hbm] * len(ins) + [vmem] * len(consts) + s_in_specs + spec,
+        out_specs=([vmem] * 3 if norms else [hbm]) + [hbm] * len(outs) + s_out_specs + spec,
         scratch_shapes=[
             pltpu.VMEM((slots, h, cols), low),
             pltpu.VMEM((n, h, cols), low),
@@ -681,11 +733,13 @@
         ),
         cost_estimate=SMALL,
         name=name,
-    )(*carries, *split, *consts, *s_ins, *more)
+    )(*norms, *split, *consts, *s_ins, *more)
+    lines = list(out[1:3]) if norms else []
+    out = [out[0]] + list(out[1 + len(lines) :])
     many = 1 + len(outs)
     sides = [] if side is None else list(out[many : many + 2])
     more = list(out[many + len(sides) :])
-    return [out[0]] + [o.reshape(2 * n * h, o.shape[2]) for o in out[1:many]] + sides + more
+    return [out[0]] + lines + [o.reshape(2 * n * h, o.shape[2]) for o in out[1:many]] + sides + more
 
 
 class Rows:
@@ -889,14 +943,16 @@
     )(x)
 
 
-def to_heads_kernel(n, nf, wide, x_ref, w_ref, a_ref, b_ref, z_ref, o_ref, g_ref, m_ref, z_out, made, send, recv, local, *extra):
+def to_heads_kernel(
+    n, nf, wide, carried, x_ref, w_ref, t_ref, a_ref, b_ref, z_ref, o_ref, g_ref, m_ref, z_out, t_out, handed, made, *extra
+):
     me = lax.axis_index("seq")
-    rider = Blocks("fsdp", nf, False, z_ref, z_out, *extra[-3:])
-    extra = extra[:-3]
-    side = Side(2 * n, (a_ref, b_ref, g_ref, m_ref) + extra)
+    send, recv, local = extra[:3]
+    side = Side(2 * n, (a_ref, b_ref, g_ref, m_ref) + extra[3:7])
+    planes = PlaneSum(nf, z_ref, 0, *extra[7:])
     side.begin()
-    greet([{"seq": place(me, r, n)} for r in range(1, n)] + rider.peers())
-    rider.start()
+    greet([{"seq": place(me, r, n)} for r in range(1, n)] + planes.peers())
+    planes.start()
 
     def copy(r):
         to = place(me, r, n)
@@ -919,39 +975,50 @@
     lax.fori_loop(0, n, step, 0)
     mine().start()
     side.run(0, 2 * n)
+    cols = t_out.shape[0]
+    for at in range(0, cols, 512):
+        end = min(at + 512, cols)
+        t_out[at:end] = lax.dot_general(
+            x_ref[:, at:end], t_ref[...], (((0,), (0,)), ((), ())), preferred_element_type=jnp.float32
+        ).astype(t_out.dtype)
+    side.end()
+    planes.finish()
+    planes.store(z_out)
     for r in range(1, n):
         dst = o_ref.at[place(me, r, n)]
         remote(dst, dst, send.at[0], recv.at[r - 1], {"seq": me}).wait_recv()
     mine().wait()
     for r in range(1, n):
         copy(r).wait_send()
-    side.end()
-    rider.finish()
-
-
-def to_heads(x, w, n, nf, wide, ident, a, b, z):
-    rows = x.shape[0]
+
+
+def to_heads(x, w, t, n, nf, wide, ident, a, b, z, count, carry):
+    rows, cols = x.shape
     vmem = pl.BlockSpec(memory_space=pltpu.VMEM)
     hbm = pl.BlockSpec(memory_space=pl.ANY)
     s_ins, s_shapes, s_in_specs, s_out_specs, s_scratch = side_parts((a, b), 2 * n)
-    out = pl.pallas_call(
+    return pl.pallas_call(
         functools.partial(to_heads_kernel, n, nf, wide),
         out_shape=[jax.ShapeDtypeStruct((n, rows, wide), x.dtype)]
         + s_shapes
-        + [blocks_shape(z, nf, False)],
-        in_specs=[vmem, vmem] + s_in_specs + [hbm],
-        out_specs=[hbm] + s_out_specs + [hbm],
+        + [
+            jax.ShapeDtypeStruct((n, count, z.shape[2] // n), z.dtype),
+            jax.ShapeDtypeStruct((cols, t.shape[1]), x.dtype),
+            jax.ShapeDtypeStruct(carry.shape, carry.dtype),
+        ],
+        in_specs=[hbm, vmem, vmem, vmem] + s_in_specs + [hbm],
+        out_specs=[hbm] + s_out_specs + [vmem, vmem, hbm],
+        input_output_aliases={0: 5},
         scratch_shapes=[pltpu.VMEM((n, rows, wide), x.dtype)]
         + Blocks.scratch(n)
         + s_scratch
-        + Blocks.scratch(nf),
+        + PlaneSum.scratch(nf, count, z.shape[2]),
         compiler_params=pltpu.CompilerParams(
             collective_id=ident, has_side_effects=True, vmem_limit_bytes=60 << 20
         ),
         cost_estimate=SMALL,
         name="to_heads",
-    )(x, w, *s_ins, z)
-    return out
+    )(carry, x, w, t, *s_ins, z)
 
 
 def contract_kernel(a_ref, b_ref, ready, o_ref, acc):
@@ -997,7 +1064,7 @@
 
 
 def give_back_kernel(
-    n, nf, rows, v_ref, w_ref, p_ref, c_ref, o_ref, v_out, w_out, p_out, c_out, o_out, planes, sums, *sems
+    n, nf, rows, v_ref, w_ref, p_ref, q_ref, c_ref, o_ref, v_out, w_out, p_out, q_out, c_out, o_out, planes, sums, *sems
 ):
     s = lax.axis_index("seq")
     f = lax.axis_index("fsdp")
@@ -1009,6 +1076,7 @@
         parts.append(rows.bind(w_ref, w_out, *take(3)))
     parts.append(Units(n, nf, True, c_ref, c_out, *take(3)))
     parts.append(Blocks("seq", n, False, p_ref, p_out, *take(3)))
+    parts.append(Blocks("seq", n, False, q_ref, q_out, *take(3)))
     parts.append(Blocks("fsdp", nf, False, o_ref, o_out, *take(3)))
     others = [{"fsdp": lax.rem(f + d, nf)} for d in range(1, nf)]
     peers = [{"seq": place(s, r, n)} for r in range(1, n)]
@@ -1042,7 +1110,7 @@
         c.wait_send()
 
 
-def give_back(vectors, w, held, p, c, o, n, nf, rows, ident):
+def give_back(vectors, w, held, p, q, c, o, n, nf, rows, ident):
     k = vectors.shape[1]
     tiles = -(-k // 1024) * 8
     padded = jnp.pad(vectors, ((0, 0), (0, tiles * 128 - k))).reshape(nf, tiles, 128)
@@ -1055,11 +1123,12 @@
             jax.ShapeDtypeStruct((tiles, 128), jnp.float32),
             jax.ShapeDtypeStruct((held, w.shape[1]), w.dtype),
             blocks_shape(p, n, False),
+            blocks_shape(q, n, False),
             blocks_shape(c, nf, False),
             blocks_shape(o, nf, False),
         ],
-        in_specs=[vmem, hbm, hbm, hbm, hbm],
-        out_specs=[vmem, hbm, hbm, hbm, hbm],
+        in_specs=[vmem, hbm, hbm, hbm, hbm, hbm],
+        out_specs=[vmem, hbm, hbm, hbm, hbm, hbm],
         scratch_shapes=[
             pltpu.VMEM((nf - 1, tiles, 128), jnp.float32),
             pltpu.VMEM((n, tiles, 128), jnp.float32),
@@ -1071,12 +1140,13 @@
         + (rows.scratch() if rows is not None else [])
         + Units.scratch(nf)
         + Blocks.scratch(n)
+        + Blocks.scratch(n)
         + Blocks.scratch(nf),
         compiler_params=pltpu.CompilerParams(collective_id=ident, has_side_effects=True),
         cost_estimate=SMALL,
         name="give_back",
-    )(padded, w, p, c, o)
-    return out[0].reshape(-1)[:k], out[1], out[2], out[3], out[4]
+    )(padded, w, p, q, c, o)
+    return (out[0].reshape(-1)[:k],) + tuple(out[1:])
 
 
 HEAD=64
@@ -1272,16 +1342,15 @@
     return out[:5] + (out[5].reshape(n * sent.shape[0], sent.shape[1]),)
 
 
-def attend_back_kernel(width, block, slots, trunk, branches, nf, count, *refs):
+def attend_back_kernel(width, block, slots, trunk, branches, nf, lows, *refs):
+    count = len(lows)
     values, qkv, kt, datt, att, tot = refs[:6]
     sources = refs[6 : 6 + count]
     out, sums = refs[6 + count : 8 + count]
-    targets = refs[8 + count : 8 + 2 * count]
+    parts = refs[8 + count : 8 + 2 * count]
     dk, dv, dqt, aug = refs[8 + 2 * count : 12 + 2 * count]
-    sems = refs[12 + 2 * count :]
-    riders = [
-        Blocks("fsdp", nf, False, sources[i], targets[i], *sems[3 * i : 3 * i + 3]) for i in range(count)
-    ]
+    rest = refs[12 + 2 * count :]
+    riders = [PlaneSum(nf, sources[i], lows[i], *rest[4 * i : 4 * i + 4]) for i in range(count)]
     p = pl.program_id(0)
     slot, key, causal, leaf, first, last = block_fields(p, slots, trunk)
     rows = lambda slot: pl.ds(pl.multiple_of(slot * block, block), block)
@@ -1389,8 +1458,9 @@
         for t in range(3):
             lanes = slice(t * width, (t + 1) * width)
             sums[:, lanes] = jnp.sum(out[:, lanes].astype(jnp.float32), 0, keepdims=True)
-        for r in riders:
+        for r, made in zip(riders, parts):
             r.finish()
+            r.store(made)
 
 
 def attend_back(values, pairs, qkv, kt, datt, att, tot, block, trunk, nf, riders, ident):
@@ -1398,29 +1468,30 @@
     by_q = lambda p: (block_fields(p, rows // block, trunk)[0], 0)
     heads = width // HEAD
     branches = (rows // block - trunk) // 3
+    made = [(k, z.shape[1] - at, z.shape[2] // k) for z, at, k in riders]
     once = lambda s: pl.BlockSpec(s, lambda p: (0,) * len(s), pipeline_mode=pl.Buffered(1))
     hbm = pl.BlockSpec(memory_space=pl.ANY)
     out = pl.pallas_call(
         functools.partial(
-            attend_back_kernel, width, block, rows // block, trunk, branches, nf, len(riders)
+            attend_back_kernel, width, block, rows // block, trunk, branches, nf, [r[1] for r in riders]
         ),
         grid=(len(pairs),),
         out_shape=[
             jax.ShapeDtypeStruct((rows, 3 * width), jnp.bfloat16),
             jax.ShapeDtypeStruct((1, 3 * width), jnp.float32),
         ]
-        + [blocks_shape(r, nf, False) for r in riders],
+        + [jax.ShapeDtypeStruct(s, jnp.bfloat16) for s in made],
         in_specs=[pl.BlockSpec(memory_space=pltpu.SMEM), once((rows, 3 * width)), once((width, rows))]
         + [pl.BlockSpec((block, width), by_q)] * 3
         + [hbm] * len(riders),
-        out_specs=[once((rows, 3 * width)), once((1, 3 * width))] + [hbm] * len(riders),
+        out_specs=[once((rows, 3 * width)), once((1, 3 * width))] + [once(s) for s in made],
         scratch_shapes=[
             pltpu.VMEM((rows, width), jnp.float32),
             pltpu.VMEM((rows, width), jnp.float32),
             pltpu.VMEM((width, block), jnp.float32),
             pltpu.VMEM((heads, block, 2 * HEAD), jnp.bfloat16),
         ]
-        + sum([Blocks.scratch(nf) for _ in riders], []),
+        + sum([PlaneSum.scratch(nf, z.shape[1] - at, z.shape[2]) for z, at, k in riders], []),
         compiler_params=pltpu.CompilerParams(
             dimension_semantics=("arbitrary",),
             vmem_limit_bytes=60 << 20,
@@ -1429,7 +1500,7 @@
         ),
         cost_estimate=SMALL,
         name="attend_back",
-    )(values, qkv, kt, datt, att, tot, *riders)
+    )(values, qkv, kt, datt, att, tot, *[r[0] for r in riders])
     return out[0], out[1], out[2:]
 
 
@@ -1579,7 +1650,7 @@
         grad = (nt(up, proj[...]) * slope.astype(wider)).astype(low)
         return nt(grad, fc[...]), grad
 
-    grad_normed_two, grad_pre, grad_proj, unused_sums, mixed = seq_scatter(
+    grad_normed_two, grad_pre, grad_proj, unused_sums = seq_scatter(
         n,
         width,
         4,
@@ -1589,20 +1660,30 @@
         (proj_mine, fc_mine),
         ((ff, low),),
         side=(hidden_act, upstream_all),
-        carry=mixed,
     )
-    mixed = lax.psum_scatter(mixed, "seq", scatter_dimension=0, tiled=True).astype(wider)
     grad_proj = grad_proj.reshape(nf, piece, width)
     cut = piece // 16 * 8
     unused_two, norm_two_back = jax.vjp(layer_norm, middle, gain_two, shift_two)
     grad_middle_norm, grad_gain_two, grad_shift_two = norm_two_back(grad_normed_two)
     grad_middle = upstream + grad_middle_norm
     grad_branch = grad_middle.astype(low)
-    grad_attended, grad_fc, hidden_sums, proj_first = to_heads(
-        grad_branch, out_turned, n, nf, wide, 5, normed_two, grad_pre, grad_proj[:, :cut]
+    grad_attended, grad_fc, hidden_sums, proj_first, grad_out, mixed = to_heads(
+        grad_branch,
+        out_turned,
+        attended_mine[:, :width],
+        n,
+        nf,
+        wide,
+        5,
+        normed_two,
+        grad_pre,
+        grad_proj,
+        cut,
+        mixed,
     )
+    mixed = lax.psum_scatter(mixed, "seq", scatter_dimension=0, tiled=True).astype(wider)
     grad_attended = grad_attended.reshape(n * block, wide)
-    grad_projected, column_sums, (fc_parts, proj_second) = attend_back(
+    grad_projected, column_sums, (fc_part, proj_second) = attend_back(
         table,
         pairs,
         projected,
@@ -1613,13 +1694,13 @@
         block,
         trunk,
         nf,
-        (grad_fc.reshape(nf, rows, ff), grad_proj[:, cut:]),
+        ((grad_fc.reshape(nf, rows, ff), 0, nf), (grad_proj, cut, n)),
         9,
     )
     output = (after(middle, grad_projected) + mixed + bias_proj).astype(low)[None]
     ready = output[0, :8, :128].astype(wider)
     grad_qkv = contract(normed_one, grad_projected, ready, block)
-    grad_normed_one, qkv_parts = seq_scatter(
+    input_grad, grad_gain_one, grad_shift_one, qkv_parts = seq_scatter(
         n,
         width,
         6,
@@ -1628,21 +1709,12 @@
         (grad_projected,),
         (qkv_mine,),
         rider=(grad_qkv.reshape(nf, rows, 3 * wide), False, nf),
+        norm=(tokens[0], gain_one.reshape(1, -1), grad_middle, low),
     )
-    unused_one, norm_one_back = jax.vjp(layer_norm, resid, gain_one, shift_one)
-    grad_resid_norm, grad_gain_one, grad_shift_one = norm_one_back(grad_normed_one)
-    input_grad = (grad_middle + grad_resid_norm).astype(low)[None]
-
-    proj_part = jnp.concatenate([proj_first, proj_second], 1)
-    proj_part = jnp.sum(proj_part.astype(wider), 0).astype(low)
-    proj_part = proj_part.reshape(piece, n, width // n).transpose(1, 0, 2)
-    fc_part = jnp.sum(fc_parts.astype(wider), 0).astype(low)
-    fc_part = fc_part.reshape(rows, nf, piece).transpose(1, 0, 2)
-    grad_out = contract_rows(
-        after(grad_branch, grad_attended), attended_mine[:, :width]
-    ).astype(low)
+    input_grad = input_grad[None]
+
     out_part = lax.psum_scatter(grad_out, "seq", scatter_dimension=0, tiled=True).T
-    out_part = after(out_part, grad_normed_one).reshape(nf, rows, width // n)
+    out_part = after(out_part, qkv_parts).reshape(nf, rows, width // n)
     qkv_part = jnp.sum(qkv_parts.astype(wider), 0).astype(low).T
 
     column_sums = column_sums.reshape(3, wide)
@@ -1664,11 +1736,12 @@
         grad_fc_bias,
         jnp.sum(upstream, 0),
     ]
-    summed, qkv_out, proj_out, fc_out, out_out = give_back(
+    summed, qkv_out, proj_first, proj_second, fc_out, out_out = give_back(
         jnp.concatenate([p.reshape(nf, -1) for p in parts], 1),
         qkv_part,
         qkv_cols,
-        proj_part,
+        proj_first,
+        proj_second,
         fc_part,
         out_part,
         n,
@@ -1683,6 +1756,7 @@
         qkv_out = lax.dynamic_slice_in_dim(qkv_out, s * qkv_cols, qkv_cols, 0)
     out_out = jnp.sum(out_out.astype(wider), 0)
     qkv_out = qkv_out.T.astype(wider)
+    proj_out = jnp.concatenate([proj_first, proj_second], 1)
     proj_out = proj_out.reshape(n * piece, width // n).astype(wider)
     fc_out = fc_out.transpose(1, 0, 2).reshape(rows, nf * piece).astype(wider)
     vector_out = []

time: 813 us -> 786 us (0.967)
  other arithmetic: 44.6 us -> 25.5 us
  Pallas kernels: 649 us -> 660 us
  local copies, waits for them, and re-layouts: 76.4 us -> 65.9 us
    reshape x4 -> x0, local copies, waits for them, and re-layouts: 11.2 us -> none  [the longest x2 5.87 us: local(): fc_part = fc_part.reshape(rows, nf, piece).transpose(1, 0, 2)]
    pallas_call x2, Pallas kernels: 148 us -> 156 us  [seq_scatter(): pl.pallas_call(functools.partial(scatter_kernel, n, h, body, len(ins), le...]
    unnamed x90 -> x74, local copies, waits for them, and re-layouts: 25.6 us -> 24.4 us
  transfers between devices with their start and end apart: 4 -> 4, of which waited for: 0 -> 0; matrix products, arithmetic and copies ran while one was open for 8% -> 6% of each run, Pallas kernels for 42% -> 51%
where the time goes in v4:
time: 786 us; the launch traced here: 777 us
  Pallas kernels  660 us (84%)
  local copies, waits for them, and re-layouts  65.9 us (8%)
  other arithmetic  25.5 us (3%)
  between operations  16.9 us (2%)
    pallas_call x2, Pallas kernels, seq_gather(): pl.pallas_call(functools.partial(gather_kernel, n, h, body, len(consts),...  165 us
    pallas_call x2, Pallas kernels, seq_scatter(): pl.pallas_call(functools.partial(scatter_kernel, n, h, body, len(ins), le...  156 us
    pallas_call x1, Pallas kernels, attend_back(): pl.pallas_call(functools.partial(attend_back_kernel, width, block, rows /...  107 us
    pallas_call x1, Pallas kernels, attend(): pl.pallas_call(functools.partial(attend_kernel, width, block, trunk, n),...  75.5 us
    pallas_call x1, Pallas kernels, to_heads(): pl.pallas_call(functools.partial(to_heads_kernel, n, nf, wide), out_shape...  45 us
    pallas_call x1, Pallas kernels, give_back(): pl.pallas_call(functools.partial(give_back_kernel, n, nf, rows), out_shap...  36.1 us
    pallas_call x1, Pallas kernels, exchange(): pl.pallas_call(functools.partial(exchange_kernel, n, nf, rows, count), ou...  32.7 us
    pallas_call x1, Pallas kernels, to_tokens(): pl.pallas_call(functools.partial(to_tokens_kernel, n, wide), out_shape=ja...  25.3 us
  transfers between devices with their start and end apart: 4, of which 0 were waited for; matrix products, arithmetic and copies ran while one was open for 6% of the time, Pallas kernels for 51%

profile of v4, /device:TPU:3, one launch (start us, length us, event | category | flops | bytes accessed | tf_op | source)
XLA Modules:
  0.0 777.4 jit_solution(11954627966754656124)
XLA Ops:
  7.2 1.3 reshape.297.refs_4_
  8.6 1.3 reshape.298.refs_5_
  9.8 1.3 reshape.300.refs_7_
  11.1 1.3 reshape.301.refs_8_
  12.3 1.3 reshape.302.refs_9_
  13.6 1.3 reshape.304.refs_11_
  14.8 1.3 reshape.299.refs_6_
  16.1 1.3 reshape.303.refs_10_
  17.4 2.1 copy.89
  19.5 2.7 reshape.296
  24.3 32.7 %exchange.1 = (bf16[768,400]{1,0:T(8,128)(2,1)}, bf16[8,200,200]{2,1,0:T(8,128)(2,1)}, bf16[4,400,200]{2,1,0:T(8,128)(2,1)}, bf16[4,400,200]{2,1,0:T(8,128)(2,1)...) custom-call(bf16[600,400]{1,0:T(8,128)(2,1)} %bitcast.98, ...), custom_call_target="tpu_custom_call" | custom-call | bytes 1048576 | tf_op jit(solution)/shard_map/exchange/pallas_call | solution.py:885
  57.0 1.6 copy.96
  58.7 1.5 reshape.310
  60.5 1.4 copy.93
  62.3 2.7 copy.88
  67.9 1.9 fusion.5.refs_0_
  69.8 92.4 %gather_one.1 = (bf16[16,256,1600]{2,1,0:T(8,128)(2,1)}, bf16[8,200,2048]{2,1,0:T(8,128)(2,1)}, bf16[4,400,768]{2,1,0:T(8,128)(2,1)}) custom-call(bf16[512,1600]{1,0:T(8,128)(2,1)} %fusion.5.refs_0_, bf16[200,2048]{1,0:T(8,128)(2,1)} %pad.12.refs_1_, bf16[400,768]{1,0:T(8,128)(2,1)} %select_bitcast_fusion.refs_2_), custom_call_target="tpu_custom_call" | custom-call | bytes 1048576 | tf_op jit(solution)/shard_map/gather_one/pallas_call | solution.py:382
  162.2 1.3 slice.84
  164.5 1.8 add.138
  168.8 2.4 copy.94
  172.0 75.5 %attend.1 = (bf16[4096,768]{1,0:T(8,128)(2,1)}, bf16[4096,256]{1,0:T(8,128)(2,1)}, f32[4096,256]{1,0:T(8,128)}, f32[4096,256]{1,0:T(8,128)}, bf16[256,4096]{1,0:T(8,128)(2,1)}, /*index=5*/bf16[8,512,1600]{2,1,0:T(8,128)(2,1)}) custom-call(s32[2,25]{1,0:T(2,128)} %pad_add_fusion.values.refs_0_, bf16[8,512,1600]{2,1,0:T(8,128)(2,1)} %bitcast.79, ...), custom_call_target="tpu_custom_call" | custom-call | bytes 1048576 | tf_op jit(solution)/shard_map/attend/pallas_call | solution.py:1312
  247.5 25.3 %to_tokens.1 = bf16[512,2048]{1,0:T(8,128)(2,1)} custom-call(bf16[8,512,256]{2,1,0:T(8,128)(2,1)} %bitcast.100), custom_call_target="tpu_custom_call" | custom-call | bytes 1048576 | tf_op jit(solution)/shard_map/to_tokens/pallas_call | solution.py:934
  272.8 2.9 slice.68.t_ref
  275.6 7.7 fusion.13
  283.8 1.9 add_convert_fusion.1.refs_0_
  285.7 72.9 %gather_two.1 = (bf16[16,256,1600]{2,1,0:T(8,128)(2,1)}, bf16[16,256,800]{2,1,0:T(8,128)(2,1)}, bf16[16,256,800]{2,1,0:T(8,128)(2,1)}, bf16[16,256,1600]{2,1,0:T(8,128)(2,1)}) custom-call(bf16[512,1600]{1,0:T(8,128)(2,1)} %add_convert_fusion.1.refs_0_, bf16[1600,800]{1,0:T(8,128)(2,1)} %all-gather.3.cloned.1.call-done.refs_1_.refs_3_, ...), custom_call_target="tpu_custom_call" | custom-call | bytes 1048576 | tf_op jit(solution)/shard_map/gather_two/pallas_call | solution.py:382
  358.6 77.5 %scatter_two.1 = (f32[512,1600]{1,0:T(8,128)}, bf16[16,256,800]{2,1,0:T(8,128)(2,1)}, bf16[800,1600]{1,0:T(8,128)(2,1)}, f32[1,1600]{1,0:T(1,128)}) custom-call(bf16[16,256,1600]{2,1,0:T(8,128)(2,1)} %bitcast.82, bf16[16,256,800]{2,1,0:T(8,128)(2,1)} %get-tuple-element.81.refs_1_, bf16[800,1600]{1,0:T(8,128)(2,1)} %all-gather.5.cloned.1.call-done.refs_3_.refs_2_, ...), custom_call_target="tpu_custom_call" | custom-call | bytes 1048576 | tf_op jit(solution)/shard_map/scatter_two/pallas_call | solution.py:701
  436.1 3.2 multiply_reduce_fusion
  440.7 3.0 convert_reduce_fusion.2
  443.7 45.0 %to_heads.1 = (bf16[8,512,256]{2,1,0:T(8,128)(2,1)}, bf16[1600,800]{1,0:T(8,128)(2,1)}, f32[1,800]{1,0:T(1,128)}, bf16[8,96,200]{2,1,0:T(8,128)(2,1)}, bf16[1600...) custom-call(bf16[4096,1600]{1,0:T(8,128)(2,1)} %bitcast.81, ...), custom_call_target="tpu_custom_call", output_to_operand_aliasing={{5}: (0, {})} | custom-call | bytes 1048576 | tf_op jit(solution)/shard_map/to_heads/pallas_call | solution.py:1000
  490.4 106.7 %attend_back.1 = (bf16[4096,768]{1,0:T(8,128)(2,1)}, f32[1,768]{1,0:T(1,128)}, bf16[4,400,200]{2,1,0:T(8,128)(2,1)}, bf16[8,104,200]{2,1,0:T(8,128)(2,1)}) custom-call(s32[2,25]{1,0:T(2,128)} %pad_add_fusion.values.refs_0_, bf16[4096,768]{1,0:T(8,128)(2,1)} %get-tuple-element.72.refs_1_, bf16[256,4096]{1,0:T(8,128)(2,1)} %get-tuple-element.73.refs_2_, ...), custom_call_target="tpu_custom_call" | custom-call | bytes 1048576 | tf_op jit(solution)/shard_map/attend_back/pallas_call | solution.py:1474
  597.1 1.2 slice.69
  600.3 3.2 fusion.7
  603.5 4.0 copy.103
  608.1 3.5 copy-done
  611.6 17.5 %contract.1 = bf16[1600,768]{1,0:T(8,128)(2,1)S(1)} custom-call(bf16[4096,1600]{1,0:T(8,128)(2,1)} %bitcast.80, bf16[4096,768]{1,0:T(8,128)(2,1)S(1)} %copy-done, f32[8,128]{1,0:T(8,128)S(1)} %fusion.9.ready), custom_call_target="tpu_custom_call" | custom-call | bytes 1048576 | tf_op jit(solution)/shard_map/contract/pallas_call | solution.py:1047
  629.1 1.4 copy-done.1
  630.5 79.0 %scatter_one.1 = (bf16[512,1600]{1,0:T(8,128)(2,1)}, f32[1,1600]{1,0:T(1,128)}, f32[1,1600]{1,0:T(1,128)}, bf16[4,400,768]{2,1,0:T(8,128)(2,1)}) custom-call(bf16[512,1600]{1,0:T(8,128)(2,1)} %bitcast.84, f32[1,1600]{1,0:T(1,128)} %reshape.339.refs_1_, f32[512,1600]{1,0:T(8,128)} %get-tuple-element.175.refs_2_, bf16[16,256,768]{2,1,0:T(8,128)(2,1)} %bitcast.76, ...), custom_call_target="tpu_custom_call" | custom-call | bytes 1048576 | tf_op jit(solution)/shard_map/scatter_one/pallas_call | solution.py:701
  710.7 2.4 reduce_sum.165
  717.3 1.2 copy.101
  719.7 36.1 %give_back.1 = (f32[40,128]{1,0:T(8,128)}, bf16[600,400]{1,0:T(8,128)(2,1)}, bf16[8,96,200]{2,1,0:T(8,128)(2,1)}, bf16[8,104,200]{2,1,0:T(8,128)(2,1)}, bf16[4,4...) custom-call(f32[4,40,128]{2,1,0:T(8,128)} %bitcast.104, bf16[768,400]{1,0:T(8,128)(2,1)} %bitcast.95, ...), custom_call_target="tpu_custom_call" | custom-call | bytes 1048576 | tf_op jit(solution)/shard_map/give_back/pallas_call | solution.py:1120
  755.8 1.5 slice.90
  757.3 1.4 slice.94
  758.6 1.4 fusion.12
  760.1 2.5 copy.104
  763.8 1.6 copy.106
  765.6 1.3 copy.105
  768.1 2.2 reshape.341
  (153 shorter events, 23.3 us)
Async XLA Ops:
  7.2 16.0 %copy-start.12 = (bf16[1600,200]{0,1:T(8,128)(2,1)S(1)}, bf16[1600,200]{0,1:T(8,128)(2,1)}, u32[]{:S(2)}) copy-start(bf16[1600,200]{0,1:T(8,128)(2,1)} %param.31) | copy-start | bytes 1920004
  7.2 278.5 %all-gather.3.cloned.1.call-start = ((), (), s32[]{:S(2)}) async-start(), calls=%async_computation.2 | async-start | bytes 3584000 | tf_op jit(solution)/shard_map/all_gather | solution.py:1615
  57.0 3.3 copy-start.22
  57.0 3.3 copy-start.23
  57.0 4.9 copy-start.9
  60.2 225.5 %all-gather.5.cloned.1.call-start = ((), (), s32[]{:S(2)}) async-start(), calls=%async_computation.3 | async-start | bytes 3328000 | tf_op jit(solution)/shard_map/all_gather | solution.py:1619
  65.0 4.8 copy-start.2
  67.9 96.3 %copy-start.8 = (bf16[8,200,200]{2,1,0:T(8,128)(2,1)S(1)}, bf16[8,200,200]{2,1,0:T(8,128)(2,1)}, u32[]{:S(2)}) copy-start(bf16[8,200,200]{2,1,0:T(8,128)(2,1)} %get-tuple-element.78) | copy-start | bytes 1920004
  162.1 4.4 copy-start.19
  162.2 4.5 copy-start.17
  162.2 5.5 copy-start.20
  162.2 5.5 copy-start.21
  162.2 5.7 copy-start.16
  162.2 6.6 copy-start.7
  164.3 6.9 copy-start.26
  164.3 6.9 copy-start.28
  164.3 7.0 copy-start.25
  164.3 7.0 copy-start.29
  164.3 7.0 copy-start.30
  164.3 7.1 copy-start.27
  166.3 434.0 %reduce-scatter.5.cloned.1.call-start = ((), (), s32[]{:S(2)}) async-start(), calls=%async_computation.4 | async-start | bytes 15335424 | tf_op jit(solution)/shard_map/reduce_scatter | solution.py:1684
  272.8 2.9 copy-start.3
  436.1 3.2 copy-start.5
  439.3 1.5 copy-start.4
  488.7 1.3 copy-start.18
  488.8 227.4 %reduce-scatter.7.cloned.1.call-start = ((), (), s32[]{:S(2)}) async-start(), calls=%async_computation.5 | async-start | bytes 5990400
  490.4 109.5 %copy-start.24 = (f32[1,800]{1,0:T(1,128)S(1)}, f32[1,800]{1,0:T(1,128)}, u32[]{:S(2)}) copy-start(f32[1,800]{1,0:T(1,128)} %get-tuple-element.98) | copy-start | bytes 9604
  608.1 3.5 copy-start
  629.1 1.4 copy-start.1
  717.3 42.8 %copy-start.6 = (bf16[512,1600]{1,0:T(8,128)(2,1)S(1)}, bf16[512,1600]{1,0:T(8,128)(2,1)}, u32[]{:S(2)}) copy-start(bf16[512,1600]{1,0:T(8,128)(2,1)} %get-tuple-element.94) | copy-start | bytes 4915204
  755.8 6.9 copy-start.11
  755.8 7.8 copy-start.14
  755.8 7.7 copy-start.15
  763.5 1.9 copy-start.13
  763.8 3.1 copy-start.10
Sparse Core Ops, SparseCore 0:
  60.3 103.9 all-gather.2
  166.4 62.9 all-gather.4
  488.9 100.7 reduce-scatter.4
  592.9 72.1 reduce-scatter.6

commit v5 on v4

--- a/solution.py
+++ b/solution.py
@@ -231,7 +231,8 @@
         w_ref, w_all = refs[at], refs[out]
         w_send, w_recv, w_keep = refs[-3:]
         refs = refs[:at] + refs[at + 1 : out] + refs[out + 1 : -3]
-        w_half = w_ref.shape[1] // 2
+        w_half = w_ref.shape[1] // 256 * 128
+        w_lanes = [pl.ds(0, w_half), pl.ds(w_half, w_ref.shape[1] - w_half)]
     refs, rider = split_rider(refs, nf, same, 1 + n_const, 1 + n_out)
     x_ref = refs[0]
     consts = refs[1 : 1 + n_const]
@@ -261,7 +262,7 @@
         if not second:
             return [first]
         owner = place(me, k, n)
-        lanes = pl.ds(half * w_half, w_half)
+        lanes = w_lanes[half]
         src = w_ref if isinstance(k, int) and k == 0 else w_all.at[owner]
         other = remote(
             src.at[:, lanes], w_all.at[owner].at[:, lanes], w_send.at[half, lane, k], w_recv.at[half, to], device(b)
@@ -273,7 +274,7 @@
             act(c)
 
     def w_arrive(half, k):
-        dst = w_all.at[place(me, k, n)].at[:, pl.ds(0, w_half)]
+        dst = w_all.at[place(me, k, n)].at[:, w_lanes[half]]
         remote(dst, dst, w_send.at[0, 0, 0], w_recv.at[half, k], device(1)).wait_recv()
 
     greet([device(b) for b in [1] + bits] + (rider.peers() if nf else []))
@@ -316,8 +317,12 @@
         @pl.when(k != 0)
         def _():
             remote(held.at[at], held.at[at], send.at[0, 0, 0], recv.at[half, k], device(1)).wait_recv()
-            if second:
-                w_arrive(half, k)
+
+        for side in (0, 1) if second else ():
+
+            @pl.when((k != 0) & (half == side))
+            def _(side=side):
+                w_arrive(side, k)
 
         for side in (0, 1):
             for i in range(nb):
@@ -488,7 +493,10 @@
     return orders, [(half, lists[half][i]) for i in range(n // 2) for half in (0, 1)]
 
 
-def scatter_kernel(n, h, body, n_in, n_const, n_out, modes, nf, same, has_side, has_norm, *refs):
+def scatter_kernel(n, h, body, n_in, n_const, n_out, modes, nf, same, has_side, has_norm, carried, *refs):
+    if carried:
+        out = 1 + n_in + n_const + 2 * has_side + min(nf, 1) + 1 + n_out + 2 * has_side + min(nf, 1)
+        refs = refs[1:out] + refs[out + 1 :]
     if has_norm:
         out = n_in + 3 + n_const + 2 * has_side + min(nf, 1)
         values, gain, joins = refs[:3]
@@ -681,7 +689,7 @@
         side.end()
 
 
-def seq_scatter(n, cols, ident, name, body, ins, consts, outs=(), modes=None, rider=None, side=None, norm=None):
+def seq_scatter(n, cols, ident, name, body, ins, consts, outs=(), modes=None, rider=None, side=None, norm=None, carry=None):
     h = ins[0].shape[0] // (2 * n)
     low = jnp.bfloat16
     slots = min(4, n)
@@ -694,20 +702,32 @@
     s_ins, s_shapes, s_in_specs, s_out_specs, s_scratch = side_parts(side, 2 * n)
     sums = [jax.ShapeDtypeStruct((2 * h, cols), jnp.float32)]
     norms = []
+    carries = [] if carry is None else [carry]
     if norm is not None:
         norms = list(norm[:3])
         line = jax.ShapeDtypeStruct((1, cols), jnp.float32)
         sums = [jax.ShapeDtypeStruct((2 * h, cols), norm[3]), line, line]
     out = pl.pallas_call(
         functools.partial(
-            scatter_kernel, n, h, body, len(ins), len(consts), len(outs), modes, nf, same, int(side is not None), norm is not None
+            scatter_kernel, n, h, body, len(ins), len(consts), len(outs), modes, nf, same, int(side is not None), norm is not None, carry is not None
         ),
         out_shape=sums
         + [jax.ShapeDtypeStruct((2 * n, h, c), d) for c, d in outs]
         + s_shapes
-        + shape,
-        in_specs=[vmem] * len(norms) + [hbm] * len(ins) + [vmem] * len(consts) + s_in_specs + spec,
-        out_specs=([vmem] * 3 if norms else [hbm]) + [hbm] * len(outs) + s_out_specs + spec,
+        + shape
+        + [jax.ShapeDtypeStruct(x.shape, x.dtype) for x in carries],
+        in_specs=[hbm] * len(carries)
+        + [vmem] * len(norms)
+        + [hbm] * len(ins)
+        + [vmem] * len(consts)
+        + s_in_specs
+        + spec,
+        out_specs=([vmem] * 3 if norms else [hbm])
+        + [hbm] * len(outs)
+        + s_out_specs
+        + spec
+        + [hbm] * len(carries),
+        input_output_aliases={0: len(sums + list(outs) + s_shapes + shape)} if carries else {},
         scratch_shapes=[
             pltpu.VMEM((slots, h, cols), low),
             pltpu.VMEM((n, h, cols), low),
@@ -733,7 +753,7 @@
         ),
         cost_estimate=SMALL,
         name=name,
-    )(*norms, *split, *consts, *s_ins, *more)
+    )(*carries, *norms, *split, *consts, *s_ins, *more)
     lines = list(out[1:3]) if norms else []
     out = [out[0]] + list(out[1 + len(lines) :])
     many = 1 + len(outs)
@@ -944,7 +964,7 @@
 
 
 def to_heads_kernel(
-    n, nf, wide, carried, x_ref, w_ref, t_ref, a_ref, b_ref, z_ref, o_ref, g_ref, m_ref, z_out, t_out, handed, made, *extra
+    n, nf, wide, x_ref, w_ref, t_ref, a_ref, b_ref, z_ref, o_ref, g_ref, m_ref, z_out, t_out, made, *extra
 ):
     me = lax.axis_index("seq")
     send, recv, local = extra[:3]
@@ -963,8 +983,23 @@
 
     def step(i, carry):
         r = n - 1 - i
-        lanes = pl.ds(pl.multiple_of(place(me, r, n) * wide, 128), wide)
-        made[r] = mm(x_ref[...], w_ref[:, lanes]).astype(made.dtype)
+        at = place(me, r, n)
+        whole, rest = w_ref.shape[1] // wide, w_ref.shape[1] % wide
+
+        @pl.when(at < whole)
+        def _():
+            lanes = pl.ds(pl.multiple_of(at * wide, 128), wide)
+            made[r] = mm(x_ref[...], w_ref[:, lanes]).astype(made.dtype)
+
+        @pl.when(at >= whole)
+        def _():
+            made[r] = jnp.zeros(made.shape[1:], made.dtype)
+
+        if rest:
+
+            @pl.when(at == whole)
+            def _():
+                made[r, :, :rest] = mm(x_ref[...], w_ref[:, whole * wide :]).astype(made.dtype)
 
         @pl.when(r > 0)
         def _():
@@ -992,7 +1027,7 @@
         copy(r).wait_send()
 
 
-def to_heads(x, w, t, n, nf, wide, ident, a, b, z, count, carry):
+def to_heads(x, w, t, n, nf, wide, ident, a, b, z, count):
     rows, cols = x.shape
     vmem = pl.BlockSpec(memory_space=pltpu.VMEM)
     hbm = pl.BlockSpec(memory_space=pl.ANY)
@@ -1004,11 +1039,9 @@
         + [
             jax.ShapeDtypeStruct((n, count, z.shape[2] // n), z.dtype),
             jax.ShapeDtypeStruct((cols, t.shape[1]), x.dtype),
-            jax.ShapeDtypeStruct(carry.shape, carry.dtype),
         ],
-        in_specs=[hbm, vmem, vmem, vmem] + s_in_specs + [hbm],
-        out_specs=[hbm] + s_out_specs + [vmem, vmem, hbm],
-        input_output_aliases={0: 5},
+        in_specs=[vmem, vmem, vmem] + s_in_specs + [hbm],
+        out_specs=[hbm] + s_out_specs + [vmem, vmem],
         scratch_shapes=[pltpu.VMEM((n, rows, wide), x.dtype)]
         + Blocks.scratch(n)
         + s_scratch
@@ -1018,11 +1051,12 @@
         ),
         cost_estimate=SMALL,
         name="to_heads",
-    )(carry, x, w, t, *s_ins, z)
-
-
-def contract_kernel(a_ref, b_ref, ready, o_ref, acc):
+    )(x, w, t, *s_ins, z)
+
+
+def contract_kernel(a_ref, b_ref, x_ref, y_ref, s_ref, o_ref, sum_ref, acc):
     i = pl.program_id(0)
+    sum_ref[...] = (x_ref[...] + y_ref[...].astype(jnp.float32) + s_ref[...]).astype(sum_ref.dtype)
     part = lax.dot_general(
         a_ref[...], b_ref[...], (((0,), (0,)), ((), ())), preferred_element_type=jnp.float32
     )
@@ -1040,27 +1074,24 @@
         o_ref[...] = acc[...].astype(o_ref.dtype)
 
 
-def contract(a, b, ready, tile):
-    rows = a.shape[0]
+def contract(a, b, x, y, s, tile):
+    steps = a.shape[0] // tile
     shape = (a.shape[1], b.shape[1])
     still = lambda s: pl.BlockSpec(s, lambda i: (0,) * len(s), pipeline_mode=pl.Buffered(1))
+    part = lambda v: pl.BlockSpec((v.shape[0] // steps, v.shape[1]), lambda i: (i, 0))
     return pl.pallas_call(
         contract_kernel,
-        out_shape=jax.ShapeDtypeStruct(shape, a.dtype),
-        grid=(rows // tile,),
-        in_specs=[
-            pl.BlockSpec((tile, shape[0]), lambda i: (i, 0)),
-            pl.BlockSpec((tile, shape[1]), lambda i: (i, 0)),
-            still(ready.shape),
-        ],
-        out_specs=still(shape),
+        out_shape=[jax.ShapeDtypeStruct(shape, a.dtype), jax.ShapeDtypeStruct(x.shape, a.dtype)],
+        grid=(steps,),
+        in_specs=[part(a), part(b), part(x), part(y), still(s.shape)],
+        out_specs=[still(shape), part(x)],
         scratch_shapes=[pltpu.VMEM(shape, jnp.float32)],
         compiler_params=pltpu.CompilerParams(
             dimension_semantics=("arbitrary",), vmem_limit_bytes=40 << 20
         ),
         cost_estimate=SMALL,
         name="contract",
-    )(a, b, ready)
+    )(a, b, x, y, s)
 
 
 def give_back_kernel(
@@ -1297,9 +1328,12 @@
             att[:, lanes] = value
             tot[:, lanes] = total
 
+    @pl.when(p == pl.num_programs(0) - 4)
+    def _():
+        spread.phase(len(spread.bits) - 1)
+
     @pl.when(p == pl.num_programs(0) - 1)
     def _():
-        spread.phase(len(spread.bits) - 1)
         spread.finish()
 
 
@@ -1573,14 +1607,18 @@
         proj_weight.reshape(n, piece, width // n),
         fc_weight.reshape(rows, nf, piece).transpose(1, 0, 2),
         out_weight,
-        [v.reshape(1, -1) for v in vectors],
+        [jnp.stack([v for v in vectors if v.shape == ln1_gain.shape])]
+        + [v.reshape(1, -1) for v in vectors if v.shape != ln1_gain.shape],
         n,
         nf,
         forth,
         wide,
         0,
     )
-    whole = [v.reshape(-1).astype(wider) for v in gathered]
+    short = iter(jnp.unstack(gathered[0], axis=1))
+    long = iter(gathered[1:])
+    whole = [next(short) if v.shape == ln1_gain.shape else next(long) for v in vectors]
+    whole = [v.reshape(-1).astype(wider) for v in whole]
     gain_one, shift_one, bias_qv, bias_out, gain_two, shift_two, bias_fc, bias_proj = whole
     bias_three = jnp.stack([bias_qv[:width], jnp.zeros((width,), wider), bias_qv[width:]])
     bias_three = jnp.pad(bias_three, ((0, 0), (0, n * wide - width)))
@@ -1600,7 +1638,7 @@
     table = block_values(seg_lengths[0], parents[0], pairs, block)
 
     resid = tokens[0].astype(wider)
-    out_turned = jnp.pad(out_blocks.reshape(width, width // n).T, ((0, 0), (0, n * wide - width)))
+    out_turned = out_blocks.reshape(width, width // n).T
     normed_one, out_turned, qkv_mine = seq_gather(
         layer_norm(resid, gain_one, shift_one).astype(low),
         n,
@@ -1609,7 +1647,7 @@
         rider=(turned.T, True, nf),
         second=out_turned,
     )
-    out_turned = out_turned.reshape(width, n * wide)
+    out_turned = out_turned.reshape(width, width)
     qkv_mine = qkv_mine.reshape(width, 3 * wide)
     fc_rows = fc_blocks.transpose(1, 0, 2).reshape(rows, nf * piece)
     fc_mine = lax.all_gather(fc_rows, "fsdp", axis=0, tiled=True)
@@ -1620,7 +1658,7 @@
     projected, attended_low, attended, totals, keys_turned, upstream_all = attend(
         table, pairs, normed_one, qkv_mine, bias_mine, block, trunk, cotangent[0], n, 8
     )
-    attended_mine = to_tokens(attended_low.reshape(n, block, wide), n, wide, 2)
+    attended_mine = to_tokens(attended_low.reshape(n, block, wide), n, wide, 2)[:, :width]
     middle = resid + contract_cols(attended_mine, out_turned) + bias_out
     normed_two = layer_norm(middle, gain_two, shift_two).astype(low)
     ff = nf * piece
@@ -1650,7 +1688,7 @@
         grad = (nt(up, proj[...]) * slope.astype(wider)).astype(low)
         return nt(grad, fc[...]), grad
 
-    grad_normed_two, grad_pre, grad_proj, unused_sums = seq_scatter(
+    grad_normed_two, grad_pre, grad_proj, unused_sums, mixed = seq_scatter(
         n,
         width,
         4,
@@ -1660,17 +1698,19 @@
         (proj_mine, fc_mine),
         ((ff, low),),
         side=(hidden_act, upstream_all),
+        carry=mixed,
     )
+    mixed = lax.psum_scatter(mixed, "seq", scatter_dimension=0, tiled=True)
     grad_proj = grad_proj.reshape(nf, piece, width)
     cut = piece // 16 * 8
     unused_two, norm_two_back = jax.vjp(layer_norm, middle, gain_two, shift_two)
     grad_middle_norm, grad_gain_two, grad_shift_two = norm_two_back(grad_normed_two)
     grad_middle = upstream + grad_middle_norm
     grad_branch = grad_middle.astype(low)
-    grad_attended, grad_fc, hidden_sums, proj_first, grad_out, mixed = to_heads(
+    grad_attended, grad_fc, hidden_sums, proj_first, grad_out = to_heads(
         grad_branch,
         out_turned,
-        attended_mine[:, :width],
+        attended_mine,
         n,
         nf,
         wide,
@@ -1679,9 +1719,7 @@
         grad_pre,
         grad_proj,
         cut,
-        mixed,
     )
-    mixed = lax.psum_scatter(mixed, "seq", scatter_dimension=0, tiled=True).astype(wider)
     grad_attended = grad_attended.reshape(n * block, wide)
     grad_projected, column_sums, (fc_part, proj_second) = attend_back(
         table,
@@ -1697,9 +1735,10 @@
         ((grad_fc.reshape(nf, rows, ff), 0, nf), (grad_proj, cut, n)),
         9,
     )
-    output = (after(middle, grad_projected) + mixed + bias_proj).astype(low)[None]
-    ready = output[0, :8, :128].astype(wider)
-    grad_qkv = contract(normed_one, grad_projected, ready, block)
+    grad_qkv, output = contract(
+        normed_one, grad_projected, middle, mixed, bias_proj.reshape(1, -1), block
+    )
+    output = output[None]
     input_grad, grad_gain_one, grad_shift_one, qkv_parts = seq_scatter(
         n,
         width,

time: 786 us -> 772 us (0.982)
    pallas_call x1, Pallas kernels: 45 us -> 60.1 us  [to_heads(): pl.pallas_call(functools.partial(to_heads_kernel, n, nf, wide), out_shape...]
    unnamed x74 -> x68, local copies, waits for them, and re-layouts: 24.4 us -> 22.1 us
  transfers between devices with their start and end apart: 4 -> 4, of which waited for: 0 -> 0; matrix products, arithmetic and copies ran while one was open for 6% -> 5% of each run, Pallas kernels for 51% -> 58%
where the time goes in v5:
time: 772 us; the launch traced here: 764 us
  Pallas kernels  662 us (86%)
  local copies, waits for them, and re-layouts  58.1 us (8%)
  other arithmetic  19.7 us (3%)
  between operations  16.2 us (2%)
    pallas_call x2, Pallas kernels, seq_gather(): pl.pallas_call(functools.partial(gather_kernel, n, h, body, len(consts),...  161 us
    pallas_call x2, Pallas kernels, seq_scatter(): pl.pallas_call(functools.partial(scatter_kernel, n, h, body, len(ins), le...  150 us
    pallas_call x1, Pallas kernels, attend_back(): pl.pallas_call(functools.partial(attend_back_kernel, width, block, rows /...  109 us
    pallas_call x1, Pallas kernels, attend(): pl.pallas_call(functools.partial(attend_kernel, width, block, trunk, n),...  69.9 us
    pallas_call x1, Pallas kernels, to_heads(): pl.pallas_call(functools.partial(to_heads_kernel, n, nf, wide), out_shape...  60.1 us
    pallas_call x1, Pallas kernels, give_back(): pl.pallas_call(functools.partial(give_back_kernel, n, nf, rows), out_shap...  36.5 us
    pallas_call x1, Pallas kernels, exchange(): pl.pallas_call(functools.partial(exchange_kernel, n, nf, rows, count), ou...  32.1 us
    pallas_call x1, Pallas kernels, to_tokens(): pl.pallas_call(functools.partial(to_tokens_kernel, n, wide), out_shape=ja...  25.3 us
  transfers between devices with their start and end apart: 4, of which 0 were waited for; matrix products, arithmetic and copies ran while one was open for 5% of the time, Pallas kernels for 58%

profile of v5, /device:TPU:3, one launch (start us, length us, event | category | flops | bytes accessed | tf_op | source)
XLA Modules:
  0.0 764.2 jit_solution(3308547242265368816)
XLA Ops:
  11.4 1.3 reshape.273.refs_5_
  12.6 1.3 reshape.274.refs_6_
  13.9 2.1 copy.89
  16.0 2.7 reshape.272
  18.7 1.0 copy.114
  19.7 1.2 copy.90
  21.5 32.1 %exchange.1 = (bf16[768,400]{1,0:T(8,128)(2,1)}, bf16[8,200,200]{2,1,0:T(8,128)(2,1)}, bf16[4,400,200]{2,1,0:T(8,128)(2,1)}, bf16[4,400,200]{2,1,0:T(8,128)(2,1)...) custom-call(bf16[600,400]{1,0:T(8,128)(2,1)} %bitcast.90, ...), custom_call_target="tpu_custom_call" | custom-call | bytes 1048576 | tf_op jit(solution)/shard_map/exchange/pallas_call | solution.py:905
  53.6 1.7 copy.96
  55.3 1.5 reshape.281
  56.9 1.1 copy.108
  58.6 2.7 copy.88
  63.1 1.9 fusion.5.refs_0_
  65.0 88.0 %gather_one.1 = (bf16[16,256,1600]{2,1,0:T(8,128)(2,1)}, bf16[8,200,1600]{2,1,0:T(8,128)(2,1)}, bf16[4,400,768]{2,1,0:T(8,128)(2,1)}) custom-call(bf16[512,1600]{1,0:T(8,128)(2,1)} %fusion.5.refs_0_, bf16[200,1600]{1,0:T(8,128)(2,1)} %bitcast.89, bf16[400,768]{1,0:T(8,128)(2,1)} %select_bitcast_fusion.refs_2_), custom_call_target="tpu_custom_call" | custom-call | bytes 1048576 | tf_op jit(solution)/shard_map/gather_one/pallas_call | solution.py:387
  153.1 1.3 slice.76
  155.4 1.8 add.119
  159.6 2.6 copy.94
  163.0 69.9 %attend.1 = (bf16[4096,768]{1,0:T(8,128)(2,1)}, bf16[4096,256]{1,0:T(8,128)(2,1)}, f32[4096,256]{1,0:T(8,128)}, f32[4096,256]{1,0:T(8,128)}, bf16[256,4096]{1,0:T(8,128)(2,1)}, /*index=5*/bf16[8,512,1600]{2,1,0:T(8,128)(2,1)}) custom-call(s32[2,25]{1,0:T(2,128)} %pad_add_fusion.values.refs_0_, bf16[8,512,1600]{2,1,0:T(8,128)(2,1)} %bitcast.70, ...), custom_call_target="tpu_custom_call" | custom-call | bytes 1048576 | tf_op jit(solution)/shard_map/attend/pallas_call | solution.py:1346
  232.9 25.3 %to_tokens.1 = bf16[512,2048]{1,0:T(8,128)(2,1)} custom-call(bf16[8,512,256]{2,1,0:T(8,128)(2,1)} %bitcast.92), custom_call_target="tpu_custom_call" | custom-call | bytes 1048576 | tf_op jit(solution)/shard_map/to_tokens/pallas_call | solution.py:954
  258.2 7.1 fusion.12
  265.8 1.8 add_convert_fusion.refs_0_
  267.7 72.9 %gather_two.1 = (bf16[16,256,1600]{2,1,0:T(8,128)(2,1)}, bf16[16,256,800]{2,1,0:T(8,128)(2,1)}, bf16[16,256,800]{2,1,0:T(8,128)(2,1)}, bf16[16,256,1600]{2,1,0:T(8,128)(2,1)}) custom-call(bf16[512,1600]{1,0:T(8,128)(2,1)} %add_convert_fusion.refs_0_, bf16[1600,800]{1,0:T(8,128)(2,1)} %all-gather.3.cloned.1.call-done.refs_1_.refs_4_, ...), custom_call_target="tpu_custom_call" | custom-call | bytes 1048576 | tf_op jit(solution)/shard_map/gather_two/pallas_call | solution.py:387
  340.6 77.5 %scatter_two.1 = (f32[512,1600]{1,0:T(8,128)}, bf16[16,256,800]{2,1,0:T(8,128)(2,1)}, bf16[800,1600]{1,0:T(8,128)(2,1)}, f32[1,1600]{1,0:T(1,128)}, bf16[4096,1600]{1,0:T(8,128)(2,1)}) custom-call(bf16[4096,1600]{1,0:T(8,128)(2,1)} %bitcast.74, bf16[16,256,1600]{2,1,0:T(8,128)(2,1)} %bitcast.72, ...), custom_call_target="tpu_custom_call", output_to_operand_aliasing={{4}: (0, {})} | custom-call | bytes 1048576 | tf_op jit(solution)/shard_map/scatter_two/pallas_call | solution.py:710
  418.3 2.9 slice.61.t_ref
  421.3 1.2 multiply_reduce_fusion
  422.5 1.1 fusion.10
  423.9 3.0 convert_reduce_fusion.2
  426.9 60.1 %to_heads.1 = (bf16[8,512,256]{2,1,0:T(8,128)(2,1)}, bf16[1600,800]{1,0:T(8,128)(2,1)}, f32[1,800]{1,0:T(1,128)}, bf16[8,96,200]{2,1,0:T(8,128)(2,1)}, bf16[1600,1600]{1,0:T(8,128)(2,1)}) custom-call(bf16[512,1600]{1,0:T(8,128)(2,1)} %get-tuple-element.174.x_ref, bf16[1600,1600]{1,0:T(8,128)(2,1)} %bitcast.83, bf16[512,1600]{1,0:T(8,128)(2,1)} %slice.61.t_ref, ...), custom_call_target="tpu_custom_call" | custom-call | bytes 1048576 | tf_op jit(solution)/shard_map/to_heads/pallas_call | solution.py:1035
  488.1 109.4 %attend_back.1 = (bf16[4096,768]{1,0:T(8,128)(2,1)}, f32[1,768]{1,0:T(1,128)}, bf16[4,400,200]{2,1,0:T(8,128)(2,1)}, bf16[8,104,200]{2,1,0:T(8,128)(2,1)}) custom-call(s32[2,25]{1,0:T(2,128)} %pad_add_fusion.values.refs_0_, bf16[4096,768]{1,0:T(8,128)(2,1)} %get-tuple-element.65.refs_1_, bf16[256,4096]{1,0:T(8,128)(2,1)} %get-tuple-element.66.refs_2_, ...), custom_call_target="tpu_custom_call" | custom-call | bytes 1048576 | tf_op jit(solution)/shard_map/attend_back/pallas_call | solution.py:1508
  598.8 1.5 copy-done.1
  600.3 18.3 %contract.1 = (bf16[1600,768]{1,0:T(8,128)(2,1)S(1)}, bf16[512,1600]{1,0:T(8,128)(2,1)S(1)}) custom-call(bf16[4096,1600]{1,0:T(8,128)(2,1)} %bitcast.71, bf16[4096,768]{1,0:T(8,128)(2,1)} %get-tuple-element.84.b_ref, f32[512,1600]{1,0:T(8,128)S(1)} %get-tuple-element.186.x_ref, bf16[512,1600]{1,0:T(8,128)(2,1)S(1)} %copy-done.1, f32[1,1600]{1,0:T(1,128)S(1)} %reshape.307.s_ref), custom_call_target="tpu_custom_call" | custom-call | bytes 1048576 | tf_op jit(solution)/shard_map/contract/pallas_call | solution.py:1082
  618.7 1.4 copy-done
  620.1 1.2 copy-done.2
  621.3 72.3 %scatter_one.1 = (bf16[512,1600]{1,0:T(8,128)(2,1)}, f32[1,1600]{1,0:T(1,128)}, f32[1,1600]{1,0:T(1,128)}, bf16[4,400,768]{2,1,0:T(8,128)(2,1)}) custom-call(bf16[512,1600]{1,0:T(8,128)(2,1)} %bitcast.75, f32[1,1600]{1,0:T(1,128)} %reshape.308.refs_1_, f32[512,1600]{1,0:T(8,128)} %get-tuple-element.175.refs_2_, bf16[16,256,768]{2,1,0:T(8,128)(2,1)} %bitcast.76, ...), custom_call_target="tpu_custom_call" | custom-call | bytes 1048576 | tf_op jit(solution)/shard_map/scatter_one/pallas_call | solution.py:710
  693.6 1.2 slice.65
  697.9 1.1 add_bitcast_fusion.1
  699.1 1.2 copy.101
  700.3 2.5 reduce_sum.165
  702.8 1.2 copy.100
  703.9 36.5 %give_back.1 = (f32[40,128]{1,0:T(8,128)}, bf16[600,400]{1,0:T(8,128)(2,1)}, bf16[8,96,200]{2,1,0:T(8,128)(2,1)}, bf16[8,104,200]{2,1,0:T(8,128)(2,1)}, bf16[4,4...) custom-call(f32[4,40,128]{2,1,0:T(8,128)} %bitcast.96, bf16[768,400]{1,0:T(8,128)(2,1)} %bitcast.87, ...), custom_call_target="tpu_custom_call" | custom-call | bytes 1048576 | tf_op jit(solution)/shard_map/give_back/pallas_call | solution.py:1151
  740.5 1.4 slice.81
  741.8 1.4 slice.85
  743.2 1.4 fusion.11
  744.7 2.3 copy.103
  746.9 2.5 copy.104
  750.7 1.6 copy.106
  752.4 1.3 copy.105
  753.9 1.1 copy.102
  754.9 2.2 reshape.309
  (141 shorter events, 18.0 us)
Async XLA Ops:
  7.2 12.5 %copy-start.14 = (bf16[1600,200]{0,1:T(8,128)(2,1)S(1)}, bf16[1600,200]{0,1:T(8,128)(2,1)}, u32[]{:S(2)}) copy-start(bf16[1600,200]{0,1:T(8,128)(2,1)} %param.31) | copy-start | bytes 1920004
  7.2 260.5 %all-gather.3.cloned.1.call-start = ((), (), s32[]{:S(2)}) async-start(), calls=%async_computation.2 | async-start | bytes 3584000 | tf_op jit(solution)/shard_map/all_gather | solution.py:1653
  53.6 3.3 copy-start.10
  53.6 4.4 copy-start.18
  53.6 4.7 copy-start.13
  56.8 210.9 %all-gather.5.cloned.1.call-start = ((), (), s32[]{:S(2)}) async-start(), calls=%async_computation.3 | async-start | bytes 3328000 | tf_op jit(solution)/shard_map/all_gather | solution.py:1657
  61.3 3.7 copy-start.4
  63.1 92.0 %copy-start.9 = (bf16[8,200,200]{2,1,0:T(8,128)(2,1)S(1)}, bf16[8,200,200]{2,1,0:T(8,128)(2,1)}, u32[]{:S(2)}) copy-start(bf16[8,200,200]{2,1,0:T(8,128)(2,1)} %get-tuple-element.71) | copy-start | bytes 1920004
  153.1 4.4 copy-start.20
  153.1 5.6 copy-start.19
  153.1 6.5 copy-start.8
  155.2 7.0 copy-start.23
  155.2 7.0 copy-start.25
  155.2 7.1 copy-start.22
  155.2 7.1 copy-start.26
  155.2 7.1 copy-start.27
  155.2 7.1 copy-start.24
  157.2 441.6 %reduce-scatter.5.cloned.1.call-start = ((), (), s32[]{:S(2)}) async-start(), calls=%async_computation.4 | async-start | bytes 15335424 | tf_op jit(solution)/shard_map/reduce_scatter | solution.py:1703
  418.1 279.8 %reduce-scatter.7.cloned.1.call-start = ((), (), s32[]{:S(2)}) async-start(), calls=%async_computation.5 | async-start | bytes 5990400
  418.3 2.9 copy-start.6
  422.5 1.5 copy-start.5
  488.1 110.3 %copy-start.21 = (f32[1,800]{1,0:T(1,128)S(1)}, f32[1,800]{1,0:T(1,128)}, u32[]{:S(2)}) copy-start(f32[1,800]{1,0:T(1,128)} %get-tuple-element.92) | copy-start | bytes 9604
  598.8 1.5 copy-start.1
  618.7 1.4 copy-start
  620.1 1.2 copy-start.2
  700.3 44.4 %copy-start.3 = (bf16[512,1600]{1,0:T(8,128)(2,1)S(1)}, bf16[512,1600]{1,0:T(8,128)(2,1)}, u32[]{:S(2)}) copy-start(bf16[512,1600]{1,0:T(8,128)(2,1)} %copy-done.2) | copy-start | bytes 4915204
  703.9 43.0 %copy-start.7 = (bf16[512,1600]{1,0:T(8,128)(2,1)S(1)}, bf16[512,1600]{1,0:T(8,128)(2,1)}, u32[]{:S(2)}) copy-start(bf16[512,1600]{1,0:T(8,128)(2,1)} %get-tuple-element.88) | copy-start | bytes 4915204
  746.9 2.5 copy-start.12
  746.9 3.4 copy-start.16
  746.9 3.4 copy-start.17
  750.4 1.9 copy-start.15
  750.7 3.1 copy-start.11
Sparse Core Ops, SparseCore 0:
  56.9 105.2 all-gather.2
  164.4 61.6 all-gather.4
  418.2 122.9 reduce-scatter.4
  544.5 64.6 reduce-scatter.6

commit v6 on v5

--- a/solution.py
+++ b/solution.py
@@ -964,7 +964,7 @@
 
 
 def to_heads_kernel(
-    n, nf, wide, x_ref, w_ref, t_ref, a_ref, b_ref, z_ref, o_ref, g_ref, m_ref, z_out, t_out, made, *extra
+    n, nf, wide, carried, x_ref, w_ref, t_ref, a_ref, b_ref, z_ref, o_ref, g_ref, m_ref, z_out, t_out, handed, made, *extra
 ):
     me = lax.axis_index("seq")
     send, recv, local = extra[:3]
@@ -1027,7 +1027,7 @@
         copy(r).wait_send()
 
 
-def to_heads(x, w, t, n, nf, wide, ident, a, b, z, count):
+def to_heads(x, w, t, n, nf, wide, ident, a, b, z, count, carry):
     rows, cols = x.shape
     vmem = pl.BlockSpec(memory_space=pltpu.VMEM)
     hbm = pl.BlockSpec(memory_space=pl.ANY)
@@ -1039,9 +1039,11 @@
         + [
             jax.ShapeDtypeStruct((n, count, z.shape[2] // n), z.dtype),
             jax.ShapeDtypeStruct((cols, t.shape[1]), x.dtype),
+            jax.ShapeDtypeStruct(carry.shape, carry.dtype),
         ],
-        in_specs=[vmem, vmem, vmem] + s_in_specs + [hbm],
-        out_specs=[hbm] + s_out_specs + [vmem, vmem],
+        in_specs=[hbm, vmem, vmem, vmem] + s_in_specs + [hbm],
+        out_specs=[hbm] + s_out_specs + [vmem, vmem, hbm],
+        input_output_aliases={0: 5},
         scratch_shapes=[pltpu.VMEM((n, rows, wide), x.dtype)]
         + Blocks.scratch(n)
         + s_scratch
@@ -1051,11 +1053,26 @@
         ),
         cost_estimate=SMALL,
         name="to_heads",
-    )(x, w, t, *s_ins, z)
-
-
-def contract_kernel(a_ref, b_ref, x_ref, y_ref, s_ref, o_ref, sum_ref, acc):
+    )(carry, x, w, t, *s_ins, z)
+
+
+def contract_kernel(
+    n, nf, a_ref, b_ref, x_ref, y_ref, s_ref, p_ref, q_ref, c_ref, o_ref, sum_ref, p_out, q_out, c_out, acc, *sems
+):
     i = pl.program_id(0)
+    parts = [
+        Blocks("seq", n, False, p_ref, p_out, *sems[:3]),
+        Blocks("seq", n, False, q_ref, q_out, *sems[3:6]),
+        Units(n, nf, True, c_ref, c_out, *sems[6:]),
+    ]
+
+    @pl.when(i == 0)
+    def _():
+        me = lax.axis_index("seq")
+        greet([{"seq": place(me, r, n)} for r in range(1, n)])
+        for part in parts:
+            part.start()
+
     sum_ref[...] = (x_ref[...] + y_ref[...].astype(jnp.float32) + s_ref[...]).astype(sum_ref.dtype)
     part = lax.dot_general(
         a_ref[...], b_ref[...], (((0,), (0,)), ((), ())), preferred_element_type=jnp.float32
@@ -1072,30 +1089,45 @@
     @pl.when(i == pl.num_programs(0) - 1)
     def _():
         o_ref[...] = acc[...].astype(o_ref.dtype)
-
-
-def contract(a, b, x, y, s, tile):
+        for part in parts:
+            part.finish()
+
+
+def contract(a, b, x, y, s, p, q, c, n, nf, tile, ident):
     steps = a.shape[0] // tile
     shape = (a.shape[1], b.shape[1])
     still = lambda s: pl.BlockSpec(s, lambda i: (0,) * len(s), pipeline_mode=pl.Buffered(1))
     part = lambda v: pl.BlockSpec((v.shape[0] // steps, v.shape[1]), lambda i: (i, 0))
+    hbm = pl.BlockSpec(memory_space=pl.ANY)
     return pl.pallas_call(
-        contract_kernel,
-        out_shape=[jax.ShapeDtypeStruct(shape, a.dtype), jax.ShapeDtypeStruct(x.shape, a.dtype)],
+        functools.partial(contract_kernel, n, nf),
+        out_shape=[
+            jax.ShapeDtypeStruct(shape, a.dtype),
+            jax.ShapeDtypeStruct(x.shape, a.dtype),
+            blocks_shape(p, n, False),
+            blocks_shape(q, n, False),
+            blocks_shape(c, nf, False),
+        ],
         grid=(steps,),
-        in_specs=[part(a), part(b), part(x), part(y), still(s.shape)],
-        out_specs=[still(shape), part(x)],
-        scratch_shapes=[pltpu.VMEM(shape, jnp.float32)],
+        in_specs=[part(a), part(b), part(x), part(y), still(s.shape), hbm, hbm, hbm],
+        out_specs=[still(shape), part(x), hbm, hbm, hbm],
+        scratch_shapes=[pltpu.VMEM(shape, jnp.float32)]
+        + Blocks.scratch(n)
+        + Blocks.scratch(n)
+        + Units.scratch(nf),
         compiler_params=pltpu.CompilerParams(
-            dimension_semantics=("arbitrary",), vmem_limit_bytes=40 << 20
+            dimension_semantics=("arbitrary",),
+            vmem_limit_bytes=40 << 20,
+            collective_id=ident,
+            has_side_effects=True,
         ),
         cost_estimate=SMALL,
         name="contract",
-    )(a, b, x, y, s)
+    )(a, b, x, y, s, p, q, c)
 
 
 def give_back_kernel(
-    n, nf, rows, v_ref, w_ref, p_ref, q_ref, c_ref, o_ref, v_out, w_out, p_out, q_out, c_out, o_out, planes, sums, *sems
+    n, nf, rows, v_ref, w_ref, o_ref, v_out, w_out, o_out, planes, sums, *sems
 ):
     s = lax.axis_index("seq")
     f = lax.axis_index("fsdp")
@@ -1105,9 +1137,6 @@
     parts = []
     if rows is not None:
         parts.append(rows.bind(w_ref, w_out, *take(3)))
-    parts.append(Units(n, nf, True, c_ref, c_out, *take(3)))
-    parts.append(Blocks("seq", n, False, p_ref, p_out, *take(3)))
-    parts.append(Blocks("seq", n, False, q_ref, q_out, *take(3)))
     parts.append(Blocks("fsdp", nf, False, o_ref, o_out, *take(3)))
     others = [{"fsdp": lax.rem(f + d, nf)} for d in range(1, nf)]
     peers = [{"seq": place(s, r, n)} for r in range(1, n)]
@@ -1117,7 +1146,7 @@
         c = remote(v_ref.at[lax.rem(f + d, nf)], planes.at[d - 1], send_z.at[d - 1], recv_z.at[d - 1], others[d - 1])
         c.start()
         copies.append(c)
-    for p in parts[:1]:
+    for p in parts:
         p.start()
     total = v_ref[f]
     for d, c in enumerate(copies):
@@ -1129,8 +1158,6 @@
         c = remote(sums.at[0], sums.at[r], send_s.at[r - 1], recv_s.at[r - 1], peers[r - 1])
         c.start()
         spread.append(c)
-    for p in parts[1:]:
-        p.start()
     for r, c in enumerate(spread):
         c.wait_recv()
         total = total + sums[r + 1]
@@ -1141,7 +1168,7 @@
         c.wait_send()
 
 
-def give_back(vectors, w, held, p, q, c, o, n, nf, rows, ident):
+def give_back(vectors, w, held, o, n, nf, rows, ident):
     k = vectors.shape[1]
     tiles = -(-k // 1024) * 8
     padded = jnp.pad(vectors, ((0, 0), (0, tiles * 128 - k))).reshape(nf, tiles, 128)
@@ -1153,13 +1180,10 @@
         out_shape=[
             jax.ShapeDtypeStruct((tiles, 128), jnp.float32),
             jax.ShapeDtypeStruct((held, w.shape[1]), w.dtype),
-            blocks_shape(p, n, False),
-            blocks_shape(q, n, False),
-            blocks_shape(c, nf, False),
             blocks_shape(o, nf, False),
         ],
-        in_specs=[vmem, hbm, hbm, hbm, hbm, hbm],
-        out_specs=[vmem, hbm, hbm, hbm, hbm, hbm],
+        in_specs=[vmem, hbm, hbm],
+        out_specs=[vmem, hbm, hbm],
         scratch_shapes=[
             pltpu.VMEM((nf - 1, tiles, 128), jnp.float32),
             pltpu.VMEM((n, tiles, 128), jnp.float32),
@@ -1169,14 +1193,11 @@
             dma((n - 1,)),
         ]
         + (rows.scratch() if rows is not None else [])
-        + Units.scratch(nf)
-        + Blocks.scratch(n)
-        + Blocks.scratch(n)
         + Blocks.scratch(nf),
         compiler_params=pltpu.CompilerParams(collective_id=ident, has_side_effects=True),
         cost_estimate=SMALL,
         name="give_back",
-    )(padded, w, p, q, c, o)
+    )(padded, w, o)
     return (out[0].reshape(-1)[:k],) + tuple(out[1:])
 
 
@@ -1424,19 +1445,18 @@
                 )
                 aug[2 * j + h] = jnp.where(here, low.astype(jnp.float32), extra).astype(jnp.bfloat16)
 
-    def add(lanes, dks, dvs):
-        @pl.when(jnp.logical_not(leaf))
-        def _():
-            at = rows(key)
+    def add(mask, lanes, dks, dvs):
+        at = rows(key)
+        if mask is None:
             dk[at, lanes] += dks
             dv[at, lanes] += dvs
-
-        @pl.when(leaf)
-        def _():
-            for b in range(branches):
+            return
+        for b in range(branches):
+            chosen = causal | (above == b) if b == 0 else leaf & (above == b)
+            if b > 0:
                 at = pl.ds((trunk + b) * block, block)
-                dk[at, lanes] += jnp.where(above == b, dks, 0.0)
-                dv[at, lanes] += jnp.where(above == b, dvs, 0.0)
+            dk[at, lanes] += jnp.where(chosen, dks, 0.0)
+            dv[at, lanes] += jnp.where(chosen, dvs, 0.0)
 
     def keyed(mask, read):
         got = read(rows(key))
@@ -1466,7 +1486,7 @@
                 dks.append(mm(ds, qh))
                 at = j * 2 * HEAD + h * HEAD
                 dqt[at : at + HEAD] += mm(keyed(mask, lambda i: kt[at : at + HEAD, i]), ds)
-            add(lanes, dks[0] + dks[1], jnp.where(left, dvs[0], dvs[1]))
+            add(mask, lanes, dks[0] + dks[1], jnp.where(left, dvs[0], dvs[1]))
 
     closes = causal | leaf
     shift = jnp.where(causal, 0, block)
@@ -1688,7 +1708,7 @@
         grad = (nt(up, proj[...]) * slope.astype(wider)).astype(low)
         return nt(grad, fc[...]), grad
 
-    grad_normed_two, grad_pre, grad_proj, unused_sums, mixed = seq_scatter(
+    grad_normed_two, grad_pre, grad_proj, unused_sums = seq_scatter(
         n,
         width,
         4,
@@ -1698,16 +1718,14 @@
         (proj_mine, fc_mine),
         ((ff, low),),
         side=(hidden_act, upstream_all),
-        carry=mixed,
     )
-    mixed = lax.psum_scatter(mixed, "seq", scatter_dimension=0, tiled=True)
     grad_proj = grad_proj.reshape(nf, piece, width)
     cut = piece // 16 * 8
     unused_two, norm_two_back = jax.vjp(layer_norm, middle, gain_two, shift_two)
     grad_middle_norm, grad_gain_two, grad_shift_two = norm_two_back(grad_normed_two)
     grad_middle = upstream + grad_middle_norm
     grad_branch = grad_middle.astype(low)
-    grad_attended, grad_fc, hidden_sums, proj_first, grad_out = to_heads(
+    grad_attended, grad_fc, hidden_sums, proj_first, grad_out, mixed = to_heads(
         grad_branch,
         out_turned,
         attended_mine,
@@ -1719,7 +1737,9 @@
         grad_pre,
         grad_proj,
         cut,
+        mixed,
     )
+    mixed = lax.psum_scatter(mixed, "seq", scatter_dimension=0, tiled=True)
     grad_attended = grad_attended.reshape(n * block, wide)
     grad_projected, column_sums, (fc_part, proj_second) = attend_back(
         table,
@@ -1735,8 +1755,19 @@
         ((grad_fc.reshape(nf, rows, ff), 0, nf), (grad_proj, cut, n)),
         9,
     )
-    grad_qkv, output = contract(
-        normed_one, grad_projected, middle, mixed, bias_proj.reshape(1, -1), block
+    grad_qkv, output, proj_first, proj_second, fc_out = contract(
+        normed_one,
+        grad_projected,
+        middle,
+        mixed,
+        bias_proj.reshape(1, -1),
+        proj_first,
+        proj_second,
+        fc_part,
+        n,
+        nf,
+        block,
+        10,
     )
     output = output[None]
     input_grad, grad_gain_one, grad_shift_one, qkv_parts = seq_scatter(
@@ -1775,13 +1806,10 @@
         grad_fc_bias,
         jnp.sum(upstream, 0),
     ]
-    summed, qkv_out, proj_first, proj_second, fc_out, out_out = give_back(
+    summed, qkv_out, out_out = give_back(
         jnp.concatenate([p.reshape(nf, -1) for p in parts], 1),
         qkv_part,
         qkv_cols,
-        proj_first,
-        proj_second,
-        fc_part,
         out_part,
         n,
         nf,

time: 772 us -> 773 us (level)
  Pallas kernels: 662 us -> 650 us
    pallas_call x2, Pallas kernels: 150 us -> 169 us  [seq_scatter(): pl.pallas_call(functools.partial(scatter_kernel, n, h, body, len(ins), le...]
    pallas_call x1, Pallas kernels: 36.5 us -> 20.4 us  [give_back(): pl.pallas_call(functools.partial(give_back_kernel, n, nf, rows), out_shap...]
    pallas_call x1, Pallas kernels: 109 us -> 98.8 us  [attend_back(): pl.pallas_call(functools.partial(attend_back_kernel, width, block, rows /...]
    pallas_call x1, Pallas kernels: 60.1 us -> 50.9 us  [to_heads(): pl.pallas_call(functools.partial(to_heads_kernel, n, nf, wide), out_shape...]
    unnamed x68 -> x80, local copies, waits for them, and re-layouts: 22.1 us -> 28.8 us
  transfers between devices with their start and end apart: 4 -> 4, of which waited for: 0 -> 0; matrix products, arithmetic and copies ran while one was open for 5% -> 5% of each run, Pallas kernels for 58% -> 52%
where the time goes in v6:
time: 773 us; the launch traced here: 761 us
  Pallas kernels  650 us (84%)
  local copies, waits for them, and re-layouts  64.9 us (8%)
  other arithmetic  21.7 us (3%)
  between operations  16.2 us (2%)
    pallas_call x2, Pallas kernels, seq_scatter(): pl.pallas_call(functools.partial(scatter_kernel, n, h, body, len(ins), le...  169 us
    pallas_call x2, Pallas kernels, seq_gather(): pl.pallas_call(functools.partial(gather_kernel, n, h, body, len(consts),...  161 us
    pallas_call x1, Pallas kernels, attend_back(): pl.pallas_call(functools.partial(attend_back_kernel, width, block, rows /...  98.8 us
    pallas_call x1, Pallas kernels, attend(): pl.pallas_call(functools.partial(attend_kernel, width, block, trunk, n),...  69.9 us
    pallas_call x1, Pallas kernels, to_heads(): pl.pallas_call(functools.partial(to_heads_kernel, n, nf, wide), out_shape...  50.9 us
    pallas_call x1, Pallas kernels, exchange(): pl.pallas_call(functools.partial(exchange_kernel, n, nf, rows, count), ou...  32.1 us
    unnamed x80, local copies, waits for them, and re-layouts  28.8 us
    pallas_call x1, Pallas kernels, to_tokens(): pl.pallas_call(functools.partial(to_tokens_kernel, n, wide), out_shape=ja...  25.3 us
  transfers between devices with their start and end apart: 4, of which 0 were waited for; matrix products, arithmetic and copies ran while one was open for 5% of the time, Pallas kernels for 52%

profile of v6, /device:TPU:3, one launch (start us, length us, event | category | flops | bytes accessed | tf_op | source)
XLA Modules:
  0.0 760.8 jit_solution(9187308083514204321)
XLA Ops:
  11.4 1.3 reshape.273.refs_5_
  12.6 1.3 reshape.274.refs_6_
  13.9 2.1 copy.89
  16.0 2.7 reshape.272
  19.7 1.2 copy.90
  21.5 32.1 %exchange.1 = (bf16[768,400]{1,0:T(8,128)(2,1)}, bf16[8,200,200]{2,1,0:T(8,128)(2,1)}, bf16[4,400,200]{2,1,0:T(8,128)(2,1)}, bf16[4,400,200]{2,1,0:T(8,128)(2,1)...) custom-call(bf16[600,400]{1,0:T(8,128)(2,1)} %bitcast.90, ...), custom_call_target="tpu_custom_call" | custom-call | bytes 1048576 | tf_op jit(solution)/shard_map/exchange/pallas_call | solution.py:905
  53.6 1.7 copy.96
  55.3 1.5 reshape.281
  56.9 1.1 copy.108
  58.6 2.7 copy.88
  63.1 1.9 fusion.5.refs_0_
  65.0 88.0 %gather_one.1 = (bf16[16,256,1600]{2,1,0:T(8,128)(2,1)}, bf16[8,200,1600]{2,1,0:T(8,128)(2,1)}, bf16[4,400,768]{2,1,0:T(8,128)(2,1)}) custom-call(bf16[512,1600]{1,0:T(8,128)(2,1)} %fusion.5.refs_0_, bf16[200,1600]{1,0:T(8,128)(2,1)} %bitcast.89, bf16[400,768]{1,0:T(8,128)(2,1)} %select_bitcast_fusion.refs_2_), custom_call_target="tpu_custom_call" | custom-call | bytes 1048576 | tf_op jit(solution)/shard_map/gather_one/pallas_call | solution.py:387
  153.1 1.3 slice.76
  155.4 1.8 add.119
  159.6 2.4 copy.94
  162.8 69.9 %attend.1 = (bf16[4096,768]{1,0:T(8,128)(2,1)}, bf16[4096,256]{1,0:T(8,128)(2,1)}, f32[4096,256]{1,0:T(8,128)}, f32[4096,256]{1,0:T(8,128)}, bf16[256,4096]{1,0:T(8,128)(2,1)}, /*index=5*/bf16[8,512,1600]{2,1,0:T(8,128)(2,1)}) custom-call(s32[2,25]{1,0:T(2,128)} %pad_add_fusion.values.refs_0_, bf16[8,512,1600]{2,1,0:T(8,128)(2,1)} %bitcast.70, ...), custom_call_target="tpu_custom_call" | custom-call | bytes 1048576 | tf_op jit(solution)/shard_map/attend/pallas_call | solution.py:1367
  232.7 25.3 %to_tokens.1 = bf16[512,2048]{1,0:T(8,128)(2,1)} custom-call(bf16[8,512,256]{2,1,0:T(8,128)(2,1)} %bitcast.92), custom_call_target="tpu_custom_call" | custom-call | bytes 1048576 | tf_op jit(solution)/shard_map/to_tokens/pallas_call | solution.py:954
  258.0 2.9 slice.61.t_ref
  261.0 6.7 fusion.12
  268.1 1.8 add_convert_fusion.refs_0_
  270.0 72.9 %gather_two.1 = (bf16[16,256,1600]{2,1,0:T(8,128)(2,1)}, bf16[16,256,800]{2,1,0:T(8,128)(2,1)}, bf16[16,256,800]{2,1,0:T(8,128)(2,1)}, bf16[16,256,1600]{2,1,0:T(8,128)(2,1)}) custom-call(bf16[512,1600]{1,0:T(8,128)(2,1)} %add_convert_fusion.refs_0_, bf16[1600,800]{1,0:T(8,128)(2,1)} %all-gather.3.cloned.1.call-done.refs_1_.refs_3_, ...), custom_call_target="tpu_custom_call" | custom-call | bytes 1048576 | tf_op jit(solution)/shard_map/gather_two/pallas_call | solution.py:387
  342.9 77.6 %scatter_two.1 = (f32[512,1600]{1,0:T(8,128)}, bf16[16,256,800]{2,1,0:T(8,128)(2,1)}, bf16[800,1600]{1,0:T(8,128)(2,1)}, f32[1,1600]{1,0:T(1,128)}) custom-call(bf16[16,256,1600]{2,1,0:T(8,128)(2,1)} %bitcast.73, bf16[16,256,800]{2,1,0:T(8,128)(2,1)} %get-tuple-element.74.refs_1_, bf16[800,1600]{1,0:T(8,128)(2,1)} %all-gather.5.cloned.1.call-done.refs_3_.refs_2_, ...), custom_call_target="tpu_custom_call" | custom-call | bytes 1048576 | tf_op jit(solution)/shard_map/scatter_two/pallas_call | solution.py:710
  420.4 3.2 multiply_reduce_fusion
  423.7 1.1 fusion.10
  425.1 3.0 convert_reduce_fusion.2
  428.1 50.9 %to_heads.1 = (bf16[8,512,256]{2,1,0:T(8,128)(2,1)}, bf16[1600,800]{1,0:T(8,128)(2,1)}, f32[1,800]{1,0:T(1,128)}, bf16[8,96,200]{2,1,0:T(8,128)(2,1)}, bf16[1600...) custom-call(bf16[4096,1600]{1,0:T(8,128)(2,1)} %bitcast.72, ...), custom_call_target="tpu_custom_call", output_to_operand_aliasing={{5}: (0, {})} | custom-call | bytes 1048576 | tf_op jit(solution)/shard_map/to_heads/pallas_call | solution.py:1035
  480.6 98.8 %attend_back.1 = (bf16[4096,768]{1,0:T(8,128)(2,1)}, f32[1,768]{1,0:T(1,128)}, bf16[4,400,200]{2,1,0:T(8,128)(2,1)}, bf16[8,104,200]{2,1,0:T(8,128)(2,1)}) custom-call(s32[2,25]{1,0:T(2,128)} %pad_add_fusion.values.refs_0_, bf16[4096,768]{1,0:T(8,128)(2,1)} %get-tuple-element.65.refs_1_, bf16[256,4096]{1,0:T(8,128)(2,1)} %get-tuple-element.66.refs_2_, ...), custom_call_target="tpu_custom_call" | custom-call | bytes 1048576 | tf_op jit(solution)/shard_map/attend_back/pallas_call | solution.py:1528
  580.7 1.4 copy-done.3
  582.2 1.1 copy-done.6
  585.3 23.5 %contract.1 = (bf16[1600,768]{1,0:T(8,128)(2,1)S(1)}, bf16[512,1600]{1,0:T(8,128)(2,1)S(1)}, bf16[8,96,200]{2,1,0:T(8,128)(2,1)S(1)}, bf16[8,104,200]{2,1,0:T(8,128)(2,1)S(1)}, bf16[4,400,200]{2,1,0:T(8,128)(2,1)S(1)}) custom-call(bf16[4096,1600]{1,0:T(8,128)(2,1)} %bitcast.71, bf16[4096,768]{1,0:T(8,128)(2,1)} %get-tuple-element.84.b_ref, ...), custom_call_target="tpu_custom_call" | custom-call | bytes 1048576 | tf_op jit(solution)/shard_map/contract/pallas_call | solution.py:1102
  608.8 1.4 copy-done
  610.3 1.2 copy-done.1
  613.9 91.0 %scatter_one.1 = (bf16[512,1600]{1,0:T(8,128)(2,1)}, f32[1,1600]{1,0:T(1,128)}, f32[1,1600]{1,0:T(1,128)}, bf16[4,400,768]{2,1,0:T(8,128)(2,1)}) custom-call(bf16[512,1600]{1,0:T(8,128)(2,1)} %bitcast.75, f32[1,1600]{1,0:T(1,128)} %reshape.308.refs_1_, f32[512,1600]{1,0:T(8,128)} %get-tuple-element.175.refs_2_, bf16[16,256,768]{2,1,0:T(8,128)(2,1)} %bitcast.76, ...), custom_call_target="tpu_custom_call" | custom-call | bytes 1048576 | tf_op jit(solution)/shard_map/scatter_one/pallas_call | solution.py:710
  704.9 1.2 slice.65
  709.2 1.1 add_bitcast_fusion.1
  710.3 1.2 copy.101
  711.5 2.5 reduce_sum.165
  714.0 1.2 copy.100
  715.2 20.4 %give_back.1 = (f32[40,128]{1,0:T(8,128)}, bf16[600,400]{1,0:T(8,128)(2,1)}, bf16[4,400,200]{2,1,0:T(8,128)(2,1)}) custom-call(f32[4,40,128]{2,1,0:T(8,128)} %bitcast.96, bf16[768,400]{1,0:T(8,128)(2,1)} %bitcast.87, bf16[4,400,200]{2,1,0:T(8,128)(2,1)} %bitcast.84), custom_call_target="tpu_custom_call" | custom-call | bytes 1048576 | tf_op jit(solution)/shard_map/give_back/pallas_call | solution.py:1178
  735.6 1.4 slice.81
  737.1 1.4 slice.85
  738.4 1.4 fusion.11
  739.9 2.3 copy.103
  742.2 3.9 copy.104
  747.3 1.6 copy.106
  749.0 1.3 copy.105
  750.5 1.1 copy.102
  751.5 2.2 reshape.309
  (153 shorter events, 23.8 us)
Async XLA Ops:
  7.2 12.5 %copy-start.22 = (bf16[1600,200]{0,1:T(8,128)(2,1)S(1)}, bf16[1600,200]{0,1:T(8,128)(2,1)}, u32[]{:S(2)}) copy-start(bf16[1600,200]{0,1:T(8,128)(2,1)} %param.31) | copy-start | bytes 1920004
  7.2 262.8 %all-gather.3.cloned.1.call-start = ((), (), s32[]{:S(2)}) async-start(), calls=%async_computation.2 | async-start | bytes 3584000 | tf_op jit(solution)/shard_map/all_gather | solution.py:1673
  53.6 3.3 copy-start.19
  53.6 4.4 copy-start.24
  53.6 4.7 copy-start.21
  56.8 213.2 %all-gather.5.cloned.1.call-start = ((), (), s32[]{:S(2)}) async-start(), calls=%async_computation.3 | async-start | bytes 3328000 | tf_op jit(solution)/shard_map/all_gather | solution.py:1677
  61.3 3.7 copy-start.13
  63.1 92.0 %copy-start.18 = (bf16[8,200,200]{2,1,0:T(8,128)(2,1)S(1)}, bf16[8,200,200]{2,1,0:T(8,128)(2,1)}, u32[]{:S(2)}) copy-start(bf16[8,200,200]{2,1,0:T(8,128)(2,1)} %get-tuple-element.71) | copy-start | bytes 1920004
  153.1 4.4 copy-start.26
  153.1 5.6 copy-start.25
  153.1 6.5 copy-start.17
  155.2 6.8 copy-start.29
  155.2 6.8 copy-start.31
  155.2 6.9 copy-start.28
  155.2 6.9 copy-start.32
  155.2 6.9 copy-start.33
  155.2 7.0 copy-start.30
  157.2 423.5 %reduce-scatter.5.cloned.1.call-start = ((), (), s32[]{:S(2)}) async-start(), calls=%async_computation.4 | async-start | bytes 15335424 | tf_op jit(solution)/shard_map/reduce_scatter | solution.py:1742
  258.0 2.9 copy-start.14
  420.4 3.2 copy-start.16
  423.7 1.5 copy-start.15
  479.0 230.2 %reduce-scatter.7.cloned.1.call-start = ((), (), s32[]{:S(2)}) async-start(), calls=%async_computation.5 | async-start | bytes 5990400
  480.6 99.7 %copy-start.27 = (f32[1,800]{1,0:T(1,128)S(1)}, f32[1,800]{1,0:T(1,128)}, u32[]{:S(2)}) copy-start(f32[1,800]{1,0:T(1,128)} %get-tuple-element.95) | copy-start | bytes 9604
  580.7 1.5 copy-start.3
  582.2 1.1 copy-start.6
  583.3 1.0 copy-start.9
  584.3 1.0 copy-start.12
  608.8 1.4 copy-start
  610.3 1.2 copy-start.1
  611.5 0.9 copy-start.4
  612.4 0.8 copy-start.7
  613.1 0.8 copy-start.10
  711.5 28.4 %copy-start.2 = (bf16[512,1600]{1,0:T(8,128)(2,1)S(1)}, bf16[512,1600]{1,0:T(8,128)(2,1)}, u32[]{:S(2)}) copy-start(bf16[512,1600]{1,0:T(8,128)(2,1)} %copy-done.1) | copy-start | bytes 4915204
  735.6 10.4 %copy-start.20 = (bf16[4,400,200]{2,1,0:T(8,128)(2,1)S(1)}, bf16[4,400,200]{2,1,0:T(8,128)(2,1)}, u32[]{:S(2)}) copy-start(bf16[4,400,200]{2,1,0:T(8,128)(2,1)} %get-tuple-element.100) | copy-start | bytes 1920004
  739.9 7.0 copy-start.8
  739.9 7.0 copy-start.11
  746.9 1.9 copy-start.23
  747.3 3.1 copy-start.5
Sparse Core Ops, SparseCore 0:
  56.9 105.2 all-gather.2
  164.4 61.6 all-gather.4
  479.1 101.4 reduce-scatter.4
  583.8 74.7 reduce-scatter.6

commit v7 on v6

--- a/solution.py
+++ b/solution.py
@@ -964,7 +964,7 @@
 
 
 def to_heads_kernel(
-    n, nf, wide, carried, x_ref, w_ref, t_ref, a_ref, b_ref, z_ref, o_ref, g_ref, m_ref, z_out, t_out, handed, made, *extra
+    n, nf, wide, x_ref, w_ref, t_ref, a_ref, b_ref, z_ref, o_ref, g_ref, m_ref, z_out, t_out, made, *extra
 ):
     me = lax.axis_index("seq")
     send, recv, local = extra[:3]
@@ -1027,7 +1027,7 @@
         copy(r).wait_send()
 
 
-def to_heads(x, w, t, n, nf, wide, ident, a, b, z, count, carry):
+def to_heads(x, w, t, n, nf, wide, ident, a, b, z, count):
     rows, cols = x.shape
     vmem = pl.BlockSpec(memory_space=pltpu.VMEM)
     hbm = pl.BlockSpec(memory_space=pl.ANY)
@@ -1039,11 +1039,9 @@
         + [
             jax.ShapeDtypeStruct((n, count, z.shape[2] // n), z.dtype),
             jax.ShapeDtypeStruct((cols, t.shape[1]), x.dtype),
-            jax.ShapeDtypeStruct(carry.shape, carry.dtype),
         ],
-        in_specs=[hbm, vmem, vmem, vmem] + s_in_specs + [hbm],
-        out_specs=[hbm] + s_out_specs + [vmem, vmem, hbm],
-        input_output_aliases={0: 5},
+        in_specs=[vmem, vmem, vmem] + s_in_specs + [hbm],
+        out_specs=[hbm] + s_out_specs + [vmem, vmem],
         scratch_shapes=[pltpu.VMEM((n, rows, wide), x.dtype)]
         + Blocks.scratch(n)
         + s_scratch
@@ -1053,7 +1051,7 @@
         ),
         cost_estimate=SMALL,
         name="to_heads",
-    )(carry, x, w, t, *s_ins, z)
+    )(x, w, t, *s_ins, z)
 
 
 def contract_kernel(
@@ -1708,7 +1706,7 @@
         grad = (nt(up, proj[...]) * slope.astype(wider)).astype(low)
         return nt(grad, fc[...]), grad
 
-    grad_normed_two, grad_pre, grad_proj, unused_sums = seq_scatter(
+    grad_normed_two, grad_pre, grad_proj, unused_sums, mixed = seq_scatter(
         n,
         width,
         4,
@@ -1718,14 +1716,16 @@
         (proj_mine, fc_mine),
         ((ff, low),),
         side=(hidden_act, upstream_all),
+        carry=mixed,
     )
+    mixed = lax.psum_scatter(mixed, "seq", scatter_dimension=0, tiled=True)
     grad_proj = grad_proj.reshape(nf, piece, width)
     cut = piece // 16 * 8
     unused_two, norm_two_back = jax.vjp(layer_norm, middle, gain_two, shift_two)
     grad_middle_norm, grad_gain_two, grad_shift_two = norm_two_back(grad_normed_two)
     grad_middle = upstream + grad_middle_norm
     grad_branch = grad_middle.astype(low)
-    grad_attended, grad_fc, hidden_sums, proj_first, grad_out, mixed = to_heads(
+    grad_attended, grad_fc, hidden_sums, proj_first, grad_out = to_heads(
         grad_branch,
         out_turned,
         attended_mine,
@@ -1737,9 +1737,7 @@
         grad_pre,
         grad_proj,
         cut,
-        mixed,
     )
-    mixed = lax.psum_scatter(mixed, "seq", scatter_dimension=0, tiled=True)
     grad_attended = grad_attended.reshape(n * block, wide)
     grad_projected, column_sums, (fc_part, proj_second) = attend_back(
         table,

time: 773 us -> 772 us (level)
    pallas_call x2, Pallas kernels: 169 us -> 152 us  [seq_scatter(): pl.pallas_call(functools.partial(scatter_kernel, n, h, body, len(ins), le...]
    pallas_call x1, Pallas kernels: 50.9 us -> 60.1 us  [to_heads(): pl.pallas_call(functools.partial(to_heads_kernel, n, nf, wide), out_shape...]
    unnamed x80 -> x78, local copies, waits for them, and re-layouts: 28.8 us -> 29.1 us
  transfers between devices with their start and end apart: 4 -> 4, of which waited for: 0 -> 0; matrix products, arithmetic and copies ran while one was open for 5% -> 5% of each run, Pallas kernels for 52% -> 59%
where the time goes in v7:
time: 772 us; the launch traced here: 759 us
  Pallas kernels  650 us (84%)
  local copies, waits for them, and re-layouts  65.2 us (8%)
  other arithmetic  19.7 us (3%)
  between operations  16.2 us (2%)
    pallas_call x2, Pallas kernels, seq_gather(): pl.pallas_call(functools.partial(gather_kernel, n, h, body, len(consts),...  161 us
    pallas_call x2, Pallas kernels, seq_scatter(): pl.pallas_call(functools.partial(scatter_kernel, n, h, body, len(ins), le...  152 us
    pallas_call x1, Pallas kernels, attend_back(): pl.pallas_call(functools.partial(attend_back_kernel, width, block, rows /...  101 us
    pallas_call x1, Pallas kernels, attend(): pl.pallas_call(functools.partial(attend_kernel, width, block, trunk, n),...  69.9 us
    pallas_call x1, Pallas kernels, to_heads(): pl.pallas_call(functools.partial(to_heads_kernel, n, nf, wide), out_shape...  60.1 us
    pallas_call x1, Pallas kernels, exchange(): pl.pallas_call(functools.partial(exchange_kernel, n, nf, rows, count), ou...  32.1 us
    pallas_call x1, Pallas kernels, contract(): pl.pallas_call(functools.partial(contract_kernel, n, nf), out_shape=[jax....  29.1 us
    unnamed x78, local copies, waits for them, and re-layouts  29.1 us
  transfers between devices with their start and end apart: 4, of which 0 were waited for; matrix products, arithmetic and copies ran while one was open for 5% of the time, Pallas kernels for 59%

profile of v7, /device:TPU:3, one launch (start us, length us, event | category | flops | bytes accessed | tf_op | source)
XLA Modules:
  0.0 759.1 jit_solution(15516672529187687623)
XLA Ops:
  11.4 1.3 reshape.273.refs_5_
  12.6 1.3 reshape.274.refs_6_
  13.9 2.1 copy.89
  16.0 2.7 reshape.272
  19.7 1.2 copy.90
  21.5 32.1 %exchange.1 = (bf16[768,400]{1,0:T(8,128)(2,1)}, bf16[8,200,200]{2,1,0:T(8,128)(2,1)}, bf16[4,400,200]{2,1,0:T(8,128)(2,1)}, bf16[4,400,200]{2,1,0:T(8,128)(2,1)...) custom-call(bf16[600,400]{1,0:T(8,128)(2,1)} %bitcast.90, ...), custom_call_target="tpu_custom_call" | custom-call | bytes 1048576 | tf_op jit(solution)/shard_map/exchange/pallas_call | solution.py:905
  53.6 1.7 copy.96
  55.3 1.5 reshape.281
  56.9 1.1 copy.108
  58.6 2.7 copy.88
  63.1 1.9 fusion.5.refs_0_
  65.0 88.0 %gather_one.1 = (bf16[16,256,1600]{2,1,0:T(8,128)(2,1)}, bf16[8,200,1600]{2,1,0:T(8,128)(2,1)}, bf16[4,400,768]{2,1,0:T(8,128)(2,1)}) custom-call(bf16[512,1600]{1,0:T(8,128)(2,1)} %fusion.5.refs_0_, bf16[200,1600]{1,0:T(8,128)(2,1)} %bitcast.89, bf16[400,768]{1,0:T(8,128)(2,1)} %select_bitcast_fusion.refs_2_), custom_call_target="tpu_custom_call" | custom-call | bytes 1048576 | tf_op jit(solution)/shard_map/gather_one/pallas_call | solution.py:387
  153.1 1.3 slice.76
  155.4 1.8 add.119
  159.6 2.6 copy.94
  163.0 69.9 %attend.1 = (bf16[4096,768]{1,0:T(8,128)(2,1)}, bf16[4096,256]{1,0:T(8,128)(2,1)}, f32[4096,256]{1,0:T(8,128)}, f32[4096,256]{1,0:T(8,128)}, bf16[256,4096]{1,0:T(8,128)(2,1)}, /*index=5*/bf16[8,512,1600]{2,1,0:T(8,128)(2,1)}) custom-call(s32[2,25]{1,0:T(2,128)} %pad_add_fusion.values.refs_0_, bf16[8,512,1600]{2,1,0:T(8,128)(2,1)} %bitcast.70, ...), custom_call_target="tpu_custom_call" | custom-call | bytes 1048576 | tf_op jit(solution)/shard_map/attend/pallas_call | solution.py:1365
  232.9 25.3 %to_tokens.1 = bf16[512,2048]{1,0:T(8,128)(2,1)} custom-call(bf16[8,512,256]{2,1,0:T(8,128)(2,1)} %bitcast.92), custom_call_target="tpu_custom_call" | custom-call | bytes 1048576 | tf_op jit(solution)/shard_map/to_tokens/pallas_call | solution.py:954
  258.2 7.1 fusion.12
  265.8 1.8 add_convert_fusion.refs_0_
  267.7 72.9 %gather_two.1 = (bf16[16,256,1600]{2,1,0:T(8,128)(2,1)}, bf16[16,256,800]{2,1,0:T(8,128)(2,1)}, bf16[16,256,800]{2,1,0:T(8,128)(2,1)}, bf16[16,256,1600]{2,1,0:T(8,128)(2,1)}) custom-call(bf16[512,1600]{1,0:T(8,128)(2,1)} %add_convert_fusion.refs_0_, bf16[1600,800]{1,0:T(8,128)(2,1)} %all-gather.3.cloned.1.call-done.refs_1_.refs_4_, ...), custom_call_target="tpu_custom_call" | custom-call | bytes 1048576 | tf_op jit(solution)/shard_map/gather_two/pallas_call | solution.py:387
  340.6 77.5 %scatter_two.1 = (f32[512,1600]{1,0:T(8,128)}, bf16[16,256,800]{2,1,0:T(8,128)(2,1)}, bf16[800,1600]{1,0:T(8,128)(2,1)}, f32[1,1600]{1,0:T(1,128)}, bf16[4096,1600]{1,0:T(8,128)(2,1)}) custom-call(bf16[4096,1600]{1,0:T(8,128)(2,1)} %bitcast.74, bf16[16,256,1600]{2,1,0:T(8,128)(2,1)} %bitcast.72, ...), custom_call_target="tpu_custom_call", output_to_operand_aliasing={{4}: (0, {})} | custom-call | bytes 1048576 | tf_op jit(solution)/shard_map/scatter_two/pallas_call | solution.py:710
  418.3 2.9 slice.61.t_ref
  421.3 1.2 multiply_reduce_fusion
  422.5 1.1 fusion.10
  423.9 3.0 convert_reduce_fusion.2
  426.9 60.1 %to_heads.1 = (bf16[8,512,256]{2,1,0:T(8,128)(2,1)}, bf16[1600,800]{1,0:T(8,128)(2,1)}, f32[1,800]{1,0:T(1,128)}, bf16[8,96,200]{2,1,0:T(8,128)(2,1)}, bf16[1600,1600]{1,0:T(8,128)(2,1)}) custom-call(bf16[512,1600]{1,0:T(8,128)(2,1)} %get-tuple-element.174.x_ref, bf16[1600,1600]{1,0:T(8,128)(2,1)} %bitcast.83, bf16[512,1600]{1,0:T(8,128)(2,1)} %slice.61.t_ref, ...), custom_call_target="tpu_custom_call" | custom-call | bytes 1048576 | tf_op jit(solution)/shard_map/to_heads/pallas_call | solution.py:1035
  488.1 101.5 %attend_back.1 = (bf16[4096,768]{1,0:T(8,128)(2,1)}, f32[1,768]{1,0:T(1,128)}, bf16[4,400,200]{2,1,0:T(8,128)(2,1)}, bf16[8,104,200]{2,1,0:T(8,128)(2,1)}) custom-call(s32[2,25]{1,0:T(2,128)} %pad_add_fusion.values.refs_0_, bf16[4096,768]{1,0:T(8,128)(2,1)} %get-tuple-element.65.refs_1_, bf16[256,4096]{1,0:T(8,128)(2,1)} %get-tuple-element.66.refs_2_, ...), custom_call_target="tpu_custom_call" | custom-call | bytes 1048576 | tf_op jit(solution)/shard_map/attend_back/pallas_call | solution.py:1526
  590.9 1.5 copy-done.3
  592.5 1.1 copy-done.6
  595.6 29.1 %contract.1 = (bf16[1600,768]{1,0:T(8,128)(2,1)S(1)}, bf16[512,1600]{1,0:T(8,128)(2,1)S(1)}, bf16[8,96,200]{2,1,0:T(8,128)(2,1)S(1)}, bf16[8,104,200]{2,1,0:T(8,128)(2,1)S(1)}, bf16[4,400,200]{2,1,0:T(8,128)(2,1)S(1)}) custom-call(bf16[4096,1600]{1,0:T(8,128)(2,1)} %bitcast.71, bf16[4096,768]{1,0:T(8,128)(2,1)} %get-tuple-element.84.b_ref, ...), custom_call_target="tpu_custom_call" | custom-call | bytes 1048576 | tf_op jit(solution)/shard_map/contract/pallas_call | solution.py:1100
  624.8 1.5 copy-done
  626.3 1.2 copy-done.1
  629.9 74.1 %scatter_one.1 = (bf16[512,1600]{1,0:T(8,128)(2,1)}, f32[1,1600]{1,0:T(1,128)}, f32[1,1600]{1,0:T(1,128)}, bf16[4,400,768]{2,1,0:T(8,128)(2,1)}) custom-call(bf16[512,1600]{1,0:T(8,128)(2,1)} %bitcast.75, f32[1,1600]{1,0:T(1,128)} %reshape.308.refs_1_, f32[512,1600]{1,0:T(8,128)} %get-tuple-element.175.refs_2_, bf16[16,256,768]{2,1,0:T(8,128)(2,1)} %bitcast.76, ...), custom_call_target="tpu_custom_call" | custom-call | bytes 1048576 | tf_op jit(solution)/shard_map/scatter_one/pallas_call | solution.py:710
  704.0 1.2 slice.65
  708.2 1.1 add_bitcast_fusion.1
  709.4 1.2 copy.101
  710.6 2.5 reduce_sum.165
  713.1 1.2 copy.100
  714.2 19.7 %give_back.1 = (f32[40,128]{1,0:T(8,128)}, bf16[600,400]{1,0:T(8,128)(2,1)}, bf16[4,400,200]{2,1,0:T(8,128)(2,1)}) custom-call(f32[4,40,128]{2,1,0:T(8,128)} %bitcast.96, bf16[768,400]{1,0:T(8,128)(2,1)} %bitcast.87, bf16[4,400,200]{2,1,0:T(8,128)(2,1)} %bitcast.84), custom_call_target="tpu_custom_call" | custom-call | bytes 1048576 | tf_op jit(solution)/shard_map/give_back/pallas_call | solution.py:1176
  733.9 1.4 slice.81
  735.4 1.4 slice.85
  736.7 1.4 fusion.11
  738.2 2.3 copy.103
  740.5 3.9 copy.104
  745.6 1.6 copy.106
  747.3 1.3 copy.105
  748.8 1.1 copy.102
  749.8 2.2 reshape.309
  (151 shorter events, 23.4 us)
Async XLA Ops:
  7.2 12.5 %copy-start.21 = (bf16[1600,200]{0,1:T(8,128)(2,1)S(1)}, bf16[1600,200]{0,1:T(8,128)(2,1)}, u32[]{:S(2)}) copy-start(bf16[1600,200]{0,1:T(8,128)(2,1)} %param.31) | copy-start | bytes 1920004
  7.2 260.5 %all-gather.3.cloned.1.call-start = ((), (), s32[]{:S(2)}) async-start(), calls=%async_computation.2 | async-start | bytes 3584000 | tf_op jit(solution)/shard_map/all_gather | solution.py:1671
  53.6 3.3 copy-start.18
  53.6 4.4 copy-start.23
  53.6 4.7 copy-start.20
  56.8 210.9 %all-gather.5.cloned.1.call-start = ((), (), s32[]{:S(2)}) async-start(), calls=%async_computation.3 | async-start | bytes 3328000 | tf_op jit(solution)/shard_map/all_gather | solution.py:1675
  61.3 3.7 copy-start.13
  63.1 92.0 %copy-start.17 = (bf16[8,200,200]{2,1,0:T(8,128)(2,1)S(1)}, bf16[8,200,200]{2,1,0:T(8,128)(2,1)}, u32[]{:S(2)}) copy-start(bf16[8,200,200]{2,1,0:T(8,128)(2,1)} %get-tuple-element.71) | copy-start | bytes 1920004
  153.1 4.4 copy-start.25
  153.1 5.6 copy-start.24
  153.1 6.5 copy-start.16
  155.2 7.0 copy-start.28
  155.2 7.0 copy-start.30
  155.2 7.1 copy-start.27
  155.2 7.1 copy-start.31
  155.2 7.1 copy-start.32
  155.2 7.1 copy-start.29
  157.2 433.7 %reduce-scatter.5.cloned.1.call-start = ((), (), s32[]{:S(2)}) async-start(), calls=%async_computation.4 | async-start | bytes 15335424 | tf_op jit(solution)/shard_map/reduce_scatter | solution.py:1721
  418.1 290.1 %reduce-scatter.7.cloned.1.call-start = ((), (), s32[]{:S(2)}) async-start(), calls=%async_computation.5 | async-start | bytes 5990400
  418.3 2.9 copy-start.15
  422.5 1.5 copy-start.14
  488.1 102.4 %copy-start.26 = (f32[1,800]{1,0:T(1,128)S(1)}, f32[1,800]{1,0:T(1,128)}, u32[]{:S(2)}) copy-start(f32[1,800]{1,0:T(1,128)} %get-tuple-element.95) | copy-start | bytes 9604
  590.9 1.5 copy-start.3
  592.5 1.1 copy-start.6
  593.6 1.0 copy-start.9
  594.6 1.0 copy-start.12
  624.8 1.5 copy-start
  626.2 1.2 copy-start.1
  627.5 0.9 copy-start.4
  628.4 0.8 copy-start.7
  629.1 0.8 copy-start.10
  710.6 27.6 %copy-start.2 = (bf16[512,1600]{1,0:T(8,128)(2,1)S(1)}, bf16[512,1600]{1,0:T(8,128)(2,1)}, u32[]{:S(2)}) copy-start(bf16[512,1600]{1,0:T(8,128)(2,1)} %copy-done.1) | copy-start | bytes 4915204
  733.9 10.4 %copy-start.19 = (bf16[4,400,200]{2,1,0:T(8,128)(2,1)S(1)}, bf16[4,400,200]{2,1,0:T(8,128)(2,1)}, u32[]{:S(2)}) copy-start(bf16[4,400,200]{2,1,0:T(8,128)(2,1)} %get-tuple-element.100) | copy-start | bytes 1920004
  738.2 7.0 copy-start.8
  738.2 7.0 copy-start.11
  745.2 1.9 copy-start.22
  745.6 3.1 copy-start.5
Sparse Core Ops, SparseCore 0:
  56.9 105.2 all-gather.2
  164.4 61.6 all-gather.4
  418.2 122.9 reduce-scatter.4
  544.5 78.5 reduce-scatter.6

commit v8 on v7

--- a/solution.py
+++ b/solution.py
@@ -1668,7 +1668,7 @@
     out_turned = out_turned.reshape(width, width)
     qkv_mine = qkv_mine.reshape(width, 3 * wide)
     fc_rows = fc_blocks.transpose(1, 0, 2).reshape(rows, nf * piece)
-    fc_mine = lax.all_gather(fc_rows, "fsdp", axis=0, tiled=True)
+    fc_mine = lax.all_gather(after(fc_rows, normed_one), "fsdp", axis=0, tiled=True)
 
     upstream = cotangent[0].astype(wider)
     proj_rows = proj_blocks.transpose(1, 0, 2).reshape(piece, width)

time: 772 us -> 762 us (0.987)
  Pallas kernels: 650 us -> 636 us
    unnamed x78 -> x72, local copies, waits for them, and re-layouts: 29.1 us -> 29 us
  transfers between devices with their start and end apart: 4 -> 4, of which waited for: 0 -> 1; matrix products, arithmetic and copies ran while one was open for 5% -> 4% of each run, Pallas kernels for 59% -> 46%
where the time goes in v8:
time: 762 us; the launch traced here: 749 us
  Pallas kernels  636 us (83%)
  local copies, waits for them, and re-layouts  66.1 us (9%)
  other arithmetic  21.9 us (3%)
  between operations  16.2 us (2%)
    pallas_call x2, Pallas kernels, seq_gather(): pl.pallas_call(functools.partial(gather_kernel, n, h, body, len(consts),...  161 us
    pallas_call x2, Pallas kernels, seq_scatter(): pl.pallas_call(functools.partial(scatter_kernel, n, h, body, len(ins), le...  153 us
    pallas_call x1, Pallas kernels, attend_back(): pl.pallas_call(functools.partial(attend_back_kernel, width, block, rows /...  95.3 us
    pallas_call x1, Pallas kernels, attend(): pl.pallas_call(functools.partial(attend_kernel, width, block, trunk, n),...  70.1 us
    pallas_call x1, Pallas kernels, to_heads(): pl.pallas_call(functools.partial(to_heads_kernel, n, nf, wide), out_shape...  52.6 us
    pallas_call x1, Pallas kernels, exchange(): pl.pallas_call(functools.partial(exchange_kernel, n, nf, rows, count), ou...  32.1 us
    unnamed x72, local copies, waits for them, and re-layouts  29 us
    pallas_call x1, Pallas kernels, contract(): pl.pallas_call(functools.partial(contract_kernel, n, nf), out_shape=[jax....  27.7 us
  transfers between devices with their start and end apart: 4, of which 1 were waited for; matrix products, arithmetic and copies ran while one was open for 4% of the time, Pallas kernels for 46%

profile of v8, /device:TPU:3, one launch (start us, length us, event | category | flops | bytes accessed | tf_op | source)
XLA Modules:
  0.0 749.2 jit_solution(12416180343835049576)
XLA Ops:
  11.4 1.3 reshape.273.refs_5_
  12.7 1.3 reshape.274.refs_6_
  14.0 2.1 copy.89
  16.1 2.7 reshape.272
  19.7 1.2 copy.90
  21.6 32.1 %exchange.1 = (bf16[768,400]{1,0:T(8,128)(2,1)}, bf16[8,200,200]{2,1,0:T(8,128)(2,1)}, bf16[4,400,200]{2,1,0:T(8,128)(2,1)}, bf16[4,400,200]{2,1,0:T(8,128)(2,1)...) custom-call(bf16[600,400]{1,0:T(8,128)(2,1)} %bitcast.91, ...), custom_call_target="tpu_custom_call" | custom-call | bytes 1048576 | tf_op jit(solution)/shard_map/exchange/pallas_call | solution.py:905
  53.6 2.3 copy.108
  57.2 1.4 copy.93
  58.6 2.7 copy.88
  63.1 1.9 fusion.5.refs_0_
  65.0 88.0 %gather_one.1 = (bf16[16,256,1600]{2,1,0:T(8,128)(2,1)}, bf16[8,200,1600]{2,1,0:T(8,128)(2,1)}, bf16[4,400,768]{2,1,0:T(8,128)(2,1)}) custom-call(bf16[512,1600]{1,0:T(8,128)(2,1)} %fusion.5.refs_0_, bf16[200,1600]{1,0:T(8,128)(2,1)} %bitcast.90, bf16[400,768]{1,0:T(8,128)(2,1)} %select_bitcast_fusion.refs_2_), custom_call_target="tpu_custom_call" | custom-call | bytes 1048576 | tf_op jit(solution)/shard_map/gather_one/pallas_call | solution.py:387
  153.0 1.3 slice.77
  154.9 1.2 add_bitcast_fusion
  156.3 1.8 add.135
  158.7 1.5 add.130
  162.6 2.6 copy.94
  166.0 70.1 %attend.1 = (bf16[4096,768]{1,0:T(8,128)(2,1)}, bf16[4096,256]{1,0:T(8,128)(2,1)}, f32[4096,256]{1,0:T(8,128)}, f32[4096,256]{1,0:T(8,128)}, bf16[256,4096]{1,0:T(8,128)(2,1)}, /*index=5*/bf16[8,512,1600]{2,1,0:T(8,128)(2,1)}) custom-call(s32[2,25]{1,0:T(2,128)} %pad_add_fusion.values.refs_0_, bf16[8,512,1600]{2,1,0:T(8,128)(2,1)} %bitcast.71, ...), custom_call_target="tpu_custom_call" | custom-call | bytes 1048576 | tf_op jit(solution)/shard_map/attend/pallas_call | solution.py:1365
  236.1 25.3 %to_tokens.1 = bf16[512,2048]{1,0:T(8,128)(2,1)} custom-call(bf16[8,512,256]{2,1,0:T(8,128)(2,1)} %bitcast.93), custom_call_target="tpu_custom_call" | custom-call | bytes 1048576 | tf_op jit(solution)/shard_map/to_tokens/pallas_call | solution.py:954
  261.3 7.1 fusion.12
  269.0 1.8 add_convert_fusion.refs_0_
  270.8 1.3 all-gather.3.cloned.1.call-done.refs_1_.refs_4_
  272.0 72.7 %gather_two.1 = (bf16[16,256,1600]{2,1,0:T(8,128)(2,1)}, bf16[16,256,800]{2,1,0:T(8,128)(2,1)}, bf16[16,256,800]{2,1,0:T(8,128)(2,1)}, bf16[16,256,1600]{2,1,0:T(8,128)(2,1)}) custom-call(bf16[512,1600]{1,0:T(8,128)(2,1)} %add_convert_fusion.refs_0_, bf16[1600,800]{1,0:T(8,128)(2,1)} %all-gather.3.cloned.1.call-done.refs_1_.refs_4_, ...), custom_call_target="tpu_custom_call" | custom-call | bytes 1048576 | tf_op jit(solution)/shard_map/gather_two/pallas_call | solution.py:387
  344.8 77.2 %scatter_two.1 = (f32[512,1600]{1,0:T(8,128)}, bf16[16,256,800]{2,1,0:T(8,128)(2,1)}, bf16[800,1600]{1,0:T(8,128)(2,1)}, f32[1,1600]{1,0:T(1,128)}, bf16[4096,1600]{1,0:T(8,128)(2,1)}) custom-call(bf16[4096,1600]{1,0:T(8,128)(2,1)} %bitcast.75, bf16[16,256,1600]{2,1,0:T(8,128)(2,1)} %bitcast.73, ...), custom_call_target="tpu_custom_call", output_to_operand_aliasing={{4}: (0, {})} | custom-call | bytes 1048576 | tf_op jit(solution)/shard_map/scatter_two/pallas_call | solution.py:710
  422.3 2.9 slice.62.t_ref
  425.2 1.2 multiply_reduce_fusion
  427.9 3.0 convert_reduce_fusion.2
  430.9 52.6 %to_heads.1 = (bf16[8,512,256]{2,1,0:T(8,128)(2,1)}, bf16[1600,800]{1,0:T(8,128)(2,1)}, f32[1,800]{1,0:T(1,128)}, bf16[8,96,200]{2,1,0:T(8,128)(2,1)}, bf16[1600,1600]{1,0:T(8,128)(2,1)}) custom-call(bf16[512,1600]{1,0:T(8,128)(2,1)} %get-tuple-element.174.x_ref, bf16[1600,1600]{1,0:T(8,128)(2,1)} %bitcast.84, bf16[512,1600]{1,0:T(8,128)(2,1)} %slice.62.t_ref, ...), custom_call_target="tpu_custom_call" | custom-call | bytes 1048576 | tf_op jit(solution)/shard_map/to_heads/pallas_call | solution.py:1035
  484.6 95.3 %attend_back.1 = (bf16[4096,768]{1,0:T(8,128)(2,1)}, f32[1,768]{1,0:T(1,128)}, bf16[4,400,200]{2,1,0:T(8,128)(2,1)}, bf16[8,104,200]{2,1,0:T(8,128)(2,1)}) custom-call(s32[2,25]{1,0:T(2,128)} %pad_add_fusion.values.refs_0_, bf16[4096,768]{1,0:T(8,128)(2,1)} %get-tuple-element.65.refs_1_, bf16[256,4096]{1,0:T(8,128)(2,1)} %get-tuple-element.66.refs_2_, ...), custom_call_target="tpu_custom_call" | custom-call | bytes 1048576 | tf_op jit(solution)/shard_map/attend_back/pallas_call | solution.py:1526
  581.2 1.4 copy-done.3
  582.7 1.1 copy-done.6
  585.8 27.7 %contract.1 = (bf16[1600,768]{1,0:T(8,128)(2,1)S(1)}, bf16[512,1600]{1,0:T(8,128)(2,1)S(1)}, bf16[8,96,200]{2,1,0:T(8,128)(2,1)S(1)}, bf16[8,104,200]{2,1,0:T(8,128)(2,1)S(1)}, bf16[4,400,200]{2,1,0:T(8,128)(2,1)S(1)}) custom-call(bf16[4096,1600]{1,0:T(8,128)(2,1)} %bitcast.72, bf16[4096,768]{1,0:T(8,128)(2,1)} %get-tuple-element.84.b_ref, ...), custom_call_target="tpu_custom_call" | custom-call | bytes 1048576 | tf_op jit(solution)/shard_map/contract/pallas_call | solution.py:1100
  613.5 1.5 copy-done
  615.0 1.2 copy-done.1
  618.6 75.8 %scatter_one.1 = (bf16[512,1600]{1,0:T(8,128)(2,1)}, f32[1,1600]{1,0:T(1,128)}, f32[1,1600]{1,0:T(1,128)}, bf16[4,400,768]{2,1,0:T(8,128)(2,1)}) custom-call(bf16[512,1600]{1,0:T(8,128)(2,1)} %bitcast.76, f32[1,1600]{1,0:T(1,128)} %reshape.307.refs_1_, f32[512,1600]{1,0:T(8,128)} %get-tuple-element.175.refs_2_, bf16[16,256,768]{2,1,0:T(8,128)(2,1)} %bitcast.77, ...), custom_call_target="tpu_custom_call" | custom-call | bytes 1048576 | tf_op jit(solution)/shard_map/scatter_one/pallas_call | solution.py:710
  694.4 1.2 slice.66
  698.7 1.1 add_bitcast_fusion.2
  699.8 1.2 copy.101
  701.0 2.5 reduce_sum.165
  703.5 1.2 copy.100
  704.7 19.3 %give_back.1 = (f32[40,128]{1,0:T(8,128)}, bf16[600,400]{1,0:T(8,128)(2,1)}, bf16[4,400,200]{2,1,0:T(8,128)(2,1)}) custom-call(f32[4,40,128]{2,1,0:T(8,128)} %bitcast.96, bf16[768,400]{1,0:T(8,128)(2,1)} %bitcast.88, bf16[4,400,200]{2,1,0:T(8,128)(2,1)} %bitcast.85), custom_call_target="tpu_custom_call" | custom-call | bytes 1048576 | tf_op jit(solution)/shard_map/give_back/pallas_call | solution.py:1176
  724.0 1.4 slice.82
  725.5 1.4 slice.86
  726.9 1.4 fusion.11
  728.3 2.3 copy.103
  730.6 3.9 copy.104
  735.7 1.6 copy.106
  737.4 1.3 copy.105
  739.9 2.2 reshape.308
  (146 shorter events, 26.7 us)
Async XLA Ops:
  7.2 12.6 %copy-start.19 = (bf16[1600,200]{0,1:T(8,128)(2,1)S(1)}, bf16[1600,200]{0,1:T(8,128)(2,1)}, u32[]{:S(2)}) copy-start(bf16[1600,200]{0,1:T(8,128)(2,1)} %param.31) | copy-start | bytes 1920004
  7.2 263.6 %all-gather.5.cloned.1.call-start = ((), (), s32[]{:S(2)}) async-start(), calls=%async_computation.3 | async-start | bytes 3328000 | tf_op jit(solution)/shard_map/all_gather | solution.py:1675
  61.3 3.7 copy-start.13
  153.0 5.2 copy-start.17
  158.1 2.4 copy-start.22
  158.1 3.7 copy-start.21
  158.1 4.5 copy-start.16
  158.1 113.9 %all-gather.3.cloned.1.call-start = ((), (), s32[]{:S(2)}) async-start(), calls=%async_computation.2 | async-start | bytes 3584000 | tf_op jit(solution)/shard_map/all_gather | solution.py:1671
  158.2 7.0 copy-start.25
  158.2 7.0 copy-start.27
  158.3 7.0 copy-start.24
  158.3 7.0 copy-start.28
  158.3 7.0 copy-start.29
  158.3 7.1 copy-start.26
  160.2 421.0 %reduce-scatter.5.cloned.1.call-start = ((), (), s32[]{:S(2)}) async-start(), calls=%async_computation.4 | async-start | bytes 15335424 | tf_op jit(solution)/shard_map/reduce_scatter | solution.py:1721
  422.0 276.6 %reduce-scatter.7.cloned.1.call-start = ((), (), s32[]{:S(2)}) async-start(), calls=%async_computation.5 | async-start | bytes 5990400
  422.3 2.9 copy-start.15
  426.4 1.5 copy-start.14
  484.6 96.2 %copy-start.23 = (f32[1,800]{1,0:T(1,128)S(1)}, f32[1,800]{1,0:T(1,128)}, u32[]{:S(2)}) copy-start(f32[1,800]{1,0:T(1,128)} %get-tuple-element.95) | copy-start | bytes 9604
  581.2 1.5 copy-start.3
  582.7 1.1 copy-start.6
  583.8 1.0 copy-start.9
  584.8 1.0 copy-start.12
  613.5 1.5 copy-start
  615.0 1.2 copy-start.1
  616.2 0.9 copy-start.4
  617.1 0.8 copy-start.7
  617.9 0.8 copy-start.10
  701.0 27.3 %copy-start.2 = (bf16[512,1600]{1,0:T(8,128)(2,1)S(1)}, bf16[512,1600]{1,0:T(8,128)(2,1)}, u32[]{:S(2)}) copy-start(bf16[512,1600]{1,0:T(8,128)(2,1)} %copy-done.1) | copy-start | bytes 4915204
  724.0 10.4 %copy-start.18 = (bf16[4,400,200]{2,1,0:T(8,128)(2,1)S(1)}, bf16[4,400,200]{2,1,0:T(8,128)(2,1)}, u32[]{:S(2)}) copy-start(bf16[4,400,200]{2,1,0:T(8,128)(2,1)} %get-tuple-element.100) | copy-start | bytes 1920004
  728.3 7.0 copy-start.8
  728.3 7.0 copy-start.11
  735.4 1.9 copy-start.20
  735.7 3.1 copy-start.5
Sparse Core Ops, SparseCore 0:
  158.2 53.8 all-gather.4
  214.2 57.7 all-gather.2
  422.2 107.7 reduce-scatter.4
  533.2 70.2 reduce-scatter.6

commit v9 on v8

--- a/solution.py
+++ b/solution.py
@@ -1720,7 +1720,7 @@
     )
     mixed = lax.psum_scatter(mixed, "seq", scatter_dimension=0, tiled=True)
     grad_proj = grad_proj.reshape(nf, piece, width)
-    cut = piece // 16 * 8
+    cut = piece * 3 // 32 * 8
     unused_two, norm_two_back = jax.vjp(layer_norm, middle, gain_two, shift_two)
     grad_middle_norm, grad_gain_two, grad_shift_two = norm_two_back(grad_normed_two)
     grad_middle = upstream + grad_middle_norm

time: 762 us -> 761 us (level)
  no operation moved by 1% of the time
where the time goes in v9:
time: 761 us; the launch traced here: 748 us
  Pallas kernels  635 us (83%)
  local copies, waits for them, and re-layouts  66.1 us (9%)
  other arithmetic  21.9 us (3%)
  between operations  16.2 us (2%)
    pallas_call x2, Pallas kernels, seq_gather(): pl.pallas_call(functools.partial(gather_kernel, n, h, body, len(consts),...  161 us
    pallas_call x2, Pallas kernels, seq_scatter(): pl.pallas_call(functools.partial(scatter_kernel, n, h, body, len(ins), le...  151 us
    pallas_call x1, Pallas kernels, attend_back(): pl.pallas_call(functools.partial(attend_back_kernel, width, block, rows /...  96.8 us
    pallas_call x1, Pallas kernels, attend(): pl.pallas_call(functools.partial(attend_kernel, width, block, trunk, n),...  70.1 us
    pallas_call x1, Pallas kernels, to_heads(): pl.pallas_call(functools.partial(to_heads_kernel, n, nf, wide), out_shape...  52.7 us
    pallas_call x1, Pallas kernels, exchange(): pl.pallas_call(functools.partial(exchange_kernel, n, nf, rows, count), ou...  32.1 us
    unnamed x72, local copies, waits for them, and re-layouts  29.1 us
    pallas_call x1, Pallas kernels, contract(): pl.pallas_call(functools.partial(contract_kernel, n, nf), out_shape=[jax....  26 us
  transfers between devices with their start and end apart: 4, of which 1 were waited for; matrix products, arithmetic and copies ran while one was open for 4% of the time, Pallas kernels for 46%

profile of v9, /device:TPU:3, one launch (start us, length us, event | category | flops | bytes accessed | tf_op | source)
XLA Modules:
  0.0 747.7 jit_solution(10650384945854302474)
XLA Ops:
  11.4 1.3 reshape.273.refs_5_
  12.7 1.3 reshape.274.refs_6_
  14.0 2.1 copy.89
  16.1 2.7 reshape.272
  19.7 1.2 copy.90
  21.6 32.1 %exchange.1 = (bf16[768,400]{1,0:T(8,128)(2,1)}, bf16[8,200,200]{2,1,0:T(8,128)(2,1)}, bf16[4,400,200]{2,1,0:T(8,128)(2,1)}, bf16[4,400,200]{2,1,0:T(8,128)(2,1)...) custom-call(bf16[600,400]{1,0:T(8,128)(2,1)} %bitcast.91, ...), custom_call_target="tpu_custom_call" | custom-call | bytes 1048576 | tf_op jit(solution)/shard_map/exchange/pallas_call | solution.py:905
  53.6 2.3 copy.108
  57.2 1.4 copy.93
  58.6 2.7 copy.88
  63.1 1.9 fusion.5.refs_0_
  65.0 88.0 %gather_one.1 = (bf16[16,256,1600]{2,1,0:T(8,128)(2,1)}, bf16[8,200,1600]{2,1,0:T(8,128)(2,1)}, bf16[4,400,768]{2,1,0:T(8,128)(2,1)}) custom-call(bf16[512,1600]{1,0:T(8,128)(2,1)} %fusion.5.refs_0_, bf16[200,1600]{1,0:T(8,128)(2,1)} %bitcast.90, bf16[400,768]{1,0:T(8,128)(2,1)} %select_bitcast_fusion.refs_2_), custom_call_target="tpu_custom_call" | custom-call | bytes 1048576 | tf_op jit(solution)/shard_map/gather_one/pallas_call | solution.py:387
  153.0 1.3 slice.77
  154.9 1.2 add_bitcast_fusion
  156.3 1.8 add.135
  158.7 1.5 add.130
  162.6 2.6 copy.94
  166.0 70.1 %attend.1 = (bf16[4096,768]{1,0:T(8,128)(2,1)}, bf16[4096,256]{1,0:T(8,128)(2,1)}, f32[4096,256]{1,0:T(8,128)}, f32[4096,256]{1,0:T(8,128)}, bf16[256,4096]{1,0:T(8,128)(2,1)}, /*index=5*/bf16[8,512,1600]{2,1,0:T(8,128)(2,1)}) custom-call(s32[2,25]{1,0:T(2,128)} %pad_add_fusion.values.refs_0_, bf16[8,512,1600]{2,1,0:T(8,128)(2,1)} %bitcast.71, ...), custom_call_target="tpu_custom_call" | custom-call | bytes 1048576 | tf_op jit(solution)/shard_map/attend/pallas_call | solution.py:1365
  236.1 25.3 %to_tokens.1 = bf16[512,2048]{1,0:T(8,128)(2,1)} custom-call(bf16[8,512,256]{2,1,0:T(8,128)(2,1)} %bitcast.93), custom_call_target="tpu_custom_call" | custom-call | bytes 1048576 | tf_op jit(solution)/shard_map/to_tokens/pallas_call | solution.py:954
  261.3 7.1 fusion.12
  269.0 1.8 add_convert_fusion.refs_0_
  270.8 1.3 all-gather.3.cloned.1.call-done.refs_1_.refs_4_
  272.0 72.7 %gather_two.1 = (bf16[16,256,1600]{2,1,0:T(8,128)(2,1)}, bf16[16,256,800]{2,1,0:T(8,128)(2,1)}, bf16[16,256,800]{2,1,0:T(8,128)(2,1)}, bf16[16,256,1600]{2,1,0:T(8,128)(2,1)}) custom-call(bf16[512,1600]{1,0:T(8,128)(2,1)} %add_convert_fusion.refs_0_, bf16[1600,800]{1,0:T(8,128)(2,1)} %all-gather.3.cloned.1.call-done.refs_1_.refs_4_, ...), custom_call_target="tpu_custom_call" | custom-call | bytes 1048576 | tf_op jit(solution)/shard_map/gather_two/pallas_call | solution.py:387
  344.8 77.2 %scatter_two.1 = (f32[512,1600]{1,0:T(8,128)}, bf16[16,256,800]{2,1,0:T(8,128)(2,1)}, bf16[800,1600]{1,0:T(8,128)(2,1)}, f32[1,1600]{1,0:T(1,128)}, bf16[4096,1600]{1,0:T(8,128)(2,1)}) custom-call(bf16[4096,1600]{1,0:T(8,128)(2,1)} %bitcast.75, bf16[16,256,1600]{2,1,0:T(8,128)(2,1)} %bitcast.73, ...), custom_call_target="tpu_custom_call", output_to_operand_aliasing={{4}: (0, {})} | custom-call | bytes 1048576 | tf_op jit(solution)/shard_map/scatter_two/pallas_call | solution.py:710
  422.3 2.9 slice.62.t_ref
  425.2 1.2 multiply_reduce_fusion
  427.9 3.0 convert_reduce_fusion.2
  430.9 52.7 %to_heads.1 = (bf16[8,512,256]{2,1,0:T(8,128)(2,1)}, bf16[1600,800]{1,0:T(8,128)(2,1)}, f32[1,800]{1,0:T(1,128)}, bf16[8,144,200]{2,1,0:T(8,128)(2,1)}, bf16[1600,1600]{1,0:T(8,128)(2,1)}) custom-call(bf16[512,1600]{1,0:T(8,128)(2,1)} %get-tuple-element.174.x_ref, bf16[1600,1600]{1,0:T(8,128)(2,1)} %bitcast.84, bf16[512,1600]{1,0:T(8,128)(2,1)} %slice.62.t_ref, ...), custom_call_target="tpu_custom_call" | custom-call | bytes 1048576 | tf_op jit(solution)/shard_map/to_heads/pallas_call | solution.py:1035
  484.7 96.8 %attend_back.1 = (bf16[4096,768]{1,0:T(8,128)(2,1)}, f32[1,768]{1,0:T(1,128)}, bf16[4,400,200]{2,1,0:T(8,128)(2,1)}, bf16[8,56,200]{2,1,0:T(8,128)(2,1)}) custom-call(s32[2,25]{1,0:T(2,128)} %pad_add_fusion.values.refs_0_, bf16[4096,768]{1,0:T(8,128)(2,1)} %get-tuple-element.65.refs_1_, bf16[256,4096]{1,0:T(8,128)(2,1)} %get-tuple-element.66.refs_2_, ...), custom_call_target="tpu_custom_call" | custom-call | bytes 1048576 | tf_op jit(solution)/shard_map/attend_back/pallas_call | solution.py:1526
  582.8 1.4 copy-done.3
  584.3 1.1 copy-done.6
  587.5 26.0 %contract.1 = (bf16[1600,768]{1,0:T(8,128)(2,1)S(1)}, bf16[512,1600]{1,0:T(8,128)(2,1)S(1)}, bf16[8,144,200]{2,1,0:T(8,128)(2,1)S(1)}, bf16[8,56,200]{2,1,0:T(8,128)(2,1)S(1)}, bf16[4,400,200]{2,1,0:T(8,128)(2,1)S(1)}) custom-call(bf16[4096,1600]{1,0:T(8,128)(2,1)} %bitcast.72, bf16[4096,768]{1,0:T(8,128)(2,1)} %get-tuple-element.84.b_ref, ...), custom_call_target="tpu_custom_call" | custom-call | bytes 1048576 | tf_op jit(solution)/shard_map/contract/pallas_call | solution.py:1100
  613.5 1.5 copy-done
  615.0 1.2 copy-done.1
  618.6 74.1 %scatter_one.1 = (bf16[512,1600]{1,0:T(8,128)(2,1)}, f32[1,1600]{1,0:T(1,128)}, f32[1,1600]{1,0:T(1,128)}, bf16[4,400,768]{2,1,0:T(8,128)(2,1)}) custom-call(bf16[512,1600]{1,0:T(8,128)(2,1)} %bitcast.76, f32[1,1600]{1,0:T(1,128)} %reshape.307.refs_1_, f32[512,1600]{1,0:T(8,128)} %get-tuple-element.175.refs_2_, bf16[16,256,768]{2,1,0:T(8,128)(2,1)} %bitcast.77, ...), custom_call_target="tpu_custom_call" | custom-call | bytes 1048576 | tf_op jit(solution)/shard_map/scatter_one/pallas_call | solution.py:710
  692.7 1.2 slice.66
  696.9 1.1 add_bitcast_fusion.2
  698.1 1.2 copy.101
  699.3 2.5 reduce_sum.165
  701.8 1.2 copy.100
  702.9 19.6 %give_back.1 = (f32[40,128]{1,0:T(8,128)}, bf16[600,400]{1,0:T(8,128)(2,1)}, bf16[4,400,200]{2,1,0:T(8,128)(2,1)}) custom-call(f32[4,40,128]{2,1,0:T(8,128)} %bitcast.96, bf16[768,400]{1,0:T(8,128)(2,1)} %bitcast.88, bf16[4,400,200]{2,1,0:T(8,128)(2,1)} %bitcast.85), custom_call_target="tpu_custom_call" | custom-call | bytes 1048576 | tf_op jit(solution)/shard_map/give_back/pallas_call | solution.py:1176
  722.6 1.4 slice.82
  724.0 1.4 slice.86
  725.4 1.4 fusion.11
  726.9 2.3 copy.103
  729.1 3.9 copy.104
  734.2 1.6 copy.106
  735.9 1.3 copy.105
  738.5 2.2 reshape.308
  (146 shorter events, 26.8 us)
Async XLA Ops:
  7.2 12.6 %copy-start.19 = (bf16[1600,200]{0,1:T(8,128)(2,1)S(1)}, bf16[1600,200]{0,1:T(8,128)(2,1)}, u32[]{:S(2)}) copy-start(bf16[1600,200]{0,1:T(8,128)(2,1)} %param.31) | copy-start | bytes 1920004
  7.2 263.6 %all-gather.5.cloned.1.call-start = ((), (), s32[]{:S(2)}) async-start(), calls=%async_computation.3 | async-start | bytes 3328000 | tf_op jit(solution)/shard_map/all_gather | solution.py:1675
  61.3 3.7 copy-start.13
  153.0 5.2 copy-start.17
  158.1 2.4 copy-start.22
  158.1 3.7 copy-start.21
  158.1 4.5 copy-start.16
  158.1 113.9 %all-gather.3.cloned.1.call-start = ((), (), s32[]{:S(2)}) async-start(), calls=%async_computation.2 | async-start | bytes 3584000 | tf_op jit(solution)/shard_map/all_gather | solution.py:1671
  158.2 7.0 copy-start.25
  158.2 7.0 copy-start.27
  158.3 7.0 copy-start.24
  158.3 7.0 copy-start.28
  158.3 7.0 copy-start.29
  158.3 7.1 copy-start.26
  160.2 422.6 %reduce-scatter.5.cloned.1.call-start = ((), (), s32[]{:S(2)}) async-start(), calls=%async_computation.4 | async-start | bytes 15335424 | tf_op jit(solution)/shard_map/reduce_scatter | solution.py:1721
  422.0 274.9 %reduce-scatter.7.cloned.1.call-start = ((), (), s32[]{:S(2)}) async-start(), calls=%async_computation.5 | async-start | bytes 5990400
  422.3 2.9 copy-start.15
  426.4 1.5 copy-start.14
  484.6 97.7 %copy-start.23 = (f32[1,800]{1,0:T(1,128)S(1)}, f32[1,800]{1,0:T(1,128)}, u32[]{:S(2)}) copy-start(f32[1,800]{1,0:T(1,128)} %get-tuple-element.95) | copy-start | bytes 9604
  582.8 1.5 copy-start.3
  584.3 1.1 copy-start.6
  585.4 1.1 copy-start.9
  586.5 1.0 copy-start.12
  613.5 1.5 copy-start
  615.0 1.2 copy-start.1
  616.2 0.9 copy-start.4
  617.1 0.8 copy-start.7
  617.9 0.7 copy-start.10
  699.3 27.6 %copy-start.2 = (bf16[512,1600]{1,0:T(8,128)(2,1)S(1)}, bf16[512,1600]{1,0:T(8,128)(2,1)}, u32[]{:S(2)}) copy-start(bf16[512,1600]{1,0:T(8,128)(2,1)} %copy-done.1) | copy-start | bytes 4915204
  722.6 10.4 %copy-start.18 = (bf16[4,400,200]{2,1,0:T(8,128)(2,1)S(1)}, bf16[4,400,200]{2,1,0:T(8,128)(2,1)}, u32[]{:S(2)}) copy-start(bf16[4,400,200]{2,1,0:T(8,128)(2,1)} %get-tuple-element.100) | copy-start | bytes 1920004
  726.8 7.0 copy-start.8
  726.8 7.0 copy-start.11
  733.9 1.9 copy-start.20
  734.2 3.1 copy-start.5
Sparse Core Ops, SparseCore 0:
  158.2 53.8 all-gather.4
  214.2 57.7 all-gather.2
  422.2 107.6 reduce-scatter.4
  533.1 66.4 reduce-scatter.6
